TPU v7x, 32 devices: a whole 2x2x4 slice. The times are simulated.
32 devices in a mesh: row: 4 (over z), col: 8 (over y, x, core).
Axes of the slice: x: 2, y: 2, z: 4, core: 2. Of those that a mesh axis runs over, the one named last changes fastest.
Arguments:
- kernel: bfloat16 [2, 2, 2048, 1024], P(None, None, 'col', 'row'), may hold values from -0.09375 to 0.09375
- probes: bfloat16 [256, 2, 2, 2048], P(None, None, None, 'col'), may hold values from -6 to 6
- noise_var: float32 [2, 2048], P(None, 'col'), may hold values from 0.05 to 0.5
- prior_diag: float32 [1024], P('row'), may hold values from 2.2 to 4
Outputs:
- hess_probes: float32 [256, 2, 2, 2048], P('row', None, None, 'col')
All inputs are finite; a program needn't handle non-finite values.
Results may differ from a plain program's by a relative error of at most 0.015.
Values may be sent and summed in bfloat16 or wider, within the bound.
No kernel may reach another device: no remote copies, remote signals or barrier semaphores. Data moves between devices by JAX's collectives and lax.ppermute only.
A program may use at most 64 MiB of HBM per device.

v0:
```python
import jax
import jax.numpy as jnp
from jax import lax
from jax.sharding import PartitionSpec as P


def extended(block, sides, width):
    for axis, dim in sides:
        count = lax.axis_size(axis)
        forward = [(i, i + 1) for i in range(count - 1)]
        backward = [(target, source) for source, target in forward]
        low = lax.ppermute(
            lax.slice_in_dim(block, block.shape[dim] - width, None, axis=dim), axis, forward
        )
        high = lax.ppermute(lax.slice_in_dim(block, 0, width, axis=dim), axis, backward)
        block = jnp.concatenate([low, block, high], axis=dim)
    return block


def sweep(field, coef, below, above):
    return coef * field - below - above


def apply_prior(block, coef):
    shape = block.shape
    par_count = shape[-1]
    flat = block.reshape(-1, par_count)
    stacked = jnp.concatenate([flat, coef[None, :]], axis=0)
    wide = extended(stacked.astype(jnp.bfloat16), (("row", 1),), 2).astype(stacked.dtype)
    values = wide[:-1]
    coefs = wide[-1]
    first = sweep(values[:, 1:-1], coefs[1:-1], values[:, :-2], values[:, 2:])
    places = lax.axis_index("row") * par_count + jnp.arange(par_count + 2, dtype=jnp.int32) - 1
    valid = (places >= 0) & (places < par_count * lax.axis_size("row"))
    first = jnp.where(valid[None, :], first, 0.0)
    result = sweep(first[:, 1:-1], coefs[2:-2], first[:, :-2], first[:, 2:])
    return result.reshape(shape)


def shards(kernel, probes, noise_var, prior_diag):
    freq_count = kernel.shape[0]
    row_count = kernel.shape[2]
    par_count = kernel.shape[3]
    col_count = probes.shape[0]
    stacks = [kernel[freq_no].reshape(2 * row_count, par_count) for freq_no in range(freq_count)]
    adjoint = []
    for freq_no in range(freq_count):
        real_part = probes[:, freq_no, 0, :]
        imag_part = probes[:, freq_no, 1, :]
        upper = jnp.concatenate([real_part, imag_part], axis=1)
        lower = jnp.concatenate([imag_part, -real_part], axis=1)
        product = jnp.dot(
            jnp.concatenate([upper, lower], axis=0),
            stacks[freq_no],
            preferred_element_type=jnp.float32,
        )
        adjoint.append(product.reshape(2, col_count, par_count))
    adjoint = jnp.stack(adjoint)
    summed = lax.psum(adjoint, "col")
    field = apply_prior(summed, prior_diag).astype(jnp.bfloat16)
    rows_own = col_count // lax.axis_size("row")
    count = lax.axis_size("row") * rows_own
    parts = []
    for freq_no in range(freq_count):
        real_rows = field[freq_no, 0]
        imag_rows = field[freq_no, 1]
        both = jnp.concatenate([real_rows, imag_rows], axis=0)
        prod = lax.dot_general(
            both, stacks[freq_no], (((1,), (1,)), ((), ())), preferred_element_type=jnp.float32
        )
        real_out = prod[:count, :row_count] - prod[count:, row_count:]
        imag_out = prod[count:, :row_count] + prod[:count, row_count:]
        parts.append(jnp.stack([real_out, imag_out], axis=1))
    total = lax.psum_scatter(
        jnp.stack(parts, axis=1).astype(jnp.bfloat16), "row", scatter_dimension=0, tiled=True
    ).astype(jnp.float32)
    first_row = lax.axis_index("row") * rows_own
    own_probes = lax.dynamic_slice_in_dim(probes, first_row, rows_own, 0).astype(jnp.float32)
    return total + noise_var[None, :, None, :] * own_probes


def solution(mesh):
    in_specs = (P(None, None, "col", "row"), P(None, None, None, "col"), P(None, "col"), P("row"))
    out_specs = P("row", None, None, "col")
    return jax.shard_map(shards, mesh=mesh, in_specs=in_specs, out_specs=out_specs, check_vma=False)
```

profile of v0, /device:TPU:0, one launch (start us, length us, event | category | flops | bytes accessed | tf_op | source)
XLA Modules:
  0.0 108.3 jit_solution(1654378138064933633)
XLA Ops:
  6.5 0.0 copy-start
  6.5 0.0 reduce-scatter.2.cloned.1.call-start
  6.5 2.1 %fusion.27 = (bf16[256,1,1,256]{3,2,1,0:T(2,128)(2,1)S(1)}, bf16[256,1,1,256]{3,2,1,0:T(2,128)(2,1)S(1)}, bf16[256,1,1,256]{3,2,1,0:T(2,128)(2,1)S(1)}, bf16[256,1,1,256]{3,2,1,0:T(2,128)(2,1)S(1)}) fusion(bf16[256,2,2,256]{3,2,1,0:T(2,128)(2,1)} %param.5), kind=kLoop, calls=%fused_computation.62 | loop fusion | bytes 1048576 | tf_op jit(solution)/shard_map/slice | solution.py:49
  8.7 0.0 copy-done
  8.9 0.3 convolution_bitcast_fusion.1
  9.2 0.3 convolution_bitcast_fusion
  9.5 0.0 copy-start.2
  9.6 0.1 pad_maximum_fusion
  9.6 52.8 %all-reduce.1 = bf16[2,2,256,256]{3,2,1,0:T(8,128)(2,1)S(1)} all-reduce(f32[2,2,256,256]{3,2,1,0:T(8,128)S(1)} %pad_maximum_fusion), channel_id=1, replica_groups=mesh['row'=4,'col'=8] {'col'}, use_global_device_ids=true, to_apply=%region_0.0 | all-reduce | flops 262144 | bytes 1572864 | tf_op jit(solution)/shard_map/psum | solution.py:59
  62.5 0.0 copy-done.2
  62.5 0.1 fusion.2
  62.6 3.5 %collective-permute-start = (bf16[1025,2]{1,0:T(8,128)(2,1)S(1)}, bf16[1025,2]{1,0:T(8,128)(2,1)S(1)}, u32[]{:S(2)}, u32[]{:S(2)}) collective-permute-start(bf16[1025,2]{1,0:T(8,128)(2,1)S(1)} %get-tuple-element.13), channel_id=1, source_target_pairs={{0,8},{8,16},{16,24},{1,9},{9,17},{17,25},{2,10},{10,18},{18,26},{... | collective-permute-start | bytes 12308 | tf_op jit(solution)/shard_map/ppermute | solution.py:12
  66.1 1.3 %collective-permute-start.1 = (bf16[1025,2]{1,0:T(8,128)(2,1)S(1)}, bf16[1025,2]{1,0:T(8,128)(2,1)S(1)}, u32[]{:S(2)}, u32[]{:S(2)}) collective-permute-start(bf16[1025,2]{1,0:T(8,128)(2,1)S(1)} %get-tuple-element.14), channel_id=1, source_target_pairs={{8,0},{16,8},{24,16},{9,1},{17,9},{25,17},{10,2},{18,10},{26,18},{... | collective-permute-start | bytes 12308 | tf_op jit(solution)/shard_map/ppermute | solution.py:15
  67.5 2.6 %collective-permute-done = bf16[1025,2]{1,0:T(8,128)(2,1)S(1)} collective-permute-done((bf16[1025,2]{1,0:T(8,128)(2,1)S(1)}, bf16[1025,2]{1,0:T(8,128)(2,1)S(1)}, u32[]{:S(2)}, u32[]{:S(2)}) %collective-permute-start) | collective-permute-done | bytes 4132 | tf_op jit(solution)/shard_map/ppermute | solution.py:12
  70.0 4.4 %collective-permute-done.1 = bf16[1025,2]{1,0:T(8,128)(2,1)S(1)} collective-permute-done((bf16[1025,2]{1,0:T(8,128)(2,1)S(1)}, bf16[1025,2]{1,0:T(8,128)(2,1)S(1)}, u32[]{:S(2)}, u32[]{:S(2)}) %collective-permute-start.1) | collective-permute-done | bytes 4132 | tf_op jit(solution)/shard_map/ppermute | solution.py:15
  74.4 0.1 convert_reduce_fusion
  74.5 0.4 maximum_convert_fusion
  74.9 0.9 fusion
  75.8 0.1 maximum_convert_fusion.1
  75.9 0.6 fusion.1
  76.6 0.3 fusion.7
  76.9 0.1 fusion.15
  77.0 0.3 fusion.11
  77.3 0.1 fusion.17
  77.4 0.0 copy-start.1
  77.4 0.8 pad_maximum_fusion.1
  78.3 0.0 reduce-scatter.2.cloned.1.call-update
  78.3 1.0 constant_dynamic-slice_fusion
  79.3 20.3 %reduce-scatter.2.cloned.1.call-done = bf16[64,2,2,256]{3,0,2,1:T(8,128)(2,1)} async-done(((bf16[256,2,2,256]{3,0,2,1:T(8,128)(2,1)}), bf16[64,2,2,256]{3,0,2,1:T(8,128)(2,1)}) %reduce-scatter.2.cloned.1.call-update) | async-done | bytes 131088 | tf_op jit(solution)/shard_map/reduce_scatter | solution.py:74
  99.6 0.0 copy-done.1
  99.6 0.9 multiply_add_fusion
  100.5 0.9 copy.14
  (11 shorter events, 0.3 us)
Async XLA Ops:
  6.5 2.2 %copy-start = (bf16[2,2,256,256]{3,2,1,0:T(8,128)(2,1)S(1)}, bf16[2,2,256,256]{3,2,1,0:T(8,128)(2,1)}, u32[]{:S(2)}) copy-start(bf16[2,2,256,256]{3,2,1,0:T(8,128)(2,1)} %param.4) | copy-start | bytes 1572868
  6.5 93.0 %reduce-scatter.2.cloned.1.call-start = ((), (), s32[]{:S(2)}) async-start(), calls=%async_computation.1 | async-start | bytes 655360 | tf_op jit(solution)/shard_map/reduce_scatter | solution.py:74
  9.5 52.9 %copy-start.2 = (f32[256]{0:T(256)S(1)}, f32[256]{0:T(256)}, u32[]{:S(2)}) copy-start(f32[256]{0:T(256)} %param.7) | copy-start | bytes 3076
  62.6 7.4 %collective-permute-start = (bf16[1025,2]{1,0:T(8,128)(2,1)S(1)}, bf16[1025,2]{1,0:T(8,128)(2,1)S(1)}, u32[]{:S(2)}, u32[]{:S(2)}) collective-permute-start(bf16[1025,2]{1,0:T(8,128)(2,1)S(1)} %get-tuple-element.13), channel_id=1, source_target_pairs={{0,8},{8,16},{16,24},{1,9},{9,17},{17,25},{2,10},{10,18},{18,26},{... | collective-permute-start | bytes 12308 | tf_op jit(solution)/shard_map/ppermute | solution.py:12
  66.1 8.3 %collective-permute-start.1 = (bf16[1025,2]{1,0:T(8,128)(2,1)S(1)}, bf16[1025,2]{1,0:T(8,128)(2,1)S(1)}, u32[]{:S(2)}, u32[]{:S(2)}) collective-permute-start(bf16[1025,2]{1,0:T(8,128)(2,1)S(1)} %get-tuple-element.14), channel_id=1, source_target_pairs={{8,0},{16,8},{24,16},{9,1},{17,9},{25,17},{10,2},{18,10},{26,18},{... | collective-permute-start | bytes 12308 | tf_op jit(solution)/shard_map/ppermute | solution.py:15
  77.4 22.2 %copy-start.1 = (f32[2,256]{1,0:T(2,128)S(1)}, f32[2,256]{1,0:T(2,128)}, u32[]{:S(2)}) copy-start(f32[2,256]{1,0:T(2,128)} %param.6) | copy-start | bytes 6148
Sparse Core Ops, SparseCore 0:
  78.4 21.1 reduce-scatter.1
where the time goes:
time: 108 us
  blocking collectives  52.8 us (49%)
  waiting for transfers between devices  27.3 us (25%)
  between operations  13.6 us (13%)
  starting transfers between devices  4.79 us (4%)
  other arithmetic  4.36 us (4%)
  local copies, waits for them, and re-layouts  4.19 us (4%)
  matrix products  1.25 us (1%)
    psum x1, blocking collectives, shards(): summed = lax.psum(adjoint, 'col')  52.8 us
    reduce_scatter x1, waiting for transfers between devices, shards(): lax.psum_scatter(jnp.stack(parts, axis=1).astype(jnp.bfloat16), 'row', sc...  20.3 us
    ppermute x1, waiting for transfers between devices, extended(): lax.ppermute(lax.slice_in_dim(block, 0, width, axis=dim), axis, backward)  4.41 us
    ppermute x1, starting transfers between devices, extended(): lax.ppermute(lax.slice_in_dim(block, block.shape[dim] - width, None, axis...  3.5 us
    ppermute x1, waiting for transfers between devices, extended(): lax.ppermute(lax.slice_in_dim(block, block.shape[dim] - width, None, axis...  2.56 us
  transfers between devices with their start and end apart: 3, of which 3 were waited for; matrix products, arithmetic and copies ran while one was open for 1% of the time, Pallas kernels for 0%

commit v1 on v0

v1 whole, which is shorter than its diff:
```python
import functools

import jax
import jax.numpy as jnp
from jax import lax
from jax.experimental import pallas as pl
from jax.experimental.pallas import tpu as pltpu
from jax.sharding import PartitionSpec as P

BF = jnp.bfloat16
F32 = jnp.float32
LANES = 128
VMEM = pl.BlockSpec(memory_space=pltpu.VMEM)


def call(body, name, ins, outs, scratch=()):
    return pl.pallas_call(
        body,
        name=name,
        in_specs=[VMEM] * len(ins),
        out_specs=[VMEM] * len(outs),
        out_shape=[jax.ShapeDtypeStruct(*o) for o in outs],
        scratch_shapes=list(scratch),
    )(*ins)


def parity():
    return lax.rem(lax.axis_index("col"), 2)


def dot_nt(left, right):
    return lax.dot_general(left, right, (((1,), (1,)), ((), ())), preferred_element_type=F32)


def dot_nn(left, right):
    return jnp.dot(left, right, preferred_element_type=F32)


def pair_perm(axis, step):
    return [(i, i ^ step) for i in range(lax.axis_size(axis))]


def adjoint_body(swap, x_ref, k_ref, o_ref, u_ref):
    rows = x_ref.shape[0] // 4
    width = k_ref.shape[3]
    freq = parity()
    if swap:
        freq = 1 - freq
    x = x_ref[...]
    tiles = width // LANES
    for part in range(2):
        y = dot_nn(x, k_ref[freq, part])
        for t in range(tiles):
            u_ref[part * tiles + t] = y[:, t * LANES:(t + 1) * LANES]
    real = pl.ds(2 * freq, rows, stride=4)
    imag = pl.ds(2 * freq + 1, rows, stride=4)
    for t in range(tiles):
        at = slice(t * LANES, (t + 1) * LANES)
        o_ref[:rows, at] = (u_ref[t, real, :] + u_ref[tiles + t, imag, :]).astype(o_ref.dtype)
        o_ref[rows:, at] = (u_ref[t, imag, :] - u_ref[tiles + t, real, :]).astype(o_ref.dtype)


def edges_body(k_ref, d_ref, low_ref, high_ref):
    freqs, _, rows, width = k_ref.shape
    at = lax.broadcasted_iota(jnp.int32, (8, width), 0)
    place = lax.broadcasted_iota(jnp.int32, (8, width), 1)
    first = jnp.where((at < 2) & (place == at), 1.0, 0.0).astype(BF)
    last = jnp.where((at < 2) & (place == at + width - 2), 1.0, 0.0).astype(BF)
    for f in range(freqs):
        for c in range(2):
            lo = (f * 2 + c) * rows
            low_ref[:, lo:lo + rows] = dot_nt(last, k_ref[f, c]).astype(BF)
            high_ref[:, lo:lo + rows] = dot_nt(first, k_ref[f, c]).astype(BF)
    coef = d_ref[...]
    spot = lax.broadcasted_iota(jnp.int32, coef.shape, 1)
    for ref, where in ((low_ref, width - 1), (high_ref, 0)):
        left = jnp.sum(jnp.where(spot == where, coef, 0.0), axis=1, keepdims=True)
        for row in range(2, 5):
            piece = left.astype(BF)
            ref[row:row + 1, :] = jnp.broadcast_to(piece, (1, ref.shape[1]))
            left = left - piece.astype(F32)


def operator_body(k_ref, d_ref, low_ref, high_ref, o_ref):
    freqs, _, rows, width = k_ref.shape
    at = lax.axis_index("row")
    coef = d_ref[...]
    row_at = lax.broadcasted_iota(jnp.int32, (width, width), 0)
    col_at = lax.broadcasted_iota(jnp.int32, (width, width), 1)
    wide = jnp.broadcast_to(coef, (width, width))
    tall = jnp.sum(jnp.where(row_at == col_at, wide, 0.0), axis=1, keepdims=True)
    gap = jnp.abs(row_at - col_at)
    edge = ((row_at == 0) & (at == 0)) | ((row_at == width - 1) & (at == lax.axis_size("row") - 1))
    centre = wide * wide + jnp.where(edge, 1.0, 2.0)
    stencil = jnp.where(gap == 0, centre, jnp.where(gap == 1, -(wide + tall), jnp.where(gap == 2, 1.0, 0.0)))
    upper = stencil.astype(BF)
    lower = (stencil - upper.astype(F32)).astype(BF)
    low = low_ref[...].astype(F32)
    high = high_ref[...].astype(F32)
    low_coef = low[2:3, :rows] + low[3:4, :rows] + low[4:5, :rows] + coef[:, :1]
    high_coef = high[2:3, :rows] + high[3:4, :rows] + high[4:5, :rows] + coef[:, width - 1:]
    for f in range(freqs):
        for c in range(2):
            block = k_ref[f, c]
            value = dot_nt(upper, block) + dot_nt(lower, block)
            lo = (f * 2 + c) * rows
            before = low[0:2, lo:lo + rows]
            after = high[0:2, lo:lo + rows]
            head = jnp.concatenate(
                [before[0:1] - low_coef * before[1:2], before[1:2]], axis=0
            )
            tail = jnp.concatenate(
                [after[0:1], after[1:2] - high_coef * after[0:1]], axis=0
            )
            value = value + jnp.concatenate(
                [head, jnp.zeros((width - 4, rows), F32), tail], axis=0
            )
            o_ref[f, c] = value.astype(BF)


def split_body(own_ref, got_ref, keep_ref, *send_refs):
    size = keep_ref.shape[0]
    me = lax.div(lax.axis_index("col"), 2)

    def piece(chip):
        rows = pl.ds(pl.multiple_of(chip * size, size), size)
        return own_ref[rows, :] + got_ref[rows, :].astype(F32)

    keep_ref[...] = piece(me)
    for step, ref in enumerate(send_refs):
        ref[...] = piece(jnp.bitwise_xor(me, step + 1)).astype(BF)


def sum_body(keep_ref, *refs):
    total = keep_ref[...]
    for ref in refs[:-1]:
        total = total + ref[...].astype(F32)
    refs[-1][...] = total.astype(BF)


def join_body(mine_ref, *refs):
    size = mine_ref.shape[0]
    me = lax.div(lax.axis_index("col"), 2)
    out = refs[-1]
    for step, ref in enumerate((mine_ref,) + refs[:-1]):
        chip = jnp.bitwise_xor(me, step)
        out[pl.ds(pl.multiple_of(chip * size, size), size), :] = ref[...]


def predict_body(swap, a_ref, k_ref, keep_ref, *refs):
    freq = parity()
    if swap:
        freq = 1 - freq
    probes = a_ref.shape[0] // 2
    size = keep_ref.shape[0] // 2
    me = lax.axis_index("row")
    k_real = k_ref[freq, 0]
    k_imag = k_ref[freq, 1]
    for step in range(len(refs), -1, -1):
        block = jnp.bitwise_xor(me, step)
        start = pl.multiple_of(block * size, size)
        real = a_ref[pl.ds(start, size), :]
        imag = a_ref[pl.ds(pl.multiple_of(probes + start, size), size), :]
        both = jnp.concatenate([real, imag], axis=0)
        by_real = dot_nn(both, k_real)
        by_imag = dot_nn(both, k_imag)
        ref = keep_ref if step == 0 else refs[step - 1]
        ref[:size] = (by_real[:size] - by_imag[size:]).astype(ref.dtype)
        ref[size:] = (by_real[size:] + by_imag[:size]).astype(ref.dtype)


def final_body(peers, x_ref, noise_ref, *refs):
    out_ref, s_ref = refs[-2:]
    rows = out_ref.shape[0]
    size = rows // 4
    me = lax.axis_index("row")
    freq = parity()
    for which in range(2):
        group = refs[which * (peers + 1):(which + 1) * (peers + 1)]
        total = group[0][...]
        for ref in group[1:]:
            total = total + ref[...].astype(F32)
        f = freq if which == 0 else 1 - freq
        for t in range(s_ref.shape[0]):
            at = slice(t * LANES, (t + 1) * LANES)
            s_ref[t, pl.ds(2 * f, size, stride=4), :] = total[:size, at]
            s_ref[t, pl.ds(2 * f + 1, size, stride=4), :] = total[size:, at]
    x = x_ref[pl.ds(pl.multiple_of(me * rows, rows), rows), :].astype(F32)
    kind = lax.rem(lax.broadcasted_iota(jnp.int32, x.shape, 0), 4)
    noise = jnp.where(kind < 2, noise_ref[0:1, :], noise_ref[1:2, :])
    extra = noise * x
    for t in range(s_ref.shape[0]):
        at = slice(t * LANES, (t + 1) * LANES)
        out_ref[:, at] = s_ref[t] + extra[:, at]


def all_sum(x, kernel):
    rows = x.shape[0] // 2
    width = kernel.shape[3]
    count = lax.axis_size("col")
    scratch = (pltpu.VMEM((2 * width // LANES, x.shape[0], LANES), F32),)
    other = call(functools.partial(adjoint_body, True), "adjoint_other", (x, kernel), [((rows, width), BF)], scratch)[0]
    got = lax.ppermute(other, "col", pair_perm("col", 1))
    own = call(functools.partial(adjoint_body, False), "adjoint_own", (x, kernel), [((rows, width), F32)], scratch)[0]
    chips = count // 2
    if chips > 4:
        part = own + got.astype(F32)
        both = jnp.where(parity() == 0, jnp.stack([part, 0 * part]), jnp.stack([0 * part, part]))
        both = lax.psum(both, "col").astype(BF)
        mine = lax.dynamic_index_in_dim(both, parity(), 0, keepdims=False)
        return mine, lax.dynamic_index_in_dim(both, 1 - parity(), 0, keepdims=False)
    size = rows // chips
    keep, *sends = call(
        split_body, "split", (own, got), [((size, width), F32)] + [((size, width), BF)] * (chips - 1)
    )
    got = [lax.ppermute(v, "col", pair_perm("col", 2 * (d + 1))) for d, v in enumerate(sends)]
    mine = call(sum_body, "sum", (keep, *got), [((size, width), BF)])[0]
    got = [lax.ppermute(mine, "col", pair_perm("col", 2 * (d + 1))) for d in range(chips - 1)]
    mine = call(join_body, "join", (mine, *got), [((rows, width), BF)])[0]
    return mine, lax.ppermute(mine, "col", pair_perm("col", 1))


def shards(kernel, probes, noise_var, prior_diag):
    rows_own = kernel.shape[2]
    width = kernel.shape[3]
    count = probes.shape[0]
    blocks = lax.axis_size("row")
    x = probes.reshape(-1, rows_own)
    coef = prior_diag[None, :]
    low, high = call(edges_body, "edges", (kernel, coef), [((8, 4 * rows_own), BF)] * 2)
    low = lax.ppermute(low, "row", [(i, i + 1) for i in range(blocks - 1)])
    high = lax.ppermute(high, "row", [(i + 1, i) for i in range(blocks - 1)])
    mine, other = all_sum(x, kernel)
    operator = call(operator_body, "operator", (kernel, coef, low, high), [((2, 2, width, rows_own), BF)])[0]
    size = count // blocks
    groups = []
    for swap, field in ((False, mine), (True, other)):
        keep, *sends = call(
            functools.partial(predict_body, swap),
            "predict_other" if swap else "predict_own",
            (field, operator),
            [((2 * size, rows_own), F32)] + [((2 * size, rows_own), BF)] * (blocks - 1),
        )
        groups.append(keep)
        groups += [lax.ppermute(v, "row", pair_perm("row", d + 1)) for d, v in enumerate(sends)]
    out = call(
        functools.partial(final_body, blocks - 1),
        "final",
        (x, noise_var, *groups),
        [((4 * size, rows_own), F32)],
        (pltpu.VMEM((rows_own // LANES, 4 * size, LANES), F32),),
    )[0]
    return out.reshape(size, 2, 2, rows_own)


def solution(mesh):
    in_specs = (P(None, None, "col", "row"), P(None, None, None, "col"), P(None, "col"), P("row"))
    out_specs = P("row", None, None, "col")
    return jax.shard_map(shards, mesh=mesh, in_specs=in_specs, out_specs=out_specs, check_vma=False)
```

time: 108 us -> 68.1 us (0.63)
  blocking collectives: 52.8 us -> 0 us
  Pallas kernels: 0 us -> 20.9 us
  starting transfers between devices: 4.79 us -> 21.2 us
  between operations: 13.6 us -> 0.09 us
  waiting for transfers between devices: 27.3 us -> 17.7 us
  other arithmetic: 4.36 us -> 0 us
  local copies, waits for them, and re-layouts: 4.19 us -> 7.67 us
  matrix products: 1.25 us -> 0 us
    psum x1 -> x0, blocking collectives: 52.8 us -> none  [shards(): summed = lax.psum(adjoint, 'col')]
    pallas_call x0 -> x10, Pallas kernels: none -> 20.9 us  [call(): pl.pallas_call(body, name=name, in_specs=[VMEM] * len(ins), out_specs=[VM...]
    reduce_scatter x1 -> x0, waiting for transfers between devices: 20.3 us -> none  [shards(): lax.psum_scatter(jnp.stack(parts, axis=1).astype(jnp.bfloat16), 'row', sc...]
    ppermute x2 -> x16, starting transfers between devices: 4.79 us -> 21.2 us  [the longest x6 8.51 us: shards(): lax.ppermute(v, 'row', pair_perm('row', d + 1))]
    ppermute x2 -> x16, waiting for transfers between devices: 6.97 us -> 17.7 us  [the longest x3 5.37 us: all_sum(): lax.ppermute(v, 'col', pair_perm('col', 2 * (d + 1)))]
    unnamed x6 -> x32, local copies, waits for them, and re-layouts: 0.02 us -> 3.85 us
    reshape x0 -> x2, local copies, waits for them, and re-layouts: none -> 3.82 us  [the longest x1 2.02 us: shards(): x = probes.reshape(-1, rows_own)]
    slice x2 -> x0, local copies, waits for them, and re-layouts: 2.18 us -> none  [the longest x1 2.14 us: shards(): imag_part = probes[:, freq_no, 1, :]]
  transfers between devices with their start and end apart: 3 -> 16, of which waited for: 3 -> 11; matrix products, arithmetic and copies ran while one was open for 1% -> 0% of each run, Pallas kernels for 0% -> 17%
where the time goes in v1:
time: 68.1 us; the launch traced here: 67.6 us
  starting transfers between devices  21.2 us (31%)
  Pallas kernels  20.9 us (31%)
  waiting for transfers between devices  17.7 us (26%)
  local copies, waits for them, and re-layouts  7.67 us (11%)
    pallas_call x10, Pallas kernels, call(): pl.pallas_call(body, name=name, in_specs=[VMEM] * len(ins), out_specs=[VM...  20.9 us
    ppermute x6, starting transfers between devices, shards(): lax.ppermute(v, 'row', pair_perm('row', d + 1))  8.51 us
    ppermute x3, waiting for transfers between devices, all_sum(): lax.ppermute(v, 'col', pair_perm('col', 2 * (d + 1)))  5.37 us
    ppermute x6, waiting for transfers between devices, shards(): lax.ppermute(v, 'row', pair_perm('row', d + 1))  4.83 us
    ppermute x1, waiting for transfers between devices, shards(): high = lax.ppermute(high, 'row', [(i + 1, i) for i in range(blocks - 1)])  4.2 us
    ppermute x3, starting transfers between devices, all_sum(): lax.ppermute(v, 'col', pair_perm('col', 2 * (d + 1)))  3.99 us
    unnamed x32, local copies, waits for them, and re-layouts  3.85 us
    ppermute x3, starting transfers between devices, all_sum(): lax.ppermute(mine, 'col', pair_perm('col', 2 * (d + 1)))  3.49 us
  transfers between devices with their start and end apart: 16, of which 11 were waited for; matrix products, arithmetic and copies ran while one was open for 0% of the time, Pallas kernels for 17%

profile of v1, /device:TPU:0, one launch (start us, length us, event | category | flops | bytes accessed | tf_op | source)
XLA Modules:
  0.0 67.6 jit_solution(8072964129495268732)
XLA Ops:
  0.0 2.0 %reshape.6.x_ref = bf16[1024,256]{1,0:T(8,128)(2,1)} reshape(bf16[256,2,2,256]{3,2,1,0:T(2,128)(2,1)} %param.5) | data formatting | bytes 1048576 | tf_op jit(solution)/shard_map/reshape | solution.py:228
  2.0 2.4 %adjoint_other.1 = bf16[512,256]{1,0:T(8,128)(2,1)} custom-call(bf16[1024,256]{1,0:T(8,128)(2,1)} %reshape.6.x_ref, bf16[2,2,256,256]{3,2,1,0:T(8,128)(2,1)} %k_ref.7), custom_call_target="tpu_custom_call" | custom-call | tf_op jit(solution)/shard_map/adjoint_other/pallas_call | solution.py:17
  4.4 0.5 collective-permute-start
  4.9 2.6 %adjoint_own.1.own_ref = f32[512,256]{1,0:T(8,128)} custom-call(bf16[1024,256]{1,0:T(8,128)(2,1)} %reshape.6.x_ref, bf16[2,2,256,256]{3,2,1,0:T(8,128)(2,1)} %k_ref.7), custom_call_target="tpu_custom_call" | custom-call | tf_op jit(solution)/shard_map/adjoint_own/pallas_call | solution.py:17
  7.5 0.0 collective-permute-done.got_ref
  7.5 0.0 copy-start.1
  7.5 0.7 %copy-done.1 = bf16[512,256]{1,0:T(8,128)(2,1)} copy-done((bf16[512,256]{1,0:T(8,128)(2,1)}, bf16[512,256]{1,0:T(8,128)(2,1)S(1)}, u32[]{:S(2)}) %copy-start.1) | copy-done | bytes 262168
  8.2 1.9 %split.1 = (f32[128,256]{1,0:T(8,128)}, bf16[128,256]{1,0:T(8,128)(2,1)}, bf16[128,256]{1,0:T(8,128)(2,1)}, bf16[128,256]{1,0:T(8,128)(2,1)}) custom-call(f32[512,256]{1,0:T(8,128)} %adjoint_own.1.own_ref, bf16[512,256]{1,0:T(8,128)(2,1)} %copy-done.1), custom_call_target="tpu_custom_call" | custom-call | tf_op jit(solution)/shard_map/split/pallas_call | solution.py:17
  10.1 2.5 %collective-permute-start.1 = (bf16[128,256]{1,0:T(8,128)(2,1)}, bf16[128,256]{1,0:T(8,128)(2,1)S(1)}, u32[]{:S(2)}, u32[]{:S(2)}) collective-permute-start(bf16[128,256]{1,0:T(8,128)(2,1)} %get-tuple-element.20), channel_id=1, source_target_pairs={{0,2},{1,3},{2,0},{3,1},{4,6},{5,7},{6,4},{7,5},{8,10},{9,11},{10,... | collective-permute-start | bytes 196616 | tf_op jit(solution)/shard_map/ppermute | solution.py:216
  12.6 1.5 %collective-permute-start.2 = (bf16[128,256]{1,0:T(8,128)(2,1)}, bf16[128,256]{1,0:T(8,128)(2,1)S(1)}, u32[]{:S(2)}, u32[]{:S(2)}) collective-permute-start(bf16[128,256]{1,0:T(8,128)(2,1)} %get-tuple-element.21), channel_id=1, source_target_pairs={{0,4},{1,5},{2,6},{3,7},{4,0},{5,1},{6,2},{7,3},{8,12},{9,13},{10,... | collective-permute-start | bytes 196616 | tf_op jit(solution)/shard_map/ppermute | solution.py:216
  14.1 0.0 collective-permute-start.3
  14.1 1.5 %collective-permute-done.1.refs_0_ = bf16[128,256]{1,0:T(8,128)(2,1)S(1)} collective-permute-done((bf16[128,256]{1,0:T(8,128)(2,1)}, bf16[128,256]{1,0:T(8,128)(2,1)S(1)}, u32[]{:S(2)}, u32[]{:S(2)}) %collective-permute-start.1) | collective-permute-done | bytes 65568 | tf_op jit(solution)/shard_map/ppermute | solution.py:216
  15.5 0.0 copy-start.8
  15.5 1.5 %collective-permute-done.2.refs_1_ = bf16[128,256]{1,0:T(8,128)(2,1)S(1)} collective-permute-done((bf16[128,256]{1,0:T(8,128)(2,1)}, bf16[128,256]{1,0:T(8,128)(2,1)S(1)}, u32[]{:S(2)}, u32[]{:S(2)}) %collective-permute-start.2) | collective-permute-done | bytes 65568 | tf_op jit(solution)/shard_map/ppermute | solution.py:216
  17.0 0.0 copy-start.9
  17.0 2.4 %collective-permute-done.3.refs_2_ = bf16[128,256]{1,0:T(8,128)(2,1)S(1)} collective-permute-done((bf16[128,256]{1,0:T(8,128)(2,1)}, bf16[128,256]{1,0:T(8,128)(2,1)S(1)}, u32[]{:S(2)}, u32[]{:S(2)}) %collective-permute-start.3) | collective-permute-done | bytes 65568 | tf_op jit(solution)/shard_map/ppermute | solution.py:216
  19.5 0.0 copy-done.8
  19.5 0.0 copy-done.9
  19.5 0.6 copy-done.10
  20.1 1.6 %sum.1.mine_ref = bf16[128,256]{1,0:T(8,128)(2,1)} custom-call(f32[128,256]{1,0:T(8,128)} %get-tuple-element.19.keep_ref, bf16[128,256]{1,0:T(8,128)(2,1)} %copy-done.8, bf16[128,256]{1,0:T(8,128)(2,1)} %copy-done.9, bf16[128,256]{1,0:T(8,128)(2,1)} %copy-done.10), custom_call_target="tpu_custom_call" | custom-call | tf_op jit(solution)/shard_map/sum/pallas_call | solution.py:17
  21.7 0.5 collective-permute-start.4
  22.2 0.5 collective-permute-start.5
  22.8 2.4 %collective-permute-start.6 = (bf16[128,256]{1,0:T(8,128)(2,1)}, bf16[128,256]{1,0:T(8,128)(2,1)S(1)}, u32[]{:S(2)}, u32[]{:S(2)}) collective-permute-start(bf16[128,256]{1,0:T(8,128)(2,1)} %sum.1.mine_ref), channel_id=1, source_target_pairs={{0,6},{1,7},{2,4},{3,5},{4,2},{5,3},{6,0},{7,1},{8,14},{9,15},{10,... | collective-permute-start | bytes 196616 | tf_op jit(solution)/shard_map/ppermute | solution.py:218
  25.2 1.0 %collective-permute-done.4.refs_0_ = bf16[128,256]{1,0:T(8,128)(2,1)S(1)} collective-permute-done((bf16[128,256]{1,0:T(8,128)(2,1)}, bf16[128,256]{1,0:T(8,128)(2,1)S(1)}, u32[]{:S(2)}, u32[]{:S(2)}) %collective-permute-start.4) | collective-permute-done | bytes 65568 | tf_op jit(solution)/shard_map/ppermute | solution.py:218
  26.2 0.6 collective-permute-done.5.refs_1_
  26.7 1.4 %collective-permute-done.6.refs_2_ = bf16[128,256]{1,0:T(8,128)(2,1)S(1)} collective-permute-done((bf16[128,256]{1,0:T(8,128)(2,1)}, bf16[128,256]{1,0:T(8,128)(2,1)S(1)}, u32[]{:S(2)}, u32[]{:S(2)}) %collective-permute-start.6) | collective-permute-done | bytes 65568 | tf_op jit(solution)/shard_map/ppermute | solution.py:218
  28.1 0.0 copy-done.11
  28.1 0.0 copy-done.12
  28.1 0.6 copy-done.13
  28.8 1.7 %join.1.a_ref = bf16[512,256]{1,0:T(8,128)(2,1)} custom-call(bf16[128,256]{1,0:T(8,128)(2,1)} %sum.1.mine_ref, bf16[128,256]{1,0:T(8,128)(2,1)} %copy-done.11, bf16[128,256]{1,0:T(8,128)(2,1)} %copy-done.12, bf16[128,256]{1,0:T(8,128)(2,1)} %copy-done.13), custom_call_target="tpu_custom_call" | custom-call | tf_op jit(solution)/shard_map/join/pallas_call | solution.py:17
  30.4 0.0 collective-permute-start.12
  30.4 2.1 %edges.1 = (bf16[8,1024]{1,0:T(8,128)(2,1)}, bf16[8,1024]{1,0:T(8,128)(2,1)}) custom-call(bf16[2,2,256,256]{3,2,1,0:T(8,128)(2,1)} %k_ref.7, f32[1,256]{1,0:T(1,128)} %bitcast.1), custom_call_target="tpu_custom_call" | custom-call | tf_op jit(solution)/shard_map/edges/pallas_call | solution.py:17
  32.5 3.4 %collective-permute-start.7 = (bf16[8,1024]{1,0:T(8,128)(2,1)}, bf16[8,1024]{1,0:T(8,128)(2,1)S(1)}, u32[]{:S(2)}, u32[]{:S(2)}) collective-permute-start(bf16[8,1024]{1,0:T(8,128)(2,1)} %get-tuple-element.23), channel_id=1, source_target_pairs={{0,8},{8,16},{16,24},{1,9},{9,17},{17,25},{2,10},{10,18},{18,26},{... | collective-permute-start | bytes 49160 | tf_op jit(solution)/shard_map/ppermute | solution.py:231
  35.9 1.3 %collective-permute-start.8 = (bf16[8,1024]{1,0:T(8,128)(2,1)}, bf16[8,1024]{1,0:T(8,128)(2,1)S(1)}, u32[]{:S(2)}, u32[]{:S(2)}) collective-permute-start(bf16[8,1024]{1,0:T(8,128)(2,1)} %get-tuple-element.24), channel_id=1, source_target_pairs={{8,0},{16,8},{24,16},{9,1},{17,9},{25,17},{10,2},{18,10},{26,18},{... | collective-permute-start | bytes 49160 | tf_op jit(solution)/shard_map/ppermute | solution.py:232
  37.2 0.3 collective-permute-done.7.low_ref
  37.6 4.2 %collective-permute-done.8.high_ref = bf16[8,1024]{1,0:T(8,128)(2,1)S(1)} collective-permute-done((bf16[8,1024]{1,0:T(8,128)(2,1)}, bf16[8,1024]{1,0:T(8,128)(2,1)S(1)}, u32[]{:S(2)}, u32[]{:S(2)}) %collective-permute-start.8) | collective-permute-done | bytes 16416 | tf_op jit(solution)/shard_map/ppermute | solution.py:232
  41.8 0.0 copy-done.14
  41.8 0.6 copy-done.15
  42.4 2.4 %operator.1.k_ref = bf16[2,2,256,256]{3,2,1,0:T(8,128)(2,1)} custom-call(bf16[2,2,256,256]{3,2,1,0:T(8,128)(2,1)} %k_ref.7, f32[1,256]{1,0:T(1,128)} %bitcast.2, bf16[8,1024]{1,0:T(8,128)(2,1)} %copy-done.14, bf16[8,1024]{1,0:T(8,128)(2,1)} %copy-done.15), custom_call_target="tpu_custom_call" | custom-call | tf_op jit(solution)/shard_map/operator/pallas_call | solution.py:17
  44.7 2.1 %predict_own.1 = (f32[128,256]{1,0:T(8,128)}, bf16[128,256]{1,0:T(8,128)(2,1)}, bf16[128,256]{1,0:T(8,128)(2,1)}, bf16[128,256]{1,0:T(8,128)(2,1)}) custom-call(bf16[512,256]{1,0:T(8,128)(2,1)} %join.1.a_ref, bf16[2,2,256,256]{3,2,1,0:T(8,128)(2,1)} %operator.1.k_ref), custom_call_target="tpu_custom_call" | custom-call | tf_op jit(solution)/shard_map/predict_own/pallas_call | solution.py:17
  46.9 2.6 %collective-permute-start.10 = (bf16[128,256]{1,0:T(8,128)(2,1)}, bf16[128,256]{1,0:T(8,128)(2,1)S(1)}, u32[]{:S(2)}, u32[]{:S(2)}) collective-permute-start(bf16[128,256]{1,0:T(8,128)(2,1)} %get-tuple-element.27), channel_id=1, source_target_pairs={{0,16},{8,24},{16,0},{24,8},{1,17},{9,25},{17,1},{25,9},{2,18},{10... | collective-permute-start | bytes 196616 | tf_op jit(solution)/shard_map/ppermute | solution.py:245
  49.5 1.3 %collective-permute-start.11 = (bf16[128,256]{1,0:T(8,128)(2,1)}, bf16[128,256]{1,0:T(8,128)(2,1)S(1)}, u32[]{:S(2)}, u32[]{:S(2)}) collective-permute-start(bf16[128,256]{1,0:T(8,128)(2,1)} %get-tuple-element.28), channel_id=1, source_target_pairs={{0,24},{8,16},{16,8},{24,0},{1,25},{9,17},{17,9},{25,1},{2,26},{10... | collective-permute-start | bytes 196616 | tf_op jit(solution)/shard_map/ppermute | solution.py:245
  50.8 0.0 collective-permute-start.9
  50.8 0.0 collective-permute-done.12.a_ref
  50.8 0.7 %copy-done = bf16[512,256]{1,0:T(8,128)(2,1)} copy-done((bf16[512,256]{1,0:T(8,128)(2,1)}, bf16[512,256]{1,0:T(8,128)(2,1)S(1)}, u32[]{:S(2)}) %copy-start) | copy-done | bytes 262168
  51.5 2.2 %predict_other.1 = (f32[128,256]{1,0:T(8,128)}, bf16[128,256]{1,0:T(8,128)(2,1)}, bf16[128,256]{1,0:T(8,128)(2,1)}, bf16[128,256]{1,0:T(8,128)(2,1)}) custom-call(bf16[512,256]{1,0:T(8,128)(2,1)} %copy-done, bf16[2,2,256,256]{3,2,1,0:T(8,128)(2,1)} %operator.1.k_ref), custom_call_target="tpu_custom_call" | custom-call | tf_op jit(solution)/shard_map/predict_other/pallas_call | solution.py:17
  53.7 2.0 %collective-permute-start.13 = (bf16[128,256]{1,0:T(8,128)(2,1)}, bf16[128,256]{1,0:T(8,128)(2,1)S(1)}, u32[]{:S(2)}, u32[]{:S(2)}) collective-permute-start(bf16[128,256]{1,0:T(8,128)(2,1)} %get-tuple-element.30), channel_id=1, source_target_pairs={{0,8},{8,0},{16,24},{24,16},{1,9},{9,1},{17,25},{25,17},{2,10},{10... | collective-permute-start | bytes 196616 | tf_op jit(solution)/shard_map/ppermute | solution.py:245
  55.7 1.0 %collective-permute-start.14 = (bf16[128,256]{1,0:T(8,128)(2,1)}, bf16[128,256]{1,0:T(8,128)(2,1)S(1)}, u32[]{:S(2)}, u32[]{:S(2)}) collective-permute-start(bf16[128,256]{1,0:T(8,128)(2,1)} %get-tuple-element.31), channel_id=1, source_target_pairs={{0,16},{8,24},{16,0},{24,8},{1,17},{9,25},{17,1},{25,9},{2,18},{10... | collective-permute-start | bytes 196616 | tf_op jit(solution)/shard_map/ppermute | solution.py:245
  56.7 0.0 collective-permute-done.10.refs_2_
  56.7 1.5 %collective-permute-start.15 = (bf16[128,256]{1,0:T(8,128)(2,1)}, bf16[128,256]{1,0:T(8,128)(2,1)S(1)}, u32[]{:S(2)}, u32[]{:S(2)}) collective-permute-start(bf16[128,256]{1,0:T(8,128)(2,1)} %get-tuple-element.32), channel_id=1, source_target_pairs={{0,24},{8,16},{16,8},{24,0},{1,25},{9,17},{17,9},{25,1},{2,26},{10... | collective-permute-start | bytes 196616 | tf_op jit(solution)/shard_map/ppermute | solution.py:245
  58.3 0.0 collective-permute-done.11.refs_3_
  58.3 0.0 collective-permute-done.9.refs_1_
  58.3 0.0 copy-start.4
  58.3 0.4 collective-permute-done.13.refs_5_
  58.7 3.1 %collective-permute-done.14.refs_6_ = bf16[128,256]{1,0:T(8,128)(2,1)S(1)} collective-permute-done((bf16[128,256]{1,0:T(8,128)(2,1)}, bf16[128,256]{1,0:T(8,128)(2,1)S(1)}, u32[]{:S(2)}, u32[]{:S(2)}) %collective-permute-start.14) | collective-permute-done | bytes 65568 | tf_op jit(solution)/shard_map/ppermute | solution.py:245
  61.8 1.3 %collective-permute-done.15.refs_7_ = bf16[128,256]{1,0:T(8,128)(2,1)S(1)} collective-permute-done((bf16[128,256]{1,0:T(8,128)(2,1)}, bf16[128,256]{1,0:T(8,128)(2,1)S(1)}, u32[]{:S(2)}, u32[]{:S(2)}) %collective-permute-start.15) | collective-permute-done | bytes 65568 | tf_op jit(solution)/shard_map/ppermute | solution.py:245
  63.1 0.0 copy-done.2
  63.1 0.0 copy-done.3
  63.1 0.0 copy-done.4
  63.1 0.0 copy-done.5
  63.1 0.0 copy-done.6
  63.1 0.6 copy-done.7
  63.7 2.1 %final.1 = f32[256,256]{1,0:T(8,128)} custom-call(bf16[1024,256]{1,0:T(8,128)(2,1)} %reshape.6.x_ref, f32[2,256]{1,0:T(2,128)} %noise_ref.1, f32[128,256]{1,0:T(8,128)} %get-tuple-element.25.refs_0_, bf16[128,256]{1,0:T(8,128)(2,1)} %copy-done.4, bf16[128,256]{1,0:T(8,128)(2,1)} %copy-done.2, bf16[128,256]{1,0:T(8,128)(2,1)} %copy-done.3, ...), custom_call_target="tpu_custom_call" | custom-call | tf_op jit(solution)/shard_map/final/pallas_call | solution.py:17
  65.8 1.8 %reshape.7 = f32[64,2,2,256]{3,2,1,0:T(2,128)} reshape(f32[256,256]{1,0:T(8,128)} %final.1) | data formatting | bytes 524288 | tf_op jit(solution)/shard_map/reshape | solution.py:253
  (12 shorter events, 0.0 us)
Async XLA Ops:
  4.4 3.1 %collective-permute-start = (bf16[512,256]{1,0:T(8,128)(2,1)}, bf16[512,256]{1,0:T(8,128)(2,1)S(1)}, u32[]{:S(2)}, u32[]{:S(2)}) collective-permute-start(bf16[512,256]{1,0:T(8,128)(2,1)} %adjoint_other.1), channel_id=1, source_target_pairs={{0,1},{1,0},{2,3},{3,2},{4,5},{5,4},{6,7},{7,6},{8,9},{9,8},{10,11... | collective-permute-start | bytes 786440 | tf_op jit(solution)/shard_map/ppermute | solution.py:203
  7.5 0.7 %copy-start.1 = (bf16[512,256]{1,0:T(8,128)(2,1)}, bf16[512,256]{1,0:T(8,128)(2,1)S(1)}, u32[]{:S(2)}) copy-start(bf16[512,256]{1,0:T(8,128)(2,1)S(1)} %collective-permute-done.got_ref) | copy-start | bytes 786436
  10.1 5.4 %collective-permute-start.1 = (bf16[128,256]{1,0:T(8,128)(2,1)}, bf16[128,256]{1,0:T(8,128)(2,1)S(1)}, u32[]{:S(2)}, u32[]{:S(2)}) collective-permute-start(bf16[128,256]{1,0:T(8,128)(2,1)} %get-tuple-element.20), channel_id=1, source_target_pairs={{0,2},{1,3},{2,0},{3,1},{4,6},{5,7},{6,4},{7,5},{8,10},{9,11},{10,... | collective-permute-start | bytes 196616 | tf_op jit(solution)/shard_map/ppermute | solution.py:216
  12.6 4.5 %collective-permute-start.2 = (bf16[128,256]{1,0:T(8,128)(2,1)}, bf16[128,256]{1,0:T(8,128)(2,1)S(1)}, u32[]{:S(2)}, u32[]{:S(2)}) collective-permute-start(bf16[128,256]{1,0:T(8,128)(2,1)} %get-tuple-element.21), channel_id=1, source_target_pairs={{0,4},{1,5},{2,6},{3,7},{4,0},{5,1},{6,2},{7,3},{8,12},{9,13},{10,... | collective-permute-start | bytes 196616 | tf_op jit(solution)/shard_map/ppermute | solution.py:216
  14.1 5.4 %collective-permute-start.3 = (bf16[128,256]{1,0:T(8,128)(2,1)}, bf16[128,256]{1,0:T(8,128)(2,1)S(1)}, u32[]{:S(2)}, u32[]{:S(2)}) collective-permute-start(bf16[128,256]{1,0:T(8,128)(2,1)} %get-tuple-element.22), channel_id=1, source_target_pairs={{0,6},{1,7},{2,4},{3,5},{4,2},{5,3},{6,0},{7,1},{8,14},{9,15},{10,... | collective-permute-start | bytes 196616 | tf_op jit(solution)/shard_map/ppermute | solution.py:216
  15.5 3.9 %copy-start.8 = (bf16[128,256]{1,0:T(8,128)(2,1)}, bf16[128,256]{1,0:T(8,128)(2,1)S(1)}, u32[]{:S(2)}) copy-start(bf16[128,256]{1,0:T(8,128)(2,1)S(1)} %collective-permute-done.1.refs_0_) | copy-start | bytes 196612
  17.0 2.4 %copy-start.9 = (bf16[128,256]{1,0:T(8,128)(2,1)}, bf16[128,256]{1,0:T(8,128)(2,1)S(1)}, u32[]{:S(2)}) copy-start(bf16[128,256]{1,0:T(8,128)(2,1)S(1)} %collective-permute-done.2.refs_1_) | copy-start | bytes 196612
  19.5 0.6 copy-start.10
  21.7 4.5 %collective-permute-start.4 = (bf16[128,256]{1,0:T(8,128)(2,1)}, bf16[128,256]{1,0:T(8,128)(2,1)S(1)}, u32[]{:S(2)}, u32[]{:S(2)}) collective-permute-start(bf16[128,256]{1,0:T(8,128)(2,1)} %sum.1.mine_ref), channel_id=1, source_target_pairs={{0,2},{1,3},{2,0},{3,1},{4,6},{5,7},{6,4},{7,5},{8,10},{9,11},{10,... | collective-permute-start | bytes 196616 | tf_op jit(solution)/shard_map/ppermute | solution.py:218
  22.2 4.5 %collective-permute-start.5 = (bf16[128,256]{1,0:T(8,128)(2,1)}, bf16[128,256]{1,0:T(8,128)(2,1)S(1)}, u32[]{:S(2)}, u32[]{:S(2)}) collective-permute-start(bf16[128,256]{1,0:T(8,128)(2,1)} %sum.1.mine_ref), channel_id=1, source_target_pairs={{0,4},{1,5},{2,6},{3,7},{4,0},{5,1},{6,2},{7,3},{8,12},{9,13},{10,... | collective-permute-start | bytes 196616 | tf_op jit(solution)/shard_map/ppermute | solution.py:218
  22.8 5.4 %collective-permute-start.6 = (bf16[128,256]{1,0:T(8,128)(2,1)}, bf16[128,256]{1,0:T(8,128)(2,1)S(1)}, u32[]{:S(2)}, u32[]{:S(2)}) collective-permute-start(bf16[128,256]{1,0:T(8,128)(2,1)} %sum.1.mine_ref), channel_id=1, source_target_pairs={{0,6},{1,7},{2,4},{3,5},{4,2},{5,3},{6,0},{7,1},{8,14},{9,15},{10,... | collective-permute-start | bytes 196616 | tf_op jit(solution)/shard_map/ppermute | solution.py:218
  26.2 2.0 %copy-start.11 = (bf16[128,256]{1,0:T(8,128)(2,1)}, bf16[128,256]{1,0:T(8,128)(2,1)S(1)}, u32[]{:S(2)}) copy-start(bf16[128,256]{1,0:T(8,128)(2,1)S(1)} %collective-permute-done.4.refs_0_) | copy-start | bytes 196612
  26.7 1.4 %copy-start.12 = (bf16[128,256]{1,0:T(8,128)(2,1)}, bf16[128,256]{1,0:T(8,128)(2,1)S(1)}, u32[]{:S(2)}) copy-start(bf16[128,256]{1,0:T(8,128)(2,1)S(1)} %collective-permute-done.5.refs_1_) | copy-start | bytes 196612
  28.1 0.6 copy-start.13
  30.4 20.4 %collective-permute-start.12 = (bf16[512,256]{1,0:T(8,128)(2,1)}, bf16[512,256]{1,0:T(8,128)(2,1)S(1)}, u32[]{:S(2)}, u32[]{:S(2)}) collective-permute-start(bf16[512,256]{1,0:T(8,128)(2,1)} %join.1.a_ref), channel_id=1, source_target_pairs={{0,1},{1,0},{2,3},{3,2},{4,5},{5,4},{6,7},{7,6},{8,9},{9,8},{10,11... | collective-permute-start | bytes 786440 | tf_op jit(solution)/shard_map/ppermute | solution.py:220
  32.5 5.1 %collective-permute-start.7 = (bf16[8,1024]{1,0:T(8,128)(2,1)}, bf16[8,1024]{1,0:T(8,128)(2,1)S(1)}, u32[]{:S(2)}, u32[]{:S(2)}) collective-permute-start(bf16[8,1024]{1,0:T(8,128)(2,1)} %get-tuple-element.23), channel_id=1, source_target_pairs={{0,8},{8,16},{16,24},{1,9},{9,17},{17,25},{2,10},{10,18},{18,26},{... | collective-permute-start | bytes 49160 | tf_op jit(solution)/shard_map/ppermute | solution.py:231
  35.9 5.8 %collective-permute-start.8 = (bf16[8,1024]{1,0:T(8,128)(2,1)}, bf16[8,1024]{1,0:T(8,128)(2,1)S(1)}, u32[]{:S(2)}, u32[]{:S(2)}) collective-permute-start(bf16[8,1024]{1,0:T(8,128)(2,1)} %get-tuple-element.24), channel_id=1, source_target_pairs={{8,0},{16,8},{24,16},{9,1},{17,9},{25,17},{10,2},{18,10},{26,18},{... | collective-permute-start | bytes 49160 | tf_op jit(solution)/shard_map/ppermute | solution.py:232
  37.6 4.2 %copy-start.14 = (bf16[8,1024]{1,0:T(8,128)(2,1)}, bf16[8,1024]{1,0:T(8,128)(2,1)S(1)}, u32[]{:S(2)}) copy-start(bf16[8,1024]{1,0:T(8,128)(2,1)S(1)} %collective-permute-done.7.low_ref) | copy-start | bytes 49156
  41.8 0.6 copy-start.15
  46.9 9.9 %collective-permute-start.10 = (bf16[128,256]{1,0:T(8,128)(2,1)}, bf16[128,256]{1,0:T(8,128)(2,1)S(1)}, u32[]{:S(2)}, u32[]{:S(2)}) collective-permute-start(bf16[128,256]{1,0:T(8,128)(2,1)} %get-tuple-element.27), channel_id=1, source_target_pairs={{0,16},{8,24},{16,0},{24,8},{1,17},{9,25},{17,1},{25,9},{2,18},{10... | collective-permute-start | bytes 196616 | tf_op jit(solution)/shard_map/ppermute | solution.py:245
  49.5 8.8 %collective-permute-start.11 = (bf16[128,256]{1,0:T(8,128)(2,1)}, bf16[128,256]{1,0:T(8,128)(2,1)S(1)}, u32[]{:S(2)}, u32[]{:S(2)}) collective-permute-start(bf16[128,256]{1,0:T(8,128)(2,1)} %get-tuple-element.28), channel_id=1, source_target_pairs={{0,24},{8,16},{16,8},{24,0},{1,25},{9,17},{17,9},{25,1},{2,26},{10... | collective-permute-start | bytes 196616 | tf_op jit(solution)/shard_map/ppermute | solution.py:245
  50.8 7.5 %collective-permute-start.9 = (bf16[128,256]{1,0:T(8,128)(2,1)}, bf16[128,256]{1,0:T(8,128)(2,1)S(1)}, u32[]{:S(2)}, u32[]{:S(2)}) collective-permute-start(bf16[128,256]{1,0:T(8,128)(2,1)} %get-tuple-element.26), channel_id=1, source_target_pairs={{0,8},{8,0},{16,24},{24,16},{1,9},{9,1},{17,25},{25,17},{2,10},{10... | collective-permute-start | bytes 196616 | tf_op jit(solution)/shard_map/ppermute | solution.py:245
  50.8 0.7 %copy-start = (bf16[512,256]{1,0:T(8,128)(2,1)}, bf16[512,256]{1,0:T(8,128)(2,1)S(1)}, u32[]{:S(2)}) copy-start(bf16[512,256]{1,0:T(8,128)(2,1)S(1)} %collective-permute-done.12.a_ref) | copy-start | bytes 786436
  53.7 5.0 %collective-permute-start.13 = (bf16[128,256]{1,0:T(8,128)(2,1)}, bf16[128,256]{1,0:T(8,128)(2,1)S(1)}, u32[]{:S(2)}, u32[]{:S(2)}) collective-permute-start(bf16[128,256]{1,0:T(8,128)(2,1)} %get-tuple-element.30), channel_id=1, source_target_pairs={{0,8},{8,0},{16,24},{24,16},{1,9},{9,1},{17,25},{25,17},{2,10},{10... | collective-permute-start | bytes 196616 | tf_op jit(solution)/shard_map/ppermute | solution.py:245
  55.7 6.1 %collective-permute-start.14 = (bf16[128,256]{1,0:T(8,128)(2,1)}, bf16[128,256]{1,0:T(8,128)(2,1)S(1)}, u32[]{:S(2)}, u32[]{:S(2)}) collective-permute-start(bf16[128,256]{1,0:T(8,128)(2,1)} %get-tuple-element.31), channel_id=1, source_target_pairs={{0,16},{8,24},{16,0},{24,8},{1,17},{9,25},{17,1},{25,9},{2,18},{10... | collective-permute-start | bytes 196616 | tf_op jit(solution)/shard_map/ppermute | solution.py:245
  56.7 6.4 %copy-start.2 = (bf16[128,256]{1,0:T(8,128)(2,1)}, bf16[128,256]{1,0:T(8,128)(2,1)S(1)}, u32[]{:S(2)}) copy-start(bf16[128,256]{1,0:T(8,128)(2,1)S(1)} %collective-permute-done.10.refs_2_) | copy-start | bytes 196612
  56.7 6.4 %collective-permute-start.15 = (bf16[128,256]{1,0:T(8,128)(2,1)}, bf16[128,256]{1,0:T(8,128)(2,1)S(1)}, u32[]{:S(2)}, u32[]{:S(2)}) collective-permute-start(bf16[128,256]{1,0:T(8,128)(2,1)} %get-tuple-element.32), channel_id=1, source_target_pairs={{0,24},{8,16},{16,8},{24,0},{1,25},{9,17},{17,9},{25,1},{2,26},{10... | collective-permute-start | bytes 196616 | tf_op jit(solution)/shard_map/ppermute | solution.py:245
  58.3 4.9 %copy-start.3 = (bf16[128,256]{1,0:T(8,128)(2,1)}, bf16[128,256]{1,0:T(8,128)(2,1)S(1)}, u32[]{:S(2)}) copy-start(bf16[128,256]{1,0:T(8,128)(2,1)S(1)} %collective-permute-done.11.refs_3_) | copy-start | bytes 196612
  58.3 4.8 %copy-start.4 = (bf16[128,256]{1,0:T(8,128)(2,1)}, bf16[128,256]{1,0:T(8,128)(2,1)S(1)}, u32[]{:S(2)}) copy-start(bf16[128,256]{1,0:T(8,128)(2,1)S(1)} %collective-permute-done.9.refs_1_) | copy-start | bytes 196612
  58.7 4.4 %copy-start.5 = (bf16[128,256]{1,0:T(8,128)(2,1)}, bf16[128,256]{1,0:T(8,128)(2,1)S(1)}, u32[]{:S(2)}) copy-start(bf16[128,256]{1,0:T(8,128)(2,1)S(1)} %collective-permute-done.13.refs_5_) | copy-start | bytes 196612
  61.8 1.4 %copy-start.6 = (bf16[128,256]{1,0:T(8,128)(2,1)}, bf16[128,256]{1,0:T(8,128)(2,1)S(1)}, u32[]{:S(2)}) copy-start(bf16[128,256]{1,0:T(8,128)(2,1)S(1)} %collective-permute-done.14.refs_6_) | copy-start | bytes 196612
  63.1 0.6 copy-start.7

commit v2 on v1

--- a/solution.py
+++ b/solution.py
@@ -19,9 +19,9 @@
         name=name,
         in_specs=[VMEM] * len(ins),
         out_specs=[VMEM] * len(outs),
-        out_shape=[jax.ShapeDtypeStruct(*o) for o in outs],
+        out_shape=[pltpu.VMEM(*o) for o in outs],
         scratch_shapes=list(scratch),
-    )(*ins)
+    )(*[pltpu.with_memory_space_constraint(v, pltpu.VMEM) for v in ins])
 
 
 def parity():
@@ -40,13 +40,17 @@
     return [(i, i ^ step) for i in range(lax.axis_size(axis))]
 
 
-def adjoint_body(swap, x_ref, k_ref, o_ref, u_ref):
-    rows = x_ref.shape[0] // 4
+def adjoint_body(swap, x_ref, k_ref, o_ref, *refs):
+    u_ref = refs[-1]
+    rows = u_ref.shape[1] // 4
     width = k_ref.shape[3]
     freq = parity()
     if swap:
         freq = 1 - freq
     x = x_ref[...]
+    if swap:
+        x = x.reshape(refs[0].shape)
+        refs[0][...] = x
     tiles = width // LANES
     for part in range(2):
         y = dot_nn(x, k_ref[freq, part])
@@ -171,8 +175,8 @@
 
 def final_body(peers, x_ref, noise_ref, *refs):
     out_ref, s_ref = refs[-2:]
-    rows = out_ref.shape[0]
-    size = rows // 4
+    size = out_ref.shape[0]
+    rows = 4 * size
     me = lax.axis_index("row")
     freq = parity()
     for which in range(2):
@@ -188,18 +192,23 @@
     x = x_ref[pl.ds(pl.multiple_of(me * rows, rows), rows), :].astype(F32)
     kind = lax.rem(lax.broadcasted_iota(jnp.int32, x.shape, 0), 4)
     noise = jnp.where(kind < 2, noise_ref[0:1, :], noise_ref[1:2, :])
-    extra = noise * x
-    for t in range(s_ref.shape[0]):
-        at = slice(t * LANES, (t + 1) * LANES)
-        out_ref[:, at] = s_ref[t] + extra[:, at]
-
-
-def all_sum(x, kernel):
-    rows = x.shape[0] // 2
+    values = jnp.concatenate([s_ref[t] for t in range(s_ref.shape[0])], axis=1) + noise * x
+    out_ref[...] = values.reshape(out_ref.shape)
+
+
+def all_sum(probes, kernel):
+    rows = 2 * probes.shape[0]
     width = kernel.shape[3]
     count = lax.axis_size("col")
-    scratch = (pltpu.VMEM((2 * width // LANES, x.shape[0], LANES), F32),)
-    other = call(functools.partial(adjoint_body, True), "adjoint_other", (x, kernel), [((rows, width), BF)], scratch)[0]
+    flat = (2 * rows, probes.shape[3])
+    scratch = (pltpu.VMEM((2 * width // LANES, 2 * rows, LANES), F32),)
+    other, x = call(
+        functools.partial(adjoint_body, True),
+        "adjoint_other",
+        (probes, kernel),
+        [((rows, width), BF), (flat, BF)],
+        scratch,
+    )
     got = lax.ppermute(other, "col", pair_perm("col", 1))
     own = call(functools.partial(adjoint_body, False), "adjoint_own", (x, kernel), [((rows, width), F32)], scratch)[0]
     chips = count // 2
@@ -208,7 +217,7 @@
         both = jnp.where(parity() == 0, jnp.stack([part, 0 * part]), jnp.stack([0 * part, part]))
         both = lax.psum(both, "col").astype(BF)
         mine = lax.dynamic_index_in_dim(both, parity(), 0, keepdims=False)
-        return mine, lax.dynamic_index_in_dim(both, 1 - parity(), 0, keepdims=False)
+        return x, mine, lax.dynamic_index_in_dim(both, 1 - parity(), 0, keepdims=False)
     size = rows // chips
     keep, *sends = call(
         split_body, "split", (own, got), [((size, width), F32)] + [((size, width), BF)] * (chips - 1)
@@ -217,7 +226,7 @@
     mine = call(sum_body, "sum", (keep, *got), [((size, width), BF)])[0]
     got = [lax.ppermute(mine, "col", pair_perm("col", 2 * (d + 1))) for d in range(chips - 1)]
     mine = call(join_body, "join", (mine, *got), [((rows, width), BF)])[0]
-    return mine, lax.ppermute(mine, "col", pair_perm("col", 1))
+    return x, mine, lax.ppermute(mine, "col", pair_perm("col", 1))
 
 
 def shards(kernel, probes, noise_var, prior_diag):
@@ -225,12 +234,11 @@
     width = kernel.shape[3]
     count = probes.shape[0]
     blocks = lax.axis_size("row")
-    x = probes.reshape(-1, rows_own)
     coef = prior_diag[None, :]
     low, high = call(edges_body, "edges", (kernel, coef), [((8, 4 * rows_own), BF)] * 2)
     low = lax.ppermute(low, "row", [(i, i + 1) for i in range(blocks - 1)])
     high = lax.ppermute(high, "row", [(i + 1, i) for i in range(blocks - 1)])
-    mine, other = all_sum(x, kernel)
+    x, mine, other = all_sum(probes, kernel)
     operator = call(operator_body, "operator", (kernel, coef, low, high), [((2, 2, width, rows_own), BF)])[0]
     size = count // blocks
     groups = []
@@ -247,10 +255,10 @@
         functools.partial(final_body, blocks - 1),
         "final",
         (x, noise_var, *groups),
-        [((4 * size, rows_own), F32)],
+        [((size,) + probes.shape[1:3] + (rows_own,), F32)],
         (pltpu.VMEM((rows_own // LANES, 4 * size, LANES), F32),),
     )[0]
-    return out.reshape(size, 2, 2, rows_own)
+    return out
 
 
 def solution(mesh):

time: 68.1 us -> 46.2 us (0.68)
  Pallas kernels: 20.9 us -> 2.9 us
  local copies, waits for them, and re-layouts: 7.67 us -> 3.39 us
  starting transfers between devices: 21.2 us -> 22.1 us
    pallas_call x10, Pallas kernels: 20.9 us -> 2.9 us  [call(): pl.pallas_call(body, name=name, in_specs=[VMEM] * len(ins), out_specs=[VM...]
    reshape x2 -> x0, local copies, waits for them, and re-layouts: 3.82 us -> none  [the longest x1 2.02 us: shards(): x = probes.reshape(-1, rows_own)]
    unnamed x32 -> x11, local copies, waits for them, and re-layouts: 3.85 us -> 3.39 us
  transfers between devices with their start and end apart: 16 -> 16, of which waited for: 11 -> 13; matrix products, arithmetic and copies ran while one was open for 0% -> 0% of each run, Pallas kernels for 17% -> 5%
where the time goes in v2:
time: 46.2 us; the launch traced here: 45.9 us
  starting transfers between devices  22.1 us (48%)
  waiting for transfers between devices  17.4 us (38%)
  local copies, waits for them, and re-layouts  3.39 us (7%)
  Pallas kernels  2.9 us (6%)
    ppermute x6, starting transfers between devices, shards(): lax.ppermute(v, 'row', pair_perm('row', d + 1))  8.63 us
    ppermute x3, waiting for transfers between devices, all_sum(): lax.ppermute(v, 'col', pair_perm('col', 2 * (d + 1)))  5.14 us
    ppermute x6, waiting for transfers between devices, shards(): lax.ppermute(v, 'row', pair_perm('row', d + 1))  4.71 us
    ppermute x3, starting transfers between devices, all_sum(): lax.ppermute(v, 'col', pair_perm('col', 2 * (d + 1)))  4.46 us
    ppermute x1, waiting for transfers between devices, shards(): high = lax.ppermute(high, 'row', [(i + 1, i) for i in range(blocks - 1)])  4.21 us
    ppermute x1, starting transfers between devices, shards(): low = lax.ppermute(low, 'row', [(i, i + 1) for i in range(blocks - 1)])  3.57 us
    ppermute x3, starting transfers between devices, all_sum(): lax.ppermute(mine, 'col', pair_perm('col', 2 * (d + 1)))  3.55 us
    unnamed x11, local copies, waits for them, and re-layouts  3.39 us
  transfers between devices with their start and end apart: 16, of which 13 were waited for; matrix products, arithmetic and copies ran while one was open for 0% of the time, Pallas kernels for 5%

profile of v2, /device:TPU:0, one launch (start us, length us, event | category | flops | bytes accessed | tf_op | source)
XLA Modules:
  0.0 45.9 jit_solution(17413448895528210729)
XLA Ops:
  0.0 0.0 copy-start
  0.0 1.0 %copy-done = bf16[2,2,256,256]{3,2,1,0:T(8,128)(2,1)S(1)} copy-done((bf16[2,2,256,256]{3,2,1,0:T(8,128)(2,1)S(1)}, bf16[2,2,256,256]{3,2,1,0:T(8,128)(2,1)}, u32[]{:S(2)}) %copy-start) | copy-done | bytes 524312
  1.0 0.0 copy-start.2
  1.0 1.0 %copy-done.2 = bf16[256,2,2,256]{3,2,1,0:T(2,128)(2,1)S(1)} copy-done((bf16[256,2,2,256]{3,2,1,0:T(2,128)(2,1)S(1)}, bf16[256,2,2,256]{3,2,1,0:T(2,128)(2,1)}, u32[]{:S(2)}) %copy-start.2) | copy-done | bytes 524312
  2.1 0.0 copy-start.1
  2.1 0.5 %adjoint_other.1 = (bf16[512,256]{1,0:T(8,128)(2,1)S(1)}, bf16[1024,256]{1,0:T(8,128)(2,1)S(1)}) custom-call(bf16[256,2,2,256]{3,2,1,0:T(2,128)(2,1)S(1)} %copy-done.2, bf16[2,2,256,256]{3,2,1,0:T(8,128)(2,1)S(1)} %copy-done), custom_call_target="tpu_custom_call" | custom-call | tf_op jit(solution)/shard_map/adjoint_other/pallas_call | solution.py:17
  2.6 0.6 %collective-permute-start = (bf16[512,256]{1,0:T(8,128)(2,1)S(1)}, bf16[512,256]{1,0:T(8,128)(2,1)S(1)}, u32[]{:S(2)}, u32[]{:S(2)}) collective-permute-start(bf16[512,256]{1,0:T(8,128)(2,1)S(1)} %get-tuple-element.22), channel_id=1, source_target_pairs={{0,1},{1,0},{2,3},{3,2},{4,5},{5,4},{6,7},{7,6},{8,9},{9,8},{10,11... | collective-permute-start | bytes 786440 | tf_op jit(solution)/shard_map/ppermute | solution.py:212
  3.2 0.0 copy-done.1
  3.2 0.6 %adjoint_own.1.own_ref = f32[512,256]{1,0:T(8,128)S(1)} custom-call(bf16[1024,256]{1,0:T(8,128)(2,1)S(1)} %get-tuple-element.21.x_ref, bf16[2,2,256,256]{3,2,1,0:T(8,128)(2,1)S(1)} %copy-done.1), custom_call_target="tpu_custom_call" | custom-call | tf_op jit(solution)/shard_map/adjoint_own/pallas_call | solution.py:17
  3.8 0.6 %collective-permute-done.got_ref = bf16[512,256]{1,0:T(8,128)(2,1)S(1)} collective-permute-done((bf16[512,256]{1,0:T(8,128)(2,1)S(1)}, bf16[512,256]{1,0:T(8,128)(2,1)S(1)}, u32[]{:S(2)}, u32[]{:S(2)}) %collective-permute-start) | collective-permute-done | bytes 262176 | tf_op jit(solution)/shard_map/ppermute | solution.py:212
  4.4 2.9 %collective-permute-start.1 = (bf16[128,256]{1,0:T(8,128)(2,1)S(1)}, bf16[128,256]{1,0:T(8,128)(2,1)S(1)}, u32[]{:S(2)}, u32[]{:S(2)}) collective-permute-start(bf16[128,256]{1,0:T(8,128)(2,1)S(1)} %get-tuple-element.24), channel_id=1, source_target_pairs={{0,2},{1,3},{2,0},{3,1},{4,6},{5,7},{6,4},{7,5},{8,10},{9,11},{10,... | collective-permute-start | bytes 196616 | tf_op jit(solution)/shard_map/ppermute | solution.py:225
  7.3 1.5 %collective-permute-start.2 = (bf16[128,256]{1,0:T(8,128)(2,1)S(1)}, bf16[128,256]{1,0:T(8,128)(2,1)S(1)}, u32[]{:S(2)}, u32[]{:S(2)}) collective-permute-start(bf16[128,256]{1,0:T(8,128)(2,1)S(1)} %get-tuple-element.25), channel_id=1, source_target_pairs={{0,4},{1,5},{2,6},{3,7},{4,0},{5,1},{6,2},{7,3},{8,12},{9,13},{10,... | collective-permute-start | bytes 196616 | tf_op jit(solution)/shard_map/ppermute | solution.py:225
  8.8 0.0 collective-permute-start.3
  8.9 0.9 %collective-permute-done.1.refs_0_ = bf16[128,256]{1,0:T(8,128)(2,1)S(1)} collective-permute-done((bf16[128,256]{1,0:T(8,128)(2,1)S(1)}, bf16[128,256]{1,0:T(8,128)(2,1)S(1)}, u32[]{:S(2)}, u32[]{:S(2)}) %collective-permute-start.1) | collective-permute-done | bytes 65568 | tf_op jit(solution)/shard_map/ppermute | solution.py:225
  9.7 1.9 %collective-permute-done.2.refs_1_ = bf16[128,256]{1,0:T(8,128)(2,1)S(1)} collective-permute-done((bf16[128,256]{1,0:T(8,128)(2,1)S(1)}, bf16[128,256]{1,0:T(8,128)(2,1)S(1)}, u32[]{:S(2)}, u32[]{:S(2)}) %collective-permute-start.2) | collective-permute-done | bytes 65568 | tf_op jit(solution)/shard_map/ppermute | solution.py:225
  11.6 2.4 %collective-permute-done.3.refs_2_ = bf16[128,256]{1,0:T(8,128)(2,1)S(1)} collective-permute-done((bf16[128,256]{1,0:T(8,128)(2,1)S(1)}, bf16[128,256]{1,0:T(8,128)(2,1)S(1)}, u32[]{:S(2)}, u32[]{:S(2)}) %collective-permute-start.3) | collective-permute-done | bytes 65568 | tf_op jit(solution)/shard_map/ppermute | solution.py:225
  14.0 0.6 %collective-permute-start.4 = (bf16[128,256]{1,0:T(8,128)(2,1)S(1)}, bf16[128,256]{1,0:T(8,128)(2,1)S(1)}, u32[]{:S(2)}, u32[]{:S(2)}) collective-permute-start(bf16[128,256]{1,0:T(8,128)(2,1)S(1)} %sum.1.mine_ref), channel_id=1, source_target_pairs={{0,2},{1,3},{2,0},{3,1},{4,6},{5,7},{6,4},{7,5},{8,10},{9,11},{10,... | collective-permute-start | bytes 196616 | tf_op jit(solution)/shard_map/ppermute | solution.py:227
  14.6 0.4 collective-permute-start.5
  15.1 2.5 %collective-permute-start.6 = (bf16[128,256]{1,0:T(8,128)(2,1)S(1)}, bf16[128,256]{1,0:T(8,128)(2,1)S(1)}, u32[]{:S(2)}, u32[]{:S(2)}) collective-permute-start(bf16[128,256]{1,0:T(8,128)(2,1)S(1)} %sum.1.mine_ref), channel_id=1, source_target_pairs={{0,6},{1,7},{2,4},{3,5},{4,2},{5,3},{6,0},{7,1},{8,14},{9,15},{10,... | collective-permute-start | bytes 196616 | tf_op jit(solution)/shard_map/ppermute | solution.py:227
  17.6 0.8 %collective-permute-done.4.refs_0_ = bf16[128,256]{1,0:T(8,128)(2,1)S(1)} collective-permute-done((bf16[128,256]{1,0:T(8,128)(2,1)S(1)}, bf16[128,256]{1,0:T(8,128)(2,1)S(1)}, u32[]{:S(2)}, u32[]{:S(2)}) %collective-permute-start.4) | collective-permute-done | bytes 65568 | tf_op jit(solution)/shard_map/ppermute | solution.py:227
  18.4 0.5 %collective-permute-done.5.refs_1_ = bf16[128,256]{1,0:T(8,128)(2,1)S(1)} collective-permute-done((bf16[128,256]{1,0:T(8,128)(2,1)S(1)}, bf16[128,256]{1,0:T(8,128)(2,1)S(1)}, u32[]{:S(2)}, u32[]{:S(2)}) %collective-permute-start.5) | collective-permute-done | bytes 65568 | tf_op jit(solution)/shard_map/ppermute | solution.py:227
  18.9 1.3 %collective-permute-done.6.refs_2_ = bf16[128,256]{1,0:T(8,128)(2,1)S(1)} collective-permute-done((bf16[128,256]{1,0:T(8,128)(2,1)S(1)}, bf16[128,256]{1,0:T(8,128)(2,1)S(1)}, u32[]{:S(2)}, u32[]{:S(2)}) %collective-permute-start.6) | collective-permute-done | bytes 65568 | tf_op jit(solution)/shard_map/ppermute | solution.py:227
  20.3 0.0 copy-start.3
  20.3 0.1 collective-permute-start.12
  20.3 0.6 %copy-done.3 = f32[256]{0:T(256)S(1)} copy-done((f32[256]{0:T(256)S(1)}, f32[256]{0:T(256)}, u32[]{:S(2)}) %copy-start.3) | copy-done | bytes 1048
  20.9 0.4 edges.1
  21.3 3.6 %collective-permute-start.7 = (bf16[8,1024]{1,0:T(8,128)(2,1)S(1)}, bf16[8,1024]{1,0:T(8,128)(2,1)S(1)}, u32[]{:S(2)}, u32[]{:S(2)}) collective-permute-start(bf16[8,1024]{1,0:T(8,128)(2,1)S(1)} %get-tuple-element.27), channel_id=1, source_target_pairs={{0,8},{8,16},{16,24},{1,9},{9,17},{17,25},{2,10},{10,18},{18,26},{... | collective-permute-start | bytes 49160 | tf_op jit(solution)/shard_map/ppermute | solution.py:239
  24.9 1.3 %collective-permute-start.8 = (bf16[8,1024]{1,0:T(8,128)(2,1)S(1)}, bf16[8,1024]{1,0:T(8,128)(2,1)S(1)}, u32[]{:S(2)}, u32[]{:S(2)}) collective-permute-start(bf16[8,1024]{1,0:T(8,128)(2,1)S(1)} %get-tuple-element.28), channel_id=1, source_target_pairs={{8,0},{16,8},{24,16},{9,1},{17,9},{25,17},{10,2},{18,10},{26,18},{... | collective-permute-start | bytes 49160 | tf_op jit(solution)/shard_map/ppermute | solution.py:240
  26.2 0.1 collective-permute-done.7.low_ref
  26.3 4.2 %collective-permute-done.8.high_ref = bf16[8,1024]{1,0:T(8,128)(2,1)S(1)} collective-permute-done((bf16[8,1024]{1,0:T(8,128)(2,1)S(1)}, bf16[8,1024]{1,0:T(8,128)(2,1)S(1)}, u32[]{:S(2)}, u32[]{:S(2)}) %collective-permute-start.8) | collective-permute-done | bytes 16416 | tf_op jit(solution)/shard_map/ppermute | solution.py:240
  30.5 0.5 %operator.1.k_ref = bf16[2,2,256,256]{3,2,1,0:T(8,128)(2,1)S(1)} custom-call(bf16[2,2,256,256]{3,2,1,0:T(8,128)(2,1)S(1)} %copy-done.1, f32[1,256]{1,0:T(1,128)S(1)} %bitcast.2, bf16[8,1024]{1,0:T(8,128)(2,1)S(1)} %collective-permute-done.7.low_ref, bf16[8,1024]{1,0:T(8,128)(2,1)S(1)} %collective-permute-done.8.high_ref), custom_call_target="tpu_custom_call" | custom-call | tf_op jit(solution)/shard_map/operator/pallas_call | solution.py:17
  31.1 0.3 predict_own.1
  31.4 2.7 %collective-permute-start.10 = (bf16[128,256]{1,0:T(8,128)(2,1)S(1)}, bf16[128,256]{1,0:T(8,128)(2,1)S(1)}, u32[]{:S(2)}, u32[]{:S(2)}) collective-permute-start(bf16[128,256]{1,0:T(8,128)(2,1)S(1)} %get-tuple-element.31), channel_id=1, source_target_pairs={{0,16},{8,24},{16,0},{24,8},{1,17},{9,25},{17,1},{25,9},{2,18},{10... | collective-permute-start | bytes 196616 | tf_op jit(solution)/shard_map/ppermute | solution.py:253
  34.0 1.3 %collective-permute-start.11 = (bf16[128,256]{1,0:T(8,128)(2,1)S(1)}, bf16[128,256]{1,0:T(8,128)(2,1)S(1)}, u32[]{:S(2)}, u32[]{:S(2)}) collective-permute-start(bf16[128,256]{1,0:T(8,128)(2,1)S(1)} %get-tuple-element.32), channel_id=1, source_target_pairs={{0,24},{8,16},{16,8},{24,0},{1,25},{9,17},{17,9},{25,1},{2,26},{10... | collective-permute-start | bytes 196616 | tf_op jit(solution)/shard_map/ppermute | solution.py:253
  35.4 0.0 collective-permute-start.9
  35.4 0.0 collective-permute-done.12.a_ref
  35.4 0.3 predict_other.1
  35.7 2.1 %collective-permute-start.13 = (bf16[128,256]{1,0:T(8,128)(2,1)S(1)}, bf16[128,256]{1,0:T(8,128)(2,1)S(1)}, u32[]{:S(2)}, u32[]{:S(2)}) collective-permute-start(bf16[128,256]{1,0:T(8,128)(2,1)S(1)} %get-tuple-element.34), channel_id=1, source_target_pairs={{0,8},{8,0},{16,24},{24,16},{1,9},{9,1},{17,25},{25,17},{2,10},{10... | collective-permute-start | bytes 196616 | tf_op jit(solution)/shard_map/ppermute | solution.py:253
  37.8 1.1 %collective-permute-start.14 = (bf16[128,256]{1,0:T(8,128)(2,1)S(1)}, bf16[128,256]{1,0:T(8,128)(2,1)S(1)}, u32[]{:S(2)}, u32[]{:S(2)}) collective-permute-start(bf16[128,256]{1,0:T(8,128)(2,1)S(1)} %get-tuple-element.35), channel_id=1, source_target_pairs={{0,16},{8,24},{16,0},{24,8},{1,17},{9,25},{17,1},{25,9},{2,18},{10... | collective-permute-start | bytes 196616 | tf_op jit(solution)/shard_map/ppermute | solution.py:253
  38.9 0.0 collective-permute-done.10.refs_2_
  38.9 0.0 copy-start.4
  38.9 1.5 %collective-permute-start.15 = (bf16[128,256]{1,0:T(8,128)(2,1)S(1)}, bf16[128,256]{1,0:T(8,128)(2,1)S(1)}, u32[]{:S(2)}, u32[]{:S(2)}) collective-permute-start(bf16[128,256]{1,0:T(8,128)(2,1)S(1)} %get-tuple-element.36), channel_id=1, source_target_pairs={{0,24},{8,16},{16,8},{24,0},{1,25},{9,17},{17,9},{25,1},{2,26},{10... | collective-permute-start | bytes 196616 | tf_op jit(solution)/shard_map/ppermute | solution.py:253
  40.4 0.5 %collective-permute-done.11.refs_3_ = bf16[128,256]{1,0:T(8,128)(2,1)S(1)} collective-permute-done((bf16[128,256]{1,0:T(8,128)(2,1)S(1)}, bf16[128,256]{1,0:T(8,128)(2,1)S(1)}, u32[]{:S(2)}, u32[]{:S(2)}) %collective-permute-start.11) | collective-permute-done | bytes 65568 | tf_op jit(solution)/shard_map/ppermute | solution.py:253
  40.9 0.0 collective-permute-done.9.refs_1_
  40.9 1.3 %collective-permute-done.13.refs_5_ = bf16[128,256]{1,0:T(8,128)(2,1)S(1)} collective-permute-done((bf16[128,256]{1,0:T(8,128)(2,1)S(1)}, bf16[128,256]{1,0:T(8,128)(2,1)S(1)}, u32[]{:S(2)}, u32[]{:S(2)}) %collective-permute-start.13) | collective-permute-done | bytes 65568 | tf_op jit(solution)/shard_map/ppermute | solution.py:253
  42.2 0.8 %collective-permute-done.14.refs_6_ = bf16[128,256]{1,0:T(8,128)(2,1)S(1)} collective-permute-done((bf16[128,256]{1,0:T(8,128)(2,1)S(1)}, bf16[128,256]{1,0:T(8,128)(2,1)S(1)}, u32[]{:S(2)}, u32[]{:S(2)}) %collective-permute-start.14) | collective-permute-done | bytes 65568 | tf_op jit(solution)/shard_map/ppermute | solution.py:253
  43.0 2.1 %collective-permute-done.15.refs_7_ = bf16[128,256]{1,0:T(8,128)(2,1)S(1)} collective-permute-done((bf16[128,256]{1,0:T(8,128)(2,1)S(1)}, bf16[128,256]{1,0:T(8,128)(2,1)S(1)}, u32[]{:S(2)}, u32[]{:S(2)}) %collective-permute-start.15) | collective-permute-done | bytes 65568 | tf_op jit(solution)/shard_map/ppermute | solution.py:253
  45.1 0.0 copy-done.4
  45.1 0.2 final.1
  45.2 0.7 %copy.5 = f32[64,2,2,256]{3,2,1,0:T(2,128)} copy(f32[64,2,2,256]{3,2,1,0:T(2,128)S(1)} %final.1) | data formatting | bytes 524288
  (3 shorter events, 0.1 us)
Async XLA Ops:
  0.0 1.0 %copy-start = (bf16[2,2,256,256]{3,2,1,0:T(8,128)(2,1)S(1)}, bf16[2,2,256,256]{3,2,1,0:T(8,128)(2,1)}, u32[]{:S(2)}) copy-start(bf16[2,2,256,256]{3,2,1,0:T(8,128)(2,1)} %k_ref.7) | copy-start | bytes 1572868
  1.0 1.0 %copy-start.2 = (bf16[256,2,2,256]{3,2,1,0:T(2,128)(2,1)S(1)}, bf16[256,2,2,256]{3,2,1,0:T(2,128)(2,1)}, u32[]{:S(2)}) copy-start(bf16[256,2,2,256]{3,2,1,0:T(2,128)(2,1)} %x_ref.1) | copy-start | bytes 1572868
  2.1 1.1 %copy-start.1 = (bf16[2,2,256,256]{3,2,1,0:T(8,128)(2,1)S(1)}, bf16[2,2,256,256]{3,2,1,0:T(8,128)(2,1)}, u32[]{:S(2)}) copy-start(bf16[2,2,256,256]{3,2,1,0:T(8,128)(2,1)} %k_ref.7) | copy-start | bytes 1572868
  2.6 1.7 %collective-permute-start = (bf16[512,256]{1,0:T(8,128)(2,1)S(1)}, bf16[512,256]{1,0:T(8,128)(2,1)S(1)}, u32[]{:S(2)}, u32[]{:S(2)}) collective-permute-start(bf16[512,256]{1,0:T(8,128)(2,1)S(1)} %get-tuple-element.22), channel_id=1, source_target_pairs={{0,1},{1,0},{2,3},{3,2},{4,5},{5,4},{6,7},{7,6},{8,9},{9,8},{10,11... | collective-permute-start | bytes 786440 | tf_op jit(solution)/shard_map/ppermute | solution.py:212
  4.4 5.3 %collective-permute-start.1 = (bf16[128,256]{1,0:T(8,128)(2,1)S(1)}, bf16[128,256]{1,0:T(8,128)(2,1)S(1)}, u32[]{:S(2)}, u32[]{:S(2)}) collective-permute-start(bf16[128,256]{1,0:T(8,128)(2,1)S(1)} %get-tuple-element.24), channel_id=1, source_target_pairs={{0,2},{1,3},{2,0},{3,1},{4,6},{5,7},{6,4},{7,5},{8,10},{9,11},{10,... | collective-permute-start | bytes 196616 | tf_op jit(solution)/shard_map/ppermute | solution.py:225
  7.3 4.3 %collective-permute-start.2 = (bf16[128,256]{1,0:T(8,128)(2,1)S(1)}, bf16[128,256]{1,0:T(8,128)(2,1)S(1)}, u32[]{:S(2)}, u32[]{:S(2)}) collective-permute-start(bf16[128,256]{1,0:T(8,128)(2,1)S(1)} %get-tuple-element.25), channel_id=1, source_target_pairs={{0,4},{1,5},{2,6},{3,7},{4,0},{5,1},{6,2},{7,3},{8,12},{9,13},{10,... | collective-permute-start | bytes 196616 | tf_op jit(solution)/shard_map/ppermute | solution.py:225
  8.8 5.2 %collective-permute-start.3 = (bf16[128,256]{1,0:T(8,128)(2,1)S(1)}, bf16[128,256]{1,0:T(8,128)(2,1)S(1)}, u32[]{:S(2)}, u32[]{:S(2)}) collective-permute-start(bf16[128,256]{1,0:T(8,128)(2,1)S(1)} %get-tuple-element.26), channel_id=1, source_target_pairs={{0,6},{1,7},{2,4},{3,5},{4,2},{5,3},{6,0},{7,1},{8,14},{9,15},{10,... | collective-permute-start | bytes 196616 | tf_op jit(solution)/shard_map/ppermute | solution.py:225
  14.0 4.3 %collective-permute-start.4 = (bf16[128,256]{1,0:T(8,128)(2,1)S(1)}, bf16[128,256]{1,0:T(8,128)(2,1)S(1)}, u32[]{:S(2)}, u32[]{:S(2)}) collective-permute-start(bf16[128,256]{1,0:T(8,128)(2,1)S(1)} %sum.1.mine_ref), channel_id=1, source_target_pairs={{0,2},{1,3},{2,0},{3,1},{4,6},{5,7},{6,4},{7,5},{8,10},{9,11},{10,... | collective-permute-start | bytes 196616 | tf_op jit(solution)/shard_map/ppermute | solution.py:227
  14.6 4.3 %collective-permute-start.5 = (bf16[128,256]{1,0:T(8,128)(2,1)S(1)}, bf16[128,256]{1,0:T(8,128)(2,1)S(1)}, u32[]{:S(2)}, u32[]{:S(2)}) collective-permute-start(bf16[128,256]{1,0:T(8,128)(2,1)S(1)} %sum.1.mine_ref), channel_id=1, source_target_pairs={{0,4},{1,5},{2,6},{3,7},{4,0},{5,1},{6,2},{7,3},{8,12},{9,13},{10,... | collective-permute-start | bytes 196616 | tf_op jit(solution)/shard_map/ppermute | solution.py:227
  15.1 5.2 %collective-permute-start.6 = (bf16[128,256]{1,0:T(8,128)(2,1)S(1)}, bf16[128,256]{1,0:T(8,128)(2,1)S(1)}, u32[]{:S(2)}, u32[]{:S(2)}) collective-permute-start(bf16[128,256]{1,0:T(8,128)(2,1)S(1)} %sum.1.mine_ref), channel_id=1, source_target_pairs={{0,6},{1,7},{2,4},{3,5},{4,2},{5,3},{6,0},{7,1},{8,14},{9,15},{10,... | collective-permute-start | bytes 196616 | tf_op jit(solution)/shard_map/ppermute | solution.py:227
  20.3 0.7 %copy-start.3 = (f32[256]{0:T(256)S(1)}, f32[256]{0:T(256)}, u32[]{:S(2)}) copy-start(f32[256]{0:T(256)} %param.7) | copy-start | bytes 3076
  20.3 15.1 %collective-permute-start.12 = (bf16[512,256]{1,0:T(8,128)(2,1)S(1)}, bf16[512,256]{1,0:T(8,128)(2,1)S(1)}, u32[]{:S(2)}, u32[]{:S(2)}) collective-permute-start(bf16[512,256]{1,0:T(8,128)(2,1)S(1)} %join.1.a_ref), channel_id=1, source_target_pairs={{0,1},{1,0},{2,3},{3,2},{4,5},{5,4},{6,7},{7,6},{8,9},{9,8},{10,11... | collective-permute-start | bytes 786440 | tf_op jit(solution)/shard_map/ppermute | solution.py:229
  21.3 5.0 %collective-permute-start.7 = (bf16[8,1024]{1,0:T(8,128)(2,1)S(1)}, bf16[8,1024]{1,0:T(8,128)(2,1)S(1)}, u32[]{:S(2)}, u32[]{:S(2)}) collective-permute-start(bf16[8,1024]{1,0:T(8,128)(2,1)S(1)} %get-tuple-element.27), channel_id=1, source_target_pairs={{0,8},{8,16},{16,24},{1,9},{9,17},{17,25},{2,10},{10,18},{18,26},{... | collective-permute-start | bytes 49160 | tf_op jit(solution)/shard_map/ppermute | solution.py:239
  24.9 5.6 %collective-permute-start.8 = (bf16[8,1024]{1,0:T(8,128)(2,1)S(1)}, bf16[8,1024]{1,0:T(8,128)(2,1)S(1)}, u32[]{:S(2)}, u32[]{:S(2)}) collective-permute-start(bf16[8,1024]{1,0:T(8,128)(2,1)S(1)} %get-tuple-element.28), channel_id=1, source_target_pairs={{8,0},{16,8},{24,16},{9,1},{17,9},{25,17},{10,2},{18,10},{26,18},{... | collective-permute-start | bytes 49160 | tf_op jit(solution)/shard_map/ppermute | solution.py:240
  31.4 7.5 %collective-permute-start.10 = (bf16[128,256]{1,0:T(8,128)(2,1)S(1)}, bf16[128,256]{1,0:T(8,128)(2,1)S(1)}, u32[]{:S(2)}, u32[]{:S(2)}) collective-permute-start(bf16[128,256]{1,0:T(8,128)(2,1)S(1)} %get-tuple-element.31), channel_id=1, source_target_pairs={{0,16},{8,24},{16,0},{24,8},{1,17},{9,25},{17,1},{25,9},{2,18},{10... | collective-permute-start | bytes 196616 | tf_op jit(solution)/shard_map/ppermute | solution.py:253
  34.0 6.9 %collective-permute-start.11 = (bf16[128,256]{1,0:T(8,128)(2,1)S(1)}, bf16[128,256]{1,0:T(8,128)(2,1)S(1)}, u32[]{:S(2)}, u32[]{:S(2)}) collective-permute-start(bf16[128,256]{1,0:T(8,128)(2,1)S(1)} %get-tuple-element.32), channel_id=1, source_target_pairs={{0,24},{8,16},{16,8},{24,0},{1,25},{9,17},{17,9},{25,1},{2,26},{10... | collective-permute-start | bytes 196616 | tf_op jit(solution)/shard_map/ppermute | solution.py:253
  35.4 5.5 %collective-permute-start.9 = (bf16[128,256]{1,0:T(8,128)(2,1)S(1)}, bf16[128,256]{1,0:T(8,128)(2,1)S(1)}, u32[]{:S(2)}, u32[]{:S(2)}) collective-permute-start(bf16[128,256]{1,0:T(8,128)(2,1)S(1)} %get-tuple-element.30), channel_id=1, source_target_pairs={{0,8},{8,0},{16,24},{24,16},{1,9},{9,1},{17,25},{25,17},{2,10},{10... | collective-permute-start | bytes 196616 | tf_op jit(solution)/shard_map/ppermute | solution.py:253
  35.7 6.5 %collective-permute-start.13 = (bf16[128,256]{1,0:T(8,128)(2,1)S(1)}, bf16[128,256]{1,0:T(8,128)(2,1)S(1)}, u32[]{:S(2)}, u32[]{:S(2)}) collective-permute-start(bf16[128,256]{1,0:T(8,128)(2,1)S(1)} %get-tuple-element.34), channel_id=1, source_target_pairs={{0,8},{8,0},{16,24},{24,16},{1,9},{9,1},{17,25},{25,17},{2,10},{10... | collective-permute-start | bytes 196616 | tf_op jit(solution)/shard_map/ppermute | solution.py:253
  37.8 5.2 %collective-permute-start.14 = (bf16[128,256]{1,0:T(8,128)(2,1)S(1)}, bf16[128,256]{1,0:T(8,128)(2,1)S(1)}, u32[]{:S(2)}, u32[]{:S(2)}) collective-permute-start(bf16[128,256]{1,0:T(8,128)(2,1)S(1)} %get-tuple-element.35), channel_id=1, source_target_pairs={{0,16},{8,24},{16,0},{24,8},{1,17},{9,25},{17,1},{25,9},{2,18},{10... | collective-permute-start | bytes 196616 | tf_op jit(solution)/shard_map/ppermute | solution.py:253
  38.9 6.2 %copy-start.4 = (f32[2,256]{1,0:T(2,128)S(1)}, f32[2,256]{1,0:T(2,128)}, u32[]{:S(2)}) copy-start(f32[2,256]{1,0:T(2,128)} %noise_ref.1) | copy-start | bytes 6148
  38.9 6.2 %collective-permute-start.15 = (bf16[128,256]{1,0:T(8,128)(2,1)S(1)}, bf16[128,256]{1,0:T(8,128)(2,1)S(1)}, u32[]{:S(2)}, u32[]{:S(2)}) collective-permute-start(bf16[128,256]{1,0:T(8,128)(2,1)S(1)} %get-tuple-element.36), channel_id=1, source_target_pairs={{0,24},{8,16},{16,8},{24,0},{1,25},{9,17},{17,9},{25,1},{2,26},{10... | collective-permute-start | bytes 196616 | tf_op jit(solution)/shard_map/ppermute | solution.py:253

commit v3 on v2

--- a/solution.py
+++ b/solution.py
@@ -7,16 +7,16 @@
 from jax.experimental.pallas import tpu as pltpu
 from jax.sharding import PartitionSpec as P
 
+
 BF = jnp.bfloat16
 F32 = jnp.float32
 LANES = 128
 VMEM = pl.BlockSpec(memory_space=pltpu.VMEM)
 
 
-def call(body, name, ins, outs, scratch=()):
+def call(body, ins, outs, scratch=()):
     return pl.pallas_call(
         body,
-        name=name,
         in_specs=[VMEM] * len(ins),
         out_specs=[VMEM] * len(outs),
         out_shape=[pltpu.VMEM(*o) for o in outs],
@@ -135,7 +135,11 @@
         ref[...] = piece(jnp.bitwise_xor(me, step + 1)).astype(BF)
 
 
-def sum_body(keep_ref, *refs):
+def fence_body(d_ref, o_ref):
+    o_ref[...] = jnp.zeros_like(o_ref)
+
+
+def sum_body(keep_ref, fence_ref, *refs):
     total = keep_ref[...]
     for ref in refs[:-1]:
         total = total + ref[...].astype(F32)
@@ -196,21 +200,15 @@
     out_ref[...] = values.reshape(out_ref.shape)
 
 
-def all_sum(probes, kernel):
+def all_sum(probes, kernel, coef):
     rows = 2 * probes.shape[0]
     width = kernel.shape[3]
     count = lax.axis_size("col")
     flat = (2 * rows, probes.shape[3])
     scratch = (pltpu.VMEM((2 * width // LANES, 2 * rows, LANES), F32),)
-    other, x = call(
-        functools.partial(adjoint_body, True),
-        "adjoint_other",
-        (probes, kernel),
-        [((rows, width), BF), (flat, BF)],
-        scratch,
-    )
+    other, x = call(functools.partial(adjoint_body, True), (probes, kernel), [((rows, width), BF), (flat, BF)], scratch)
     got = lax.ppermute(other, "col", pair_perm("col", 1))
-    own = call(functools.partial(adjoint_body, False), "adjoint_own", (x, kernel), [((rows, width), F32)], scratch)[0]
+    own = call(functools.partial(adjoint_body, False), (x, kernel), [((rows, width), F32)], scratch)[0]
     chips = count // 2
     if chips > 4:
         part = own + got.astype(F32)
@@ -219,33 +217,31 @@
         mine = lax.dynamic_index_in_dim(both, parity(), 0, keepdims=False)
         return x, mine, lax.dynamic_index_in_dim(both, 1 - parity(), 0, keepdims=False)
     size = rows // chips
-    keep, *sends = call(
-        split_body, "split", (own, got), [((size, width), F32)] + [((size, width), BF)] * (chips - 1)
-    )
+    keep, *sends = call(split_body, (own, got), [((size, width), F32)] + [((size, width), BF)] * (chips - 1))
     got = [lax.ppermute(v, "col", pair_perm("col", 2 * (d + 1))) for d, v in enumerate(sends)]
-    mine = call(sum_body, "sum", (keep, *got), [((size, width), BF)])[0]
+    fence = call(fence_body, (coef,), [((8, LANES), F32)])[0]
+    mine = call(sum_body, (keep, fence, *got), [((size, width), BF)])[0]
     got = [lax.ppermute(mine, "col", pair_perm("col", 2 * (d + 1))) for d in range(chips - 1)]
-    mine = call(join_body, "join", (mine, *got), [((rows, width), BF)])[0]
+    mine = call(join_body, (mine, *got), [((rows, width), BF)])[0]
     return x, mine, lax.ppermute(mine, "col", pair_perm("col", 1))
 
 
-def shards(kernel, probes, noise_var, prior_diag):
+def apply(kernel, probes, noise_var, prior_diag):
     rows_own = kernel.shape[2]
     width = kernel.shape[3]
     count = probes.shape[0]
     blocks = lax.axis_size("row")
     coef = prior_diag[None, :]
-    low, high = call(edges_body, "edges", (kernel, coef), [((8, 4 * rows_own), BF)] * 2)
+    low, high = call(edges_body, (kernel, coef), [((8, 4 * rows_own), BF)] * 2)
     low = lax.ppermute(low, "row", [(i, i + 1) for i in range(blocks - 1)])
     high = lax.ppermute(high, "row", [(i + 1, i) for i in range(blocks - 1)])
-    x, mine, other = all_sum(probes, kernel)
-    operator = call(operator_body, "operator", (kernel, coef, low, high), [((2, 2, width, rows_own), BF)])[0]
+    x, mine, other = all_sum(probes, kernel, coef)
+    operator = call(operator_body, (kernel, coef, low, high), [((2, 2, width, rows_own), BF)])[0]
     size = count // blocks
     groups = []
     for swap, field in ((False, mine), (True, other)):
         keep, *sends = call(
             functools.partial(predict_body, swap),
-            "predict_other" if swap else "predict_own",
             (field, operator),
             [((2 * size, rows_own), F32)] + [((2 * size, rows_own), BF)] * (blocks - 1),
         )
@@ -253,7 +249,6 @@
         groups += [lax.ppermute(v, "row", pair_perm("row", d + 1)) for d, v in enumerate(sends)]
     out = call(
         functools.partial(final_body, blocks - 1),
-        "final",
         (x, noise_var, *groups),
         [((size,) + probes.shape[1:3] + (rows_own,), F32)],
         (pltpu.VMEM((rows_own // LANES, 4 * size, LANES), F32),),
@@ -264,4 +259,4 @@
 def solution(mesh):
     in_specs = (P(None, None, "col", "row"), P(None, None, None, "col"), P(None, "col"), P("row"))
     out_specs = P("row", None, None, "col")
-    return jax.shard_map(shards, mesh=mesh, in_specs=in_specs, out_specs=out_specs, check_vma=False)
+    return jax.shard_map(apply, mesh=mesh, in_specs=in_specs, out_specs=out_specs, check_vma=False)

time: 46.2 us -> 45.5 us (0.985)
  waiting for transfers between devices: 17.4 us -> 16.7 us
    ppermute x3, waiting for transfers between devices: 5.14 us -> 4.48 us  [all_sum(): lax.ppermute(v, 'col', pair_perm('col', 2 * (d + 1)))]
    pallas_call x10 -> x11, Pallas kernels: 2.9 us -> 2.9 us  [call(): pl.pallas_call(body, in_specs=[VMEM] * len(ins), out_specs=[VMEM] * len(o...]
  transfers between devices with their start and end apart: 16 -> 16, of which waited for: 13 -> 14; matrix products, arithmetic and copies ran while one was open for 0% -> 0% of each run, Pallas kernels for 5% -> 5%
where the time goes in v3:
time: 45.5 us; the launch traced here: 45.2 us
  starting transfers between devices  22.1 us (49%)
  waiting for transfers between devices  16.7 us (37%)
  local copies, waits for them, and re-layouts  3.45 us (8%)
  Pallas kernels  2.9 us (6%)
    ppermute x6, starting transfers between devices, apply(): lax.ppermute(v, 'row', pair_perm('row', d + 1))  8.64 us
    ppermute x6, waiting for transfers between devices, apply(): lax.ppermute(v, 'row', pair_perm('row', d + 1))  4.61 us
    ppermute x3, waiting for transfers between devices, all_sum(): lax.ppermute(v, 'col', pair_perm('col', 2 * (d + 1)))  4.48 us
    ppermute x3, starting transfers between devices, all_sum(): lax.ppermute(v, 'col', pair_perm('col', 2 * (d + 1)))  4.46 us
    ppermute x1, waiting for transfers between devices, apply(): high = lax.ppermute(high, 'row', [(i + 1, i) for i in range(blocks - 1)])  4.21 us
    ppermute x1, starting transfers between devices, apply(): low = lax.ppermute(low, 'row', [(i, i + 1) for i in range(blocks - 1)])  3.57 us
    ppermute x3, starting transfers between devices, all_sum(): lax.ppermute(mine, 'col', pair_perm('col', 2 * (d + 1)))  3.55 us
    unnamed x11, local copies, waits for them, and re-layouts  3.45 us
  transfers between devices with their start and end apart: 16, of which 14 were waited for; matrix products, arithmetic and copies ran while one was open for 0% of the time, Pallas kernels for 5%

profile of v3, /device:TPU:0, one launch (start us, length us, event | category | flops | bytes accessed | tf_op | source)
XLA Modules:
  0.0 45.2 jit_solution(17923941770762673351)
XLA Ops:
  0.0 0.0 copy-start
  0.0 1.0 %copy-done = bf16[2,2,256,256]{3,2,1,0:T(8,128)(2,1)S(1)} copy-done((bf16[2,2,256,256]{3,2,1,0:T(8,128)(2,1)S(1)}, bf16[2,2,256,256]{3,2,1,0:T(8,128)(2,1)}, u32[]{:S(2)}) %copy-start) | copy-done | bytes 524312
  1.0 0.0 copy-start.2
  1.0 1.0 %copy-done.2 = bf16[256,2,2,256]{3,2,1,0:T(2,128)(2,1)S(1)} copy-done((bf16[256,2,2,256]{3,2,1,0:T(2,128)(2,1)S(1)}, bf16[256,2,2,256]{3,2,1,0:T(2,128)(2,1)}, u32[]{:S(2)}) %copy-start.2) | copy-done | bytes 524312
  2.1 0.0 copy-start.1
  2.1 0.5 %shard_map.46 = (bf16[512,256]{1,0:T(8,128)(2,1)S(1)}, bf16[1024,256]{1,0:T(8,128)(2,1)S(1)}) custom-call(bf16[256,2,2,256]{3,2,1,0:T(2,128)(2,1)S(1)} %copy-done.2, bf16[2,2,256,256]{3,2,1,0:T(8,128)(2,1)S(1)} %copy-done), custom_call_target="tpu_custom_call" | custom-call | tf_op jit(solution)/shard_map/pallas_call | solution.py:18
  2.6 0.6 %collective-permute-start = (bf16[512,256]{1,0:T(8,128)(2,1)S(1)}, bf16[512,256]{1,0:T(8,128)(2,1)S(1)}, u32[]{:S(2)}, u32[]{:S(2)}) collective-permute-start(bf16[512,256]{1,0:T(8,128)(2,1)S(1)} %get-tuple-element.22), channel_id=1, source_target_pairs={{0,1},{1,0},{2,3},{3,2},{4,5},{5,4},{6,7},{7,6},{8,9},{9,8},{10,11... | collective-permute-start | bytes 786440 | tf_op jit(solution)/shard_map/ppermute | solution.py:210
  3.2 0.0 copy-done.1
  3.2 0.6 %shard_map.47.own_ref = f32[512,256]{1,0:T(8,128)S(1)} custom-call(bf16[1024,256]{1,0:T(8,128)(2,1)S(1)} %get-tuple-element.21.x_ref, bf16[2,2,256,256]{3,2,1,0:T(8,128)(2,1)S(1)} %copy-done.1), custom_call_target="tpu_custom_call" | custom-call | tf_op jit(solution)/shard_map/pallas_call | solution.py:18
  3.8 0.6 %collective-permute-done.got_ref = bf16[512,256]{1,0:T(8,128)(2,1)S(1)} collective-permute-done((bf16[512,256]{1,0:T(8,128)(2,1)S(1)}, bf16[512,256]{1,0:T(8,128)(2,1)S(1)}, u32[]{:S(2)}, u32[]{:S(2)}) %collective-permute-start) | collective-permute-done | bytes 262176 | tf_op jit(solution)/shard_map/ppermute | solution.py:210
  4.4 2.9 %collective-permute-start.1 = (bf16[128,256]{1,0:T(8,128)(2,1)S(1)}, bf16[128,256]{1,0:T(8,128)(2,1)S(1)}, u32[]{:S(2)}, u32[]{:S(2)}) collective-permute-start(bf16[128,256]{1,0:T(8,128)(2,1)S(1)} %get-tuple-element.24), channel_id=1, source_target_pairs={{0,2},{1,3},{2,0},{3,1},{4,6},{5,7},{6,4},{7,5},{8,10},{9,11},{10,... | collective-permute-start | bytes 196616 | tf_op jit(solution)/shard_map/ppermute | solution.py:221
  7.3 1.5 %collective-permute-start.2 = (bf16[128,256]{1,0:T(8,128)(2,1)S(1)}, bf16[128,256]{1,0:T(8,128)(2,1)S(1)}, u32[]{:S(2)}, u32[]{:S(2)}) collective-permute-start(bf16[128,256]{1,0:T(8,128)(2,1)S(1)} %get-tuple-element.25), channel_id=1, source_target_pairs={{0,4},{1,5},{2,6},{3,7},{4,0},{5,1},{6,2},{7,3},{8,12},{9,13},{10,... | collective-permute-start | bytes 196616 | tf_op jit(solution)/shard_map/ppermute | solution.py:221
  8.8 0.0 copy-start.3
  8.8 0.0 collective-permute-start.3
  8.9 0.7 %copy-done.3 = f32[256]{0:T(256)S(1)} copy-done((f32[256]{0:T(256)S(1)}, f32[256]{0:T(256)}, u32[]{:S(2)}) %copy-start.3) | copy-done | bytes 1048
  9.5 0.2 collective-permute-done.1.refs_0_
  9.7 1.9 %collective-permute-done.2.refs_1_ = bf16[128,256]{1,0:T(8,128)(2,1)S(1)} collective-permute-done((bf16[128,256]{1,0:T(8,128)(2,1)S(1)}, bf16[128,256]{1,0:T(8,128)(2,1)S(1)}, u32[]{:S(2)}, u32[]{:S(2)}) %collective-permute-start.2) | collective-permute-done | bytes 65568 | tf_op jit(solution)/shard_map/ppermute | solution.py:221
  11.6 2.4 %collective-permute-done.3.refs_2_ = bf16[128,256]{1,0:T(8,128)(2,1)S(1)} collective-permute-done((bf16[128,256]{1,0:T(8,128)(2,1)S(1)}, bf16[128,256]{1,0:T(8,128)(2,1)S(1)}, u32[]{:S(2)}, u32[]{:S(2)}) %collective-permute-start.3) | collective-permute-done | bytes 65568 | tf_op jit(solution)/shard_map/ppermute | solution.py:221
  14.0 0.6 %collective-permute-start.4 = (bf16[128,256]{1,0:T(8,128)(2,1)S(1)}, bf16[128,256]{1,0:T(8,128)(2,1)S(1)}, u32[]{:S(2)}, u32[]{:S(2)}) collective-permute-start(bf16[128,256]{1,0:T(8,128)(2,1)S(1)} %shard_map.50.mine_ref), channel_id=1, source_target_pairs={{0,2},{1,3},{2,0},{3,1},{4,6},{5,7},{6,4},{7,5},{8,10},{9,11},{10,... | collective-permute-start | bytes 196616 | tf_op jit(solution)/shard_map/ppermute | solution.py:224
  14.6 0.4 collective-permute-start.5
  15.1 2.5 %collective-permute-start.6 = (bf16[128,256]{1,0:T(8,128)(2,1)S(1)}, bf16[128,256]{1,0:T(8,128)(2,1)S(1)}, u32[]{:S(2)}, u32[]{:S(2)}) collective-permute-start(bf16[128,256]{1,0:T(8,128)(2,1)S(1)} %shard_map.50.mine_ref), channel_id=1, source_target_pairs={{0,6},{1,7},{2,4},{3,5},{4,2},{5,3},{6,0},{7,1},{8,14},{9,15},{10,... | collective-permute-start | bytes 196616 | tf_op jit(solution)/shard_map/ppermute | solution.py:224
  17.6 0.8 %collective-permute-done.4.refs_0_ = bf16[128,256]{1,0:T(8,128)(2,1)S(1)} collective-permute-done((bf16[128,256]{1,0:T(8,128)(2,1)S(1)}, bf16[128,256]{1,0:T(8,128)(2,1)S(1)}, u32[]{:S(2)}, u32[]{:S(2)}) %collective-permute-start.4) | collective-permute-done | bytes 65568 | tf_op jit(solution)/shard_map/ppermute | solution.py:224
  18.4 0.5 %collective-permute-done.5.refs_1_ = bf16[128,256]{1,0:T(8,128)(2,1)S(1)} collective-permute-done((bf16[128,256]{1,0:T(8,128)(2,1)S(1)}, bf16[128,256]{1,0:T(8,128)(2,1)S(1)}, u32[]{:S(2)}, u32[]{:S(2)}) %collective-permute-start.5) | collective-permute-done | bytes 65568 | tf_op jit(solution)/shard_map/ppermute | solution.py:224
  18.9 1.3 %collective-permute-done.6.refs_2_ = bf16[128,256]{1,0:T(8,128)(2,1)S(1)} collective-permute-done((bf16[128,256]{1,0:T(8,128)(2,1)S(1)}, bf16[128,256]{1,0:T(8,128)(2,1)S(1)}, u32[]{:S(2)}, u32[]{:S(2)}) %collective-permute-start.6) | collective-permute-done | bytes 65568 | tf_op jit(solution)/shard_map/ppermute | solution.py:224
  20.3 0.1 collective-permute-start.12
  20.3 0.4 shard_map.52
  20.7 3.6 %collective-permute-start.7 = (bf16[8,1024]{1,0:T(8,128)(2,1)S(1)}, bf16[8,1024]{1,0:T(8,128)(2,1)S(1)}, u32[]{:S(2)}, u32[]{:S(2)}) collective-permute-start(bf16[8,1024]{1,0:T(8,128)(2,1)S(1)} %get-tuple-element.27), channel_id=1, source_target_pairs={{0,8},{8,16},{16,24},{1,9},{9,17},{17,25},{2,10},{10,18},{18,26},{... | collective-permute-start | bytes 49160 | tf_op jit(solution)/shard_map/ppermute | solution.py:236
  24.3 1.3 %collective-permute-start.8 = (bf16[8,1024]{1,0:T(8,128)(2,1)S(1)}, bf16[8,1024]{1,0:T(8,128)(2,1)S(1)}, u32[]{:S(2)}, u32[]{:S(2)}) collective-permute-start(bf16[8,1024]{1,0:T(8,128)(2,1)S(1)} %get-tuple-element.28), channel_id=1, source_target_pairs={{8,0},{16,8},{24,16},{9,1},{17,9},{25,17},{10,2},{18,10},{26,18},{... | collective-permute-start | bytes 49160 | tf_op jit(solution)/shard_map/ppermute | solution.py:237
  25.6 0.1 collective-permute-done.7.low_ref
  25.7 4.2 %collective-permute-done.8.high_ref = bf16[8,1024]{1,0:T(8,128)(2,1)S(1)} collective-permute-done((bf16[8,1024]{1,0:T(8,128)(2,1)S(1)}, bf16[8,1024]{1,0:T(8,128)(2,1)S(1)}, u32[]{:S(2)}, u32[]{:S(2)}) %collective-permute-start.8) | collective-permute-done | bytes 16416 | tf_op jit(solution)/shard_map/ppermute | solution.py:237
  29.9 0.5 %shard_map.53.k_ref = bf16[2,2,256,256]{3,2,1,0:T(8,128)(2,1)S(1)} custom-call(bf16[2,2,256,256]{3,2,1,0:T(8,128)(2,1)S(1)} %copy-done.1, f32[1,256]{1,0:T(1,128)S(1)} %bitcast.3, bf16[8,1024]{1,0:T(8,128)(2,1)S(1)} %collective-permute-done.7.low_ref, bf16[8,1024]{1,0:T(8,128)(2,1)S(1)} %collective-permute-done.8.high_ref), custom_call_target="tpu_custom_call" | custom-call | tf_op jit(solution)/shard_map/pallas_call | solution.py:18
  30.5 0.3 shard_map.54
  30.8 2.7 %collective-permute-start.10 = (bf16[128,256]{1,0:T(8,128)(2,1)S(1)}, bf16[128,256]{1,0:T(8,128)(2,1)S(1)}, u32[]{:S(2)}, u32[]{:S(2)}) collective-permute-start(bf16[128,256]{1,0:T(8,128)(2,1)S(1)} %get-tuple-element.31), channel_id=1, source_target_pairs={{0,16},{8,24},{16,0},{24,8},{1,17},{9,25},{17,1},{25,9},{2,18},{10... | collective-permute-start | bytes 196616 | tf_op jit(solution)/shard_map/ppermute | solution.py:249
  33.4 1.3 %collective-permute-start.11 = (bf16[128,256]{1,0:T(8,128)(2,1)S(1)}, bf16[128,256]{1,0:T(8,128)(2,1)S(1)}, u32[]{:S(2)}, u32[]{:S(2)}) collective-permute-start(bf16[128,256]{1,0:T(8,128)(2,1)S(1)} %get-tuple-element.32), channel_id=1, source_target_pairs={{0,24},{8,16},{16,8},{24,0},{1,25},{9,17},{17,9},{25,1},{2,26},{10... | collective-permute-start | bytes 196616 | tf_op jit(solution)/shard_map/ppermute | solution.py:249
  34.8 0.0 collective-permute-start.9
  34.8 0.0 collective-permute-done.12.a_ref
  34.8 0.3 shard_map.55
  35.1 2.1 %collective-permute-start.13 = (bf16[128,256]{1,0:T(8,128)(2,1)S(1)}, bf16[128,256]{1,0:T(8,128)(2,1)S(1)}, u32[]{:S(2)}, u32[]{:S(2)}) collective-permute-start(bf16[128,256]{1,0:T(8,128)(2,1)S(1)} %get-tuple-element.34), channel_id=1, source_target_pairs={{0,8},{8,0},{16,24},{24,16},{1,9},{9,1},{17,25},{25,17},{2,10},{10... | collective-permute-start | bytes 196616 | tf_op jit(solution)/shard_map/ppermute | solution.py:249
  37.2 1.1 %collective-permute-start.14 = (bf16[128,256]{1,0:T(8,128)(2,1)S(1)}, bf16[128,256]{1,0:T(8,128)(2,1)S(1)}, u32[]{:S(2)}, u32[]{:S(2)}) collective-permute-start(bf16[128,256]{1,0:T(8,128)(2,1)S(1)} %get-tuple-element.35), channel_id=1, source_target_pairs={{0,16},{8,24},{16,0},{24,8},{1,17},{9,25},{17,1},{25,9},{2,18},{10... | collective-permute-start | bytes 196616 | tf_op jit(solution)/shard_map/ppermute | solution.py:249
  38.3 0.0 collective-permute-done.10.refs_2_
  38.3 0.0 copy-start.4
  38.3 1.5 %collective-permute-start.15 = (bf16[128,256]{1,0:T(8,128)(2,1)S(1)}, bf16[128,256]{1,0:T(8,128)(2,1)S(1)}, u32[]{:S(2)}, u32[]{:S(2)}) collective-permute-start(bf16[128,256]{1,0:T(8,128)(2,1)S(1)} %get-tuple-element.36), channel_id=1, source_target_pairs={{0,24},{8,16},{16,8},{24,0},{1,25},{9,17},{17,9},{25,1},{2,26},{10... | collective-permute-start | bytes 196616 | tf_op jit(solution)/shard_map/ppermute | solution.py:249
  39.8 0.6 %collective-permute-done.11.refs_3_ = bf16[128,256]{1,0:T(8,128)(2,1)S(1)} collective-permute-done((bf16[128,256]{1,0:T(8,128)(2,1)S(1)}, bf16[128,256]{1,0:T(8,128)(2,1)S(1)}, u32[]{:S(2)}, u32[]{:S(2)}) %collective-permute-start.11) | collective-permute-done | bytes 65568 | tf_op jit(solution)/shard_map/ppermute | solution.py:249
  40.3 0.1 collective-permute-done.9.refs_1_
  40.5 1.0 %collective-permute-done.13.refs_5_ = bf16[128,256]{1,0:T(8,128)(2,1)S(1)} collective-permute-done((bf16[128,256]{1,0:T(8,128)(2,1)S(1)}, bf16[128,256]{1,0:T(8,128)(2,1)S(1)}, u32[]{:S(2)}, u32[]{:S(2)}) %collective-permute-start.13) | collective-permute-done | bytes 65568 | tf_op jit(solution)/shard_map/ppermute | solution.py:249
  41.5 2.1 %collective-permute-done.14.refs_6_ = bf16[128,256]{1,0:T(8,128)(2,1)S(1)} collective-permute-done((bf16[128,256]{1,0:T(8,128)(2,1)S(1)}, bf16[128,256]{1,0:T(8,128)(2,1)S(1)}, u32[]{:S(2)}, u32[]{:S(2)}) %collective-permute-start.14) | collective-permute-done | bytes 65568 | tf_op jit(solution)/shard_map/ppermute | solution.py:249
  43.6 0.8 %collective-permute-done.15.refs_7_ = bf16[128,256]{1,0:T(8,128)(2,1)S(1)} collective-permute-done((bf16[128,256]{1,0:T(8,128)(2,1)S(1)}, bf16[128,256]{1,0:T(8,128)(2,1)S(1)}, u32[]{:S(2)}, u32[]{:S(2)}) %collective-permute-start.15) | collective-permute-done | bytes 65568 | tf_op jit(solution)/shard_map/ppermute | solution.py:249
  44.4 0.0 copy-done.4
  44.4 0.2 shard_map.56
  44.5 0.7 %copy.5 = f32[64,2,2,256]{3,2,1,0:T(2,128)} copy(f32[64,2,2,256]{3,2,1,0:T(2,128)S(1)} %shard_map.56) | data formatting | bytes 524288
  (4 shorter events, 0.1 us)
Async XLA Ops:
  0.0 1.0 %copy-start = (bf16[2,2,256,256]{3,2,1,0:T(8,128)(2,1)S(1)}, bf16[2,2,256,256]{3,2,1,0:T(8,128)(2,1)}, u32[]{:S(2)}) copy-start(bf16[2,2,256,256]{3,2,1,0:T(8,128)(2,1)} %k_ref.7) | copy-start | bytes 1572868
  1.0 1.0 %copy-start.2 = (bf16[256,2,2,256]{3,2,1,0:T(2,128)(2,1)S(1)}, bf16[256,2,2,256]{3,2,1,0:T(2,128)(2,1)}, u32[]{:S(2)}) copy-start(bf16[256,2,2,256]{3,2,1,0:T(2,128)(2,1)} %x_ref.1) | copy-start | bytes 1572868
  2.1 1.1 %copy-start.1 = (bf16[2,2,256,256]{3,2,1,0:T(8,128)(2,1)S(1)}, bf16[2,2,256,256]{3,2,1,0:T(8,128)(2,1)}, u32[]{:S(2)}) copy-start(bf16[2,2,256,256]{3,2,1,0:T(8,128)(2,1)} %k_ref.7) | copy-start | bytes 1572868
  2.6 1.7 %collective-permute-start = (bf16[512,256]{1,0:T(8,128)(2,1)S(1)}, bf16[512,256]{1,0:T(8,128)(2,1)S(1)}, u32[]{:S(2)}, u32[]{:S(2)}) collective-permute-start(bf16[512,256]{1,0:T(8,128)(2,1)S(1)} %get-tuple-element.22), channel_id=1, source_target_pairs={{0,1},{1,0},{2,3},{3,2},{4,5},{5,4},{6,7},{7,6},{8,9},{9,8},{10,11... | collective-permute-start | bytes 786440 | tf_op jit(solution)/shard_map/ppermute | solution.py:210
  4.4 5.3 %collective-permute-start.1 = (bf16[128,256]{1,0:T(8,128)(2,1)S(1)}, bf16[128,256]{1,0:T(8,128)(2,1)S(1)}, u32[]{:S(2)}, u32[]{:S(2)}) collective-permute-start(bf16[128,256]{1,0:T(8,128)(2,1)S(1)} %get-tuple-element.24), channel_id=1, source_target_pairs={{0,2},{1,3},{2,0},{3,1},{4,6},{5,7},{6,4},{7,5},{8,10},{9,11},{10,... | collective-permute-start | bytes 196616 | tf_op jit(solution)/shard_map/ppermute | solution.py:221
  7.3 4.3 %collective-permute-start.2 = (bf16[128,256]{1,0:T(8,128)(2,1)S(1)}, bf16[128,256]{1,0:T(8,128)(2,1)S(1)}, u32[]{:S(2)}, u32[]{:S(2)}) collective-permute-start(bf16[128,256]{1,0:T(8,128)(2,1)S(1)} %get-tuple-element.25), channel_id=1, source_target_pairs={{0,4},{1,5},{2,6},{3,7},{4,0},{5,1},{6,2},{7,3},{8,12},{9,13},{10,... | collective-permute-start | bytes 196616 | tf_op jit(solution)/shard_map/ppermute | solution.py:221
  8.8 0.7 %copy-start.3 = (f32[256]{0:T(256)S(1)}, f32[256]{0:T(256)}, u32[]{:S(2)}) copy-start(f32[256]{0:T(256)} %param.7) | copy-start | bytes 3076
  8.8 5.2 %collective-permute-start.3 = (bf16[128,256]{1,0:T(8,128)(2,1)S(1)}, bf16[128,256]{1,0:T(8,128)(2,1)S(1)}, u32[]{:S(2)}, u32[]{:S(2)}) collective-permute-start(bf16[128,256]{1,0:T(8,128)(2,1)S(1)} %get-tuple-element.26), channel_id=1, source_target_pairs={{0,6},{1,7},{2,4},{3,5},{4,2},{5,3},{6,0},{7,1},{8,14},{9,15},{10,... | collective-permute-start | bytes 196616 | tf_op jit(solution)/shard_map/ppermute | solution.py:221
  14.0 4.3 %collective-permute-start.4 = (bf16[128,256]{1,0:T(8,128)(2,1)S(1)}, bf16[128,256]{1,0:T(8,128)(2,1)S(1)}, u32[]{:S(2)}, u32[]{:S(2)}) collective-permute-start(bf16[128,256]{1,0:T(8,128)(2,1)S(1)} %shard_map.50.mine_ref), channel_id=1, source_target_pairs={{0,2},{1,3},{2,0},{3,1},{4,6},{5,7},{6,4},{7,5},{8,10},{9,11},{10,... | collective-permute-start | bytes 196616 | tf_op jit(solution)/shard_map/ppermute | solution.py:224
  14.6 4.3 %collective-permute-start.5 = (bf16[128,256]{1,0:T(8,128)(2,1)S(1)}, bf16[128,256]{1,0:T(8,128)(2,1)S(1)}, u32[]{:S(2)}, u32[]{:S(2)}) collective-permute-start(bf16[128,256]{1,0:T(8,128)(2,1)S(1)} %shard_map.50.mine_ref), channel_id=1, source_target_pairs={{0,4},{1,5},{2,6},{3,7},{4,0},{5,1},{6,2},{7,3},{8,12},{9,13},{10,... | collective-permute-start | bytes 196616 | tf_op jit(solution)/shard_map/ppermute | solution.py:224
  15.1 5.2 %collective-permute-start.6 = (bf16[128,256]{1,0:T(8,128)(2,1)S(1)}, bf16[128,256]{1,0:T(8,128)(2,1)S(1)}, u32[]{:S(2)}, u32[]{:S(2)}) collective-permute-start(bf16[128,256]{1,0:T(8,128)(2,1)S(1)} %shard_map.50.mine_ref), channel_id=1, source_target_pairs={{0,6},{1,7},{2,4},{3,5},{4,2},{5,3},{6,0},{7,1},{8,14},{9,15},{10,... | collective-permute-start | bytes 196616 | tf_op jit(solution)/shard_map/ppermute | solution.py:224
  20.3 14.5 %collective-permute-start.12 = (bf16[512,256]{1,0:T(8,128)(2,1)S(1)}, bf16[512,256]{1,0:T(8,128)(2,1)S(1)}, u32[]{:S(2)}, u32[]{:S(2)}) collective-permute-start(bf16[512,256]{1,0:T(8,128)(2,1)S(1)} %shard_map.51.a_ref), channel_id=1, source_target_pairs={{0,1},{1,0},{2,3},{3,2},{4,5},{5,4},{6,7},{7,6},{8,9},{9,8},{10,11... | collective-permute-start | bytes 786440 | tf_op jit(solution)/shard_map/ppermute | solution.py:226
  20.7 5.0 %collective-permute-start.7 = (bf16[8,1024]{1,0:T(8,128)(2,1)S(1)}, bf16[8,1024]{1,0:T(8,128)(2,1)S(1)}, u32[]{:S(2)}, u32[]{:S(2)}) collective-permute-start(bf16[8,1024]{1,0:T(8,128)(2,1)S(1)} %get-tuple-element.27), channel_id=1, source_target_pairs={{0,8},{8,16},{16,24},{1,9},{9,17},{17,25},{2,10},{10,18},{18,26},{... | collective-permute-start | bytes 49160 | tf_op jit(solution)/shard_map/ppermute | solution.py:236
  24.3 5.6 %collective-permute-start.8 = (bf16[8,1024]{1,0:T(8,128)(2,1)S(1)}, bf16[8,1024]{1,0:T(8,128)(2,1)S(1)}, u32[]{:S(2)}, u32[]{:S(2)}) collective-permute-start(bf16[8,1024]{1,0:T(8,128)(2,1)S(1)} %get-tuple-element.28), channel_id=1, source_target_pairs={{8,0},{16,8},{24,16},{9,1},{17,9},{25,17},{10,2},{18,10},{26,18},{... | collective-permute-start | bytes 49160 | tf_op jit(solution)/shard_map/ppermute | solution.py:237
  30.8 7.5 %collective-permute-start.10 = (bf16[128,256]{1,0:T(8,128)(2,1)S(1)}, bf16[128,256]{1,0:T(8,128)(2,1)S(1)}, u32[]{:S(2)}, u32[]{:S(2)}) collective-permute-start(bf16[128,256]{1,0:T(8,128)(2,1)S(1)} %get-tuple-element.31), channel_id=1, source_target_pairs={{0,16},{8,24},{16,0},{24,8},{1,17},{9,25},{17,1},{25,9},{2,18},{10... | collective-permute-start | bytes 196616 | tf_op jit(solution)/shard_map/ppermute | solution.py:249
  33.4 6.9 %collective-permute-start.11 = (bf16[128,256]{1,0:T(8,128)(2,1)S(1)}, bf16[128,256]{1,0:T(8,128)(2,1)S(1)}, u32[]{:S(2)}, u32[]{:S(2)}) collective-permute-start(bf16[128,256]{1,0:T(8,128)(2,1)S(1)} %get-tuple-element.32), channel_id=1, source_target_pairs={{0,24},{8,16},{16,8},{24,0},{1,25},{9,17},{17,9},{25,1},{2,26},{10... | collective-permute-start | bytes 196616 | tf_op jit(solution)/shard_map/ppermute | solution.py:249
  34.8 5.7 %collective-permute-start.9 = (bf16[128,256]{1,0:T(8,128)(2,1)S(1)}, bf16[128,256]{1,0:T(8,128)(2,1)S(1)}, u32[]{:S(2)}, u32[]{:S(2)}) collective-permute-start(bf16[128,256]{1,0:T(8,128)(2,1)S(1)} %get-tuple-element.30), channel_id=1, source_target_pairs={{0,8},{8,0},{16,24},{24,16},{1,9},{9,1},{17,25},{25,17},{2,10},{10... | collective-permute-start | bytes 196616 | tf_op jit(solution)/shard_map/ppermute | solution.py:249
  35.1 6.4 %collective-permute-start.13 = (bf16[128,256]{1,0:T(8,128)(2,1)S(1)}, bf16[128,256]{1,0:T(8,128)(2,1)S(1)}, u32[]{:S(2)}, u32[]{:S(2)}) collective-permute-start(bf16[128,256]{1,0:T(8,128)(2,1)S(1)} %get-tuple-element.34), channel_id=1, source_target_pairs={{0,8},{8,0},{16,24},{24,16},{1,9},{9,1},{17,25},{25,17},{2,10},{10... | collective-permute-start | bytes 196616 | tf_op jit(solution)/shard_map/ppermute | solution.py:249
  37.2 6.4 %collective-permute-start.14 = (bf16[128,256]{1,0:T(8,128)(2,1)S(1)}, bf16[128,256]{1,0:T(8,128)(2,1)S(1)}, u32[]{:S(2)}, u32[]{:S(2)}) collective-permute-start(bf16[128,256]{1,0:T(8,128)(2,1)S(1)} %get-tuple-element.35), channel_id=1, source_target_pairs={{0,16},{8,24},{16,0},{24,8},{1,17},{9,25},{17,1},{25,9},{2,18},{10... | collective-permute-start | bytes 196616 | tf_op jit(solution)/shard_map/ppermute | solution.py:249
  38.3 6.1 %copy-start.4 = (f32[2,256]{1,0:T(2,128)S(1)}, f32[2,256]{1,0:T(2,128)}, u32[]{:S(2)}) copy-start(f32[2,256]{1,0:T(2,128)} %noise_ref.1) | copy-start | bytes 6148
  38.3 6.1 %collective-permute-start.15 = (bf16[128,256]{1,0:T(8,128)(2,1)S(1)}, bf16[128,256]{1,0:T(8,128)(2,1)S(1)}, u32[]{:S(2)}, u32[]{:S(2)}) collective-permute-start(bf16[128,256]{1,0:T(8,128)(2,1)S(1)} %get-tuple-element.36), channel_id=1, source_target_pairs={{0,24},{8,16},{16,8},{24,0},{1,25},{9,17},{17,9},{25,1},{2,26},{10... | collective-permute-start | bytes 196616 | tf_op jit(solution)/shard_map/ppermute | solution.py:249

commit v4 on v3

v4 whole, which is shorter than its diff:
```python
import functools

import jax
import jax.numpy as jnp
from jax import lax
from jax.experimental import pallas as pl
from jax.experimental.pallas import tpu as pltpu
from jax.sharding import PartitionSpec as P


BF = jnp.bfloat16
F32 = jnp.float32
LANES = 128
VMEM = pl.BlockSpec(memory_space=pltpu.VMEM)
HBM = pl.BlockSpec(memory_space=pl.ANY)


def call(body, ins, outs, scratch=(), raw=()):
    return pl.pallas_call(
        body,
        in_specs=[HBM] * len(raw) + [VMEM] * len(ins),
        out_specs=[VMEM] * len(outs),
        out_shape=[pltpu.VMEM(*o) for o in outs],
        scratch_shapes=list(scratch),
    )(*raw, *[pltpu.with_memory_space_constraint(v, pltpu.VMEM) for v in ins])


def move(value, axis, perm):
    return lax.ppermute(value, axis, perm)


def pair_perm(axis, step):
    return [(i, i ^ step) for i in range(lax.axis_size(axis))]


def parity():
    return lax.rem(lax.axis_index("col"), 2)


def xor(a, b):
    return jnp.bitwise_xor(a, b)


def part(start, size):
    return pl.ds(pl.multiple_of(start, size), size)


def dot_nt(left, right):
    return lax.dot_general(left, right, (((1,), (1,)), ((), ())), preferred_element_type=F32)


def dot_nn(left, right):
    return jnp.dot(left, right, preferred_element_type=F32)


def three(value):
    pieces = []
    for _ in range(3):
        pieces.append(value.astype(BF))
        value = value - pieces[-1].astype(F32)
    return pieces


def adjoint(freq, x, k_ref, o_ref, u_ref):
    rows = x.shape[0] // 4
    width = k_ref.shape[3]
    tiles = width // LANES
    for c in range(2):
        y = dot_nn(x, k_ref[freq, c])
        for t in range(tiles):
            u_ref[c * tiles + t] = y[:, t * LANES:(t + 1) * LANES]
    real = pl.ds(2 * freq, rows, stride=4)
    imag = pl.ds(2 * freq + 1, rows, stride=4)
    for t in range(tiles):
        at = slice(t * LANES, (t + 1) * LANES)
        o_ref[:rows, at] = (u_ref[t, real, :] + u_ref[tiles + t, imag, :]).astype(o_ref.dtype)
        o_ref[rows:, at] = (u_ref[t, imag, :] - u_ref[tiles + t, real, :]).astype(o_ref.dtype)


def adjoint_other_body(v_hbm, k_hbm, o_ref, x_ref, k_ref, v_ref, u_ref, sems):
    freq = 1 - parity()
    copies = [
        pltpu.make_async_copy(v_hbm, v_ref, sems.at[0]),
        pltpu.make_async_copy(k_hbm.at[freq], k_ref.at[freq], sems.at[1]),
        pltpu.make_async_copy(k_hbm.at[1 - freq], k_ref.at[1 - freq], sems.at[2]),
    ]
    for copy in copies:
        copy.start()
    copies[0].wait()
    x = v_ref[...].reshape(x_ref.shape)
    x_ref[...] = x
    copies[1].wait()
    adjoint(freq, x, k_ref, o_ref, u_ref)
    copies[2].wait()


def adjoint_own_body(x_ref, k_ref, o_ref, u_ref):
    adjoint(parity(), x_ref[...], k_ref, o_ref, u_ref)


def seam_body(k_ref, d_ref, o_ref):
    freqs, _, rows, width = k_ref.shape
    odd = lax.rem(lax.axis_index("row"), 2)
    at = lax.broadcasted_iota(jnp.int32, (8, width), 0)
    place = lax.broadcasted_iota(jnp.int32, (8, width), 1)
    pick = jnp.where((at < 2) & (place == at + odd * (width - 2)), 1.0, 0.0).astype(BF)
    for f in range(freqs):
        for c in range(2):
            lo = (f * 2 + c) * rows
            o_ref[:, lo:lo + rows] = dot_nt(pick, k_ref[f, c]).astype(BF)
    coef = d_ref[...]
    spot = lax.broadcasted_iota(jnp.int32, coef.shape, 1)
    edge = jnp.sum(jnp.where(spot == odd * (width - 1), coef, 0.0), axis=1, keepdims=True)
    for n, piece in enumerate(three(edge)):
        o_ref[2 + n:3 + n, :] = jnp.broadcast_to(piece, (1, o_ref.shape[1]))


def fence_body(d_ref, o_ref):
    o_ref[...] = jnp.zeros_like(o_ref)


def stencil_matrix(coef, block):
    width = coef.shape[1]
    row_at = lax.broadcasted_iota(jnp.int32, (width, width), 0)
    col_at = lax.broadcasted_iota(jnp.int32, (width, width), 1)
    wide = jnp.broadcast_to(coef, (width, width))
    tall = jnp.sum(jnp.where(row_at == col_at, wide, 0.0), axis=1, keepdims=True)
    gap = jnp.abs(row_at - col_at)
    first = (row_at == 0) & (block == 0)
    last = (row_at == width - 1) & (block == lax.axis_size("row") - 1)
    centre = wide * wide + jnp.where(first | last, 1.0, 2.0)
    matrix = jnp.where(gap == 0, centre, jnp.where(gap == 1, -(wide + tall), jnp.where(gap == 2, 1.0, 0.0)))
    upper = matrix.astype(BF)
    return upper, (matrix - upper.astype(F32)).astype(BF)


def operator_body(k_ref, mate_ref, d_ref, got_ref, near_ref, far_ref, o_ref):
    freqs, _, rows, width = k_ref.shape
    me = lax.axis_index("row")
    odd = lax.rem(me, 2)
    is_odd = odd == 1
    at = lax.broadcasted_iota(jnp.int32, (8, width), 0)
    place = lax.broadcasted_iota(jnp.int32, (8, width), 1)
    own_pick = jnp.where((at < 2) & (place == at + (1 - odd) * (width - 2)), 1.0, 0.0).astype(BF)
    mate_pick = jnp.where((at < 2) & (place == at + odd * (width - 2)), 1.0, 0.0).astype(BF)
    coef = d_ref[...]
    tail = got_ref[got_ref.shape[0] - 16:, :].astype(F32)
    mate_coef = tail[0:1] + tail[1:2] + tail[2:3]

    def last_or_first(value, last):
        return jnp.where(last, value[:, width - 1:], value[:, :1])

    def outer(ref):
        full = ref[...].astype(F32)
        return full[0:2], full[2:3, :1] + full[3:4, :1] + full[4:5, :1]

    near, near_coef = outer(near_ref)
    far, far_coef = outer(far_ref)
    sides = (
        (k_ref, coef, me, near, near_coef, mate_ref, mate_pick, last_or_first(mate_coef, is_odd), is_odd),
        (mate_ref, mate_coef, xor(me, 1), far, far_coef, k_ref, own_pick, last_or_first(coef, ~is_odd), ~is_odd),
    )
    for n, (ref, c_block, block, outside, outside_coef, inner_ref, pick, inside_coef, inner_left) in enumerate(sides):
        upper, lower = stencil_matrix(c_block, block)
        left_coef = jnp.where(inner_left, inside_coef, outside_coef) + c_block[:, :1]
        right_coef = jnp.where(inner_left, outside_coef, inside_coef) + c_block[:, width - 1:]
        for f in range(freqs):
            for c in range(2):
                own = ref[f, c]
                value = dot_nt(upper, own) + dot_nt(lower, own)
                inside = dot_nt(pick, inner_ref[f, c])[0:2]
                lo = (f * 2 + c) * rows
                beyond = outside[:, lo:lo + rows]
                left = jnp.where(inner_left, inside, beyond)
                right = jnp.where(inner_left, beyond, inside)
                extra = jnp.concatenate(
                    [
                        left[0:1] - left_coef * left[1:2],
                        left[1:2],
                        jnp.zeros((width - 4, rows), F32),
                        right[0:1],
                        right[1:2] - right_coef * right[0:1],
                    ],
                    axis=0,
                )
                o_ref[f, c, n * width:(n + 1) * width] = (value + extra).astype(BF)


def split_body(own_ref, got_ref, keep_ref, *send_refs):
    chips = len(send_refs) + 1
    blocks = lax.axis_size("row")
    probes = own_ref.shape[0] // 2
    block = probes // blocks
    size = block // chips
    chip = lax.div(lax.axis_index("col"), 2)
    me = lax.axis_index("row")
    for step, ref in enumerate((keep_ref,) + send_refs):
        target = xor(chip, step)
        at = 0
        for mate in range(2):
            for slot in range(blocks // 2):
                for c in range(2):
                    lo = c * probes + xor(me, mate + 2 * slot) * block + target * size
                    rows = part(lo, size)
                    ref[at:at + size] = (own_ref[rows, :] + got_ref[rows, :].astype(F32)).astype(ref.dtype)
                    at += size


def sum_body(keep_ref, d_ref, fence_ref, *refs):
    stay_ref, give_ref = refs[-2:]
    size = stay_ref.shape[0]
    total = keep_ref[...]
    for ref in refs[:-2]:
        total = total + ref[...].astype(F32)
    stay_ref[...] = total[:size].astype(BF)
    give_ref[:size] = total[size:].astype(BF)
    pad = jnp.zeros((13, d_ref.shape[1]), BF)
    give_ref[size:] = jnp.concatenate(three(d_ref[...]) + [pad], axis=0)


def pack_body(stay_ref, got_ref, fence_ref, o_ref):
    size = stay_ref.shape[0]
    o_ref[:size] = stay_ref[...]
    o_ref[size:] = got_ref[:size]


def join_body(mine_ref, *refs):
    out_ref = refs[-1]
    pieces = (mine_ref,) + refs[:-1]
    chips = len(pieces)
    groups = 2 * lax.axis_size("row")
    size = mine_ref.shape[0] // groups
    chip = lax.div(lax.axis_index("col"), 2)
    for step, ref in enumerate(pieces):
        source = xor(chip, step)
        for n in range(groups):
            lo = n * chips * size + source * size
            out_ref[part(lo, size), :] = ref[n * size:(n + 1) * size]


def predict_body(swap, a_ref, k_ref, keep_ref, *refs):
    freq = parity()
    if swap:
        freq = 1 - freq
    half = a_ref.shape[0] // 2
    width = a_ref.shape[1]
    size = keep_ref.shape[0] // 2
    total = []
    for c in range(2):
        value = dot_nn(a_ref[:half], k_ref[freq, c, :width])
        total.append(value + dot_nn(a_ref[half:], k_ref[freq, c, width:]))
    by_real, by_imag = total
    for slot, ref in enumerate((keep_ref,) + refs):
        lo = 2 * slot * size
        mid = lo + size
        hi = mid + size
        ref[:size] = (by_real[lo:mid] - by_imag[mid:hi]).astype(ref.dtype)
        ref[size:] = (by_real[mid:hi] + by_imag[lo:mid]).astype(ref.dtype)


def final_body(peers, x_ref, noise_ref, *refs):
    out_ref, s_ref = refs[-2:]
    size = out_ref.shape[0]
    rows = 4 * size
    me = lax.axis_index("row")
    freq = parity()
    for which in range(2):
        group = refs[which * (peers + 1):(which + 1) * (peers + 1)]
        total = group[0][...]
        for ref in group[1:]:
            total = total + ref[...].astype(F32)
        f = freq if which == 0 else 1 - freq
        for t in range(s_ref.shape[0]):
            at = slice(t * LANES, (t + 1) * LANES)
            s_ref[t, pl.ds(2 * f, size, stride=4), :] = total[:size, at]
            s_ref[t, pl.ds(2 * f + 1, size, stride=4), :] = total[size:, at]
    x = x_ref[part(me * rows, rows), :].astype(F32)
    kind = lax.rem(lax.broadcasted_iota(jnp.int32, x.shape, 0), 4)
    noise = jnp.where(kind < 2, noise_ref[0:1, :], noise_ref[1:2, :])
    values = jnp.concatenate([s_ref[t] for t in range(s_ref.shape[0])], axis=1) + noise * x
    out_ref[...] = values.reshape(out_ref.shape)


def wide_sum(own, got, coef, blocks):
    rows, width = own.shape
    a = parity()
    value = own + got.astype(F32)
    both = jnp.where(a == 0, jnp.stack([value, 0 * value]), jnp.stack([0 * value, value]))
    both = lax.psum(both, "col").astype(BF).reshape(2, 2, blocks, -1, width)
    slots = 2 * jnp.arange(blocks // 2)
    me = lax.axis_index("row")

    def chosen(freq, mate):
        value = lax.dynamic_index_in_dim(both, freq, 0, keepdims=False)
        value = jnp.take(value, xor(me, mate + slots), axis=1)
        return value.transpose(1, 0, 2, 3).reshape(-1, width)

    tail = jnp.concatenate(three(coef) + [jnp.zeros((13, width), BF)], axis=0)
    give = jnp.concatenate([chosen(1 - a, 1), chosen(a, 1), tail], axis=0)
    give = move(give, "row", pair_perm("row", 1))
    half = rows // 2
    mine = jnp.concatenate([chosen(a, 0), give[half:rows]], axis=0)
    other = jnp.concatenate([chosen(1 - a, 0), give[:half]], axis=0)
    return mine, other, give


def chip_sum(own, got, coef, chips):
    rows, width = own.shape
    size = rows // chips
    keep, *sends = call(split_body, (own, got), [((size, width), F32)] + [((size, width), BF)] * (chips - 1))
    fence = call(fence_body, (coef,), [((8, LANES), F32)])[0]
    got = [move(v, "col", pair_perm("col", 2 * (d + 1))) for d, v in enumerate(sends)]
    stay, give = call(sum_body, (keep, coef, fence, *got), [((size // 2, width), BF), ((size // 2 + 16, width), BF)])
    fence = call(fence_body, (coef,), [((8, LANES), F32)])[0]
    give = move(give, "row", pair_perm("row", 1))
    mine = call(pack_body, (stay, give, fence), [((size, width), BF)])[0]
    got = [move(mine, "col", pair_perm("col", 2 * (d + 1))) for d in range(chips - 1)]
    mine = call(join_body, (mine, *got), [((rows, width), BF)])[0]
    return mine, move(mine, "col", pair_perm("col", 1)), give


def apply(kernel, probes, noise_var, prior_diag):
    count = probes.shape[0]
    rows, width = kernel.shape[2:]
    blocks = lax.axis_size("row")
    chips = lax.axis_size("col") // 2
    coef = prior_diag[None, :]
    flat = (4 * count, rows)
    scratch = pltpu.VMEM((2 * width // LANES, 4 * count, LANES), F32)
    mate = move(kernel, "row", pair_perm("row", 1))
    other, x, kernel = call(
        adjoint_other_body,
        (),
        [((2 * count, width), BF), (flat, BF), (kernel.shape, BF)],
        (pltpu.VMEM(probes.shape, BF), scratch, pltpu.SemaphoreType.DMA((3,))),
        raw=(probes, kernel),
    )
    got = move(other, "col", pair_perm("col", 1))
    own = call(adjoint_own_body, (x, kernel), [((2 * count, width), F32)], (scratch,))[0]
    seam = call(seam_body, (kernel, coef), [((8, 4 * rows), BF)])[0]
    odd = [i for i in range(blocks) if i % 2]
    even = [i for i in range(blocks) if i % 2 == 0]
    near = [(i, i + 1) for i in odd if i + 1 < blocks] + [(i, i - 1) for i in even if i]
    far = [(i, i + 2) for i in odd if i + 2 < blocks] + [(i, i - 2) for i in even if i]
    near = move(seam, "row", near)
    far = move(seam, "row", far)
    if chips > 4:
        mine, other, give = wide_sum(own, got, coef, blocks)
    else:
        mine, other, give = chip_sum(own, got, coef, chips)
    operator = call(operator_body, (kernel, mate, coef, give, near, far), [((2, 2, 2 * width, rows), BF)])[0]
    size = count // blocks
    peers = blocks // 2 - 1
    groups = []
    for swap, field in ((False, mine), (True, other)):
        keep, *sends = call(
            functools.partial(predict_body, swap),
            (field, operator),
            [((2 * size, rows), F32)] + [((2 * size, rows), BF)] * peers,
        )
        groups.append(keep)
        groups += [move(v, "row", pair_perm("row", 2 * (d + 1))) for d, v in enumerate(sends)]
    return call(
        functools.partial(final_body, peers),
        (x, noise_var, *groups),
        [((size,) + probes.shape[1:3] + (rows,), F32)],
        (pltpu.VMEM((rows // LANES, 4 * size, LANES), F32),),
    )[0]


def solution(mesh):
    in_specs = (P(None, None, "col", "row"), P(None, None, None, "col"), P(None, "col"), P("row"))
    out_specs = P("row", None, None, "col")
    return jax.shard_map(apply, mesh=mesh, in_specs=in_specs, out_specs=out_specs, check_vma=False)
```

time: 45.5 us -> 48.6 us (1.068)
  waiting for transfers between devices: 16.7 us -> 23 us
  starting transfers between devices: 22.1 us -> 18 us
  Pallas kernels: 2.9 us -> 4.51 us
  local copies, waits for them, and re-layouts: 3.45 us -> 2.76 us
    ppermute x16 -> x14, waiting for transfers between devices: 16.7 us -> 23 us  [move(): return lax.ppermute(value, axis, perm)]
    ppermute x16 -> x14, starting transfers between devices: 22.1 us -> 18 us  [move(): return lax.ppermute(value, axis, perm)]
    pallas_call x11 -> x12, Pallas kernels: 2.9 us -> 4.51 us  [call(): pl.pallas_call(body, in_specs=[HBM] * len(raw) + [VMEM] * len(ins), out_s...]
    unnamed x11 -> x13, local copies, waits for them, and re-layouts: 3.45 us -> 2.76 us
  transfers between devices with their start and end apart: 16 -> 14, of which waited for: 14 -> 10; matrix products, arithmetic and copies ran while one was open for 0% -> 0% of each run, Pallas kernels for 5% -> 5%
where the time goes in v4:
time: 48.6 us; the launch traced here: 48.4 us
  waiting for transfers between devices  23 us (47%)
  starting transfers between devices  18 us (37%)
  Pallas kernels  4.51 us (9%)
  local copies, waits for them, and re-layouts  2.76 us (6%)
    ppermute x14, waiting for transfers between devices, move(): return lax.ppermute(value, axis, perm)  23 us
    ppermute x14, starting transfers between devices, move(): return lax.ppermute(value, axis, perm)  18 us
    pallas_call x12, Pallas kernels, call(): pl.pallas_call(body, in_specs=[HBM] * len(raw) + [VMEM] * len(ins), out_s...  4.51 us
    unnamed x13, local copies, waits for them, and re-layouts  2.76 us
  transfers between devices with their start and end apart: 14, of which 10 were waited for; matrix products, arithmetic and copies ran while one was open for 0% of the time, Pallas kernels for 5%

profile of v4, /device:TPU:0, one launch (start us, length us, event | category | flops | bytes accessed | tf_op | source)
XLA Modules:
  0.0 48.4 jit_solution(7718735721964439406)
XLA Ops:
  0.0 1.7 %shard_map.46 = (bf16[512,256]{1,0:T(8,128)(2,1)S(1)}, bf16[1024,256]{1,0:T(8,128)(2,1)S(1)}, bf16[2,2,256,256]{3,2,1,0:T(8,128)(2,1)S(1)}) custom-call(bf16[256,2,2,256]{3,2,1,0:T(2,128)(2,1)} %v_hbm.1, bf16[2,2,256,256]{3,2,1,0:T(8,128)(2,1)} %k_hbm.1), custom_call_target="tpu_custom_call" | custom-call | tf_op jit(solution)/shard_map/pallas_call | solution.py:19
  1.8 0.0 copy-start
  1.8 0.6 %collective-permute-start = (bf16[512,256]{1,0:T(8,128)(2,1)S(1)}, bf16[512,256]{1,0:T(8,128)(2,1)S(1)}, u32[]{:S(2)}, u32[]{:S(2)}) collective-permute-start(bf16[512,256]{1,0:T(8,128)(2,1)S(1)} %get-tuple-element.20), channel_id=1, source_target_pairs={{0,1},{1,0},{2,3},{3,2},{4,5},{5,4},{6,7},{7,6},{8,9},{9,8},{10,11... | collective-permute-start | bytes 786440 | tf_op jit(solution)/shard_map/ppermute | solution.py:29
  2.3 2.6 %collective-permute-start.8 = (bf16[2,2,256,256]{3,2,1,0:T(8,128)(2,1)}, bf16[2,2,256,256]{3,2,1,0:T(8,128)(2,1)S(1)}, u32[]{:S(2)}, u32[]{:S(2)}) collective-permute-start(bf16[2,2,256,256]{3,2,1,0:T(8,128)(2,1)} %k_hbm.1), channel_id=1, source_target_pairs={{0,8},{8,0},{16,24},{24,16},{1,9},{9,1},{17,25},{25,17},{2,10},{10... | collective-permute-start | bytes 1572872 | tf_op jit(solution)/shard_map/ppermute | solution.py:29
  5.0 0.6 %shard_map.47.own_ref = f32[512,256]{1,0:T(8,128)S(1)} custom-call(bf16[1024,256]{1,0:T(8,128)(2,1)S(1)} %get-tuple-element.18.x_ref, bf16[2,2,256,256]{3,2,1,0:T(8,128)(2,1)S(1)} %get-tuple-element.19.k_ref), custom_call_target="tpu_custom_call" | custom-call | tf_op jit(solution)/shard_map/pallas_call | solution.py:19
  5.5 0.0 copy-done
  5.5 0.0 collective-permute-done.got_ref
  5.6 0.1 shard_map.48
  5.6 1.6 %collective-permute-start.1 = (bf16[128,256]{1,0:T(8,128)(2,1)S(1)}, bf16[128,256]{1,0:T(8,128)(2,1)S(1)}, u32[]{:S(2)}, u32[]{:S(2)}) collective-permute-start(bf16[128,256]{1,0:T(8,128)(2,1)S(1)} %get-tuple-element.22), channel_id=1, source_target_pairs={{0,2},{1,3},{2,0},{3,1},{4,6},{5,7},{6,4},{7,5},{8,10},{9,11},{10,... | collective-permute-start | bytes 196616 | tf_op jit(solution)/shard_map/ppermute | solution.py:29
  7.2 1.5 %collective-permute-start.2 = (bf16[128,256]{1,0:T(8,128)(2,1)S(1)}, bf16[128,256]{1,0:T(8,128)(2,1)S(1)}, u32[]{:S(2)}, u32[]{:S(2)}) collective-permute-start(bf16[128,256]{1,0:T(8,128)(2,1)S(1)} %get-tuple-element.23), channel_id=1, source_target_pairs={{0,4},{1,5},{2,6},{3,7},{4,0},{5,1},{6,2},{7,3},{8,12},{9,13},{10,... | collective-permute-start | bytes 196616 | tf_op jit(solution)/shard_map/ppermute | solution.py:29
  8.7 0.0 copy-start.4
  8.7 0.5 %collective-permute-start.3 = (bf16[128,256]{1,0:T(8,128)(2,1)S(1)}, bf16[128,256]{1,0:T(8,128)(2,1)S(1)}, u32[]{:S(2)}, u32[]{:S(2)}) collective-permute-start(bf16[128,256]{1,0:T(8,128)(2,1)S(1)} %get-tuple-element.24), channel_id=1, source_target_pairs={{0,6},{1,7},{2,4},{3,5},{4,2},{5,3},{6,0},{7,1},{8,14},{9,15},{10,... | collective-permute-start | bytes 196616 | tf_op jit(solution)/shard_map/ppermute | solution.py:29
  9.2 0.2 copy-done.4
  9.4 0.6 %collective-permute-done.1.refs_0_ = bf16[128,256]{1,0:T(8,128)(2,1)S(1)} collective-permute-done((bf16[128,256]{1,0:T(8,128)(2,1)S(1)}, bf16[128,256]{1,0:T(8,128)(2,1)S(1)}, u32[]{:S(2)}, u32[]{:S(2)}) %collective-permute-start.1) | collective-permute-done | bytes 65568 | tf_op jit(solution)/shard_map/ppermute | solution.py:29
  10.0 1.5 %collective-permute-done.2.refs_1_ = bf16[128,256]{1,0:T(8,128)(2,1)S(1)} collective-permute-done((bf16[128,256]{1,0:T(8,128)(2,1)S(1)}, bf16[128,256]{1,0:T(8,128)(2,1)S(1)}, u32[]{:S(2)}, u32[]{:S(2)}) %collective-permute-start.2) | collective-permute-done | bytes 65568 | tf_op jit(solution)/shard_map/ppermute | solution.py:29
  11.5 2.4 %collective-permute-done.3.refs_2_ = bf16[128,256]{1,0:T(8,128)(2,1)S(1)} collective-permute-done((bf16[128,256]{1,0:T(8,128)(2,1)S(1)}, bf16[128,256]{1,0:T(8,128)(2,1)S(1)}, u32[]{:S(2)}, u32[]{:S(2)}) %collective-permute-start.3) | collective-permute-done | bytes 65568 | tf_op jit(solution)/shard_map/ppermute | solution.py:29
  13.9 0.1 shard_map.50
  13.9 0.9 %collective-permute-start.4 = (bf16[80,256]{1,0:T(8,128)(2,1)S(1)}, bf16[80,256]{1,0:T(8,128)(2,1)S(1)}, u32[]{:S(2)}, u32[]{:S(2)}) collective-permute-start(bf16[80,256]{1,0:T(8,128)(2,1)S(1)} %get-tuple-element.26), channel_id=1, source_target_pairs={{0,8},{8,0},{16,24},{24,16},{1,9},{9,1},{17,25},{25,17},{2,10},{10... | collective-permute-start | bytes 122888 | tf_op jit(solution)/shard_map/ppermute | solution.py:29
  14.8 3.7 %collective-permute-done.4.got_ref = bf16[80,256]{1,0:T(8,128)(2,1)S(1)} collective-permute-done((bf16[80,256]{1,0:T(8,128)(2,1)S(1)}, bf16[80,256]{1,0:T(8,128)(2,1)S(1)}, u32[]{:S(2)}, u32[]{:S(2)}) %collective-permute-start.4) | collective-permute-done | bytes 40992 | tf_op jit(solution)/shard_map/ppermute | solution.py:29
  18.6 2.6 %collective-permute-start.7 = (bf16[128,256]{1,0:T(8,128)(2,1)S(1)}, bf16[128,256]{1,0:T(8,128)(2,1)S(1)}, u32[]{:S(2)}, u32[]{:S(2)}) collective-permute-start(bf16[128,256]{1,0:T(8,128)(2,1)S(1)} %shard_map.51.mine_ref), channel_id=1, source_target_pairs={{0,6},{1,7},{2,4},{3,5},{4,2},{5,3},{6,0},{7,1},{8,14},{9,15},{10,... | collective-permute-start | bytes 196616 | tf_op jit(solution)/shard_map/ppermute | solution.py:29
  21.2 0.5 %collective-permute-start.6 = (bf16[128,256]{1,0:T(8,128)(2,1)S(1)}, bf16[128,256]{1,0:T(8,128)(2,1)S(1)}, u32[]{:S(2)}, u32[]{:S(2)}) collective-permute-start(bf16[128,256]{1,0:T(8,128)(2,1)S(1)} %shard_map.51.mine_ref), channel_id=1, source_target_pairs={{0,4},{1,5},{2,6},{3,7},{4,0},{5,1},{6,2},{7,3},{8,12},{9,13},{10,... | collective-permute-start | bytes 196616 | tf_op jit(solution)/shard_map/ppermute | solution.py:29
  21.7 0.4 collective-permute-start.5
  22.1 1.7 %collective-permute-done.7.refs_2_ = bf16[128,256]{1,0:T(8,128)(2,1)S(1)} collective-permute-done((bf16[128,256]{1,0:T(8,128)(2,1)S(1)}, bf16[128,256]{1,0:T(8,128)(2,1)S(1)}, u32[]{:S(2)}, u32[]{:S(2)}) %collective-permute-start.7) | collective-permute-done | bytes 65568 | tf_op jit(solution)/shard_map/ppermute | solution.py:29
  23.8 1.6 %collective-permute-done.6.refs_1_ = bf16[128,256]{1,0:T(8,128)(2,1)S(1)} collective-permute-done((bf16[128,256]{1,0:T(8,128)(2,1)S(1)}, bf16[128,256]{1,0:T(8,128)(2,1)S(1)}, u32[]{:S(2)}, u32[]{:S(2)}) %collective-permute-start.6) | collective-permute-done | bytes 65568 | tf_op jit(solution)/shard_map/ppermute | solution.py:29
  25.4 0.5 %collective-permute-done.5.refs_0_ = bf16[128,256]{1,0:T(8,128)(2,1)S(1)} collective-permute-done((bf16[128,256]{1,0:T(8,128)(2,1)S(1)}, bf16[128,256]{1,0:T(8,128)(2,1)S(1)}, u32[]{:S(2)}, u32[]{:S(2)}) %collective-permute-start.5) | collective-permute-done | bytes 65568 | tf_op jit(solution)/shard_map/ppermute | solution.py:29
  26.0 0.1 collective-permute-start.12
  26.1 0.2 shard_map.53
  26.3 1.3 %collective-permute-start.10 = (bf16[8,1024]{1,0:T(8,128)(2,1)S(1)}, bf16[8,1024]{1,0:T(8,128)(2,1)S(1)}, u32[]{:S(2)}, u32[]{:S(2)}) collective-permute-start(bf16[8,1024]{1,0:T(8,128)(2,1)S(1)} %shard_map.53), channel_id=1, source_target_pairs={{8,24},{16,0},{9,25},{17,1},{10,26},{18,2},{11,27},{19,3},{12,28},... | collective-permute-start | bytes 49160 | tf_op jit(solution)/shard_map/ppermute | solution.py:29
  27.6 0.7 %collective-permute-start.9 = (bf16[8,1024]{1,0:T(8,128)(2,1)S(1)}, bf16[8,1024]{1,0:T(8,128)(2,1)S(1)}, u32[]{:S(2)}, u32[]{:S(2)}) collective-permute-start(bf16[8,1024]{1,0:T(8,128)(2,1)S(1)} %shard_map.53), channel_id=1, source_target_pairs={{8,16},{16,8},{9,17},{17,9},{10,18},{18,10},{11,19},{19,11},{12,20... | collective-permute-start | bytes 49160 | tf_op jit(solution)/shard_map/ppermute | solution.py:29
  28.3 4.6 %collective-permute-done.10.far_ref = bf16[8,1024]{1,0:T(8,128)(2,1)S(1)} collective-permute-done((bf16[8,1024]{1,0:T(8,128)(2,1)S(1)}, bf16[8,1024]{1,0:T(8,128)(2,1)S(1)}, u32[]{:S(2)}, u32[]{:S(2)}) %collective-permute-start.10) | collective-permute-done | bytes 16416 | tf_op jit(solution)/shard_map/ppermute | solution.py:29
  32.9 0.0 collective-permute-done.9.near_ref
  32.9 0.0 collective-permute-done.8.mate_ref
  32.9 0.0 copy-start.2
  32.9 0.8 %copy-done.2 = bf16[2,2,256,256]{3,2,1,0:T(8,128)(2,1)} copy-done((bf16[2,2,256,256]{3,2,1,0:T(8,128)(2,1)}, bf16[2,2,256,256]{3,2,1,0:T(8,128)(2,1)S(1)}, u32[]{:S(2)}) %copy-start.2) | copy-done | bytes 524312
  33.7 0.0 copy-start.3
  33.7 1.0 %copy-done.3 = bf16[2,2,256,256]{3,2,1,0:T(8,128)(2,1)S(1)} copy-done((bf16[2,2,256,256]{3,2,1,0:T(8,128)(2,1)S(1)}, bf16[2,2,256,256]{3,2,1,0:T(8,128)(2,1)}, u32[]{:S(2)}) %copy-start.3) | copy-done | bytes 524312
  34.7 1.0 %shard_map.54.k_ref = bf16[2,2,512,256]{3,2,1,0:T(8,128)(2,1)S(1)} custom-call(bf16[2,2,256,256]{3,2,1,0:T(8,128)(2,1)S(1)} %get-tuple-element.19.k_ref, bf16[2,2,256,256]{3,2,1,0:T(8,128)(2,1)S(1)} %copy-done.3, f32[1,256]{1,0:T(1,128)S(1)} %bitcast.4, bf16[80,256]{1,0:T(8,128)(2,1)S(1)} %collective-permute-done.4.got_ref, ...), custom_call_target="tpu_custom_call" | custom-call | tf_op jit(solution)/shard_map/pallas_call | solution.py:19
  35.8 0.3 shard_map.55
  36.1 0.0 copy-start.1
  36.1 4.7 %collective-permute-start.11 = (bf16[128,256]{1,0:T(8,128)(2,1)S(1)}, bf16[128,256]{1,0:T(8,128)(2,1)S(1)}, u32[]{:S(2)}, u32[]{:S(2)}) collective-permute-start(bf16[128,256]{1,0:T(8,128)(2,1)S(1)} %get-tuple-element.28), channel_id=1, source_target_pairs={{0,16},{8,24},{16,0},{24,8},{1,17},{9,25},{17,1},{25,9},{2,18},{10... | collective-permute-start | bytes 196616 | tf_op jit(solution)/shard_map/ppermute | solution.py:29
  40.8 0.0 collective-permute-done.12.a_ref
  40.8 0.3 shard_map.56
  41.1 0.0 copy-start.5
  41.1 0.1 collective-permute-start.13
  41.2 1.8 %collective-permute-done.11.refs_1_ = bf16[128,256]{1,0:T(8,128)(2,1)S(1)} collective-permute-done((bf16[128,256]{1,0:T(8,128)(2,1)S(1)}, bf16[128,256]{1,0:T(8,128)(2,1)S(1)}, u32[]{:S(2)}, u32[]{:S(2)}) %collective-permute-start.11) | collective-permute-done | bytes 65568 | tf_op jit(solution)/shard_map/ppermute | solution.py:29
  43.0 4.5 %collective-permute-done.13.refs_3_ = bf16[128,256]{1,0:T(8,128)(2,1)S(1)} collective-permute-done((bf16[128,256]{1,0:T(8,128)(2,1)S(1)}, bf16[128,256]{1,0:T(8,128)(2,1)S(1)}, u32[]{:S(2)}, u32[]{:S(2)}) %collective-permute-start.13) | collective-permute-done | bytes 65568 | tf_op jit(solution)/shard_map/ppermute | solution.py:29
  47.5 0.0 copy-done.1
  47.5 0.0 copy-done.5
  47.5 0.1 shard_map.57
  47.7 0.7 %copy.5 = f32[64,2,2,256]{3,2,1,0:T(2,128)} copy(f32[64,2,2,256]{3,2,1,0:T(2,128)S(1)} %shard_map.57) | data formatting | bytes 524288
  (3 shorter events, 0.0 us)
Async XLA Ops:
  1.8 3.8 %copy-start = (bf16[1024,256]{1,0:T(8,128)(2,1)}, bf16[1024,256]{1,0:T(8,128)(2,1)S(1)}, u32[]{:S(2)}) copy-start(bf16[1024,256]{1,0:T(8,128)(2,1)S(1)} %get-tuple-element.18.x_ref) | copy-start | bytes 1572868
  1.8 3.8 %collective-permute-start = (bf16[512,256]{1,0:T(8,128)(2,1)S(1)}, bf16[512,256]{1,0:T(8,128)(2,1)S(1)}, u32[]{:S(2)}, u32[]{:S(2)}) collective-permute-start(bf16[512,256]{1,0:T(8,128)(2,1)S(1)} %get-tuple-element.20), channel_id=1, source_target_pairs={{0,1},{1,0},{2,3},{3,2},{4,5},{5,4},{6,7},{7,6},{8,9},{9,8},{10,11... | collective-permute-start | bytes 786440 | tf_op jit(solution)/shard_map/ppermute | solution.py:29
  2.3 30.5 %collective-permute-start.8 = (bf16[2,2,256,256]{3,2,1,0:T(8,128)(2,1)}, bf16[2,2,256,256]{3,2,1,0:T(8,128)(2,1)S(1)}, u32[]{:S(2)}, u32[]{:S(2)}) collective-permute-start(bf16[2,2,256,256]{3,2,1,0:T(8,128)(2,1)} %k_hbm.1), channel_id=1, source_target_pairs={{0,8},{8,0},{16,24},{24,16},{1,9},{9,1},{17,25},{25,17},{2,10},{10... | collective-permute-start | bytes 1572872 | tf_op jit(solution)/shard_map/ppermute | solution.py:29
  5.6 4.3 %collective-permute-start.1 = (bf16[128,256]{1,0:T(8,128)(2,1)S(1)}, bf16[128,256]{1,0:T(8,128)(2,1)S(1)}, u32[]{:S(2)}, u32[]{:S(2)}) collective-permute-start(bf16[128,256]{1,0:T(8,128)(2,1)S(1)} %get-tuple-element.22), channel_id=1, source_target_pairs={{0,2},{1,3},{2,0},{3,1},{4,6},{5,7},{6,4},{7,5},{8,10},{9,11},{10,... | collective-permute-start | bytes 196616 | tf_op jit(solution)/shard_map/ppermute | solution.py:29
  7.2 4.3 %collective-permute-start.2 = (bf16[128,256]{1,0:T(8,128)(2,1)S(1)}, bf16[128,256]{1,0:T(8,128)(2,1)S(1)}, u32[]{:S(2)}, u32[]{:S(2)}) collective-permute-start(bf16[128,256]{1,0:T(8,128)(2,1)S(1)} %get-tuple-element.23), channel_id=1, source_target_pairs={{0,4},{1,5},{2,6},{3,7},{4,0},{5,1},{6,2},{7,3},{8,12},{9,13},{10,... | collective-permute-start | bytes 196616 | tf_op jit(solution)/shard_map/ppermute | solution.py:29
  8.7 0.7 %copy-start.4 = (f32[256]{0:T(256)S(1)}, f32[256]{0:T(256)}, u32[]{:S(2)}) copy-start(f32[256]{0:T(256)} %param.7) | copy-start | bytes 3076
  8.7 5.2 %collective-permute-start.3 = (bf16[128,256]{1,0:T(8,128)(2,1)S(1)}, bf16[128,256]{1,0:T(8,128)(2,1)S(1)}, u32[]{:S(2)}, u32[]{:S(2)}) collective-permute-start(bf16[128,256]{1,0:T(8,128)(2,1)S(1)} %get-tuple-element.24), channel_id=1, source_target_pairs={{0,6},{1,7},{2,4},{3,5},{4,2},{5,3},{6,0},{7,1},{8,14},{9,15},{10,... | collective-permute-start | bytes 196616 | tf_op jit(solution)/shard_map/ppermute | solution.py:29
  13.9 4.6 %collective-permute-start.4 = (bf16[80,256]{1,0:T(8,128)(2,1)S(1)}, bf16[80,256]{1,0:T(8,128)(2,1)S(1)}, u32[]{:S(2)}, u32[]{:S(2)}) collective-permute-start(bf16[80,256]{1,0:T(8,128)(2,1)S(1)} %get-tuple-element.26), channel_id=1, source_target_pairs={{0,8},{8,0},{16,24},{24,16},{1,9},{9,1},{17,25},{25,17},{2,10},{10... | collective-permute-start | bytes 122888 | tf_op jit(solution)/shard_map/ppermute | solution.py:29
  18.6 5.2 %collective-permute-start.7 = (bf16[128,256]{1,0:T(8,128)(2,1)S(1)}, bf16[128,256]{1,0:T(8,128)(2,1)S(1)}, u32[]{:S(2)}, u32[]{:S(2)}) collective-permute-start(bf16[128,256]{1,0:T(8,128)(2,1)S(1)} %shard_map.51.mine_ref), channel_id=1, source_target_pairs={{0,6},{1,7},{2,4},{3,5},{4,2},{5,3},{6,0},{7,1},{8,14},{9,15},{10,... | collective-permute-start | bytes 196616 | tf_op jit(solution)/shard_map/ppermute | solution.py:29
  21.2 4.3 %collective-permute-start.6 = (bf16[128,256]{1,0:T(8,128)(2,1)S(1)}, bf16[128,256]{1,0:T(8,128)(2,1)S(1)}, u32[]{:S(2)}, u32[]{:S(2)}) collective-permute-start(bf16[128,256]{1,0:T(8,128)(2,1)S(1)} %shard_map.51.mine_ref), channel_id=1, source_target_pairs={{0,4},{1,5},{2,6},{3,7},{4,0},{5,1},{6,2},{7,3},{8,12},{9,13},{10,... | collective-permute-start | bytes 196616 | tf_op jit(solution)/shard_map/ppermute | solution.py:29
  21.7 4.3 %collective-permute-start.5 = (bf16[128,256]{1,0:T(8,128)(2,1)S(1)}, bf16[128,256]{1,0:T(8,128)(2,1)S(1)}, u32[]{:S(2)}, u32[]{:S(2)}) collective-permute-start(bf16[128,256]{1,0:T(8,128)(2,1)S(1)} %shard_map.51.mine_ref), channel_id=1, source_target_pairs={{0,2},{1,3},{2,0},{3,1},{4,6},{5,7},{6,4},{7,5},{8,10},{9,11},{10,... | collective-permute-start | bytes 196616 | tf_op jit(solution)/shard_map/ppermute | solution.py:29
  26.0 14.8 %collective-permute-start.12 = (bf16[512,256]{1,0:T(8,128)(2,1)S(1)}, bf16[512,256]{1,0:T(8,128)(2,1)S(1)}, u32[]{:S(2)}, u32[]{:S(2)}) collective-permute-start(bf16[512,256]{1,0:T(8,128)(2,1)S(1)} %shard_map.52.a_ref), channel_id=1, source_target_pairs={{0,1},{1,0},{2,3},{3,2},{4,5},{5,4},{6,7},{7,6},{8,9},{9,8},{10,11... | collective-permute-start | bytes 786440 | tf_op jit(solution)/shard_map/ppermute | solution.py:29
  26.3 6.5 %collective-permute-start.10 = (bf16[8,1024]{1,0:T(8,128)(2,1)S(1)}, bf16[8,1024]{1,0:T(8,128)(2,1)S(1)}, u32[]{:S(2)}, u32[]{:S(2)}) collective-permute-start(bf16[8,1024]{1,0:T(8,128)(2,1)S(1)} %shard_map.53), channel_id=1, source_target_pairs={{8,24},{16,0},{9,25},{17,1},{10,26},{18,2},{11,27},{19,3},{12,28},... | collective-permute-start | bytes 49160 | tf_op jit(solution)/shard_map/ppermute | solution.py:29
  27.6 5.2 %collective-permute-start.9 = (bf16[8,1024]{1,0:T(8,128)(2,1)S(1)}, bf16[8,1024]{1,0:T(8,128)(2,1)S(1)}, u32[]{:S(2)}, u32[]{:S(2)}) collective-permute-start(bf16[8,1024]{1,0:T(8,128)(2,1)S(1)} %shard_map.53), channel_id=1, source_target_pairs={{8,16},{16,8},{9,17},{17,9},{10,18},{18,10},{11,19},{19,11},{12,20... | collective-permute-start | bytes 49160 | tf_op jit(solution)/shard_map/ppermute | solution.py:29
  32.9 0.8 %copy-start.2 = (bf16[2,2,256,256]{3,2,1,0:T(8,128)(2,1)}, bf16[2,2,256,256]{3,2,1,0:T(8,128)(2,1)S(1)}, u32[]{:S(2)}) copy-start(bf16[2,2,256,256]{3,2,1,0:T(8,128)(2,1)S(1)} %collective-permute-done.8.mate_ref) | copy-start | bytes 1572868
  33.7 1.0 %copy-start.3 = (bf16[2,2,256,256]{3,2,1,0:T(8,128)(2,1)S(1)}, bf16[2,2,256,256]{3,2,1,0:T(8,128)(2,1)}, u32[]{:S(2)}) copy-start(bf16[2,2,256,256]{3,2,1,0:T(8,128)(2,1)} %copy-done.2) | copy-start | bytes 1572868
  36.1 11.5 %copy-start.1 = (bf16[1024,256]{1,0:T(8,128)(2,1)S(1)}, bf16[1024,256]{1,0:T(8,128)(2,1)}, u32[]{:S(2)}) copy-start(bf16[1024,256]{1,0:T(8,128)(2,1)} %copy-done) | copy-start | bytes 1572868
  36.1 6.9 %collective-permute-start.11 = (bf16[128,256]{1,0:T(8,128)(2,1)S(1)}, bf16[128,256]{1,0:T(8,128)(2,1)S(1)}, u32[]{:S(2)}, u32[]{:S(2)}) collective-permute-start(bf16[128,256]{1,0:T(8,128)(2,1)S(1)} %get-tuple-element.28), channel_id=1, source_target_pairs={{0,16},{8,24},{16,0},{24,8},{1,17},{9,25},{17,1},{25,9},{2,18},{10... | collective-permute-start | bytes 196616 | tf_op jit(solution)/shard_map/ppermute | solution.py:29
  41.1 6.4 %copy-start.5 = (f32[2,256]{1,0:T(2,128)S(1)}, f32[2,256]{1,0:T(2,128)}, u32[]{:S(2)}) copy-start(f32[2,256]{1,0:T(2,128)} %noise_ref.1) | copy-start | bytes 6148
  41.1 6.4 %collective-permute-start.13 = (bf16[128,256]{1,0:T(8,128)(2,1)S(1)}, bf16[128,256]{1,0:T(8,128)(2,1)S(1)}, u32[]{:S(2)}, u32[]{:S(2)}) collective-permute-start(bf16[128,256]{1,0:T(8,128)(2,1)S(1)} %get-tuple-element.30), channel_id=1, source_target_pairs={{0,16},{8,24},{16,0},{24,8},{1,17},{9,25},{17,1},{25,9},{2,18},{10... | collective-permute-start | bytes 196616 | tf_op jit(solution)/shard_map/ppermute | solution.py:29

commit v5 on v4

--- a/solution.py
+++ b/solution.py
@@ -11,8 +11,9 @@
 BF = jnp.bfloat16
 F32 = jnp.float32
 LANES = 128
+LIMIT = 24 * 2**20
 VMEM = pl.BlockSpec(memory_space=pltpu.VMEM)
-HBM = pl.BlockSpec(memory_space=pl.ANY)
+HBM = pl.BlockSpec(memory_space=pltpu.HBM)
 
 
 def call(body, ins, outs, scratch=(), raw=()):
@@ -22,11 +23,8 @@
         out_specs=[VMEM] * len(outs),
         out_shape=[pltpu.VMEM(*o) for o in outs],
         scratch_shapes=list(scratch),
-    )(*raw, *[pltpu.with_memory_space_constraint(v, pltpu.VMEM) for v in ins])
-
-
-def move(value, axis, perm):
-    return lax.ppermute(value, axis, perm)
+        compiler_params=pltpu.CompilerParams(vmem_limit_bytes=LIMIT),
+    )(*[pltpu.with_memory_space_constraint(v, pltpu.HBM) for v in raw], *[pltpu.with_memory_space_constraint(v, pltpu.VMEM) for v in ins])
 
 
 def pair_perm(axis, step):
@@ -77,12 +75,14 @@
         o_ref[rows:, at] = (u_ref[t, imag, :] - u_ref[tiles + t, real, :]).astype(o_ref.dtype)
 
 
-def adjoint_other_body(v_hbm, k_hbm, o_ref, x_ref, k_ref, v_ref, u_ref, sems):
+def adjoint_other_body(v_hbm, k_hbm, d_hbm, n_hbm, o_ref, x_ref, k_ref, d_ref, n_ref, v_ref, u_ref, sems):
     freq = 1 - parity()
     copies = [
         pltpu.make_async_copy(v_hbm, v_ref, sems.at[0]),
         pltpu.make_async_copy(k_hbm.at[freq], k_ref.at[freq], sems.at[1]),
         pltpu.make_async_copy(k_hbm.at[1 - freq], k_ref.at[1 - freq], sems.at[2]),
+        pltpu.make_async_copy(d_hbm, d_ref, sems.at[3]),
+        pltpu.make_async_copy(n_hbm, n_ref, sems.at[4]),
     ]
     for copy in copies:
         copy.start()
@@ -91,7 +91,8 @@
     x_ref[...] = x
     copies[1].wait()
     adjoint(freq, x, k_ref, o_ref, u_ref)
-    copies[2].wait()
+    for copy in copies[2:]:
+        copy.wait()
 
 
 def adjoint_own_body(x_ref, k_ref, o_ref, u_ref):
@@ -297,7 +298,7 @@
 
     tail = jnp.concatenate(three(coef) + [jnp.zeros((13, width), BF)], axis=0)
     give = jnp.concatenate([chosen(1 - a, 1), chosen(a, 1), tail], axis=0)
-    give = move(give, "row", pair_perm("row", 1))
+    give = lax.ppermute(give, "row", pair_perm("row", 1))
     half = rows // 2
     mine = jnp.concatenate([chosen(a, 0), give[half:rows]], axis=0)
     other = jnp.concatenate([chosen(1 - a, 0), give[:half]], axis=0)
@@ -309,14 +310,14 @@
     size = rows // chips
     keep, *sends = call(split_body, (own, got), [((size, width), F32)] + [((size, width), BF)] * (chips - 1))
     fence = call(fence_body, (coef,), [((8, LANES), F32)])[0]
-    got = [move(v, "col", pair_perm("col", 2 * (d + 1))) for d, v in enumerate(sends)]
+    got = [lax.ppermute(v, "col", pair_perm("col", 2 * (d + 1))) for d, v in enumerate(sends)]
     stay, give = call(sum_body, (keep, coef, fence, *got), [((size // 2, width), BF), ((size // 2 + 16, width), BF)])
     fence = call(fence_body, (coef,), [((8, LANES), F32)])[0]
-    give = move(give, "row", pair_perm("row", 1))
+    give = lax.ppermute(give, "row", pair_perm("row", 1))
     mine = call(pack_body, (stay, give, fence), [((size, width), BF)])[0]
-    got = [move(mine, "col", pair_perm("col", 2 * (d + 1))) for d in range(chips - 1)]
+    got = [lax.ppermute(mine, "col", pair_perm("col", 2 * (d + 1))) for d in range(chips - 1)]
     mine = call(join_body, (mine, *got), [((rows, width), BF)])[0]
-    return mine, move(mine, "col", pair_perm("col", 1)), give
+    return mine, lax.ppermute(mine, "col", pair_perm("col", 1)), give
 
 
 def apply(kernel, probes, noise_var, prior_diag):
@@ -327,23 +328,23 @@
     coef = prior_diag[None, :]
     flat = (4 * count, rows)
     scratch = pltpu.VMEM((2 * width // LANES, 4 * count, LANES), F32)
-    mate = move(kernel, "row", pair_perm("row", 1))
-    other, x, kernel = call(
+    mate = lax.ppermute(kernel, "row", pair_perm("row", 1))
+    other, x, kernel, coef, noise = call(
         adjoint_other_body,
         (),
-        [((2 * count, width), BF), (flat, BF), (kernel.shape, BF)],
-        (pltpu.VMEM(probes.shape, BF), scratch, pltpu.SemaphoreType.DMA((3,))),
-        raw=(probes, kernel),
+        [((2 * count, width), BF), (flat, BF), (kernel.shape, BF), (coef.shape, F32), (noise_var.shape, F32)],
+        (pltpu.VMEM(probes.shape, BF), scratch, pltpu.SemaphoreType.DMA((5,))),
+        raw=(probes, kernel, coef, noise_var),
     )
-    got = move(other, "col", pair_perm("col", 1))
+    got = lax.ppermute(other, "col", pair_perm("col", 1))
     own = call(adjoint_own_body, (x, kernel), [((2 * count, width), F32)], (scratch,))[0]
     seam = call(seam_body, (kernel, coef), [((8, 4 * rows), BF)])[0]
     odd = [i for i in range(blocks) if i % 2]
     even = [i for i in range(blocks) if i % 2 == 0]
     near = [(i, i + 1) for i in odd if i + 1 < blocks] + [(i, i - 1) for i in even if i]
     far = [(i, i + 2) for i in odd if i + 2 < blocks] + [(i, i - 2) for i in even if i]
-    near = move(seam, "row", near)
-    far = move(seam, "row", far)
+    near = lax.ppermute(seam, "row", near)
+    far = lax.ppermute(seam, "row", far)
     if chips > 4:
         mine, other, give = wide_sum(own, got, coef, blocks)
     else:
@@ -359,10 +360,10 @@
             [((2 * size, rows), F32)] + [((2 * size, rows), BF)] * peers,
         )
         groups.append(keep)
-        groups += [move(v, "row", pair_perm("row", 2 * (d + 1))) for d, v in enumerate(sends)]
+        groups += [lax.ppermute(v, "row", pair_perm("row", 2 * (d + 1))) for d, v in enumerate(sends)]
     return call(
         functools.partial(final_body, peers),
-        (x, noise_var, *groups),
+        (x, noise, *groups),
         [((size,) + probes.shape[1:3] + (rows,), F32)],
         (pltpu.VMEM((rows // LANES, 4 * size, LANES), F32),),
     )[0]

time: 48.6 us -> 46.5 us (0.957)
  local copies, waits for them, and re-layouts: 2.76 us -> 0.71 us
    unnamed x13 -> x3, local copies, waits for them, and re-layouts: 2.76 us -> 0.71 us
  transfers between devices with their start and end apart: 14 -> 14, of which waited for: 10 -> 10; matrix products, arithmetic and copies ran while one was open for 0% -> 0% of each run, Pallas kernels for 5% -> 6%
where the time goes in v5:
time: 46.5 us; the launch traced here: 46.4 us
  waiting for transfers between devices  23 us (49%)
  starting transfers between devices  18 us (39%)
  Pallas kernels  4.58 us (10%)
  local copies, waits for them, and re-layouts  0.71 us (2%)
    ppermute x2, waiting for transfers between devices, apply(): lax.ppermute(v, 'row', pair_perm('row', 2 * (d + 1)))  6.35 us
    ppermute x2, starting transfers between devices, apply(): lax.ppermute(v, 'row', pair_perm('row', 2 * (d + 1)))  4.78 us
    ppermute x3, waiting for transfers between devices, chip_sum(): lax.ppermute(v, 'col', pair_perm('col', 2 * (d + 1)))  4.69 us
    pallas_call x12, Pallas kernels, call(): pl.pallas_call(body, in_specs=[HBM] * len(raw) + [VMEM] * len(ins), out_s...  4.58 us
    ppermute x1, waiting for transfers between devices, apply(): far = lax.ppermute(seam, 'row', far)  4.56 us
    ppermute x3, waiting for transfers between devices, chip_sum(): lax.ppermute(mine, 'col', pair_perm('col', 2 * (d + 1)))  3.9 us
    ppermute x3, starting transfers between devices, chip_sum(): lax.ppermute(v, 'col', pair_perm('col', 2 * (d + 1)))  3.55 us
    ppermute x1, waiting for transfers between devices, chip_sum(): give = lax.ppermute(give, 'row', pair_perm('row', 1))  3.51 us
  transfers between devices with their start and end apart: 14, of which 10 were waited for; matrix products, arithmetic and copies ran while one was open for 0% of the time, Pallas kernels for 6%

profile of v5, /device:TPU:0, one launch (start us, length us, event | category | flops | bytes accessed | tf_op | source)
XLA Modules:
  0.0 46.4 jit_solution(13367346128752677071)
XLA Ops:
  0.0 0.0 copy-start
  0.0 1.8 %shard_map.46 = (bf16[512,256]{1,0:T(8,128)(2,1)S(1)}, bf16[1024,256]{1,0:T(8,128)(2,1)S(1)}, bf16[2,2,256,256]{3,2,1,0:T(8,128)(2,1)S(1)}, f32[1,256]{1,0:T(1,128)S(1)}, f32[2,256]{1,0:T(2,128)S(1)}) custom-call(bf16[256,2,2,256]{3,2,1,0:T(2,128)(2,1)} %v_hbm.1, bf16[2,2,256,256]{3,2,1,0:T(8,128)(2,1)} %k_hbm.1, f32[1,256]{1,0:T(1,128)} %bitcast.1, ...), custom_call_target="tpu_custom_call" | custom-call | tf_op jit(solution)/shard_map/pallas_call | solution.py:20
  1.8 0.6 %collective-permute-start = (bf16[512,256]{1,0:T(8,128)(2,1)S(1)}, bf16[512,256]{1,0:T(8,128)(2,1)S(1)}, u32[]{:S(2)}, u32[]{:S(2)}) collective-permute-start(bf16[512,256]{1,0:T(8,128)(2,1)S(1)} %get-tuple-element.23), channel_id=1, source_target_pairs={{0,1},{1,0},{2,3},{3,2},{4,5},{5,4},{6,7},{7,6},{8,9},{9,8},{10,11... | collective-permute-start | bytes 786440 | tf_op jit(solution)/shard_map/ppermute | solution.py:339
  2.4 0.0 copy-done
  2.4 2.6 %collective-permute-start.8 = (bf16[2,2,256,256]{3,2,1,0:T(8,128)(2,1)S(1)}, bf16[2,2,256,256]{3,2,1,0:T(8,128)(2,1)S(1)}, u32[]{:S(2)}, u32[]{:S(2)}) collective-permute-start(bf16[2,2,256,256]{3,2,1,0:T(8,128)(2,1)S(1)} %copy-done), channel_id=1, source_target_pairs={{0,8},{8,0},{16,24},{24,16},{1,9},{9,1},{17,25},{25,17},{2,10},{10... | collective-permute-start | bytes 1572872 | tf_op jit(solution)/shard_map/ppermute | solution.py:331
  5.0 0.6 %shard_map.47.own_ref = f32[512,256]{1,0:T(8,128)S(1)} custom-call(bf16[1024,256]{1,0:T(8,128)(2,1)S(1)} %get-tuple-element.20.x_ref, bf16[2,2,256,256]{3,2,1,0:T(8,128)(2,1)S(1)} %get-tuple-element.22.k_ref), custom_call_target="tpu_custom_call" | custom-call | tf_op jit(solution)/shard_map/pallas_call | solution.py:20
  5.6 0.0 collective-permute-done.got_ref
  5.6 0.1 shard_map.48
  5.7 1.5 %collective-permute-start.1 = (bf16[128,256]{1,0:T(8,128)(2,1)S(1)}, bf16[128,256]{1,0:T(8,128)(2,1)S(1)}, u32[]{:S(2)}, u32[]{:S(2)}) collective-permute-start(bf16[128,256]{1,0:T(8,128)(2,1)S(1)} %get-tuple-element.26), channel_id=1, source_target_pairs={{0,2},{1,3},{2,0},{3,1},{4,6},{5,7},{6,4},{7,5},{8,10},{9,11},{10,... | collective-permute-start | bytes 196616 | tf_op jit(solution)/shard_map/ppermute | solution.py:313
  7.3 1.5 %collective-permute-start.2 = (bf16[128,256]{1,0:T(8,128)(2,1)S(1)}, bf16[128,256]{1,0:T(8,128)(2,1)S(1)}, u32[]{:S(2)}, u32[]{:S(2)}) collective-permute-start(bf16[128,256]{1,0:T(8,128)(2,1)S(1)} %get-tuple-element.27), channel_id=1, source_target_pairs={{0,4},{1,5},{2,6},{3,7},{4,0},{5,1},{6,2},{7,3},{8,12},{9,13},{10,... | collective-permute-start | bytes 196616 | tf_op jit(solution)/shard_map/ppermute | solution.py:313
  8.8 0.5 %collective-permute-start.3 = (bf16[128,256]{1,0:T(8,128)(2,1)S(1)}, bf16[128,256]{1,0:T(8,128)(2,1)S(1)}, u32[]{:S(2)}, u32[]{:S(2)}) collective-permute-start(bf16[128,256]{1,0:T(8,128)(2,1)S(1)} %get-tuple-element.28), channel_id=1, source_target_pairs={{0,6},{1,7},{2,4},{3,5},{4,2},{5,3},{6,0},{7,1},{8,14},{9,15},{10,... | collective-permute-start | bytes 196616 | tf_op jit(solution)/shard_map/ppermute | solution.py:313
  9.3 0.8 %collective-permute-done.1.refs_0_ = bf16[128,256]{1,0:T(8,128)(2,1)S(1)} collective-permute-done((bf16[128,256]{1,0:T(8,128)(2,1)S(1)}, bf16[128,256]{1,0:T(8,128)(2,1)S(1)}, u32[]{:S(2)}, u32[]{:S(2)}) %collective-permute-start.1) | collective-permute-done | bytes 65568 | tf_op jit(solution)/shard_map/ppermute | solution.py:313
  10.0 1.5 %collective-permute-done.2.refs_1_ = bf16[128,256]{1,0:T(8,128)(2,1)S(1)} collective-permute-done((bf16[128,256]{1,0:T(8,128)(2,1)S(1)}, bf16[128,256]{1,0:T(8,128)(2,1)S(1)}, u32[]{:S(2)}, u32[]{:S(2)}) %collective-permute-start.2) | collective-permute-done | bytes 65568 | tf_op jit(solution)/shard_map/ppermute | solution.py:313
  11.5 2.4 %collective-permute-done.3.refs_2_ = bf16[128,256]{1,0:T(8,128)(2,1)S(1)} collective-permute-done((bf16[128,256]{1,0:T(8,128)(2,1)S(1)}, bf16[128,256]{1,0:T(8,128)(2,1)S(1)}, u32[]{:S(2)}, u32[]{:S(2)}) %collective-permute-start.3) | collective-permute-done | bytes 65568 | tf_op jit(solution)/shard_map/ppermute | solution.py:313
  14.0 0.1 shard_map.50
  14.0 0.9 %collective-permute-start.4 = (bf16[80,256]{1,0:T(8,128)(2,1)S(1)}, bf16[80,256]{1,0:T(8,128)(2,1)S(1)}, u32[]{:S(2)}, u32[]{:S(2)}) collective-permute-start(bf16[80,256]{1,0:T(8,128)(2,1)S(1)} %get-tuple-element.30), channel_id=1, source_target_pairs={{0,8},{8,0},{16,24},{24,16},{1,9},{9,1},{17,25},{25,17},{2,10},{10... | collective-permute-start | bytes 122888 | tf_op jit(solution)/shard_map/ppermute | solution.py:316
  14.9 3.5 %collective-permute-done.4.got_ref = bf16[80,256]{1,0:T(8,128)(2,1)S(1)} collective-permute-done((bf16[80,256]{1,0:T(8,128)(2,1)S(1)}, bf16[80,256]{1,0:T(8,128)(2,1)S(1)}, u32[]{:S(2)}, u32[]{:S(2)}) %collective-permute-start.4) | collective-permute-done | bytes 40992 | tf_op jit(solution)/shard_map/ppermute | solution.py:316
  18.4 2.6 %collective-permute-start.7 = (bf16[128,256]{1,0:T(8,128)(2,1)S(1)}, bf16[128,256]{1,0:T(8,128)(2,1)S(1)}, u32[]{:S(2)}, u32[]{:S(2)}) collective-permute-start(bf16[128,256]{1,0:T(8,128)(2,1)S(1)} %shard_map.51.mine_ref), channel_id=1, source_target_pairs={{0,6},{1,7},{2,4},{3,5},{4,2},{5,3},{6,0},{7,1},{8,14},{9,15},{10,... | collective-permute-start | bytes 196616 | tf_op jit(solution)/shard_map/ppermute | solution.py:318
  21.1 0.5 %collective-permute-start.6 = (bf16[128,256]{1,0:T(8,128)(2,1)S(1)}, bf16[128,256]{1,0:T(8,128)(2,1)S(1)}, u32[]{:S(2)}, u32[]{:S(2)}) collective-permute-start(bf16[128,256]{1,0:T(8,128)(2,1)S(1)} %shard_map.51.mine_ref), channel_id=1, source_target_pairs={{0,4},{1,5},{2,6},{3,7},{4,0},{5,1},{6,2},{7,3},{8,12},{9,13},{10,... | collective-permute-start | bytes 196616 | tf_op jit(solution)/shard_map/ppermute | solution.py:318
  21.6 0.4 collective-permute-start.5
  21.9 1.7 %collective-permute-done.7.refs_2_ = bf16[128,256]{1,0:T(8,128)(2,1)S(1)} collective-permute-done((bf16[128,256]{1,0:T(8,128)(2,1)S(1)}, bf16[128,256]{1,0:T(8,128)(2,1)S(1)}, u32[]{:S(2)}, u32[]{:S(2)}) %collective-permute-start.7) | collective-permute-done | bytes 65568 | tf_op jit(solution)/shard_map/ppermute | solution.py:318
  23.7 1.6 %collective-permute-done.6.refs_1_ = bf16[128,256]{1,0:T(8,128)(2,1)S(1)} collective-permute-done((bf16[128,256]{1,0:T(8,128)(2,1)S(1)}, bf16[128,256]{1,0:T(8,128)(2,1)S(1)}, u32[]{:S(2)}, u32[]{:S(2)}) %collective-permute-start.6) | collective-permute-done | bytes 65568 | tf_op jit(solution)/shard_map/ppermute | solution.py:318
  25.3 0.5 %collective-permute-done.5.refs_0_ = bf16[128,256]{1,0:T(8,128)(2,1)S(1)} collective-permute-done((bf16[128,256]{1,0:T(8,128)(2,1)S(1)}, bf16[128,256]{1,0:T(8,128)(2,1)S(1)}, u32[]{:S(2)}, u32[]{:S(2)}) %collective-permute-start.5) | collective-permute-done | bytes 65568 | tf_op jit(solution)/shard_map/ppermute | solution.py:318
  25.9 0.1 collective-permute-start.12
  25.9 0.2 shard_map.53
  26.2 1.3 %collective-permute-start.10 = (bf16[8,1024]{1,0:T(8,128)(2,1)S(1)}, bf16[8,1024]{1,0:T(8,128)(2,1)S(1)}, u32[]{:S(2)}, u32[]{:S(2)}) collective-permute-start(bf16[8,1024]{1,0:T(8,128)(2,1)S(1)} %shard_map.53), channel_id=1, source_target_pairs={{8,24},{16,0},{9,25},{17,1},{10,26},{18,2},{11,27},{19,3},{12,28},... | collective-permute-start | bytes 49160 | tf_op jit(solution)/shard_map/ppermute | solution.py:347
  27.5 0.7 %collective-permute-start.9 = (bf16[8,1024]{1,0:T(8,128)(2,1)S(1)}, bf16[8,1024]{1,0:T(8,128)(2,1)S(1)}, u32[]{:S(2)}, u32[]{:S(2)}) collective-permute-start(bf16[8,1024]{1,0:T(8,128)(2,1)S(1)} %shard_map.53), channel_id=1, source_target_pairs={{8,16},{16,8},{9,17},{17,9},{10,18},{18,10},{11,19},{19,11},{12,20... | collective-permute-start | bytes 49160 | tf_op jit(solution)/shard_map/ppermute | solution.py:346
  28.2 4.6 %collective-permute-done.10.far_ref = bf16[8,1024]{1,0:T(8,128)(2,1)S(1)} collective-permute-done((bf16[8,1024]{1,0:T(8,128)(2,1)S(1)}, bf16[8,1024]{1,0:T(8,128)(2,1)S(1)}, u32[]{:S(2)}, u32[]{:S(2)}) %collective-permute-start.10) | collective-permute-done | bytes 16416 | tf_op jit(solution)/shard_map/ppermute | solution.py:347
  32.7 0.0 collective-permute-done.9.near_ref
  32.7 0.0 collective-permute-done.8.mate_ref
  32.7 1.0 %shard_map.54.k_ref = bf16[2,2,512,256]{3,2,1,0:T(8,128)(2,1)S(1)} custom-call(bf16[2,2,256,256]{3,2,1,0:T(8,128)(2,1)S(1)} %get-tuple-element.22.k_ref, bf16[2,2,256,256]{3,2,1,0:T(8,128)(2,1)S(1)} %collective-permute-done.8.mate_ref, f32[1,256]{1,0:T(1,128)S(1)} %get-tuple-element.25.d_ref, bf16[80,256]{1,0:T(8,128)(2,1)S(1)} %collective-permute-done.4.got_ref, ...), custom_call_target="tpu_custom_call" | custom-call | tf_op jit(solution)/shard_map/pallas_call | solution.py:20
  33.8 0.3 shard_map.55
  34.1 4.7 %collective-permute-start.11 = (bf16[128,256]{1,0:T(8,128)(2,1)S(1)}, bf16[128,256]{1,0:T(8,128)(2,1)S(1)}, u32[]{:S(2)}, u32[]{:S(2)}) collective-permute-start(bf16[128,256]{1,0:T(8,128)(2,1)S(1)} %get-tuple-element.32), channel_id=1, source_target_pairs={{0,16},{8,24},{16,0},{24,8},{1,17},{9,25},{17,1},{25,9},{2,18},{10... | collective-permute-start | bytes 196616 | tf_op jit(solution)/shard_map/ppermute | solution.py:363
  38.8 0.0 collective-permute-done.12.a_ref
  38.8 0.3 shard_map.56
  39.1 0.1 collective-permute-start.13
  39.2 1.8 %collective-permute-done.11.refs_1_ = bf16[128,256]{1,0:T(8,128)(2,1)S(1)} collective-permute-done((bf16[128,256]{1,0:T(8,128)(2,1)S(1)}, bf16[128,256]{1,0:T(8,128)(2,1)S(1)}, u32[]{:S(2)}, u32[]{:S(2)}) %collective-permute-start.11) | collective-permute-done | bytes 65568 | tf_op jit(solution)/shard_map/ppermute | solution.py:363
  41.0 4.5 %collective-permute-done.13.refs_3_ = bf16[128,256]{1,0:T(8,128)(2,1)S(1)} collective-permute-done((bf16[128,256]{1,0:T(8,128)(2,1)S(1)}, bf16[128,256]{1,0:T(8,128)(2,1)S(1)}, u32[]{:S(2)}, u32[]{:S(2)}) %collective-permute-start.13) | collective-permute-done | bytes 65568 | tf_op jit(solution)/shard_map/ppermute | solution.py:363
  45.5 0.1 shard_map.57
  45.7 0.7 %copy.5 = f32[64,2,2,256]{3,2,1,0:T(2,128)} copy(f32[64,2,2,256]{3,2,1,0:T(2,128)S(1)} %shard_map.57) | data formatting | bytes 524288
  (3 shorter events, 0.0 us)
Async XLA Ops:
  0.0 2.4 %copy-start = (bf16[2,2,256,256]{3,2,1,0:T(8,128)(2,1)S(1)}, bf16[2,2,256,256]{3,2,1,0:T(8,128)(2,1)}, u32[]{:S(2)}) copy-start(bf16[2,2,256,256]{3,2,1,0:T(8,128)(2,1)} %k_hbm.1) | copy-start | bytes 1572868
  1.8 3.8 %collective-permute-start = (bf16[512,256]{1,0:T(8,128)(2,1)S(1)}, bf16[512,256]{1,0:T(8,128)(2,1)S(1)}, u32[]{:S(2)}, u32[]{:S(2)}) collective-permute-start(bf16[512,256]{1,0:T(8,128)(2,1)S(1)} %get-tuple-element.23), channel_id=1, source_target_pairs={{0,1},{1,0},{2,3},{3,2},{4,5},{5,4},{6,7},{7,6},{8,9},{9,8},{10,11... | collective-permute-start | bytes 786440 | tf_op jit(solution)/shard_map/ppermute | solution.py:339
  2.4 30.3 %collective-permute-start.8 = (bf16[2,2,256,256]{3,2,1,0:T(8,128)(2,1)S(1)}, bf16[2,2,256,256]{3,2,1,0:T(8,128)(2,1)S(1)}, u32[]{:S(2)}, u32[]{:S(2)}) collective-permute-start(bf16[2,2,256,256]{3,2,1,0:T(8,128)(2,1)S(1)} %copy-done), channel_id=1, source_target_pairs={{0,8},{8,0},{16,24},{24,16},{1,9},{9,1},{17,25},{25,17},{2,10},{10... | collective-permute-start | bytes 1572872 | tf_op jit(solution)/shard_map/ppermute | solution.py:331
  5.7 4.3 %collective-permute-start.1 = (bf16[128,256]{1,0:T(8,128)(2,1)S(1)}, bf16[128,256]{1,0:T(8,128)(2,1)S(1)}, u32[]{:S(2)}, u32[]{:S(2)}) collective-permute-start(bf16[128,256]{1,0:T(8,128)(2,1)S(1)} %get-tuple-element.26), channel_id=1, source_target_pairs={{0,2},{1,3},{2,0},{3,1},{4,6},{5,7},{6,4},{7,5},{8,10},{9,11},{10,... | collective-permute-start | bytes 196616 | tf_op jit(solution)/shard_map/ppermute | solution.py:313
  7.3 4.3 %collective-permute-start.2 = (bf16[128,256]{1,0:T(8,128)(2,1)S(1)}, bf16[128,256]{1,0:T(8,128)(2,1)S(1)}, u32[]{:S(2)}, u32[]{:S(2)}) collective-permute-start(bf16[128,256]{1,0:T(8,128)(2,1)S(1)} %get-tuple-element.27), channel_id=1, source_target_pairs={{0,4},{1,5},{2,6},{3,7},{4,0},{5,1},{6,2},{7,3},{8,12},{9,13},{10,... | collective-permute-start | bytes 196616 | tf_op jit(solution)/shard_map/ppermute | solution.py:313
  8.8 5.2 %collective-permute-start.3 = (bf16[128,256]{1,0:T(8,128)(2,1)S(1)}, bf16[128,256]{1,0:T(8,128)(2,1)S(1)}, u32[]{:S(2)}, u32[]{:S(2)}) collective-permute-start(bf16[128,256]{1,0:T(8,128)(2,1)S(1)} %get-tuple-element.28), channel_id=1, source_target_pairs={{0,6},{1,7},{2,4},{3,5},{4,2},{5,3},{6,0},{7,1},{8,14},{9,15},{10,... | collective-permute-start | bytes 196616 | tf_op jit(solution)/shard_map/ppermute | solution.py:313
  14.0 4.4 %collective-permute-start.4 = (bf16[80,256]{1,0:T(8,128)(2,1)S(1)}, bf16[80,256]{1,0:T(8,128)(2,1)S(1)}, u32[]{:S(2)}, u32[]{:S(2)}) collective-permute-start(bf16[80,256]{1,0:T(8,128)(2,1)S(1)} %get-tuple-element.30), channel_id=1, source_target_pairs={{0,8},{8,0},{16,24},{24,16},{1,9},{9,1},{17,25},{25,17},{2,10},{10... | collective-permute-start | bytes 122888 | tf_op jit(solution)/shard_map/ppermute | solution.py:316
  18.4 5.2 %collective-permute-start.7 = (bf16[128,256]{1,0:T(8,128)(2,1)S(1)}, bf16[128,256]{1,0:T(8,128)(2,1)S(1)}, u32[]{:S(2)}, u32[]{:S(2)}) collective-permute-start(bf16[128,256]{1,0:T(8,128)(2,1)S(1)} %shard_map.51.mine_ref), channel_id=1, source_target_pairs={{0,6},{1,7},{2,4},{3,5},{4,2},{5,3},{6,0},{7,1},{8,14},{9,15},{10,... | collective-permute-start | bytes 196616 | tf_op jit(solution)/shard_map/ppermute | solution.py:318
  21.1 4.3 %collective-permute-start.6 = (bf16[128,256]{1,0:T(8,128)(2,1)S(1)}, bf16[128,256]{1,0:T(8,128)(2,1)S(1)}, u32[]{:S(2)}, u32[]{:S(2)}) collective-permute-start(bf16[128,256]{1,0:T(8,128)(2,1)S(1)} %shard_map.51.mine_ref), channel_id=1, source_target_pairs={{0,4},{1,5},{2,6},{3,7},{4,0},{5,1},{6,2},{7,3},{8,12},{9,13},{10,... | collective-permute-start | bytes 196616 | tf_op jit(solution)/shard_map/ppermute | solution.py:318
  21.6 4.3 %collective-permute-start.5 = (bf16[128,256]{1,0:T(8,128)(2,1)S(1)}, bf16[128,256]{1,0:T(8,128)(2,1)S(1)}, u32[]{:S(2)}, u32[]{:S(2)}) collective-permute-start(bf16[128,256]{1,0:T(8,128)(2,1)S(1)} %shard_map.51.mine_ref), channel_id=1, source_target_pairs={{0,2},{1,3},{2,0},{3,1},{4,6},{5,7},{6,4},{7,5},{8,10},{9,11},{10,... | collective-permute-start | bytes 196616 | tf_op jit(solution)/shard_map/ppermute | solution.py:318
  25.9 12.9 %collective-permute-start.12 = (bf16[512,256]{1,0:T(8,128)(2,1)S(1)}, bf16[512,256]{1,0:T(8,128)(2,1)S(1)}, u32[]{:S(2)}, u32[]{:S(2)}) collective-permute-start(bf16[512,256]{1,0:T(8,128)(2,1)S(1)} %shard_map.52.a_ref), channel_id=1, source_target_pairs={{0,1},{1,0},{2,3},{3,2},{4,5},{5,4},{6,7},{7,6},{8,9},{9,8},{10,11... | collective-permute-start | bytes 786440 | tf_op jit(solution)/shard_map/ppermute | solution.py:320
  26.2 6.5 %collective-permute-start.10 = (bf16[8,1024]{1,0:T(8,128)(2,1)S(1)}, bf16[8,1024]{1,0:T(8,128)(2,1)S(1)}, u32[]{:S(2)}, u32[]{:S(2)}) collective-permute-start(bf16[8,1024]{1,0:T(8,128)(2,1)S(1)} %shard_map.53), channel_id=1, source_target_pairs={{8,24},{16,0},{9,25},{17,1},{10,26},{18,2},{11,27},{19,3},{12,28},... | collective-permute-start | bytes 49160 | tf_op jit(solution)/shard_map/ppermute | solution.py:347
  27.5 5.2 %collective-permute-start.9 = (bf16[8,1024]{1,0:T(8,128)(2,1)S(1)}, bf16[8,1024]{1,0:T(8,128)(2,1)S(1)}, u32[]{:S(2)}, u32[]{:S(2)}) collective-permute-start(bf16[8,1024]{1,0:T(8,128)(2,1)S(1)} %shard_map.53), channel_id=1, source_target_pairs={{8,16},{16,8},{9,17},{17,9},{10,18},{18,10},{11,19},{19,11},{12,20... | collective-permute-start | bytes 49160 | tf_op jit(solution)/shard_map/ppermute | solution.py:346
  34.1 6.9 %collective-permute-start.11 = (bf16[128,256]{1,0:T(8,128)(2,1)S(1)}, bf16[128,256]{1,0:T(8,128)(2,1)S(1)}, u32[]{:S(2)}, u32[]{:S(2)}) collective-permute-start(bf16[128,256]{1,0:T(8,128)(2,1)S(1)} %get-tuple-element.32), channel_id=1, source_target_pairs={{0,16},{8,24},{16,0},{24,8},{1,17},{9,25},{17,1},{25,9},{2,18},{10... | collective-permute-start | bytes 196616 | tf_op jit(solution)/shard_map/ppermute | solution.py:363
  39.1 6.4 %collective-permute-start.13 = (bf16[128,256]{1,0:T(8,128)(2,1)S(1)}, bf16[128,256]{1,0:T(8,128)(2,1)S(1)}, u32[]{:S(2)}, u32[]{:S(2)}) collective-permute-start(bf16[128,256]{1,0:T(8,128)(2,1)S(1)} %get-tuple-element.34), channel_id=1, source_target_pairs={{0,16},{8,24},{16,0},{24,8},{1,17},{9,25},{17,1},{25,9},{2,18},{10... | collective-permute-start | bytes 196616 | tf_op jit(solution)/shard_map/ppermute | solution.py:363

commit v6 on v5

--- a/solution.py
+++ b/solution.py
@@ -12,6 +12,7 @@
 F32 = jnp.float32
 LANES = 128
 LIMIT = 24 * 2**20
+TAIL = 48
 VMEM = pl.BlockSpec(memory_space=pltpu.VMEM)
 HBM = pl.BlockSpec(memory_space=pltpu.HBM)
 
@@ -135,7 +136,7 @@
     return upper, (matrix - upper.astype(F32)).astype(BF)
 
 
-def operator_body(k_ref, mate_ref, d_ref, got_ref, near_ref, far_ref, o_ref):
+def operator_body(k_ref, mate_ref, d_ref, got_ref, near_ref, o_ref):
     freqs, _, rows, width = k_ref.shape
     me = lax.axis_index("row")
     odd = lax.rem(me, 2)
@@ -145,18 +146,24 @@
     own_pick = jnp.where((at < 2) & (place == at + (1 - odd) * (width - 2)), 1.0, 0.0).astype(BF)
     mate_pick = jnp.where((at < 2) & (place == at + odd * (width - 2)), 1.0, 0.0).astype(BF)
     coef = d_ref[...]
-    tail = got_ref[got_ref.shape[0] - 16:, :].astype(F32)
+    base = got_ref.shape[0] - TAIL
+    tail = got_ref[base:, :].astype(F32)
     mate_coef = tail[0:1] + tail[1:2] + tail[2:3]
 
     def last_or_first(value, last):
         return jnp.where(last, value[:, width - 1:], value[:, :1])
 
-    def outer(ref):
-        full = ref[...].astype(F32)
-        return full[0:2], full[2:3, :1] + full[3:4, :1] + full[4:5, :1]
-
-    near, near_coef = outer(near_ref)
-    far, far_coef = outer(far_ref)
+    def outer(full):
+        return full, full[2:3, :1] + full[3:4, :1] + full[4:5, :1]
+
+    def beyond_of(full, block):
+        last = lax.axis_size("row") - 1
+        there = jnp.where(lax.rem(block, 2) == 1, block < last, block > 0)
+        return jnp.where(there, full, 0.0)
+
+    near, near_coef = outer(near_ref[...].astype(F32))
+    far = jnp.concatenate([tail[16 + 8 * n:24 + 8 * n] for n in range(2 * freqs)], axis=1)
+    far, far_coef = outer(far)
     sides = (
         (k_ref, coef, me, near, near_coef, mate_ref, mate_pick, last_or_first(mate_coef, is_odd), is_odd),
         (mate_ref, mate_coef, xor(me, 1), far, far_coef, k_ref, own_pick, last_or_first(coef, ~is_odd), ~is_odd),
@@ -171,7 +178,7 @@
                 value = dot_nt(upper, own) + dot_nt(lower, own)
                 inside = dot_nt(pick, inner_ref[f, c])[0:2]
                 lo = (f * 2 + c) * rows
-                beyond = outside[:, lo:lo + rows]
+                beyond = beyond_of(outside[0:2, lo:lo + rows], block)
                 left = jnp.where(inner_left, inside, beyond)
                 right = jnp.where(inner_left, beyond, inside)
                 extra = jnp.concatenate(
@@ -187,7 +194,7 @@
                 o_ref[f, c, n * width:(n + 1) * width] = (value + extra).astype(BF)
 
 
-def split_body(own_ref, got_ref, keep_ref, *send_refs):
+def split_body(own_ref, got_ref, fence_ref, keep_ref, *send_refs):
     chips = len(send_refs) + 1
     blocks = lax.axis_size("row")
     probes = own_ref.shape[0] // 2
@@ -207,36 +214,34 @@
                     at += size
 
 
-def sum_body(keep_ref, d_ref, fence_ref, *refs):
-    stay_ref, give_ref = refs[-2:]
-    size = stay_ref.shape[0]
+def sum_body(keep_ref, d_ref, near_ref, *refs):
+    stay_ref, give_ref, long_ref = refs[-3:]
+    size, width = stay_ref.shape
     total = keep_ref[...]
-    for ref in refs[:-2]:
+    for ref in refs[:-3]:
         total = total + ref[...].astype(F32)
     stay_ref[...] = total[:size].astype(BF)
-    give_ref[:size] = total[size:].astype(BF)
-    pad = jnp.zeros((13, d_ref.shape[1]), BF)
-    give_ref[size:] = jnp.concatenate(three(d_ref[...]) + [pad], axis=0)
-
-
-def pack_body(stay_ref, got_ref, fence_ref, o_ref):
-    size = stay_ref.shape[0]
-    o_ref[:size] = stay_ref[...]
-    o_ref[size:] = got_ref[:size]
-
-
-def join_body(mine_ref, *refs):
+    give = total[size:].astype(BF)
+    give_ref[...] = give
+    long_ref[:size] = give
+    pad = jnp.zeros((13, width), BF)
+    long_ref[size:size + 16] = jnp.concatenate(three(d_ref[...]) + [pad], axis=0)
+    for n in range(4):
+        lo = size + 16 + 8 * n
+        long_ref[lo:lo + 8] = near_ref[:, n * width:(n + 1) * width]
+
+
+def join_body(*refs):
     out_ref = refs[-1]
-    pieces = (mine_ref,) + refs[:-1]
-    chips = len(pieces)
-    groups = 2 * lax.axis_size("row")
-    size = mine_ref.shape[0] // groups
+    chips = len(refs) // 2
+    groups = lax.axis_size("row")
+    size = refs[0].shape[0] // groups
     chip = lax.div(lax.axis_index("col"), 2)
-    for step, ref in enumerate(pieces):
-        source = xor(chip, step)
-        for n in range(groups):
-            lo = n * chips * size + source * size
-            out_ref[part(lo, size), :] = ref[n * size:(n + 1) * size]
+    for n, ref in enumerate(refs[:-1]):
+        source = xor(chip, n % chips)
+        for g in range(groups):
+            lo = (n // chips * groups + g) * chips * size + source * size
+            out_ref[part(lo, size), :] = ref[g * size:(g + 1) * size]
 
 
 def predict_body(swap, a_ref, k_ref, keep_ref, *refs):
@@ -282,7 +287,7 @@
     out_ref[...] = values.reshape(out_ref.shape)
 
 
-def wide_sum(own, got, coef, blocks):
+def wide_sum(own, got, coef, near, blocks):
     rows, width = own.shape
     a = parity()
     value = own + got.astype(F32)
@@ -296,8 +301,9 @@
         value = jnp.take(value, xor(me, mate + slots), axis=1)
         return value.transpose(1, 0, 2, 3).reshape(-1, width)
 
-    tail = jnp.concatenate(three(coef) + [jnp.zeros((13, width), BF)], axis=0)
-    give = jnp.concatenate([chosen(1 - a, 1), chosen(a, 1), tail], axis=0)
+    tail = three(coef) + [jnp.zeros((13, width), BF)]
+    tail += [near[:, n * width:(n + 1) * width] for n in range(4)]
+    give = jnp.concatenate([chosen(1 - a, 1), chosen(a, 1)] + tail, axis=0)
     give = lax.ppermute(give, "row", pair_perm("row", 1))
     half = rows // 2
     mine = jnp.concatenate([chosen(a, 0), give[half:rows]], axis=0)
@@ -305,19 +311,28 @@
     return mine, other, give
 
 
-def chip_sum(own, got, coef, chips):
+def cross_perm(step):
+    cols = lax.axis_size("col")
+    return [(i * cols + j, (i ^ 1) * cols + (j ^ step)) for i in range(lax.axis_size("row")) for j in range(cols)]
+
+
+def chip_sum(own, got, coef, near, chips):
     rows, width = own.shape
     size = rows // chips
-    keep, *sends = call(split_body, (own, got), [((size, width), F32)] + [((size, width), BF)] * (chips - 1))
+    half = size // 2
     fence = call(fence_body, (coef,), [((8, LANES), F32)])[0]
+    keep, *sends = call(split_body, (own, got, fence), [((size, width), F32)] + [((size, width), BF)] * (chips - 1))
     got = [lax.ppermute(v, "col", pair_perm("col", 2 * (d + 1))) for d, v in enumerate(sends)]
-    stay, give = call(sum_body, (keep, coef, fence, *got), [((size // 2, width), BF), ((size // 2 + 16, width), BF)])
-    fence = call(fence_body, (coef,), [((8, LANES), F32)])[0]
-    give = lax.ppermute(give, "row", pair_perm("row", 1))
-    mine = call(pack_body, (stay, give, fence), [((size, width), BF)])[0]
-    got = [lax.ppermute(mine, "col", pair_perm("col", 2 * (d + 1))) for d in range(chips - 1)]
-    mine = call(join_body, (mine, *got), [((rows, width), BF)])[0]
-    return mine, lax.ppermute(mine, "col", pair_perm("col", 1)), give
+    stay, give, long = call(
+        sum_body, (keep, coef, near, *got), [((half, width), BF), ((half, width), BF), ((half + TAIL, width), BF)]
+    )
+    long = lax.ppermute(long, "row", pair_perm("row", 1))
+    pieces = [stay]
+    pieces += [lax.ppermute(stay, "col", pair_perm("col", 2 * (d + 1))) for d in range(chips - 1)]
+    pieces.append(long)
+    pieces += [lax.ppermute(give, ("row", "col"), cross_perm(2 * (d + 1))) for d in range(chips - 1)]
+    mine = call(join_body, pieces, [((rows, width), BF)])[0]
+    return mine, lax.ppermute(mine, "col", pair_perm("col", 1)), long
 
 
 def apply(kernel, probes, noise_var, prior_diag):
@@ -341,15 +356,13 @@
     seam = call(seam_body, (kernel, coef), [((8, 4 * rows), BF)])[0]
     odd = [i for i in range(blocks) if i % 2]
     even = [i for i in range(blocks) if i % 2 == 0]
-    near = [(i, i + 1) for i in odd if i + 1 < blocks] + [(i, i - 1) for i in even if i]
-    far = [(i, i + 2) for i in odd if i + 2 < blocks] + [(i, i - 2) for i in even if i]
+    near = [(i, min(i + 1, blocks - 1)) for i in odd] + [(i, max(i - 1, 0)) for i in even]
     near = lax.ppermute(seam, "row", near)
-    far = lax.ppermute(seam, "row", far)
     if chips > 4:
-        mine, other, give = wide_sum(own, got, coef, blocks)
+        mine, other, give = wide_sum(own, got, coef, near, blocks)
     else:
-        mine, other, give = chip_sum(own, got, coef, chips)
-    operator = call(operator_body, (kernel, mate, coef, give, near, far), [((2, 2, 2 * width, rows), BF)])[0]
+        mine, other, give = chip_sum(own, got, coef, near, chips)
+    operator = call(operator_body, (kernel, mate, coef, give, near), [((2, 2, 2 * width, rows), BF)])[0]
     size = count // blocks
     peers = blocks // 2 - 1
     groups = []

time: 46.5 us -> 41.5 us (0.89)
  waiting for transfers between devices: 23 us -> 14.9 us
  starting transfers between devices: 18 us -> 21.1 us
    ppermute x6 -> x8, waiting for transfers between devices: 12 us -> 4.82 us  [the longest x3 2.62 us: chip_sum(): lax.ppermute(stay, 'col', pair_perm('col', 2 * (d + 1)))]
    ppermute x6 -> x8, starting transfers between devices: 5.77 us -> 10.6 us  [the longest x3 5.13 us: chip_sum(): lax.ppermute(give, ('row', 'col'), cross_perm(2 * (d + 1)))]
    ppermute x2, starting transfers between devices: 4.78 us -> 3.05 us  [apply(): lax.ppermute(v, 'row', pair_perm('row', 2 * (d + 1)))]
    ppermute x3, waiting for transfers between devices: 4.69 us -> 3.75 us  [chip_sum(): lax.ppermute(v, 'col', pair_perm('col', 2 * (d + 1)))]
    pallas_call x12 -> x11, Pallas kernels: 4.58 us -> 4.6 us  [call(): pl.pallas_call(body, in_specs=[HBM] * len(raw) + [VMEM] * len(ins), out_s...]
  transfers between devices with their start and end apart: 14 -> 16, of which waited for: 10 -> 7; matrix products, arithmetic and copies ran while one was open for 0% -> 0% of each run, Pallas kernels for 6% -> 6%
where the time goes in v6:
time: 41.5 us; the launch traced here: 41.4 us
  starting transfers between devices  21.1 us (51%)
  waiting for transfers between devices  14.9 us (36%)
  Pallas kernels  4.6 us (11%)
  local copies, waits for them, and re-layouts  0.71 us (2%)
    ppermute x2, waiting for transfers between devices, apply(): lax.ppermute(v, 'row', pair_perm('row', 2 * (d + 1)))  6.29 us
    ppermute x3, starting transfers between devices, chip_sum(): lax.ppermute(give, ('row', 'col'), cross_perm(2 * (d + 1)))  5.13 us
    pallas_call x11, Pallas kernels, call(): pl.pallas_call(body, in_specs=[HBM] * len(raw) + [VMEM] * len(ins), out_s...  4.6 us
    ppermute x3, waiting for transfers between devices, chip_sum(): lax.ppermute(v, 'col', pair_perm('col', 2 * (d + 1)))  3.75 us
    ppermute x3, starting transfers between devices, chip_sum(): lax.ppermute(v, 'col', pair_perm('col', 2 * (d + 1)))  3.55 us
    ppermute x3, starting transfers between devices, chip_sum(): lax.ppermute(stay, 'col', pair_perm('col', 2 * (d + 1)))  3.49 us
    ppermute x2, starting transfers between devices, apply(): lax.ppermute(v, 'row', pair_perm('row', 2 * (d + 1)))  3.05 us
    ppermute x1, starting transfers between devices, apply(): mate = lax.ppermute(kernel, 'row', pair_perm('row', 1))  2.64 us
  transfers between devices with their start and end apart: 16, of which 7 were waited for; matrix products, arithmetic and copies ran while one was open for 0% of the time, Pallas kernels for 6%

profile of v6, /device:TPU:0, one launch (start us, length us, event | category | flops | bytes accessed | tf_op | source)
XLA Modules:
  0.0 41.4 jit_solution(4987754582208484111)
XLA Ops:
  0.0 0.0 copy-start
  0.0 1.8 %shard_map.46 = (bf16[512,256]{1,0:T(8,128)(2,1)S(1)}, bf16[1024,256]{1,0:T(8,128)(2,1)S(1)}, bf16[2,2,256,256]{3,2,1,0:T(8,128)(2,1)S(1)}, f32[1,256]{1,0:T(1,128)S(1)}, f32[2,256]{1,0:T(2,128)S(1)}) custom-call(bf16[256,2,2,256]{3,2,1,0:T(2,128)(2,1)} %v_hbm.1, bf16[2,2,256,256]{3,2,1,0:T(8,128)(2,1)} %k_hbm.1, f32[1,256]{1,0:T(1,128)} %bitcast.1, ...), custom_call_target="tpu_custom_call" | custom-call | tf_op jit(solution)/shard_map/pallas_call | solution.py:21
  1.8 0.6 %collective-permute-start = (bf16[512,256]{1,0:T(8,128)(2,1)S(1)}, bf16[512,256]{1,0:T(8,128)(2,1)S(1)}, u32[]{:S(2)}, u32[]{:S(2)}) collective-permute-start(bf16[512,256]{1,0:T(8,128)(2,1)S(1)} %get-tuple-element.24), channel_id=1, source_target_pairs={{0,1},{1,0},{2,3},{3,2},{4,5},{5,4},{6,7},{7,6},{8,9},{9,8},{10,11... | collective-permute-start | bytes 786440 | tf_op jit(solution)/shard_map/ppermute | solution.py:354
  2.4 0.0 copy-done
  2.4 2.6 %collective-permute-start.12 = (bf16[2,2,256,256]{3,2,1,0:T(8,128)(2,1)S(1)}, bf16[2,2,256,256]{3,2,1,0:T(8,128)(2,1)S(1)}, u32[]{:S(2)}, u32[]{:S(2)}) collective-permute-start(bf16[2,2,256,256]{3,2,1,0:T(8,128)(2,1)S(1)} %copy-done), channel_id=1, source_target_pairs={{0,8},{8,0},{16,24},{24,16},{1,9},{9,1},{17,25},{25,17},{2,10},{10... | collective-permute-start | bytes 1572872 | tf_op jit(solution)/shard_map/ppermute | solution.py:346
  5.0 0.6 %shard_map.47.own_ref = f32[512,256]{1,0:T(8,128)S(1)} custom-call(bf16[1024,256]{1,0:T(8,128)(2,1)S(1)} %get-tuple-element.21.x_ref, bf16[2,2,256,256]{3,2,1,0:T(8,128)(2,1)S(1)} %get-tuple-element.23.k_ref), custom_call_target="tpu_custom_call" | custom-call | tf_op jit(solution)/shard_map/pallas_call | solution.py:21
  5.6 0.0 collective-permute-done.got_ref
  5.6 0.1 shard_map.49
  5.7 1.6 %collective-permute-start.2 = (bf16[128,256]{1,0:T(8,128)(2,1)S(1)}, bf16[128,256]{1,0:T(8,128)(2,1)S(1)}, u32[]{:S(2)}, u32[]{:S(2)}) collective-permute-start(bf16[128,256]{1,0:T(8,128)(2,1)S(1)} %get-tuple-element.27), channel_id=1, source_target_pairs={{0,2},{1,3},{2,0},{3,1},{4,6},{5,7},{6,4},{7,5},{8,10},{9,11},{10,... | collective-permute-start | bytes 196616 | tf_op jit(solution)/shard_map/ppermute | solution.py:325
  7.3 1.5 %collective-permute-start.3 = (bf16[128,256]{1,0:T(8,128)(2,1)S(1)}, bf16[128,256]{1,0:T(8,128)(2,1)S(1)}, u32[]{:S(2)}, u32[]{:S(2)}) collective-permute-start(bf16[128,256]{1,0:T(8,128)(2,1)S(1)} %get-tuple-element.28), channel_id=1, source_target_pairs={{0,4},{1,5},{2,6},{3,7},{4,0},{5,1},{6,2},{7,3},{8,12},{9,13},{10,... | collective-permute-start | bytes 196616 | tf_op jit(solution)/shard_map/ppermute | solution.py:325
  8.8 0.5 %collective-permute-start.4 = (bf16[128,256]{1,0:T(8,128)(2,1)S(1)}, bf16[128,256]{1,0:T(8,128)(2,1)S(1)}, u32[]{:S(2)}, u32[]{:S(2)}) collective-permute-start(bf16[128,256]{1,0:T(8,128)(2,1)S(1)} %get-tuple-element.29), channel_id=1, source_target_pairs={{0,6},{1,7},{2,4},{3,5},{4,2},{5,3},{6,0},{7,1},{8,14},{9,15},{10,... | collective-permute-start | bytes 196616 | tf_op jit(solution)/shard_map/ppermute | solution.py:325
  9.3 0.2 shard_map.50
  9.5 0.7 %collective-permute-start.1 = (bf16[8,1024]{1,0:T(8,128)(2,1)S(1)}, bf16[8,1024]{1,0:T(8,128)(2,1)S(1)}, u32[]{:S(2)}, u32[]{:S(2)}) collective-permute-start(bf16[8,1024]{1,0:T(8,128)(2,1)S(1)} %shard_map.50), channel_id=1, source_target_pairs={{8,16},{24,24},{0,0},{16,8},{9,17},{25,25},{1,1},{17,9},{10,18},{2... | collective-permute-start | bytes 49160 | tf_op jit(solution)/shard_map/ppermute | solution.py:360
  10.2 0.0 collective-permute-done.1.near_ref
  10.2 0.0 collective-permute-done.2.refs_0_
  10.2 1.3 %collective-permute-done.3.refs_1_ = bf16[128,256]{1,0:T(8,128)(2,1)S(1)} collective-permute-done((bf16[128,256]{1,0:T(8,128)(2,1)S(1)}, bf16[128,256]{1,0:T(8,128)(2,1)S(1)}, u32[]{:S(2)}, u32[]{:S(2)}) %collective-permute-start.3) | collective-permute-done | bytes 65568 | tf_op jit(solution)/shard_map/ppermute | solution.py:325
  11.5 2.4 %collective-permute-done.4.refs_2_ = bf16[128,256]{1,0:T(8,128)(2,1)S(1)} collective-permute-done((bf16[128,256]{1,0:T(8,128)(2,1)S(1)}, bf16[128,256]{1,0:T(8,128)(2,1)S(1)}, u32[]{:S(2)}, u32[]{:S(2)}) %collective-permute-start.4) | collective-permute-done | bytes 65568 | tf_op jit(solution)/shard_map/ppermute | solution.py:325
  14.0 3.4 %collective-permute-start.10 = (bf16[64,256]{1,0:T(8,128)(2,1)S(1)}, bf16[64,256]{1,0:T(8,128)(2,1)S(1)}, u32[]{:S(2)}, u32[]{:S(2)}) collective-permute-start(bf16[64,256]{1,0:T(8,128)(2,1)S(1)} %get-tuple-element.32), channel_id=1, source_target_pairs={{0,12},{1,13},{2,14},{3,15},{4,8},{5,9},{6,10},{7,11},{8,4},{9,5},... | collective-permute-start | bytes 98312 | tf_op jit(solution)/shard_map/ppermute | solution.py:333
  17.4 1.0 %collective-permute-start.11 = (bf16[64,256]{1,0:T(8,128)(2,1)S(1)}, bf16[64,256]{1,0:T(8,128)(2,1)S(1)}, u32[]{:S(2)}, u32[]{:S(2)}) collective-permute-start(bf16[64,256]{1,0:T(8,128)(2,1)S(1)} %get-tuple-element.32), channel_id=1, source_target_pairs={{0,14},{1,15},{2,12},{3,13},{4,10},{5,11},{6,8},{7,9},{8,6},{9,7},... | collective-permute-start | bytes 98312 | tf_op jit(solution)/shard_map/ppermute | solution.py:333
  18.4 0.5 %collective-permute-start.5 = (bf16[64,256]{1,0:T(8,128)(2,1)S(1)}, bf16[64,256]{1,0:T(8,128)(2,1)S(1)}, u32[]{:S(2)}, u32[]{:S(2)}) collective-permute-start(bf16[64,256]{1,0:T(8,128)(2,1)S(1)} %get-tuple-element.30.refs_0_), channel_id=1, source_target_pairs={{0,2},{1,3},{2,0},{3,1},{4,6},{5,7},{6,4},{7,5},{8,10},{9,11},{10,... | collective-permute-start | bytes 98312 | tf_op jit(solution)/shard_map/ppermute | solution.py:331
  18.9 1.9 %collective-permute-start.8 = (bf16[112,256]{1,0:T(8,128)(2,1)S(1)}, bf16[112,256]{1,0:T(8,128)(2,1)S(1)}, u32[]{:S(2)}, u32[]{:S(2)}) collective-permute-start(bf16[112,256]{1,0:T(8,128)(2,1)S(1)} %get-tuple-element.31), channel_id=1, source_target_pairs={{0,8},{8,0},{16,24},{24,16},{1,9},{9,1},{17,25},{25,17},{2,10},{10... | collective-permute-start | bytes 172040 | tf_op jit(solution)/shard_map/ppermute | solution.py:329
  20.8 0.0 collective-permute-done.10.refs_6_
  20.8 1.5 %collective-permute-start.6 = (bf16[64,256]{1,0:T(8,128)(2,1)S(1)}, bf16[64,256]{1,0:T(8,128)(2,1)S(1)}, u32[]{:S(2)}, u32[]{:S(2)}) collective-permute-start(bf16[64,256]{1,0:T(8,128)(2,1)S(1)} %get-tuple-element.30.refs_0_), channel_id=1, source_target_pairs={{0,4},{1,5},{2,6},{3,7},{4,0},{5,1},{6,2},{7,3},{8,12},{9,13},{10,... | collective-permute-start | bytes 98312 | tf_op jit(solution)/shard_map/ppermute | solution.py:331
  22.3 0.8 %collective-permute-done.11.refs_7_ = bf16[64,256]{1,0:T(8,128)(2,1)S(1)} collective-permute-done((bf16[64,256]{1,0:T(8,128)(2,1)S(1)}, bf16[64,256]{1,0:T(8,128)(2,1)S(1)}, u32[]{:S(2)}, u32[]{:S(2)}) %collective-permute-start.11) | collective-permute-done | bytes 32800 | tf_op jit(solution)/shard_map/ppermute | solution.py:333
  23.1 1.4 %collective-permute-start.7 = (bf16[64,256]{1,0:T(8,128)(2,1)S(1)}, bf16[64,256]{1,0:T(8,128)(2,1)S(1)}, u32[]{:S(2)}, u32[]{:S(2)}) collective-permute-start(bf16[64,256]{1,0:T(8,128)(2,1)S(1)} %get-tuple-element.30.refs_0_), channel_id=1, source_target_pairs={{0,6},{1,7},{2,4},{3,5},{4,2},{5,3},{6,0},{7,1},{8,14},{9,15},{10,... | collective-permute-start | bytes 98312 | tf_op jit(solution)/shard_map/ppermute | solution.py:331
  24.5 0.0 collective-permute-done.5.refs_1_
  24.5 0.8 %collective-permute-start.9 = (bf16[64,256]{1,0:T(8,128)(2,1)S(1)}, bf16[64,256]{1,0:T(8,128)(2,1)S(1)}, u32[]{:S(2)}, u32[]{:S(2)}) collective-permute-start(bf16[64,256]{1,0:T(8,128)(2,1)S(1)} %get-tuple-element.32), channel_id=1, source_target_pairs={{0,10},{1,11},{2,8},{3,9},{4,14},{5,15},{6,12},{7,13},{8,2},{9,3},... | collective-permute-start | bytes 98312 | tf_op jit(solution)/shard_map/ppermute | solution.py:333
  25.3 0.0 collective-permute-done.6.refs_2_
  25.3 2.6 %collective-permute-done.7.refs_3_ = bf16[64,256]{1,0:T(8,128)(2,1)S(1)} collective-permute-done((bf16[64,256]{1,0:T(8,128)(2,1)S(1)}, bf16[64,256]{1,0:T(8,128)(2,1)S(1)}, u32[]{:S(2)}, u32[]{:S(2)}) %collective-permute-start.7) | collective-permute-done | bytes 32800 | tf_op jit(solution)/shard_map/ppermute | solution.py:331
  27.9 1.4 %collective-permute-done.9.refs_5_ = bf16[64,256]{1,0:T(8,128)(2,1)S(1)} collective-permute-done((bf16[64,256]{1,0:T(8,128)(2,1)S(1)}, bf16[64,256]{1,0:T(8,128)(2,1)S(1)}, u32[]{:S(2)}, u32[]{:S(2)}) %collective-permute-start.9) | collective-permute-done | bytes 32800 | tf_op jit(solution)/shard_map/ppermute | solution.py:333
  29.3 0.0 collective-permute-done.8.refs_4_.got_ref
  29.3 0.1 shard_map.52.a_ref
  29.4 0.1 collective-permute-start.14
  29.5 0.0 collective-permute-done.12.mate_ref
  29.5 1.0 %shard_map.53.k_ref = bf16[2,2,512,256]{3,2,1,0:T(8,128)(2,1)S(1)} custom-call(bf16[2,2,256,256]{3,2,1,0:T(8,128)(2,1)S(1)} %get-tuple-element.23.k_ref, bf16[2,2,256,256]{3,2,1,0:T(8,128)(2,1)S(1)} %collective-permute-done.12.mate_ref, f32[1,256]{1,0:T(1,128)S(1)} %get-tuple-element.25.d_ref, bf16[112,256]{1,0:T(8,128)(2,1)S(1)} %collective-permute-done.8.refs_4_.got_ref, ...), custom_call_target="tpu_custom_call" | custom-call | tf_op jit(solution)/shard_map/pallas_call | solution.py:21
  30.5 0.3 shard_map.54
  30.9 1.6 %collective-permute-start.13 = (bf16[128,256]{1,0:T(8,128)(2,1)S(1)}, bf16[128,256]{1,0:T(8,128)(2,1)S(1)}, u32[]{:S(2)}, u32[]{:S(2)}) collective-permute-start(bf16[128,256]{1,0:T(8,128)(2,1)S(1)} %get-tuple-element.34), channel_id=1, source_target_pairs={{0,16},{8,24},{16,0},{24,8},{1,17},{9,25},{17,1},{25,9},{2,18},{10... | collective-permute-start | bytes 196616 | tf_op jit(solution)/shard_map/ppermute | solution.py:376
  32.5 0.0 collective-permute-done.14.a_ref
  32.5 0.3 shard_map.55
  32.8 1.4 %collective-permute-start.15 = (bf16[128,256]{1,0:T(8,128)(2,1)S(1)}, bf16[128,256]{1,0:T(8,128)(2,1)S(1)}, u32[]{:S(2)}, u32[]{:S(2)}) collective-permute-start(bf16[128,256]{1,0:T(8,128)(2,1)S(1)} %get-tuple-element.36), channel_id=1, source_target_pairs={{0,16},{8,24},{16,0},{24,8},{1,17},{9,25},{17,1},{25,9},{2,18},{10... | collective-permute-start | bytes 196616 | tf_op jit(solution)/shard_map/ppermute | solution.py:376
  34.2 5.3 %collective-permute-done.13.refs_1_ = bf16[128,256]{1,0:T(8,128)(2,1)S(1)} collective-permute-done((bf16[128,256]{1,0:T(8,128)(2,1)S(1)}, bf16[128,256]{1,0:T(8,128)(2,1)S(1)}, u32[]{:S(2)}, u32[]{:S(2)}) %collective-permute-start.13) | collective-permute-done | bytes 65568 | tf_op jit(solution)/shard_map/ppermute | solution.py:376
  39.5 1.0 %collective-permute-done.15.refs_3_ = bf16[128,256]{1,0:T(8,128)(2,1)S(1)} collective-permute-done((bf16[128,256]{1,0:T(8,128)(2,1)S(1)}, bf16[128,256]{1,0:T(8,128)(2,1)S(1)}, u32[]{:S(2)}, u32[]{:S(2)}) %collective-permute-start.15) | collective-permute-done | bytes 65568 | tf_op jit(solution)/shard_map/ppermute | solution.py:376
  40.5 0.1 shard_map.56
  40.7 0.7 %copy.5 = f32[64,2,2,256]{3,2,1,0:T(2,128)} copy(f32[64,2,2,256]{3,2,1,0:T(2,128)S(1)} %shard_map.56) | data formatting | bytes 524288
  (2 shorter events, 0.0 us)
Async XLA Ops:
  0.0 2.4 %copy-start = (bf16[2,2,256,256]{3,2,1,0:T(8,128)(2,1)S(1)}, bf16[2,2,256,256]{3,2,1,0:T(8,128)(2,1)}, u32[]{:S(2)}) copy-start(bf16[2,2,256,256]{3,2,1,0:T(8,128)(2,1)} %k_hbm.1) | copy-start | bytes 1572868
  1.8 3.8 %collective-permute-start = (bf16[512,256]{1,0:T(8,128)(2,1)S(1)}, bf16[512,256]{1,0:T(8,128)(2,1)S(1)}, u32[]{:S(2)}, u32[]{:S(2)}) collective-permute-start(bf16[512,256]{1,0:T(8,128)(2,1)S(1)} %get-tuple-element.24), channel_id=1, source_target_pairs={{0,1},{1,0},{2,3},{3,2},{4,5},{5,4},{6,7},{7,6},{8,9},{9,8},{10,11... | collective-permute-start | bytes 786440 | tf_op jit(solution)/shard_map/ppermute | solution.py:354
  2.4 27.1 %collective-permute-start.12 = (bf16[2,2,256,256]{3,2,1,0:T(8,128)(2,1)S(1)}, bf16[2,2,256,256]{3,2,1,0:T(8,128)(2,1)S(1)}, u32[]{:S(2)}, u32[]{:S(2)}) collective-permute-start(bf16[2,2,256,256]{3,2,1,0:T(8,128)(2,1)S(1)} %copy-done), channel_id=1, source_target_pairs={{0,8},{8,0},{16,24},{24,16},{1,9},{9,1},{17,25},{25,17},{2,10},{10... | collective-permute-start | bytes 1572872 | tf_op jit(solution)/shard_map/ppermute | solution.py:346
  5.7 4.5 %collective-permute-start.2 = (bf16[128,256]{1,0:T(8,128)(2,1)S(1)}, bf16[128,256]{1,0:T(8,128)(2,1)S(1)}, u32[]{:S(2)}, u32[]{:S(2)}) collective-permute-start(bf16[128,256]{1,0:T(8,128)(2,1)S(1)} %get-tuple-element.27), channel_id=1, source_target_pairs={{0,2},{1,3},{2,0},{3,1},{4,6},{5,7},{6,4},{7,5},{8,10},{9,11},{10,... | collective-permute-start | bytes 196616 | tf_op jit(solution)/shard_map/ppermute | solution.py:325
  7.3 4.3 %collective-permute-start.3 = (bf16[128,256]{1,0:T(8,128)(2,1)S(1)}, bf16[128,256]{1,0:T(8,128)(2,1)S(1)}, u32[]{:S(2)}, u32[]{:S(2)}) collective-permute-start(bf16[128,256]{1,0:T(8,128)(2,1)S(1)} %get-tuple-element.28), channel_id=1, source_target_pairs={{0,4},{1,5},{2,6},{3,7},{4,0},{5,1},{6,2},{7,3},{8,12},{9,13},{10,... | collective-permute-start | bytes 196616 | tf_op jit(solution)/shard_map/ppermute | solution.py:325
  8.8 5.2 %collective-permute-start.4 = (bf16[128,256]{1,0:T(8,128)(2,1)S(1)}, bf16[128,256]{1,0:T(8,128)(2,1)S(1)}, u32[]{:S(2)}, u32[]{:S(2)}) collective-permute-start(bf16[128,256]{1,0:T(8,128)(2,1)S(1)} %get-tuple-element.29), channel_id=1, source_target_pairs={{0,6},{1,7},{2,4},{3,5},{4,2},{5,3},{6,0},{7,1},{8,14},{9,15},{10,... | collective-permute-start | bytes 196616 | tf_op jit(solution)/shard_map/ppermute | solution.py:325
  9.5 0.7 %collective-permute-start.1 = (bf16[8,1024]{1,0:T(8,128)(2,1)S(1)}, bf16[8,1024]{1,0:T(8,128)(2,1)S(1)}, u32[]{:S(2)}, u32[]{:S(2)}) collective-permute-start(bf16[8,1024]{1,0:T(8,128)(2,1)S(1)} %shard_map.50), channel_id=1, source_target_pairs={{8,16},{24,24},{0,0},{16,8},{9,17},{25,25},{1,1},{17,9},{10,18},{2... | collective-permute-start | bytes 49160 | tf_op jit(solution)/shard_map/ppermute | solution.py:360
  14.0 6.8 %collective-permute-start.10 = (bf16[64,256]{1,0:T(8,128)(2,1)S(1)}, bf16[64,256]{1,0:T(8,128)(2,1)S(1)}, u32[]{:S(2)}, u32[]{:S(2)}) collective-permute-start(bf16[64,256]{1,0:T(8,128)(2,1)S(1)} %get-tuple-element.32), channel_id=1, source_target_pairs={{0,12},{1,13},{2,14},{3,15},{4,8},{5,9},{6,10},{7,11},{8,4},{9,5},... | collective-permute-start | bytes 98312 | tf_op jit(solution)/shard_map/ppermute | solution.py:333
  17.4 5.7 %collective-permute-start.11 = (bf16[64,256]{1,0:T(8,128)(2,1)S(1)}, bf16[64,256]{1,0:T(8,128)(2,1)S(1)}, u32[]{:S(2)}, u32[]{:S(2)}) collective-permute-start(bf16[64,256]{1,0:T(8,128)(2,1)S(1)} %get-tuple-element.32), channel_id=1, source_target_pairs={{0,14},{1,15},{2,12},{3,13},{4,10},{5,11},{6,8},{7,9},{8,6},{9,7},... | collective-permute-start | bytes 98312 | tf_op jit(solution)/shard_map/ppermute | solution.py:333
  18.4 6.1 %collective-permute-start.5 = (bf16[64,256]{1,0:T(8,128)(2,1)S(1)}, bf16[64,256]{1,0:T(8,128)(2,1)S(1)}, u32[]{:S(2)}, u32[]{:S(2)}) collective-permute-start(bf16[64,256]{1,0:T(8,128)(2,1)S(1)} %get-tuple-element.30.refs_0_), channel_id=1, source_target_pairs={{0,2},{1,3},{2,0},{3,1},{4,6},{5,7},{6,4},{7,5},{8,10},{9,11},{10,... | collective-permute-start | bytes 98312 | tf_op jit(solution)/shard_map/ppermute | solution.py:331
  18.9 10.4 %collective-permute-start.8 = (bf16[112,256]{1,0:T(8,128)(2,1)S(1)}, bf16[112,256]{1,0:T(8,128)(2,1)S(1)}, u32[]{:S(2)}, u32[]{:S(2)}) collective-permute-start(bf16[112,256]{1,0:T(8,128)(2,1)S(1)} %get-tuple-element.31), channel_id=1, source_target_pairs={{0,8},{8,0},{16,24},{24,16},{1,9},{9,1},{17,25},{25,17},{2,10},{10... | collective-permute-start | bytes 172040 | tf_op jit(solution)/shard_map/ppermute | solution.py:329
  20.8 4.5 %collective-permute-start.6 = (bf16[64,256]{1,0:T(8,128)(2,1)S(1)}, bf16[64,256]{1,0:T(8,128)(2,1)S(1)}, u32[]{:S(2)}, u32[]{:S(2)}) collective-permute-start(bf16[64,256]{1,0:T(8,128)(2,1)S(1)} %get-tuple-element.30.refs_0_), channel_id=1, source_target_pairs={{0,4},{1,5},{2,6},{3,7},{4,0},{5,1},{6,2},{7,3},{8,12},{9,13},{10,... | collective-permute-start | bytes 98312 | tf_op jit(solution)/shard_map/ppermute | solution.py:331
  23.1 4.8 %collective-permute-start.7 = (bf16[64,256]{1,0:T(8,128)(2,1)S(1)}, bf16[64,256]{1,0:T(8,128)(2,1)S(1)}, u32[]{:S(2)}, u32[]{:S(2)}) collective-permute-start(bf16[64,256]{1,0:T(8,128)(2,1)S(1)} %get-tuple-element.30.refs_0_), channel_id=1, source_target_pairs={{0,6},{1,7},{2,4},{3,5},{4,2},{5,3},{6,0},{7,1},{8,14},{9,15},{10,... | collective-permute-start | bytes 98312 | tf_op jit(solution)/shard_map/ppermute | solution.py:331
  24.5 4.8 %collective-permute-start.9 = (bf16[64,256]{1,0:T(8,128)(2,1)S(1)}, bf16[64,256]{1,0:T(8,128)(2,1)S(1)}, u32[]{:S(2)}, u32[]{:S(2)}) collective-permute-start(bf16[64,256]{1,0:T(8,128)(2,1)S(1)} %get-tuple-element.32), channel_id=1, source_target_pairs={{0,10},{1,11},{2,8},{3,9},{4,14},{5,15},{6,12},{7,13},{8,2},{9,3},... | collective-permute-start | bytes 98312 | tf_op jit(solution)/shard_map/ppermute | solution.py:333
  29.4 3.1 %collective-permute-start.14 = (bf16[512,256]{1,0:T(8,128)(2,1)S(1)}, bf16[512,256]{1,0:T(8,128)(2,1)S(1)}, u32[]{:S(2)}, u32[]{:S(2)}) collective-permute-start(bf16[512,256]{1,0:T(8,128)(2,1)S(1)} %shard_map.52.a_ref), channel_id=1, source_target_pairs={{0,1},{1,0},{2,3},{3,2},{4,5},{5,4},{6,7},{7,6},{8,9},{9,8},{10,11... | collective-permute-start | bytes 786440 | tf_op jit(solution)/shard_map/ppermute | solution.py:335
  30.9 8.6 %collective-permute-start.13 = (bf16[128,256]{1,0:T(8,128)(2,1)S(1)}, bf16[128,256]{1,0:T(8,128)(2,1)S(1)}, u32[]{:S(2)}, u32[]{:S(2)}) collective-permute-start(bf16[128,256]{1,0:T(8,128)(2,1)S(1)} %get-tuple-element.34), channel_id=1, source_target_pairs={{0,16},{8,24},{16,0},{24,8},{1,17},{9,25},{17,1},{25,9},{2,18},{10... | collective-permute-start | bytes 196616 | tf_op jit(solution)/shard_map/ppermute | solution.py:376
  32.8 7.7 %collective-permute-start.15 = (bf16[128,256]{1,0:T(8,128)(2,1)S(1)}, bf16[128,256]{1,0:T(8,128)(2,1)S(1)}, u32[]{:S(2)}, u32[]{:S(2)}) collective-permute-start(bf16[128,256]{1,0:T(8,128)(2,1)S(1)} %get-tuple-element.36), channel_id=1, source_target_pairs={{0,16},{8,24},{16,0},{24,8},{1,17},{9,25},{17,1},{25,9},{2,18},{10... | collective-permute-start | bytes 196616 | tf_op jit(solution)/shard_map/ppermute | solution.py:376

commit v7 on v6

--- a/solution.py
+++ b/solution.py
@@ -13,6 +13,7 @@
 LANES = 128
 LIMIT = 24 * 2**20
 TAIL = 48
+CHUNKS = 4
 VMEM = pl.BlockSpec(memory_space=pltpu.VMEM)
 HBM = pl.BlockSpec(memory_space=pltpu.HBM)
 
@@ -60,14 +61,17 @@
     return pieces
 
 
-def adjoint(freq, x, k_ref, o_ref, u_ref):
-    rows = x.shape[0] // 4
-    width = k_ref.shape[3]
-    tiles = width // LANES
+def products(freq, x, k_ref, u_ref, start):
+    tiles = u_ref.shape[0] // 2
     for c in range(2):
         y = dot_nn(x, k_ref[freq, c])
         for t in range(tiles):
-            u_ref[c * tiles + t] = y[:, t * LANES:(t + 1) * LANES]
+            u_ref[c * tiles + t, start:start + x.shape[0]] = y[:, t * LANES:(t + 1) * LANES]
+
+
+def combine(freq, o_ref, u_ref):
+    rows = o_ref.shape[0] // 2
+    tiles = u_ref.shape[0] // 2
     real = pl.ds(2 * freq, rows, stride=4)
     imag = pl.ds(2 * freq + 1, rows, stride=4)
     for t in range(tiles):
@@ -78,26 +82,36 @@
 
 def adjoint_other_body(v_hbm, k_hbm, d_hbm, n_hbm, o_ref, x_ref, k_ref, d_ref, n_ref, v_ref, u_ref, sems):
     freq = 1 - parity()
-    copies = [
-        pltpu.make_async_copy(v_hbm, v_ref, sems.at[0]),
-        pltpu.make_async_copy(k_hbm.at[freq], k_ref.at[freq], sems.at[1]),
-        pltpu.make_async_copy(k_hbm.at[1 - freq], k_ref.at[1 - freq], sems.at[2]),
-        pltpu.make_async_copy(d_hbm, d_ref, sems.at[3]),
-        pltpu.make_async_copy(n_hbm, n_ref, sems.at[4]),
-    ]
-    for copy in copies:
+    size = v_ref.shape[0] // CHUNKS
+    rows = x_ref.shape[0] // CHUNKS
+    first = pltpu.make_async_copy(k_hbm.at[freq], k_ref.at[freq], sems.at[0])
+    first.start()
+    copies = []
+    for n in range(CHUNKS):
+        at = pl.ds(n * size, size)
+        copies.append(pltpu.make_async_copy(v_hbm.at[at], v_ref.at[at], sems.at[n + 1]))
+    rest = (
+        (k_hbm.at[1 - freq], k_ref.at[1 - freq]),
+        (d_hbm, d_ref),
+        (n_hbm, n_ref),
+    )
+    others = [pltpu.make_async_copy(*pair, sems.at[CHUNKS + 1 + n]) for n, pair in enumerate(rest)]
+    for copy in copies + others:
         copy.start()
-    copies[0].wait()
-    x = v_ref[...].reshape(x_ref.shape)
-    x_ref[...] = x
-    copies[1].wait()
-    adjoint(freq, x, k_ref, o_ref, u_ref)
-    for copy in copies[2:]:
+    first.wait()
+    for n, copy in enumerate(copies):
         copy.wait()
+        x = v_ref[n * size:(n + 1) * size].reshape(rows, x_ref.shape[1])
+        x_ref[n * rows:(n + 1) * rows] = x
+        products(freq, x, k_ref, u_ref, n * rows)
+    combine(freq, o_ref, u_ref)
+    for copy in others:
+        copy.wait()
 
 
 def adjoint_own_body(x_ref, k_ref, o_ref, u_ref):
-    adjoint(parity(), x_ref[...], k_ref, o_ref, u_ref)
+    products(parity(), x_ref[...], k_ref, u_ref, 0)
+    combine(parity(), o_ref, u_ref)
 
 
 def seam_body(k_ref, d_ref, o_ref):
@@ -194,7 +208,7 @@
                 o_ref[f, c, n * width:(n + 1) * width] = (value + extra).astype(BF)
 
 
-def split_body(own_ref, got_ref, fence_ref, keep_ref, *send_refs):
+def split_body(own_ref, got_ref, keep_ref, *send_refs):
     chips = len(send_refs) + 1
     blocks = lax.axis_size("row")
     probes = own_ref.shape[0] // 2
@@ -214,21 +228,23 @@
                     at += size
 
 
-def sum_body(keep_ref, d_ref, near_ref, *refs):
-    stay_ref, give_ref, long_ref = refs[-3:]
+def sum_body(keep_ref, d_ref, near_ref, fence_ref, *refs):
+    stay_ref, long_ref = refs[-2:]
     size, width = stay_ref.shape
     total = keep_ref[...]
-    for ref in refs[:-3]:
+    for ref in refs[:-2]:
         total = total + ref[...].astype(F32)
     stay_ref[...] = total[:size].astype(BF)
-    give = total[size:].astype(BF)
-    give_ref[...] = give
-    long_ref[:size] = give
+    long_ref[:size] = total[size:].astype(BF)
     pad = jnp.zeros((13, width), BF)
     long_ref[size:size + 16] = jnp.concatenate(three(d_ref[...]) + [pad], axis=0)
     for n in range(4):
         lo = size + 16 + 8 * n
         long_ref[lo:lo + 8] = near_ref[:, n * width:(n + 1) * width]
+
+
+def pack_body(got_ref, fence_ref, o_ref):
+    o_ref[...] = got_ref[:o_ref.shape[0]]
 
 
 def join_body(*refs):
@@ -264,27 +280,75 @@
         ref[size:] = (by_real[mid:hi] + by_imag[lo:mid]).astype(ref.dtype)
 
 
-def final_body(peers, x_ref, noise_ref, *refs):
-    out_ref, s_ref = refs[-2:]
-    size = out_ref.shape[0]
-    rows = 4 * size
-    me = lax.axis_index("row")
-    freq = parity()
-    for which in range(2):
-        group = refs[which * (peers + 1):(which + 1) * (peers + 1)]
-        total = group[0][...]
-        for ref in group[1:]:
+def final_body(slot, keeps, peers, x_ref, noise_ref, *refs):
+    out_hbm, v_ref, s_ref, w_ref, sem = refs[-5:]
+    keep_refs = refs[:keeps]
+    got_refs = refs[keeps:keeps + peers]
+    odd = lax.rem(lax.axis_index("row"), 2)
+
+    def write(keep_ref, freq):
+        size = v_ref.shape[0]
+        me = lax.axis_index("row")
+        total = keep_ref[...]
+        for ref in got_refs:
             total = total + ref[...].astype(F32)
-        f = freq if which == 0 else 1 - freq
-        for t in range(s_ref.shape[0]):
+        x = x_ref[part(me * 4 * size, 4 * size), :].astype(F32)
+        noise = noise_ref[pl.ds(freq, 1), :]
+        tiles = s_ref.shape[0]
+        for t in range(tiles):
             at = slice(t * LANES, (t + 1) * LANES)
-            s_ref[t, pl.ds(2 * f, size, stride=4), :] = total[:size, at]
-            s_ref[t, pl.ds(2 * f + 1, size, stride=4), :] = total[size:, at]
-    x = x_ref[part(me * rows, rows), :].astype(F32)
-    kind = lax.rem(lax.broadcasted_iota(jnp.int32, x.shape, 0), 4)
-    noise = jnp.where(kind < 2, noise_ref[0:1, :], noise_ref[1:2, :])
-    values = jnp.concatenate([s_ref[t] for t in range(s_ref.shape[0])], axis=1) + noise * x
-    out_ref[...] = values.reshape(out_ref.shape)
+            w_ref[t] = x[:, at]
+            for c in range(2):
+                probe = w_ref[t, pl.ds(2 * freq + c, size, stride=4), :]
+                s_ref[t, pl.ds(c, size, stride=2), :] = total[c * size:(c + 1) * size, at] + noise[:, at] * probe
+        values = jnp.concatenate([s_ref[t] for t in range(tiles)], axis=1)
+        v_ref[...] = values.reshape(v_ref.shape)
+        copy = pltpu.make_async_copy(v_ref, out_hbm.at[:, freq], sem)
+        copy.start()
+        copy.wait()
+
+    if slot < 2:
+
+        @pl.when(odd == 0)
+        def _():
+            write(keep_refs[-1] if slot else keep_refs[0], 1 - parity() if slot else parity())
+
+    if slot > 0:
+
+        @pl.when(odd == 1)
+        def _():
+            write(keep_refs[0], parity() if slot == 1 else 1 - parity())
+
+
+def finish(slot, shape, x, noise, keeps, got, before=()):
+    size, _, parts, rows = shape
+    ins = [pltpu.with_memory_space_constraint(v, pltpu.VMEM) for v in (x, noise, *keeps, *got)]
+    return pl.pallas_call(
+        functools.partial(final_body, slot, len(keeps), len(got)),
+        in_specs=[VMEM] * len(ins) + [HBM] * len(before),
+        out_specs=HBM,
+        out_shape=jax.ShapeDtypeStruct(shape, F32),
+        input_output_aliases={len(ins): 0} if before else {},
+        scratch_shapes=[
+            pltpu.VMEM((size, parts, rows), F32),
+            pltpu.VMEM((rows // LANES, 2 * size, LANES), F32),
+            pltpu.VMEM((rows // LANES, 4 * size, LANES), F32),
+            pltpu.SemaphoreType.DMA,
+        ],
+        compiler_params=pltpu.CompilerParams(vmem_limit_bytes=LIMIT),
+    )(*ins, *before)
+
+
+def choose_body(own_ref, other_ref, o_ref):
+    odd = lax.rem(lax.axis_index("row"), 2)
+
+    @pl.when(odd == 1)
+    def _():
+        o_ref[...] = own_ref[...]
+
+    @pl.when(odd == 0)
+    def _():
+        o_ref[...] = other_ref[...]
 
 
 def wide_sum(own, got, coef, near, blocks):
@@ -311,26 +375,21 @@
     return mine, other, give
 
 
-def cross_perm(step):
-    cols = lax.axis_size("col")
-    return [(i * cols + j, (i ^ 1) * cols + (j ^ step)) for i in range(lax.axis_size("row")) for j in range(cols)]
-
-
 def chip_sum(own, got, coef, near, chips):
     rows, width = own.shape
     size = rows // chips
     half = size // 2
+    keep, *sends = call(split_body, (own, got), [((size, width), F32)] + [((size, width), BF)] * (chips - 1))
     fence = call(fence_body, (coef,), [((8, LANES), F32)])[0]
-    keep, *sends = call(split_body, (own, got, fence), [((size, width), F32)] + [((size, width), BF)] * (chips - 1))
     got = [lax.ppermute(v, "col", pair_perm("col", 2 * (d + 1))) for d, v in enumerate(sends)]
-    stay, give, long = call(
-        sum_body, (keep, coef, near, *got), [((half, width), BF), ((half, width), BF), ((half + TAIL, width), BF)]
-    )
-    long = lax.ppermute(long, "row", pair_perm("row", 1))
+    stay, long = call(sum_body, (keep, coef, near, fence, *got), [((half, width), BF), ((half + TAIL, width), BF)])
+    fence = call(fence_body, (coef,), [((8, LANES), F32)])[0]
     pieces = [stay]
     pieces += [lax.ppermute(stay, "col", pair_perm("col", 2 * (d + 1))) for d in range(chips - 1)]
-    pieces.append(long)
-    pieces += [lax.ppermute(give, ("row", "col"), cross_perm(2 * (d + 1))) for d in range(chips - 1)]
+    long = lax.ppermute(long, "row", pair_perm("row", 1))
+    give = call(pack_body, (long, fence), [((half, width), BF)])[0]
+    pieces.append(give)
+    pieces += [lax.ppermute(give, "col", pair_perm("col", 2 * (d + 1))) for d in range(chips - 1)]
     mine = call(join_body, pieces, [((rows, width), BF)])[0]
     return mine, lax.ppermute(mine, "col", pair_perm("col", 1)), long
 
@@ -348,7 +407,7 @@
         adjoint_other_body,
         (),
         [((2 * count, width), BF), (flat, BF), (kernel.shape, BF), (coef.shape, F32), (noise_var.shape, F32)],
-        (pltpu.VMEM(probes.shape, BF), scratch, pltpu.SemaphoreType.DMA((5,))),
+        (pltpu.VMEM(probes.shape, BF), scratch, pltpu.SemaphoreType.DMA((CHUNKS + 4,))),
         raw=(probes, kernel, coef, noise_var),
     )
     got = lax.ppermute(other, "col", pair_perm("col", 1))
@@ -365,21 +424,29 @@
     operator = call(operator_body, (kernel, mate, coef, give, near), [((2, 2, 2 * width, rows), BF)])[0]
     size = count // blocks
     peers = blocks // 2 - 1
-    groups = []
+    keeps, sends = [], []
     for swap, field in ((False, mine), (True, other)):
-        keep, *sends = call(
+        keep, *send = call(
             functools.partial(predict_body, swap),
             (field, operator),
             [((2 * size, rows), F32)] + [((2 * size, rows), BF)] * peers,
         )
-        groups.append(keep)
-        groups += [lax.ppermute(v, "row", pair_perm("row", 2 * (d + 1))) for d, v in enumerate(sends)]
-    return call(
-        functools.partial(final_body, peers),
-        (x, noise, *groups),
-        [((size,) + probes.shape[1:3] + (rows,), F32)],
-        (pltpu.VMEM((rows // LANES, 4 * size, LANES), F32),),
-    )[0]
+        keeps.append(keep)
+        sends.append(send)
+    shape = (size,) + probes.shape[1:3] + (rows,)
+    got = [[], [], []]
+    for d in range(peers):
+        step = 2 * (d + 1)
+        evens = [(i, i if i % 2 else i ^ step) for i in range(blocks)]
+        odds = [(i, i ^ step if i % 2 else i) for i in range(blocks)]
+        own, other = sends[0][d], sends[1][d]
+        middle = call(choose_body, (own, other), [(own.shape, BF)])[0]
+        got[0].append(lax.ppermute(own, "row", evens))
+        got[1].append(lax.ppermute(middle, "row", pair_perm("row", step)))
+        got[2].append(lax.ppermute(other, "row", odds))
+    out = finish(0, shape, x, noise, keeps[:1], got[0])
+    out = finish(1, shape, x, noise, keeps, got[1], (out,))
+    return finish(2, shape, x, noise, keeps[1:], got[2], (out,))
 
 
 def solution(mesh):

time: 41.5 us -> 39.2 us (0.945)
  waiting for transfers between devices: 14.9 us -> 9.99 us
  Pallas kernels: 4.6 us -> 6.31 us
  starting transfers between devices: 21.1 us -> 22.6 us
  local copies, waits for them, and re-layouts: 0.71 us -> 0.01 us
    ppermute x5 -> x6, waiting for transfers between devices: 8.49 us -> 5.52 us  [the longest x3 2.53 us: chip_sum(): lax.ppermute(give, 'col', pair_perm('col', 2 * (d + 1)))]
    ppermute x3, waiting for transfers between devices: 2.62 us -> 0.71 us  [chip_sum(): lax.ppermute(stay, 'col', pair_perm('col', 2 * (d + 1)))]
    pallas_call x0 -> x3, Pallas kernels: none -> 1.5 us  [finish(): pl.pallas_call(functools.partial(final_body, slot, len(keeps), len(got)),...]
    ppermute x5 -> x6, starting transfers between devices: 8.19 us -> 9.18 us  [the longest x1 4.04 us: apply(): got[0].append(lax.ppermute(own, 'row', evens))]
    unnamed x3 -> x2, local copies, waits for them, and re-layouts: 0.71 us -> 0.01 us
    ppermute x1, starting transfers between devices: 1.89 us -> 2.41 us  [chip_sum(): long = lax.ppermute(long, 'row', pair_perm('row', 1))]
    pallas_call x11 -> x12, Pallas kernels: 4.6 us -> 4.81 us  [call(): pl.pallas_call(body, in_specs=[HBM] * len(raw) + [VMEM] * len(ins), out_s...]
  transfers between devices with their start and end apart: 16 -> 17, of which waited for: 7 -> 7; matrix products, arithmetic and copies ran while one was open for 0% -> 0% of each run, Pallas kernels for 6% -> 11%
where the time goes in v7:
time: 39.2 us; the launch traced here: 39 us
  starting transfers between devices  22.6 us (58%)
  waiting for transfers between devices  9.99 us (25%)
  Pallas kernels  6.31 us (16%)
    pallas_call x12, Pallas kernels, call(): pl.pallas_call(body, in_specs=[HBM] * len(raw) + [VMEM] * len(ins), out_s...  4.81 us
    ppermute x1, starting transfers between devices, apply(): got[0].append(lax.ppermute(own, 'row', evens))  4.04 us
    ppermute x3, waiting for transfers between devices, chip_sum(): lax.ppermute(v, 'col', pair_perm('col', 2 * (d + 1)))  3.74 us
    ppermute x3, starting transfers between devices, chip_sum(): lax.ppermute(give, 'col', pair_perm('col', 2 * (d + 1)))  3.63 us
    ppermute x3, starting transfers between devices, chip_sum(): lax.ppermute(v, 'col', pair_perm('col', 2 * (d + 1)))  3.55 us
    ppermute x3, starting transfers between devices, chip_sum(): lax.ppermute(stay, 'col', pair_perm('col', 2 * (d + 1)))  3.49 us
    ppermute x1, starting transfers between devices, apply(): mate = lax.ppermute(kernel, 'row', pair_perm('row', 1))  2.64 us
    ppermute x3, waiting for transfers between devices, chip_sum(): lax.ppermute(give, 'col', pair_perm('col', 2 * (d + 1)))  2.53 us
  transfers between devices with their start and end apart: 17, of which 7 were waited for; matrix products, arithmetic and copies ran while one was open for 0% of the time, Pallas kernels for 11%

profile of v7, /device:TPU:0, one launch (start us, length us, event | category | flops | bytes accessed | tf_op | source)
XLA Modules:
  0.0 39.0 jit_solution(9954748253857438059)
XLA Ops:
  0.0 0.0 copy-start
  0.0 2.1 %shard_map.46 = (bf16[512,256]{1,0:T(8,128)(2,1)S(1)}, bf16[1024,256]{1,0:T(8,128)(2,1)S(1)}, bf16[2,2,256,256]{3,2,1,0:T(8,128)(2,1)S(1)}, f32[1,256]{1,0:T(1,128)S(1)}, f32[2,256]{1,0:T(2,128)S(1)}) custom-call(bf16[256,2,2,256]{3,2,1,0:T(2,128)(2,1)} %v_hbm.1, bf16[2,2,256,256]{3,2,1,0:T(8,128)(2,1)} %k_hbm.1, f32[1,256]{1,0:T(1,128)} %bitcast.1, ...), custom_call_target="tpu_custom_call" | custom-call | tf_op jit(solution)/shard_map/pallas_call | solution.py:22
  2.2 0.6 %collective-permute-start = (bf16[512,256]{1,0:T(8,128)(2,1)S(1)}, bf16[512,256]{1,0:T(8,128)(2,1)S(1)}, u32[]{:S(2)}, u32[]{:S(2)}) collective-permute-start(bf16[512,256]{1,0:T(8,128)(2,1)S(1)} %get-tuple-element.23), channel_id=1, source_target_pairs={{0,1},{1,0},{2,3},{3,2},{4,5},{5,4},{6,7},{7,6},{8,9},{9,8},{10,11... | collective-permute-start | bytes 786440 | tf_op jit(solution)/shard_map/ppermute | solution.py:413
  2.7 0.0 copy-done
  2.7 2.6 %collective-permute-start.13 = (bf16[2,2,256,256]{3,2,1,0:T(8,128)(2,1)S(1)}, bf16[2,2,256,256]{3,2,1,0:T(8,128)(2,1)S(1)}, u32[]{:S(2)}, u32[]{:S(2)}) collective-permute-start(bf16[2,2,256,256]{3,2,1,0:T(8,128)(2,1)S(1)} %copy-done), channel_id=1, source_target_pairs={{0,8},{8,0},{16,24},{24,16},{1,9},{9,1},{17,25},{25,17},{2,10},{10... | collective-permute-start | bytes 1572872 | tf_op jit(solution)/shard_map/ppermute | solution.py:405
  5.4 0.6 %shard_map.47.own_ref = f32[512,256]{1,0:T(8,128)S(1)} custom-call(bf16[1024,256]{1,0:T(8,128)(2,1)S(1)} %get-tuple-element.20.x_ref, bf16[2,2,256,256]{3,2,1,0:T(8,128)(2,1)S(1)} %get-tuple-element.22.k_ref), custom_call_target="tpu_custom_call" | custom-call | tf_op jit(solution)/shard_map/pallas_call | solution.py:22
  5.9 0.0 collective-permute-done.got_ref
  5.9 0.1 shard_map.48
  6.0 1.6 %collective-permute-start.2 = (bf16[128,256]{1,0:T(8,128)(2,1)S(1)}, bf16[128,256]{1,0:T(8,128)(2,1)S(1)}, u32[]{:S(2)}, u32[]{:S(2)}) collective-permute-start(bf16[128,256]{1,0:T(8,128)(2,1)S(1)} %get-tuple-element.26), channel_id=1, source_target_pairs={{0,2},{1,3},{2,0},{3,1},{4,6},{5,7},{6,4},{7,5},{8,10},{9,11},{10,... | collective-permute-start | bytes 196616 | tf_op jit(solution)/shard_map/ppermute | solution.py:384
  7.6 1.5 %collective-permute-start.3 = (bf16[128,256]{1,0:T(8,128)(2,1)S(1)}, bf16[128,256]{1,0:T(8,128)(2,1)S(1)}, u32[]{:S(2)}, u32[]{:S(2)}) collective-permute-start(bf16[128,256]{1,0:T(8,128)(2,1)S(1)} %get-tuple-element.27), channel_id=1, source_target_pairs={{0,4},{1,5},{2,6},{3,7},{4,0},{5,1},{6,2},{7,3},{8,12},{9,13},{10,... | collective-permute-start | bytes 196616 | tf_op jit(solution)/shard_map/ppermute | solution.py:384
  9.1 0.5 %collective-permute-start.4 = (bf16[128,256]{1,0:T(8,128)(2,1)S(1)}, bf16[128,256]{1,0:T(8,128)(2,1)S(1)}, u32[]{:S(2)}, u32[]{:S(2)}) collective-permute-start(bf16[128,256]{1,0:T(8,128)(2,1)S(1)} %get-tuple-element.28), channel_id=1, source_target_pairs={{0,6},{1,7},{2,4},{3,5},{4,2},{5,3},{6,0},{7,1},{8,14},{9,15},{10,... | collective-permute-start | bytes 196616 | tf_op jit(solution)/shard_map/ppermute | solution.py:384
  9.6 0.2 shard_map.49
  9.8 0.7 %collective-permute-start.1 = (bf16[8,1024]{1,0:T(8,128)(2,1)S(1)}, bf16[8,1024]{1,0:T(8,128)(2,1)S(1)}, u32[]{:S(2)}, u32[]{:S(2)}) collective-permute-start(bf16[8,1024]{1,0:T(8,128)(2,1)S(1)} %shard_map.49), channel_id=1, source_target_pairs={{8,16},{24,24},{0,0},{16,8},{9,17},{25,25},{1,1},{17,9},{10,18},{2... | collective-permute-start | bytes 49160 | tf_op jit(solution)/shard_map/ppermute | solution.py:419
  10.5 0.0 collective-permute-done.1.near_ref
  10.5 0.0 collective-permute-done.2.refs_0_
  10.5 1.3 %collective-permute-done.3.refs_1_ = bf16[128,256]{1,0:T(8,128)(2,1)S(1)} collective-permute-done((bf16[128,256]{1,0:T(8,128)(2,1)S(1)}, bf16[128,256]{1,0:T(8,128)(2,1)S(1)}, u32[]{:S(2)}, u32[]{:S(2)}) %collective-permute-start.3) | collective-permute-done | bytes 65568 | tf_op jit(solution)/shard_map/ppermute | solution.py:384
  11.9 2.4 %collective-permute-done.4.refs_2_ = bf16[128,256]{1,0:T(8,128)(2,1)S(1)} collective-permute-done((bf16[128,256]{1,0:T(8,128)(2,1)S(1)}, bf16[128,256]{1,0:T(8,128)(2,1)S(1)}, u32[]{:S(2)}, u32[]{:S(2)}) %collective-permute-start.4) | collective-permute-done | bytes 65568 | tf_op jit(solution)/shard_map/ppermute | solution.py:384
  14.3 0.1 shard_map.51
  14.3 2.4 %collective-permute-start.8 = (bf16[112,256]{1,0:T(8,128)(2,1)S(1)}, bf16[112,256]{1,0:T(8,128)(2,1)S(1)}, u32[]{:S(2)}, u32[]{:S(2)}) collective-permute-start(bf16[112,256]{1,0:T(8,128)(2,1)S(1)} %get-tuple-element.30), channel_id=1, source_target_pairs={{0,8},{8,0},{16,24},{24,16},{1,9},{9,1},{17,25},{25,17},{2,10},{10... | collective-permute-start | bytes 172040 | tf_op jit(solution)/shard_map/ppermute | solution.py:389
  16.7 1.5 %collective-permute-start.5 = (bf16[64,256]{1,0:T(8,128)(2,1)S(1)}, bf16[64,256]{1,0:T(8,128)(2,1)S(1)}, u32[]{:S(2)}, u32[]{:S(2)}) collective-permute-start(bf16[64,256]{1,0:T(8,128)(2,1)S(1)} %get-tuple-element.29.refs_0_), channel_id=1, source_target_pairs={{0,2},{1,3},{2,0},{3,1},{4,6},{5,7},{6,4},{7,5},{8,10},{9,11},{10,... | collective-permute-start | bytes 98312 | tf_op jit(solution)/shard_map/ppermute | solution.py:388
  18.2 1.5 %collective-permute-start.6 = (bf16[64,256]{1,0:T(8,128)(2,1)S(1)}, bf16[64,256]{1,0:T(8,128)(2,1)S(1)}, u32[]{:S(2)}, u32[]{:S(2)}) collective-permute-start(bf16[64,256]{1,0:T(8,128)(2,1)S(1)} %get-tuple-element.29.refs_0_), channel_id=1, source_target_pairs={{0,4},{1,5},{2,6},{3,7},{4,0},{5,1},{6,2},{7,3},{8,12},{9,13},{10,... | collective-permute-start | bytes 98312 | tf_op jit(solution)/shard_map/ppermute | solution.py:388
  19.8 0.5 %collective-permute-start.7 = (bf16[64,256]{1,0:T(8,128)(2,1)S(1)}, bf16[64,256]{1,0:T(8,128)(2,1)S(1)}, u32[]{:S(2)}, u32[]{:S(2)}) collective-permute-start(bf16[64,256]{1,0:T(8,128)(2,1)S(1)} %get-tuple-element.29.refs_0_), channel_id=1, source_target_pairs={{0,6},{1,7},{2,4},{3,5},{4,2},{5,3},{6,0},{7,1},{8,14},{9,15},{10,... | collective-permute-start | bytes 98312 | tf_op jit(solution)/shard_map/ppermute | solution.py:388
  20.2 0.0 collective-permute-done.8.got_ref
  20.2 1.5 %collective-permute-start.10 = (bf16[64,256]{1,0:T(8,128)(2,1)S(1)}, bf16[64,256]{1,0:T(8,128)(2,1)S(1)}, u32[]{:S(2)}, u32[]{:S(2)}) collective-permute-start(bf16[64,256]{1,0:T(8,128)(2,1)S(1)} %shard_map.52.refs_4_), channel_id=1, source_target_pairs={{0,4},{1,5},{2,6},{3,7},{4,0},{5,1},{6,2},{7,3},{8,12},{9,13},{10,... | collective-permute-start | bytes 98312 | tf_op jit(solution)/shard_map/ppermute | solution.py:392
  21.8 0.0 collective-permute-done.5.refs_1_
  21.8 1.4 %collective-permute-start.11 = (bf16[64,256]{1,0:T(8,128)(2,1)S(1)}, bf16[64,256]{1,0:T(8,128)(2,1)S(1)}, u32[]{:S(2)}, u32[]{:S(2)}) collective-permute-start(bf16[64,256]{1,0:T(8,128)(2,1)S(1)} %shard_map.52.refs_4_), channel_id=1, source_target_pairs={{0,6},{1,7},{2,4},{3,5},{4,2},{5,3},{6,0},{7,1},{8,14},{9,15},{10,... | collective-permute-start | bytes 98312 | tf_op jit(solution)/shard_map/ppermute | solution.py:392
  23.2 0.0 collective-permute-done.6.refs_2_
  23.2 0.7 %collective-permute-start.9 = (bf16[64,256]{1,0:T(8,128)(2,1)S(1)}, bf16[64,256]{1,0:T(8,128)(2,1)S(1)}, u32[]{:S(2)}, u32[]{:S(2)}) collective-permute-start(bf16[64,256]{1,0:T(8,128)(2,1)S(1)} %shard_map.52.refs_4_), channel_id=1, source_target_pairs={{0,2},{1,3},{2,0},{3,1},{4,6},{5,7},{6,4},{7,5},{8,10},{9,11},{10,... | collective-permute-start | bytes 98312 | tf_op jit(solution)/shard_map/ppermute | solution.py:392
  23.9 0.7 %collective-permute-done.7.refs_3_ = bf16[64,256]{1,0:T(8,128)(2,1)S(1)} collective-permute-done((bf16[64,256]{1,0:T(8,128)(2,1)S(1)}, bf16[64,256]{1,0:T(8,128)(2,1)S(1)}, u32[]{:S(2)}, u32[]{:S(2)}) %collective-permute-start.7) | collective-permute-done | bytes 32800 | tf_op jit(solution)/shard_map/ppermute | solution.py:388
  24.6 0.0 collective-permute-done.10.refs_6_
  24.6 1.9 %collective-permute-done.11.refs_7_ = bf16[64,256]{1,0:T(8,128)(2,1)S(1)} collective-permute-done((bf16[64,256]{1,0:T(8,128)(2,1)S(1)}, bf16[64,256]{1,0:T(8,128)(2,1)S(1)}, u32[]{:S(2)}, u32[]{:S(2)}) %collective-permute-start.11) | collective-permute-done | bytes 32800 | tf_op jit(solution)/shard_map/ppermute | solution.py:392
  26.6 0.5 %collective-permute-done.9.refs_5_ = bf16[64,256]{1,0:T(8,128)(2,1)S(1)} collective-permute-done((bf16[64,256]{1,0:T(8,128)(2,1)S(1)}, bf16[64,256]{1,0:T(8,128)(2,1)S(1)}, u32[]{:S(2)}, u32[]{:S(2)}) %collective-permute-start.9) | collective-permute-done | bytes 32800 | tf_op jit(solution)/shard_map/ppermute | solution.py:392
  27.2 0.1 collective-permute-start.12
  27.2 0.0 collective-permute-done.13.mate_ref
  27.2 1.0 %shard_map.54.k_ref = bf16[2,2,512,256]{3,2,1,0:T(8,128)(2,1)S(1)} custom-call(bf16[2,2,256,256]{3,2,1,0:T(8,128)(2,1)S(1)} %get-tuple-element.22.k_ref, bf16[2,2,256,256]{3,2,1,0:T(8,128)(2,1)S(1)} %collective-permute-done.13.mate_ref, f32[1,256]{1,0:T(1,128)S(1)} %get-tuple-element.25.d_ref, bf16[112,256]{1,0:T(8,128)(2,1)S(1)} %collective-permute-done.8.got_ref, ...), custom_call_target="tpu_custom_call" | custom-call | tf_op jit(solution)/shard_map/pallas_call | solution.py:22
  28.3 0.3 shard_map.56
  28.6 4.0 %collective-permute-start.16 = (bf16[128,256]{1,0:T(8,128)(2,1)S(1)}, bf16[128,256]{1,0:T(8,128)(2,1)S(1)}, u32[]{:S(2)}, u32[]{:S(2)}) collective-permute-start(bf16[128,256]{1,0:T(8,128)(2,1)S(1)} %get-tuple-element.34.own_ref), channel_id=1, source_target_pairs={{0,16},{8,8},{16,0},{24,24},{1,17},{9,9},{17,1},{25,25},{2,18},{10... | collective-permute-start | bytes 196616 | tf_op jit(solution)/shard_map/ppermute | solution.py:444
  32.7 0.0 collective-permute-done.12.a_ref
  32.7 0.3 shard_map.55
  33.0 0.9 %collective-permute-start.15 = (bf16[128,256]{1,0:T(8,128)(2,1)S(1)}, bf16[128,256]{1,0:T(8,128)(2,1)S(1)}, u32[]{:S(2)}, u32[]{:S(2)}) collective-permute-start(bf16[128,256]{1,0:T(8,128)(2,1)S(1)} %shard_map.57), channel_id=1, source_target_pairs={{0,16},{8,24},{16,0},{24,8},{1,17},{9,25},{17,1},{25,9},{2,18},{10... | collective-permute-start | bytes 196616 | tf_op jit(solution)/shard_map/ppermute | solution.py:445
  33.9 0.7 %collective-permute-start.14 = (bf16[128,256]{1,0:T(8,128)(2,1)S(1)}, bf16[128,256]{1,0:T(8,128)(2,1)S(1)}, u32[]{:S(2)}, u32[]{:S(2)}) collective-permute-start(bf16[128,256]{1,0:T(8,128)(2,1)S(1)} %get-tuple-element.32.other_ref), channel_id=1, source_target_pairs={{0,0},{8,24},{16,16},{24,8},{1,1},{9,25},{17,17},{25,9},{2,2},{10,... | collective-permute-start | bytes 196616 | tf_op jit(solution)/shard_map/ppermute | solution.py:446
  34.5 2.2 %collective-permute-done.16.refs_1_ = bf16[128,256]{1,0:T(8,128)(2,1)S(1)} collective-permute-done((bf16[128,256]{1,0:T(8,128)(2,1)S(1)}, bf16[128,256]{1,0:T(8,128)(2,1)S(1)}, u32[]{:S(2)}, u32[]{:S(2)}) %collective-permute-start.16) | collective-permute-done | bytes 65568 | tf_op jit(solution)/shard_map/ppermute | solution.py:444
  36.8 0.7 %shard_map.58.refs_3_ = f32[64,2,2,256]{3,2,1,0:T(2,128)} custom-call(bf16[1024,256]{1,0:T(8,128)(2,1)S(1)} %get-tuple-element.20.x_ref, f32[2,256]{1,0:T(2,128)S(1)} %get-tuple-element.21.noise_ref, f32[128,256]{1,0:T(8,128)S(1)} %get-tuple-element.33.refs_0_, bf16[128,256]{1,0:T(8,128)(2,1)S(1)} %collective-permute-done.16.refs_1_), custom_call_target="tpu_custom_call" | custom-call | tf_op jit(solution)/shard_map/pallas_call | solution.py:326
  37.5 0.7 %collective-permute-done.15.refs_2_ = bf16[128,256]{1,0:T(8,128)(2,1)S(1)} collective-permute-done((bf16[128,256]{1,0:T(8,128)(2,1)S(1)}, bf16[128,256]{1,0:T(8,128)(2,1)S(1)}, u32[]{:S(2)}, u32[]{:S(2)}) %collective-permute-start.15) | collective-permute-done | bytes 65568 | tf_op jit(solution)/shard_map/ppermute | solution.py:445
  38.3 0.7 %shard_map.59.refs_2_ = f32[64,2,2,256]{3,2,1,0:T(2,128)} custom-call(bf16[1024,256]{1,0:T(8,128)(2,1)S(1)} %get-tuple-element.20.x_ref, f32[2,256]{1,0:T(2,128)S(1)} %get-tuple-element.21.noise_ref, f32[128,256]{1,0:T(8,128)S(1)} %get-tuple-element.33.refs_0_, f32[128,256]{1,0:T(8,128)S(1)} %get-tuple-element.31.refs_1_.refs_0_, ...), custom_call_target="tpu_custom_call", output_to_operand_aliasing={{}: (5, {})} | custom-call | tf_op jit(solution)/shard_map/pallas_call | solution.py:326
  39.0 0.0 collective-permute-done.14.refs_1_
  (5 shorter events, 0.1 us)
Async XLA Ops:
  0.0 2.7 %copy-start = (bf16[2,2,256,256]{3,2,1,0:T(8,128)(2,1)S(1)}, bf16[2,2,256,256]{3,2,1,0:T(8,128)(2,1)}, u32[]{:S(2)}) copy-start(bf16[2,2,256,256]{3,2,1,0:T(8,128)(2,1)} %k_hbm.1) | copy-start | bytes 1572868
  2.2 3.8 %collective-permute-start = (bf16[512,256]{1,0:T(8,128)(2,1)S(1)}, bf16[512,256]{1,0:T(8,128)(2,1)S(1)}, u32[]{:S(2)}, u32[]{:S(2)}) collective-permute-start(bf16[512,256]{1,0:T(8,128)(2,1)S(1)} %get-tuple-element.23), channel_id=1, source_target_pairs={{0,1},{1,0},{2,3},{3,2},{4,5},{5,4},{6,7},{7,6},{8,9},{9,8},{10,11... | collective-permute-start | bytes 786440 | tf_op jit(solution)/shard_map/ppermute | solution.py:413
  2.7 24.5 %collective-permute-start.13 = (bf16[2,2,256,256]{3,2,1,0:T(8,128)(2,1)S(1)}, bf16[2,2,256,256]{3,2,1,0:T(8,128)(2,1)S(1)}, u32[]{:S(2)}, u32[]{:S(2)}) collective-permute-start(bf16[2,2,256,256]{3,2,1,0:T(8,128)(2,1)S(1)} %copy-done), channel_id=1, source_target_pairs={{0,8},{8,0},{16,24},{24,16},{1,9},{9,1},{17,25},{25,17},{2,10},{10... | collective-permute-start | bytes 1572872 | tf_op jit(solution)/shard_map/ppermute | solution.py:405
  6.0 4.5 %collective-permute-start.2 = (bf16[128,256]{1,0:T(8,128)(2,1)S(1)}, bf16[128,256]{1,0:T(8,128)(2,1)S(1)}, u32[]{:S(2)}, u32[]{:S(2)}) collective-permute-start(bf16[128,256]{1,0:T(8,128)(2,1)S(1)} %get-tuple-element.26), channel_id=1, source_target_pairs={{0,2},{1,3},{2,0},{3,1},{4,6},{5,7},{6,4},{7,5},{8,10},{9,11},{10,... | collective-permute-start | bytes 196616 | tf_op jit(solution)/shard_map/ppermute | solution.py:384
  7.6 4.3 %collective-permute-start.3 = (bf16[128,256]{1,0:T(8,128)(2,1)S(1)}, bf16[128,256]{1,0:T(8,128)(2,1)S(1)}, u32[]{:S(2)}, u32[]{:S(2)}) collective-permute-start(bf16[128,256]{1,0:T(8,128)(2,1)S(1)} %get-tuple-element.27), channel_id=1, source_target_pairs={{0,4},{1,5},{2,6},{3,7},{4,0},{5,1},{6,2},{7,3},{8,12},{9,13},{10,... | collective-permute-start | bytes 196616 | tf_op jit(solution)/shard_map/ppermute | solution.py:384
  9.1 5.2 %collective-permute-start.4 = (bf16[128,256]{1,0:T(8,128)(2,1)S(1)}, bf16[128,256]{1,0:T(8,128)(2,1)S(1)}, u32[]{:S(2)}, u32[]{:S(2)}) collective-permute-start(bf16[128,256]{1,0:T(8,128)(2,1)S(1)} %get-tuple-element.28), channel_id=1, source_target_pairs={{0,6},{1,7},{2,4},{3,5},{4,2},{5,3},{6,0},{7,1},{8,14},{9,15},{10,... | collective-permute-start | bytes 196616 | tf_op jit(solution)/shard_map/ppermute | solution.py:384
  9.8 0.7 %collective-permute-start.1 = (bf16[8,1024]{1,0:T(8,128)(2,1)S(1)}, bf16[8,1024]{1,0:T(8,128)(2,1)S(1)}, u32[]{:S(2)}, u32[]{:S(2)}) collective-permute-start(bf16[8,1024]{1,0:T(8,128)(2,1)S(1)} %shard_map.49), channel_id=1, source_target_pairs={{8,16},{24,24},{0,0},{16,8},{9,17},{25,25},{1,1},{17,9},{10,18},{2... | collective-permute-start | bytes 49160 | tf_op jit(solution)/shard_map/ppermute | solution.py:419
  14.3 5.9 %collective-permute-start.8 = (bf16[112,256]{1,0:T(8,128)(2,1)S(1)}, bf16[112,256]{1,0:T(8,128)(2,1)S(1)}, u32[]{:S(2)}, u32[]{:S(2)}) collective-permute-start(bf16[112,256]{1,0:T(8,128)(2,1)S(1)} %get-tuple-element.30), channel_id=1, source_target_pairs={{0,8},{8,0},{16,24},{24,16},{1,9},{9,1},{17,25},{25,17},{2,10},{10... | collective-permute-start | bytes 172040 | tf_op jit(solution)/shard_map/ppermute | solution.py:389
  16.7 5.0 %collective-permute-start.5 = (bf16[64,256]{1,0:T(8,128)(2,1)S(1)}, bf16[64,256]{1,0:T(8,128)(2,1)S(1)}, u32[]{:S(2)}, u32[]{:S(2)}) collective-permute-start(bf16[64,256]{1,0:T(8,128)(2,1)S(1)} %get-tuple-element.29.refs_0_), channel_id=1, source_target_pairs={{0,2},{1,3},{2,0},{3,1},{4,6},{5,7},{6,4},{7,5},{8,10},{9,11},{10,... | collective-permute-start | bytes 98312 | tf_op jit(solution)/shard_map/ppermute | solution.py:388
  18.2 5.0 %collective-permute-start.6 = (bf16[64,256]{1,0:T(8,128)(2,1)S(1)}, bf16[64,256]{1,0:T(8,128)(2,1)S(1)}, u32[]{:S(2)}, u32[]{:S(2)}) collective-permute-start(bf16[64,256]{1,0:T(8,128)(2,1)S(1)} %get-tuple-element.29.refs_0_), channel_id=1, source_target_pairs={{0,4},{1,5},{2,6},{3,7},{4,0},{5,1},{6,2},{7,3},{8,12},{9,13},{10,... | collective-permute-start | bytes 98312 | tf_op jit(solution)/shard_map/ppermute | solution.py:388
  19.8 4.8 %collective-permute-start.7 = (bf16[64,256]{1,0:T(8,128)(2,1)S(1)}, bf16[64,256]{1,0:T(8,128)(2,1)S(1)}, u32[]{:S(2)}, u32[]{:S(2)}) collective-permute-start(bf16[64,256]{1,0:T(8,128)(2,1)S(1)} %get-tuple-element.29.refs_0_), channel_id=1, source_target_pairs={{0,6},{1,7},{2,4},{3,5},{4,2},{5,3},{6,0},{7,1},{8,14},{9,15},{10,... | collective-permute-start | bytes 98312 | tf_op jit(solution)/shard_map/ppermute | solution.py:388
  20.2 4.4 %collective-permute-start.10 = (bf16[64,256]{1,0:T(8,128)(2,1)S(1)}, bf16[64,256]{1,0:T(8,128)(2,1)S(1)}, u32[]{:S(2)}, u32[]{:S(2)}) collective-permute-start(bf16[64,256]{1,0:T(8,128)(2,1)S(1)} %shard_map.52.refs_4_), channel_id=1, source_target_pairs={{0,4},{1,5},{2,6},{3,7},{4,0},{5,1},{6,2},{7,3},{8,12},{9,13},{10,... | collective-permute-start | bytes 98312 | tf_op jit(solution)/shard_map/ppermute | solution.py:392
  21.8 4.8 %collective-permute-start.11 = (bf16[64,256]{1,0:T(8,128)(2,1)S(1)}, bf16[64,256]{1,0:T(8,128)(2,1)S(1)}, u32[]{:S(2)}, u32[]{:S(2)}) collective-permute-start(bf16[64,256]{1,0:T(8,128)(2,1)S(1)} %shard_map.52.refs_4_), channel_id=1, source_target_pairs={{0,6},{1,7},{2,4},{3,5},{4,2},{5,3},{6,0},{7,1},{8,14},{9,15},{10,... | collective-permute-start | bytes 98312 | tf_op jit(solution)/shard_map/ppermute | solution.py:392
  23.2 3.9 %collective-permute-start.9 = (bf16[64,256]{1,0:T(8,128)(2,1)S(1)}, bf16[64,256]{1,0:T(8,128)(2,1)S(1)}, u32[]{:S(2)}, u32[]{:S(2)}) collective-permute-start(bf16[64,256]{1,0:T(8,128)(2,1)S(1)} %shard_map.52.refs_4_), channel_id=1, source_target_pairs={{0,2},{1,3},{2,0},{3,1},{4,6},{5,7},{6,4},{7,5},{8,10},{9,11},{10,... | collective-permute-start | bytes 98312 | tf_op jit(solution)/shard_map/ppermute | solution.py:392
  27.2 5.5 %collective-permute-start.12 = (bf16[512,256]{1,0:T(8,128)(2,1)S(1)}, bf16[512,256]{1,0:T(8,128)(2,1)S(1)}, u32[]{:S(2)}, u32[]{:S(2)}) collective-permute-start(bf16[512,256]{1,0:T(8,128)(2,1)S(1)} %shard_map.53.a_ref), channel_id=1, source_target_pairs={{0,1},{1,0},{2,3},{3,2},{4,5},{5,4},{6,7},{7,6},{8,9},{9,8},{10,11... | collective-permute-start | bytes 786440 | tf_op jit(solution)/shard_map/ppermute | solution.py:394
  28.6 8.2 %collective-permute-start.16 = (bf16[128,256]{1,0:T(8,128)(2,1)S(1)}, bf16[128,256]{1,0:T(8,128)(2,1)S(1)}, u32[]{:S(2)}, u32[]{:S(2)}) collective-permute-start(bf16[128,256]{1,0:T(8,128)(2,1)S(1)} %get-tuple-element.34.own_ref), channel_id=1, source_target_pairs={{0,16},{8,8},{16,0},{24,24},{1,17},{9,9},{17,1},{25,25},{2,18},{10... | collective-permute-start | bytes 196616 | tf_op jit(solution)/shard_map/ppermute | solution.py:444
  33.0 5.2 %collective-permute-start.15 = (bf16[128,256]{1,0:T(8,128)(2,1)S(1)}, bf16[128,256]{1,0:T(8,128)(2,1)S(1)}, u32[]{:S(2)}, u32[]{:S(2)}) collective-permute-start(bf16[128,256]{1,0:T(8,128)(2,1)S(1)} %shard_map.57), channel_id=1, source_target_pairs={{0,16},{8,24},{16,0},{24,8},{1,17},{9,25},{17,1},{25,9},{2,18},{10... | collective-permute-start | bytes 196616 | tf_op jit(solution)/shard_map/ppermute | solution.py:445
  33.9 5.1 %collective-permute-start.14 = (bf16[128,256]{1,0:T(8,128)(2,1)S(1)}, bf16[128,256]{1,0:T(8,128)(2,1)S(1)}, u32[]{:S(2)}, u32[]{:S(2)}) collective-permute-start(bf16[128,256]{1,0:T(8,128)(2,1)S(1)} %get-tuple-element.32.other_ref), channel_id=1, source_target_pairs={{0,0},{8,24},{16,16},{24,8},{1,1},{9,25},{17,17},{25,9},{2,2},{10,... | collective-permute-start | bytes 196616 | tf_op jit(solution)/shard_map/ppermute | solution.py:446

commit v8 on v5

--- a/solution.py
+++ b/solution.py
@@ -84,12 +84,14 @@
         pltpu.make_async_copy(d_hbm, d_ref, sems.at[3]),
         pltpu.make_async_copy(n_hbm, n_ref, sems.at[4]),
     ]
-    for copy in copies:
+    for copy in copies[:2]:
         copy.start()
     copies[0].wait()
     x = v_ref[...].reshape(x_ref.shape)
     x_ref[...] = x
     copies[1].wait()
+    for copy in copies[2:]:
+        copy.start()
     adjoint(freq, x, k_ref, o_ref, u_ref)
     for copy in copies[2:]:
         copy.wait()
@@ -151,12 +153,14 @@
     def last_or_first(value, last):
         return jnp.where(last, value[:, width - 1:], value[:, :1])
 
-    def outer(ref):
-        full = ref[...].astype(F32)
+    def outer(ref, block):
+        last = lax.axis_size("row") - 1
+        there = jnp.where(lax.rem(block, 2) == 1, block < last, block > 0)
+        full = jnp.where(there, ref[...].astype(F32), 0.0)
         return full[0:2], full[2:3, :1] + full[3:4, :1] + full[4:5, :1]
 
-    near, near_coef = outer(near_ref)
-    far, far_coef = outer(far_ref)
+    near, near_coef = outer(near_ref, me)
+    far, far_coef = outer(far_ref, xor(me, 1))
     sides = (
         (k_ref, coef, me, near, near_coef, mate_ref, mate_pick, last_or_first(mate_coef, is_odd), is_odd),
         (mate_ref, mate_coef, xor(me, 1), far, far_coef, k_ref, own_pick, last_or_first(coef, ~is_odd), ~is_odd),
@@ -342,7 +346,7 @@
     odd = [i for i in range(blocks) if i % 2]
     even = [i for i in range(blocks) if i % 2 == 0]
     near = [(i, i + 1) for i in odd if i + 1 < blocks] + [(i, i - 1) for i in even if i]
-    far = [(i, i + 2) for i in odd if i + 2 < blocks] + [(i, i - 2) for i in even if i]
+    far = [(i, i + 2 if i + 2 < blocks else 1) for i in odd] + [(i, i - 2 if i else blocks - 2) for i in even]
     near = lax.ppermute(seam, "row", near)
     far = lax.ppermute(seam, "row", far)
     if chips > 4:

time: 46.5 us -> 45.1 us (0.970)
  waiting for transfers between devices: 23 us -> 19.8 us
  starting transfers between devices: 18 us -> 19.2 us
    ppermute x1, waiting for transfers between devices: 4.56 us -> 1.39 us  [apply(): far = lax.ppermute(seam, 'row', far)]
    ppermute x1, starting transfers between devices: 1.3 us -> 2.62 us  [apply(): far = lax.ppermute(seam, 'row', far)]
where the time goes in v8:
time: 45.1 us; the launch traced here: 44.9 us
  waiting for transfers between devices  19.8 us (44%)
  starting transfers between devices  19.2 us (43%)
  Pallas kernels  5.02 us (11%)
  local copies, waits for them, and re-layouts  0.71 us (2%)
    ppermute x2, waiting for transfers between devices, apply(): lax.ppermute(v, 'row', pair_perm('row', 2 * (d + 1)))  6.35 us
    pallas_call x12, Pallas kernels, call(): pl.pallas_call(body, in_specs=[HBM] * len(raw) + [VMEM] * len(ins), out_s...  5.02 us
    ppermute x2, starting transfers between devices, apply(): lax.ppermute(v, 'row', pair_perm('row', 2 * (d + 1)))  4.76 us
    ppermute x3, waiting for transfers between devices, chip_sum(): lax.ppermute(v, 'col', pair_perm('col', 2 * (d + 1)))  4.69 us
    ppermute x3, waiting for transfers between devices, chip_sum(): lax.ppermute(mine, 'col', pair_perm('col', 2 * (d + 1)))  3.9 us
    ppermute x3, starting transfers between devices, chip_sum(): lax.ppermute(v, 'col', pair_perm('col', 2 * (d + 1)))  3.55 us
    ppermute x1, waiting for transfers between devices, chip_sum(): give = lax.ppermute(give, 'row', pair_perm('row', 1))  3.51 us
    ppermute x3, starting transfers between devices, chip_sum(): lax.ppermute(mine, 'col', pair_perm('col', 2 * (d + 1)))  3.49 us
  transfers between devices with their start and end apart: 14, of which 10 were waited for; matrix products, arithmetic and copies ran while one was open for 0% of the time, Pallas kernels for 6%

profile of v8, /device:TPU:0, one launch (start us, length us, event | category | flops | bytes accessed | tf_op | source)
XLA Modules:
  0.0 44.9 jit_solution(3911505812999963012)
XLA Ops:
  0.0 0.0 copy-start
  0.0 2.3 %shard_map.46 = (bf16[512,256]{1,0:T(8,128)(2,1)S(1)}, bf16[1024,256]{1,0:T(8,128)(2,1)S(1)}, bf16[2,2,256,256]{3,2,1,0:T(8,128)(2,1)S(1)}, f32[1,256]{1,0:T(1,128)S(1)}, f32[2,256]{1,0:T(2,128)S(1)}) custom-call(bf16[256,2,2,256]{3,2,1,0:T(2,128)(2,1)} %v_hbm.1, bf16[2,2,256,256]{3,2,1,0:T(8,128)(2,1)} %k_hbm.1, f32[1,256]{1,0:T(1,128)} %bitcast.1, ...), custom_call_target="tpu_custom_call" | custom-call | tf_op jit(solution)/shard_map/pallas_call | solution.py:20
  2.3 0.6 %collective-permute-start = (bf16[512,256]{1,0:T(8,128)(2,1)S(1)}, bf16[512,256]{1,0:T(8,128)(2,1)S(1)}, u32[]{:S(2)}, u32[]{:S(2)}) collective-permute-start(bf16[512,256]{1,0:T(8,128)(2,1)S(1)} %get-tuple-element.23), channel_id=1, source_target_pairs={{0,1},{1,0},{2,3},{3,2},{4,5},{5,4},{6,7},{7,6},{8,9},{9,8},{10,11... | collective-permute-start | bytes 786440 | tf_op jit(solution)/shard_map/ppermute | solution.py:343
  2.8 0.0 copy-done
  2.8 2.6 %collective-permute-start.8 = (bf16[2,2,256,256]{3,2,1,0:T(8,128)(2,1)S(1)}, bf16[2,2,256,256]{3,2,1,0:T(8,128)(2,1)S(1)}, u32[]{:S(2)}, u32[]{:S(2)}) collective-permute-start(bf16[2,2,256,256]{3,2,1,0:T(8,128)(2,1)S(1)} %copy-done), channel_id=1, source_target_pairs={{0,8},{8,0},{16,24},{24,16},{1,9},{9,1},{17,25},{25,17},{2,10},{10... | collective-permute-start | bytes 1572872 | tf_op jit(solution)/shard_map/ppermute | solution.py:335
  5.5 0.6 %shard_map.47.own_ref = f32[512,256]{1,0:T(8,128)S(1)} custom-call(bf16[1024,256]{1,0:T(8,128)(2,1)S(1)} %get-tuple-element.20.x_ref, bf16[2,2,256,256]{3,2,1,0:T(8,128)(2,1)S(1)} %get-tuple-element.22.k_ref), custom_call_target="tpu_custom_call" | custom-call | tf_op jit(solution)/shard_map/pallas_call | solution.py:20
  6.1 0.0 collective-permute-done.got_ref
  6.1 0.1 shard_map.48
  6.1 1.6 %collective-permute-start.1 = (bf16[128,256]{1,0:T(8,128)(2,1)S(1)}, bf16[128,256]{1,0:T(8,128)(2,1)S(1)}, u32[]{:S(2)}, u32[]{:S(2)}) collective-permute-start(bf16[128,256]{1,0:T(8,128)(2,1)S(1)} %get-tuple-element.26), channel_id=1, source_target_pairs={{0,2},{1,3},{2,0},{3,1},{4,6},{5,7},{6,4},{7,5},{8,10},{9,11},{10,... | collective-permute-start | bytes 196616 | tf_op jit(solution)/shard_map/ppermute | solution.py:317
  7.7 1.5 %collective-permute-start.2 = (bf16[128,256]{1,0:T(8,128)(2,1)S(1)}, bf16[128,256]{1,0:T(8,128)(2,1)S(1)}, u32[]{:S(2)}, u32[]{:S(2)}) collective-permute-start(bf16[128,256]{1,0:T(8,128)(2,1)S(1)} %get-tuple-element.27), channel_id=1, source_target_pairs={{0,4},{1,5},{2,6},{3,7},{4,0},{5,1},{6,2},{7,3},{8,12},{9,13},{10,... | collective-permute-start | bytes 196616 | tf_op jit(solution)/shard_map/ppermute | solution.py:317
  9.2 0.5 %collective-permute-start.3 = (bf16[128,256]{1,0:T(8,128)(2,1)S(1)}, bf16[128,256]{1,0:T(8,128)(2,1)S(1)}, u32[]{:S(2)}, u32[]{:S(2)}) collective-permute-start(bf16[128,256]{1,0:T(8,128)(2,1)S(1)} %get-tuple-element.28), channel_id=1, source_target_pairs={{0,6},{1,7},{2,4},{3,5},{4,2},{5,3},{6,0},{7,1},{8,14},{9,15},{10,... | collective-permute-start | bytes 196616 | tf_op jit(solution)/shard_map/ppermute | solution.py:317
  9.7 0.8 %collective-permute-done.1.refs_0_ = bf16[128,256]{1,0:T(8,128)(2,1)S(1)} collective-permute-done((bf16[128,256]{1,0:T(8,128)(2,1)S(1)}, bf16[128,256]{1,0:T(8,128)(2,1)S(1)}, u32[]{:S(2)}, u32[]{:S(2)}) %collective-permute-start.1) | collective-permute-done | bytes 65568 | tf_op jit(solution)/shard_map/ppermute | solution.py:317
  10.5 1.5 %collective-permute-done.2.refs_1_ = bf16[128,256]{1,0:T(8,128)(2,1)S(1)} collective-permute-done((bf16[128,256]{1,0:T(8,128)(2,1)S(1)}, bf16[128,256]{1,0:T(8,128)(2,1)S(1)}, u32[]{:S(2)}, u32[]{:S(2)}) %collective-permute-start.2) | collective-permute-done | bytes 65568 | tf_op jit(solution)/shard_map/ppermute | solution.py:317
  12.0 2.4 %collective-permute-done.3.refs_2_ = bf16[128,256]{1,0:T(8,128)(2,1)S(1)} collective-permute-done((bf16[128,256]{1,0:T(8,128)(2,1)S(1)}, bf16[128,256]{1,0:T(8,128)(2,1)S(1)}, u32[]{:S(2)}, u32[]{:S(2)}) %collective-permute-start.3) | collective-permute-done | bytes 65568 | tf_op jit(solution)/shard_map/ppermute | solution.py:317
  14.4 0.1 shard_map.50
  14.5 0.9 %collective-permute-start.4 = (bf16[80,256]{1,0:T(8,128)(2,1)S(1)}, bf16[80,256]{1,0:T(8,128)(2,1)S(1)}, u32[]{:S(2)}, u32[]{:S(2)}) collective-permute-start(bf16[80,256]{1,0:T(8,128)(2,1)S(1)} %get-tuple-element.30), channel_id=1, source_target_pairs={{0,8},{8,0},{16,24},{24,16},{1,9},{9,1},{17,25},{25,17},{2,10},{10... | collective-permute-start | bytes 122888 | tf_op jit(solution)/shard_map/ppermute | solution.py:320
  15.4 3.5 %collective-permute-done.4.got_ref = bf16[80,256]{1,0:T(8,128)(2,1)S(1)} collective-permute-done((bf16[80,256]{1,0:T(8,128)(2,1)S(1)}, bf16[80,256]{1,0:T(8,128)(2,1)S(1)}, u32[]{:S(2)}, u32[]{:S(2)}) %collective-permute-start.4) | collective-permute-done | bytes 40992 | tf_op jit(solution)/shard_map/ppermute | solution.py:320
  18.9 2.6 %collective-permute-start.7 = (bf16[128,256]{1,0:T(8,128)(2,1)S(1)}, bf16[128,256]{1,0:T(8,128)(2,1)S(1)}, u32[]{:S(2)}, u32[]{:S(2)}) collective-permute-start(bf16[128,256]{1,0:T(8,128)(2,1)S(1)} %shard_map.51.mine_ref), channel_id=1, source_target_pairs={{0,6},{1,7},{2,4},{3,5},{4,2},{5,3},{6,0},{7,1},{8,14},{9,15},{10,... | collective-permute-start | bytes 196616 | tf_op jit(solution)/shard_map/ppermute | solution.py:322
  21.5 0.5 %collective-permute-start.6 = (bf16[128,256]{1,0:T(8,128)(2,1)S(1)}, bf16[128,256]{1,0:T(8,128)(2,1)S(1)}, u32[]{:S(2)}, u32[]{:S(2)}) collective-permute-start(bf16[128,256]{1,0:T(8,128)(2,1)S(1)} %shard_map.51.mine_ref), channel_id=1, source_target_pairs={{0,4},{1,5},{2,6},{3,7},{4,0},{5,1},{6,2},{7,3},{8,12},{9,13},{10,... | collective-permute-start | bytes 196616 | tf_op jit(solution)/shard_map/ppermute | solution.py:322
  22.0 0.4 collective-permute-start.5
  22.4 1.7 %collective-permute-done.7.refs_2_ = bf16[128,256]{1,0:T(8,128)(2,1)S(1)} collective-permute-done((bf16[128,256]{1,0:T(8,128)(2,1)S(1)}, bf16[128,256]{1,0:T(8,128)(2,1)S(1)}, u32[]{:S(2)}, u32[]{:S(2)}) %collective-permute-start.7) | collective-permute-done | bytes 65568 | tf_op jit(solution)/shard_map/ppermute | solution.py:322
  24.1 1.6 %collective-permute-done.6.refs_1_ = bf16[128,256]{1,0:T(8,128)(2,1)S(1)} collective-permute-done((bf16[128,256]{1,0:T(8,128)(2,1)S(1)}, bf16[128,256]{1,0:T(8,128)(2,1)S(1)}, u32[]{:S(2)}, u32[]{:S(2)}) %collective-permute-start.6) | collective-permute-done | bytes 65568 | tf_op jit(solution)/shard_map/ppermute | solution.py:322
  25.8 0.5 %collective-permute-done.5.refs_0_ = bf16[128,256]{1,0:T(8,128)(2,1)S(1)} collective-permute-done((bf16[128,256]{1,0:T(8,128)(2,1)S(1)}, bf16[128,256]{1,0:T(8,128)(2,1)S(1)}, u32[]{:S(2)}, u32[]{:S(2)}) %collective-permute-start.5) | collective-permute-done | bytes 65568 | tf_op jit(solution)/shard_map/ppermute | solution.py:322
  26.3 0.1 collective-permute-start.12
  26.4 0.2 shard_map.53
  26.6 2.6 %collective-permute-start.10 = (bf16[8,1024]{1,0:T(8,128)(2,1)S(1)}, bf16[8,1024]{1,0:T(8,128)(2,1)S(1)}, u32[]{:S(2)}, u32[]{:S(2)}) collective-permute-start(bf16[8,1024]{1,0:T(8,128)(2,1)S(1)} %shard_map.53), channel_id=1, source_target_pairs={{8,24},{24,8},{0,16},{16,0},{9,25},{25,9},{1,17},{17,1},{10,26},{2... | collective-permute-start | bytes 49160 | tf_op jit(solution)/shard_map/ppermute | solution.py:351
  29.2 0.7 %collective-permute-start.9 = (bf16[8,1024]{1,0:T(8,128)(2,1)S(1)}, bf16[8,1024]{1,0:T(8,128)(2,1)S(1)}, u32[]{:S(2)}, u32[]{:S(2)}) collective-permute-start(bf16[8,1024]{1,0:T(8,128)(2,1)S(1)} %shard_map.53), channel_id=1, source_target_pairs={{8,16},{16,8},{9,17},{17,9},{10,18},{18,10},{11,19},{19,11},{12,20... | collective-permute-start | bytes 49160 | tf_op jit(solution)/shard_map/ppermute | solution.py:350
  29.9 1.4 %collective-permute-done.10.far_ref = bf16[8,1024]{1,0:T(8,128)(2,1)S(1)} collective-permute-done((bf16[8,1024]{1,0:T(8,128)(2,1)S(1)}, bf16[8,1024]{1,0:T(8,128)(2,1)S(1)}, u32[]{:S(2)}, u32[]{:S(2)}) %collective-permute-start.10) | collective-permute-done | bytes 16416 | tf_op jit(solution)/shard_map/ppermute | solution.py:351
  31.3 0.0 collective-permute-done.9.near_ref
  31.3 0.0 collective-permute-done.8.mate_ref
  31.3 1.0 %shard_map.54.k_ref = bf16[2,2,512,256]{3,2,1,0:T(8,128)(2,1)S(1)} custom-call(bf16[2,2,256,256]{3,2,1,0:T(8,128)(2,1)S(1)} %get-tuple-element.22.k_ref, bf16[2,2,256,256]{3,2,1,0:T(8,128)(2,1)S(1)} %collective-permute-done.8.mate_ref, f32[1,256]{1,0:T(1,128)S(1)} %get-tuple-element.25.d_ref, bf16[80,256]{1,0:T(8,128)(2,1)S(1)} %collective-permute-done.4.got_ref, ...), custom_call_target="tpu_custom_call" | custom-call | tf_op jit(solution)/shard_map/pallas_call | solution.py:20
  32.3 0.3 shard_map.55
  32.7 4.7 %collective-permute-start.11 = (bf16[128,256]{1,0:T(8,128)(2,1)S(1)}, bf16[128,256]{1,0:T(8,128)(2,1)S(1)}, u32[]{:S(2)}, u32[]{:S(2)}) collective-permute-start(bf16[128,256]{1,0:T(8,128)(2,1)S(1)} %get-tuple-element.32), channel_id=1, source_target_pairs={{0,16},{8,24},{16,0},{24,8},{1,17},{9,25},{17,1},{25,9},{2,18},{10... | collective-permute-start | bytes 196616 | tf_op jit(solution)/shard_map/ppermute | solution.py:367
  37.3 0.0 collective-permute-done.12.a_ref
  37.3 0.3 shard_map.56
  37.6 0.1 collective-permute-start.13
  37.7 1.8 %collective-permute-done.11.refs_1_ = bf16[128,256]{1,0:T(8,128)(2,1)S(1)} collective-permute-done((bf16[128,256]{1,0:T(8,128)(2,1)S(1)}, bf16[128,256]{1,0:T(8,128)(2,1)S(1)}, u32[]{:S(2)}, u32[]{:S(2)}) %collective-permute-start.11) | collective-permute-done | bytes 65568 | tf_op jit(solution)/shard_map/ppermute | solution.py:367
  39.6 4.5 %collective-permute-done.13.refs_3_ = bf16[128,256]{1,0:T(8,128)(2,1)S(1)} collective-permute-done((bf16[128,256]{1,0:T(8,128)(2,1)S(1)}, bf16[128,256]{1,0:T(8,128)(2,1)S(1)}, u32[]{:S(2)}, u32[]{:S(2)}) %collective-permute-start.13) | collective-permute-done | bytes 65568 | tf_op jit(solution)/shard_map/ppermute | solution.py:367
  44.1 0.1 shard_map.57
  44.2 0.7 %copy.5 = f32[64,2,2,256]{3,2,1,0:T(2,128)} copy(f32[64,2,2,256]{3,2,1,0:T(2,128)S(1)} %shard_map.57) | data formatting | bytes 524288
  (3 shorter events, 0.0 us)
Async XLA Ops:
  0.0 2.8 %copy-start = (bf16[2,2,256,256]{3,2,1,0:T(8,128)(2,1)S(1)}, bf16[2,2,256,256]{3,2,1,0:T(8,128)(2,1)}, u32[]{:S(2)}) copy-start(bf16[2,2,256,256]{3,2,1,0:T(8,128)(2,1)} %k_hbm.1) | copy-start | bytes 1572868
  2.3 3.8 %collective-permute-start = (bf16[512,256]{1,0:T(8,128)(2,1)S(1)}, bf16[512,256]{1,0:T(8,128)(2,1)S(1)}, u32[]{:S(2)}, u32[]{:S(2)}) collective-permute-start(bf16[512,256]{1,0:T(8,128)(2,1)S(1)} %get-tuple-element.23), channel_id=1, source_target_pairs={{0,1},{1,0},{2,3},{3,2},{4,5},{5,4},{6,7},{7,6},{8,9},{9,8},{10,11... | collective-permute-start | bytes 786440 | tf_op jit(solution)/shard_map/ppermute | solution.py:343
  2.8 28.5 %collective-permute-start.8 = (bf16[2,2,256,256]{3,2,1,0:T(8,128)(2,1)S(1)}, bf16[2,2,256,256]{3,2,1,0:T(8,128)(2,1)S(1)}, u32[]{:S(2)}, u32[]{:S(2)}) collective-permute-start(bf16[2,2,256,256]{3,2,1,0:T(8,128)(2,1)S(1)} %copy-done), channel_id=1, source_target_pairs={{0,8},{8,0},{16,24},{24,16},{1,9},{9,1},{17,25},{25,17},{2,10},{10... | collective-permute-start | bytes 1572872 | tf_op jit(solution)/shard_map/ppermute | solution.py:335
  6.1 4.3 %collective-permute-start.1 = (bf16[128,256]{1,0:T(8,128)(2,1)S(1)}, bf16[128,256]{1,0:T(8,128)(2,1)S(1)}, u32[]{:S(2)}, u32[]{:S(2)}) collective-permute-start(bf16[128,256]{1,0:T(8,128)(2,1)S(1)} %get-tuple-element.26), channel_id=1, source_target_pairs={{0,2},{1,3},{2,0},{3,1},{4,6},{5,7},{6,4},{7,5},{8,10},{9,11},{10,... | collective-permute-start | bytes 196616 | tf_op jit(solution)/shard_map/ppermute | solution.py:317
  7.7 4.3 %collective-permute-start.2 = (bf16[128,256]{1,0:T(8,128)(2,1)S(1)}, bf16[128,256]{1,0:T(8,128)(2,1)S(1)}, u32[]{:S(2)}, u32[]{:S(2)}) collective-permute-start(bf16[128,256]{1,0:T(8,128)(2,1)S(1)} %get-tuple-element.27), channel_id=1, source_target_pairs={{0,4},{1,5},{2,6},{3,7},{4,0},{5,1},{6,2},{7,3},{8,12},{9,13},{10,... | collective-permute-start | bytes 196616 | tf_op jit(solution)/shard_map/ppermute | solution.py:317
  9.2 5.2 %collective-permute-start.3 = (bf16[128,256]{1,0:T(8,128)(2,1)S(1)}, bf16[128,256]{1,0:T(8,128)(2,1)S(1)}, u32[]{:S(2)}, u32[]{:S(2)}) collective-permute-start(bf16[128,256]{1,0:T(8,128)(2,1)S(1)} %get-tuple-element.28), channel_id=1, source_target_pairs={{0,6},{1,7},{2,4},{3,5},{4,2},{5,3},{6,0},{7,1},{8,14},{9,15},{10,... | collective-permute-start | bytes 196616 | tf_op jit(solution)/shard_map/ppermute | solution.py:317
  14.5 4.4 %collective-permute-start.4 = (bf16[80,256]{1,0:T(8,128)(2,1)S(1)}, bf16[80,256]{1,0:T(8,128)(2,1)S(1)}, u32[]{:S(2)}, u32[]{:S(2)}) collective-permute-start(bf16[80,256]{1,0:T(8,128)(2,1)S(1)} %get-tuple-element.30), channel_id=1, source_target_pairs={{0,8},{8,0},{16,24},{24,16},{1,9},{9,1},{17,25},{25,17},{2,10},{10... | collective-permute-start | bytes 122888 | tf_op jit(solution)/shard_map/ppermute | solution.py:320
  18.9 5.2 %collective-permute-start.7 = (bf16[128,256]{1,0:T(8,128)(2,1)S(1)}, bf16[128,256]{1,0:T(8,128)(2,1)S(1)}, u32[]{:S(2)}, u32[]{:S(2)}) collective-permute-start(bf16[128,256]{1,0:T(8,128)(2,1)S(1)} %shard_map.51.mine_ref), channel_id=1, source_target_pairs={{0,6},{1,7},{2,4},{3,5},{4,2},{5,3},{6,0},{7,1},{8,14},{9,15},{10,... | collective-permute-start | bytes 196616 | tf_op jit(solution)/shard_map/ppermute | solution.py:322
  21.5 4.3 %collective-permute-start.6 = (bf16[128,256]{1,0:T(8,128)(2,1)S(1)}, bf16[128,256]{1,0:T(8,128)(2,1)S(1)}, u32[]{:S(2)}, u32[]{:S(2)}) collective-permute-start(bf16[128,256]{1,0:T(8,128)(2,1)S(1)} %shard_map.51.mine_ref), channel_id=1, source_target_pairs={{0,4},{1,5},{2,6},{3,7},{4,0},{5,1},{6,2},{7,3},{8,12},{9,13},{10,... | collective-permute-start | bytes 196616 | tf_op jit(solution)/shard_map/ppermute | solution.py:322
  22.0 4.3 %collective-permute-start.5 = (bf16[128,256]{1,0:T(8,128)(2,1)S(1)}, bf16[128,256]{1,0:T(8,128)(2,1)S(1)}, u32[]{:S(2)}, u32[]{:S(2)}) collective-permute-start(bf16[128,256]{1,0:T(8,128)(2,1)S(1)} %shard_map.51.mine_ref), channel_id=1, source_target_pairs={{0,2},{1,3},{2,0},{3,1},{4,6},{5,7},{6,4},{7,5},{8,10},{9,11},{10,... | collective-permute-start | bytes 196616 | tf_op jit(solution)/shard_map/ppermute | solution.py:322
  26.3 11.0 %collective-permute-start.12 = (bf16[512,256]{1,0:T(8,128)(2,1)S(1)}, bf16[512,256]{1,0:T(8,128)(2,1)S(1)}, u32[]{:S(2)}, u32[]{:S(2)}) collective-permute-start(bf16[512,256]{1,0:T(8,128)(2,1)S(1)} %shard_map.52.a_ref), channel_id=1, source_target_pairs={{0,1},{1,0},{2,3},{3,2},{4,5},{5,4},{6,7},{7,6},{8,9},{9,8},{10,11... | collective-permute-start | bytes 786440 | tf_op jit(solution)/shard_map/ppermute | solution.py:324
  26.6 4.7 %collective-permute-start.10 = (bf16[8,1024]{1,0:T(8,128)(2,1)S(1)}, bf16[8,1024]{1,0:T(8,128)(2,1)S(1)}, u32[]{:S(2)}, u32[]{:S(2)}) collective-permute-start(bf16[8,1024]{1,0:T(8,128)(2,1)S(1)} %shard_map.53), channel_id=1, source_target_pairs={{8,24},{24,8},{0,16},{16,0},{9,25},{25,9},{1,17},{17,1},{10,26},{2... | collective-permute-start | bytes 49160 | tf_op jit(solution)/shard_map/ppermute | solution.py:351
  29.2 2.1 %collective-permute-start.9 = (bf16[8,1024]{1,0:T(8,128)(2,1)S(1)}, bf16[8,1024]{1,0:T(8,128)(2,1)S(1)}, u32[]{:S(2)}, u32[]{:S(2)}) collective-permute-start(bf16[8,1024]{1,0:T(8,128)(2,1)S(1)} %shard_map.53), channel_id=1, source_target_pairs={{8,16},{16,8},{9,17},{17,9},{10,18},{18,10},{11,19},{19,11},{12,20... | collective-permute-start | bytes 49160 | tf_op jit(solution)/shard_map/ppermute | solution.py:350
  32.7 6.9 %collective-permute-start.11 = (bf16[128,256]{1,0:T(8,128)(2,1)S(1)}, bf16[128,256]{1,0:T(8,128)(2,1)S(1)}, u32[]{:S(2)}, u32[]{:S(2)}) collective-permute-start(bf16[128,256]{1,0:T(8,128)(2,1)S(1)} %get-tuple-element.32), channel_id=1, source_target_pairs={{0,16},{8,24},{16,0},{24,8},{1,17},{9,25},{17,1},{25,9},{2,18},{10... | collective-permute-start | bytes 196616 | tf_op jit(solution)/shard_map/ppermute | solution.py:367
  37.6 6.4 %collective-permute-start.13 = (bf16[128,256]{1,0:T(8,128)(2,1)S(1)}, bf16[128,256]{1,0:T(8,128)(2,1)S(1)}, u32[]{:S(2)}, u32[]{:S(2)}) collective-permute-start(bf16[128,256]{1,0:T(8,128)(2,1)S(1)} %get-tuple-element.34), channel_id=1, source_target_pairs={{0,16},{8,24},{16,0},{24,8},{1,17},{9,25},{17,1},{25,9},{2,18},{10... | collective-permute-start | bytes 196616 | tf_op jit(solution)/shard_map/ppermute | solution.py:367

commit v9 on v8

--- a/solution.py
+++ b/solution.py
@@ -84,14 +84,12 @@
         pltpu.make_async_copy(d_hbm, d_ref, sems.at[3]),
         pltpu.make_async_copy(n_hbm, n_ref, sems.at[4]),
     ]
-    for copy in copies[:2]:
+    for copy in copies:
         copy.start()
     copies[0].wait()
     x = v_ref[...].reshape(x_ref.shape)
     x_ref[...] = x
     copies[1].wait()
-    for copy in copies[2:]:
-        copy.start()
     adjoint(freq, x, k_ref, o_ref, u_ref)
     for copy in copies[2:]:
         copy.wait()
@@ -243,19 +241,16 @@
             out_ref[part(lo, size), :] = ref[n * size:(n + 1) * size]
 
 
-def predict_body(swap, a_ref, k_ref, keep_ref, *refs):
-    freq = parity()
-    if swap:
-        freq = 1 - freq
+def predict(freq, a_ref, k_ref, targets):
     half = a_ref.shape[0] // 2
     width = a_ref.shape[1]
-    size = keep_ref.shape[0] // 2
+    size = targets[0].shape[0] // 2
     total = []
     for c in range(2):
         value = dot_nn(a_ref[:half], k_ref[freq, c, :width])
         total.append(value + dot_nn(a_ref[half:], k_ref[freq, c, width:]))
     by_real, by_imag = total
-    for slot, ref in enumerate((keep_ref,) + refs):
+    for slot, ref in enumerate(targets):
         lo = 2 * slot * size
         mid = lo + size
         hi = mid + size
@@ -263,17 +258,29 @@
         ref[size:] = (by_real[mid:hi] + by_imag[lo:mid]).astype(ref.dtype)
 
 
-def final_body(peers, x_ref, noise_ref, *refs):
+def predict_own_body(a_ref, k_ref, *outs):
+    predict(parity(), a_ref, k_ref, outs)
+
+
+def predict_other_body(peers, a_ref, k_ref, *refs):
+    owns, keep_ref, sends = refs[:peers], refs[peers], refs[peers + 1:]
+    size = keep_ref.shape[0]
+    for own, send in zip(owns, sends):
+        send[:size] = own[...]
+    predict(1 - parity(), a_ref, k_ref, (keep_ref,) + tuple(send.at[size:] for send in sends))
+
+
+def final_body(x_ref, noise_ref, own_ref, other_ref, *refs):
     out_ref, s_ref = refs[-2:]
     size = out_ref.shape[0]
     rows = 4 * size
+    half = 2 * size
     me = lax.axis_index("row")
     freq = parity()
-    for which in range(2):
-        group = refs[which * (peers + 1):(which + 1) * (peers + 1)]
-        total = group[0][...]
-        for ref in group[1:]:
-            total = total + ref[...].astype(F32)
+    for which, keep_ref in enumerate((own_ref, other_ref)):
+        total = keep_ref[...]
+        for ref in refs[:-2]:
+            total = total + ref[which * half:(which + 1) * half].astype(F32)
         f = freq if which == 0 else 1 - freq
         for t in range(s_ref.shape[0]):
             at = slice(t * LANES, (t + 1) * LANES)
@@ -356,18 +363,17 @@
     operator = call(operator_body, (kernel, mate, coef, give, near, far), [((2, 2, 2 * width, rows), BF)])[0]
     size = count // blocks
     peers = blocks // 2 - 1
-    groups = []
-    for swap, field in ((False, mine), (True, other)):
-        keep, *sends = call(
-            functools.partial(predict_body, swap),
-            (field, operator),
-            [((2 * size, rows), F32)] + [((2 * size, rows), BF)] * peers,
-        )
-        groups.append(keep)
-        groups += [lax.ppermute(v, "row", pair_perm("row", 2 * (d + 1))) for d, v in enumerate(sends)]
+    half = (2 * size, rows)
+    keep_own, *owns = call(predict_own_body, (mine, operator), [(half, F32)] + [(half, BF)] * peers)
+    keep_other, *sends = call(
+        functools.partial(predict_other_body, peers),
+        (other, operator, *owns),
+        [(half, F32)] + [((4 * size, rows), BF)] * peers,
+    )
+    got = [lax.ppermute(v, "row", pair_perm("row", 2 * (d + 1))) for d, v in enumerate(sends)]
     return call(
-        functools.partial(final_body, peers),
-        (x, noise, *groups),
+        final_body,
+        (x, noise, keep_own, keep_other, *got),
         [((size,) + probes.shape[1:3] + (rows,), F32)],
         (pltpu.VMEM((rows // LANES, 4 * size, LANES), F32),),
     )[0]

time: 45.1 us -> 42.6 us (0.945)
  waiting for transfers between devices: 19.8 us -> 17.9 us
    ppermute x2 -> x1, waiting for transfers between devices: 6.35 us -> 4.41 us  [apply(): lax.ppermute(v, 'row', pair_perm('row', 2 * (d + 1)))]
    ppermute x2 -> x1, starting transfers between devices: 4.76 us -> 4.65 us  [apply(): lax.ppermute(v, 'row', pair_perm('row', 2 * (d + 1)))]
  transfers between devices with their start and end apart: 14 -> 13, of which waited for: 10 -> 9; matrix products, arithmetic and copies ran while one was open for 0% -> 0% of each run, Pallas kernels for 6% -> 5%
where the time goes in v9:
time: 42.6 us; the launch traced here: 42.5 us
  starting transfers between devices  19.1 us (45%)
  waiting for transfers between devices  17.9 us (42%)
  Pallas kernels  4.6 us (11%)
  local copies, waits for them, and re-layouts  0.71 us (2%)
    ppermute x3, waiting for transfers between devices, chip_sum(): lax.ppermute(v, 'col', pair_perm('col', 2 * (d + 1)))  4.69 us
    ppermute x1, starting transfers between devices, apply(): lax.ppermute(v, 'row', pair_perm('row', 2 * (d + 1)))  4.65 us
    pallas_call x12, Pallas kernels, call(): pl.pallas_call(body, in_specs=[HBM] * len(raw) + [VMEM] * len(ins), out_s...  4.6 us
    ppermute x1, waiting for transfers between devices, apply(): lax.ppermute(v, 'row', pair_perm('row', 2 * (d + 1)))  4.41 us
    ppermute x3, waiting for transfers between devices, chip_sum(): lax.ppermute(mine, 'col', pair_perm('col', 2 * (d + 1)))  3.9 us
    ppermute x3, starting transfers between devices, chip_sum(): lax.ppermute(v, 'col', pair_perm('col', 2 * (d + 1)))  3.55 us
    ppermute x1, waiting for transfers between devices, chip_sum(): give = lax.ppermute(give, 'row', pair_perm('row', 1))  3.51 us
    ppermute x3, starting transfers between devices, chip_sum(): lax.ppermute(mine, 'col', pair_perm('col', 2 * (d + 1)))  3.49 us
  transfers between devices with their start and end apart: 13, of which 9 were waited for; matrix products, arithmetic and copies ran while one was open for 0% of the time, Pallas kernels for 5%

profile of v9, /device:TPU:0, one launch (start us, length us, event | category | flops | bytes accessed | tf_op | source)
XLA Modules:
  0.0 42.5 jit_solution(15767442545037229550)
XLA Ops:
  0.0 0.0 copy-start
  0.0 1.8 %shard_map.46 = (bf16[512,256]{1,0:T(8,128)(2,1)S(1)}, bf16[1024,256]{1,0:T(8,128)(2,1)S(1)}, bf16[2,2,256,256]{3,2,1,0:T(8,128)(2,1)S(1)}, f32[1,256]{1,0:T(1,128)S(1)}, f32[2,256]{1,0:T(2,128)S(1)}) custom-call(bf16[256,2,2,256]{3,2,1,0:T(2,128)(2,1)} %v_hbm.1, bf16[2,2,256,256]{3,2,1,0:T(8,128)(2,1)} %k_hbm.1, f32[1,256]{1,0:T(1,128)} %bitcast.1, ...), custom_call_target="tpu_custom_call" | custom-call | tf_op jit(solution)/shard_map/pallas_call | solution.py:20
  1.8 0.6 %collective-permute-start = (bf16[512,256]{1,0:T(8,128)(2,1)S(1)}, bf16[512,256]{1,0:T(8,128)(2,1)S(1)}, u32[]{:S(2)}, u32[]{:S(2)}) collective-permute-start(bf16[512,256]{1,0:T(8,128)(2,1)S(1)} %get-tuple-element.23), channel_id=1, source_target_pairs={{0,1},{1,0},{2,3},{3,2},{4,5},{5,4},{6,7},{7,6},{8,9},{9,8},{10,11... | collective-permute-start | bytes 786440 | tf_op jit(solution)/shard_map/ppermute | solution.py:350
  2.4 0.0 copy-done
  2.4 2.6 %collective-permute-start.8 = (bf16[2,2,256,256]{3,2,1,0:T(8,128)(2,1)S(1)}, bf16[2,2,256,256]{3,2,1,0:T(8,128)(2,1)S(1)}, u32[]{:S(2)}, u32[]{:S(2)}) collective-permute-start(bf16[2,2,256,256]{3,2,1,0:T(8,128)(2,1)S(1)} %copy-done), channel_id=1, source_target_pairs={{0,8},{8,0},{16,24},{24,16},{1,9},{9,1},{17,25},{25,17},{2,10},{10... | collective-permute-start | bytes 1572872 | tf_op jit(solution)/shard_map/ppermute | solution.py:342
  5.0 0.6 %shard_map.47.own_ref = f32[512,256]{1,0:T(8,128)S(1)} custom-call(bf16[1024,256]{1,0:T(8,128)(2,1)S(1)} %get-tuple-element.20.x_ref, bf16[2,2,256,256]{3,2,1,0:T(8,128)(2,1)S(1)} %get-tuple-element.22.k_ref), custom_call_target="tpu_custom_call" | custom-call | tf_op jit(solution)/shard_map/pallas_call | solution.py:20
  5.6 0.0 collective-permute-done.got_ref
  5.6 0.1 shard_map.48
  5.7 1.5 %collective-permute-start.1 = (bf16[128,256]{1,0:T(8,128)(2,1)S(1)}, bf16[128,256]{1,0:T(8,128)(2,1)S(1)}, u32[]{:S(2)}, u32[]{:S(2)}) collective-permute-start(bf16[128,256]{1,0:T(8,128)(2,1)S(1)} %get-tuple-element.26), channel_id=1, source_target_pairs={{0,2},{1,3},{2,0},{3,1},{4,6},{5,7},{6,4},{7,5},{8,10},{9,11},{10,... | collective-permute-start | bytes 196616 | tf_op jit(solution)/shard_map/ppermute | solution.py:324
  7.3 1.5 %collective-permute-start.2 = (bf16[128,256]{1,0:T(8,128)(2,1)S(1)}, bf16[128,256]{1,0:T(8,128)(2,1)S(1)}, u32[]{:S(2)}, u32[]{:S(2)}) collective-permute-start(bf16[128,256]{1,0:T(8,128)(2,1)S(1)} %get-tuple-element.27), channel_id=1, source_target_pairs={{0,4},{1,5},{2,6},{3,7},{4,0},{5,1},{6,2},{7,3},{8,12},{9,13},{10,... | collective-permute-start | bytes 196616 | tf_op jit(solution)/shard_map/ppermute | solution.py:324
  8.8 0.5 %collective-permute-start.3 = (bf16[128,256]{1,0:T(8,128)(2,1)S(1)}, bf16[128,256]{1,0:T(8,128)(2,1)S(1)}, u32[]{:S(2)}, u32[]{:S(2)}) collective-permute-start(bf16[128,256]{1,0:T(8,128)(2,1)S(1)} %get-tuple-element.28), channel_id=1, source_target_pairs={{0,6},{1,7},{2,4},{3,5},{4,2},{5,3},{6,0},{7,1},{8,14},{9,15},{10,... | collective-permute-start | bytes 196616 | tf_op jit(solution)/shard_map/ppermute | solution.py:324
  9.3 0.8 %collective-permute-done.1.refs_0_ = bf16[128,256]{1,0:T(8,128)(2,1)S(1)} collective-permute-done((bf16[128,256]{1,0:T(8,128)(2,1)S(1)}, bf16[128,256]{1,0:T(8,128)(2,1)S(1)}, u32[]{:S(2)}, u32[]{:S(2)}) %collective-permute-start.1) | collective-permute-done | bytes 65568 | tf_op jit(solution)/shard_map/ppermute | solution.py:324
  10.0 1.5 %collective-permute-done.2.refs_1_ = bf16[128,256]{1,0:T(8,128)(2,1)S(1)} collective-permute-done((bf16[128,256]{1,0:T(8,128)(2,1)S(1)}, bf16[128,256]{1,0:T(8,128)(2,1)S(1)}, u32[]{:S(2)}, u32[]{:S(2)}) %collective-permute-start.2) | collective-permute-done | bytes 65568 | tf_op jit(solution)/shard_map/ppermute | solution.py:324
  11.5 2.4 %collective-permute-done.3.refs_2_ = bf16[128,256]{1,0:T(8,128)(2,1)S(1)} collective-permute-done((bf16[128,256]{1,0:T(8,128)(2,1)S(1)}, bf16[128,256]{1,0:T(8,128)(2,1)S(1)}, u32[]{:S(2)}, u32[]{:S(2)}) %collective-permute-start.3) | collective-permute-done | bytes 65568 | tf_op jit(solution)/shard_map/ppermute | solution.py:324
  14.0 0.1 shard_map.50
  14.0 0.9 %collective-permute-start.4 = (bf16[80,256]{1,0:T(8,128)(2,1)S(1)}, bf16[80,256]{1,0:T(8,128)(2,1)S(1)}, u32[]{:S(2)}, u32[]{:S(2)}) collective-permute-start(bf16[80,256]{1,0:T(8,128)(2,1)S(1)} %get-tuple-element.30), channel_id=1, source_target_pairs={{0,8},{8,0},{16,24},{24,16},{1,9},{9,1},{17,25},{25,17},{2,10},{10... | collective-permute-start | bytes 122888 | tf_op jit(solution)/shard_map/ppermute | solution.py:327
  14.9 3.5 %collective-permute-done.4.got_ref = bf16[80,256]{1,0:T(8,128)(2,1)S(1)} collective-permute-done((bf16[80,256]{1,0:T(8,128)(2,1)S(1)}, bf16[80,256]{1,0:T(8,128)(2,1)S(1)}, u32[]{:S(2)}, u32[]{:S(2)}) %collective-permute-start.4) | collective-permute-done | bytes 40992 | tf_op jit(solution)/shard_map/ppermute | solution.py:327
  18.4 2.6 %collective-permute-start.7 = (bf16[128,256]{1,0:T(8,128)(2,1)S(1)}, bf16[128,256]{1,0:T(8,128)(2,1)S(1)}, u32[]{:S(2)}, u32[]{:S(2)}) collective-permute-start(bf16[128,256]{1,0:T(8,128)(2,1)S(1)} %shard_map.51.mine_ref), channel_id=1, source_target_pairs={{0,6},{1,7},{2,4},{3,5},{4,2},{5,3},{6,0},{7,1},{8,14},{9,15},{10,... | collective-permute-start | bytes 196616 | tf_op jit(solution)/shard_map/ppermute | solution.py:329
  21.1 0.5 %collective-permute-start.6 = (bf16[128,256]{1,0:T(8,128)(2,1)S(1)}, bf16[128,256]{1,0:T(8,128)(2,1)S(1)}, u32[]{:S(2)}, u32[]{:S(2)}) collective-permute-start(bf16[128,256]{1,0:T(8,128)(2,1)S(1)} %shard_map.51.mine_ref), channel_id=1, source_target_pairs={{0,4},{1,5},{2,6},{3,7},{4,0},{5,1},{6,2},{7,3},{8,12},{9,13},{10,... | collective-permute-start | bytes 196616 | tf_op jit(solution)/shard_map/ppermute | solution.py:329
  21.6 0.4 collective-permute-start.5
  21.9 1.7 %collective-permute-done.7.refs_2_ = bf16[128,256]{1,0:T(8,128)(2,1)S(1)} collective-permute-done((bf16[128,256]{1,0:T(8,128)(2,1)S(1)}, bf16[128,256]{1,0:T(8,128)(2,1)S(1)}, u32[]{:S(2)}, u32[]{:S(2)}) %collective-permute-start.7) | collective-permute-done | bytes 65568 | tf_op jit(solution)/shard_map/ppermute | solution.py:329
  23.7 1.6 %collective-permute-done.6.refs_1_ = bf16[128,256]{1,0:T(8,128)(2,1)S(1)} collective-permute-done((bf16[128,256]{1,0:T(8,128)(2,1)S(1)}, bf16[128,256]{1,0:T(8,128)(2,1)S(1)}, u32[]{:S(2)}, u32[]{:S(2)}) %collective-permute-start.6) | collective-permute-done | bytes 65568 | tf_op jit(solution)/shard_map/ppermute | solution.py:329
  25.3 0.5 %collective-permute-done.5.refs_0_ = bf16[128,256]{1,0:T(8,128)(2,1)S(1)} collective-permute-done((bf16[128,256]{1,0:T(8,128)(2,1)S(1)}, bf16[128,256]{1,0:T(8,128)(2,1)S(1)}, u32[]{:S(2)}, u32[]{:S(2)}) %collective-permute-start.5) | collective-permute-done | bytes 65568 | tf_op jit(solution)/shard_map/ppermute | solution.py:329
  25.9 0.1 collective-permute-start.11
  25.9 0.2 shard_map.53
  26.2 2.6 %collective-permute-start.10 = (bf16[8,1024]{1,0:T(8,128)(2,1)S(1)}, bf16[8,1024]{1,0:T(8,128)(2,1)S(1)}, u32[]{:S(2)}, u32[]{:S(2)}) collective-permute-start(bf16[8,1024]{1,0:T(8,128)(2,1)S(1)} %shard_map.53), channel_id=1, source_target_pairs={{8,24},{24,8},{0,16},{16,0},{9,25},{25,9},{1,17},{17,1},{10,26},{2... | collective-permute-start | bytes 49160 | tf_op jit(solution)/shard_map/ppermute | solution.py:358
  28.8 0.7 %collective-permute-start.9 = (bf16[8,1024]{1,0:T(8,128)(2,1)S(1)}, bf16[8,1024]{1,0:T(8,128)(2,1)S(1)}, u32[]{:S(2)}, u32[]{:S(2)}) collective-permute-start(bf16[8,1024]{1,0:T(8,128)(2,1)S(1)} %shard_map.53), channel_id=1, source_target_pairs={{8,16},{16,8},{9,17},{17,9},{10,18},{18,10},{11,19},{19,11},{12,20... | collective-permute-start | bytes 49160 | tf_op jit(solution)/shard_map/ppermute | solution.py:357
  29.5 1.4 %collective-permute-done.10.far_ref = bf16[8,1024]{1,0:T(8,128)(2,1)S(1)} collective-permute-done((bf16[8,1024]{1,0:T(8,128)(2,1)S(1)}, bf16[8,1024]{1,0:T(8,128)(2,1)S(1)}, u32[]{:S(2)}, u32[]{:S(2)}) %collective-permute-start.10) | collective-permute-done | bytes 16416 | tf_op jit(solution)/shard_map/ppermute | solution.py:358
  30.8 0.0 collective-permute-done.9.near_ref
  30.9 0.0 collective-permute-done.8.mate_ref
  30.9 1.0 %shard_map.54.k_ref = bf16[2,2,512,256]{3,2,1,0:T(8,128)(2,1)S(1)} custom-call(bf16[2,2,256,256]{3,2,1,0:T(8,128)(2,1)S(1)} %get-tuple-element.22.k_ref, bf16[2,2,256,256]{3,2,1,0:T(8,128)(2,1)S(1)} %collective-permute-done.8.mate_ref, f32[1,256]{1,0:T(1,128)S(1)} %get-tuple-element.25.d_ref, bf16[80,256]{1,0:T(8,128)(2,1)S(1)} %collective-permute-done.4.got_ref, ...), custom_call_target="tpu_custom_call" | custom-call | tf_op jit(solution)/shard_map/pallas_call | solution.py:20
  31.9 0.3 shard_map.55
  32.2 0.0 collective-permute-done.11.a_ref
  32.2 0.3 shard_map.56
  32.6 4.7 %collective-permute-start.12 = (bf16[256,256]{1,0:T(8,128)(2,1)S(1)}, bf16[256,256]{1,0:T(8,128)(2,1)S(1)}, u32[]{:S(2)}, u32[]{:S(2)}) collective-permute-start(bf16[256,256]{1,0:T(8,128)(2,1)S(1)} %get-tuple-element.34), channel_id=1, source_target_pairs={{0,16},{8,24},{16,0},{24,8},{1,17},{9,25},{17,1},{25,9},{2,18},{10... | collective-permute-start | bytes 393224 | tf_op jit(solution)/shard_map/ppermute | solution.py:373
  37.2 4.4 %collective-permute-done.12.refs_0_ = bf16[256,256]{1,0:T(8,128)(2,1)S(1)} collective-permute-done((bf16[256,256]{1,0:T(8,128)(2,1)S(1)}, bf16[256,256]{1,0:T(8,128)(2,1)S(1)}, u32[]{:S(2)}, u32[]{:S(2)}) %collective-permute-start.12) | collective-permute-done | bytes 131104 | tf_op jit(solution)/shard_map/ppermute | solution.py:373
  41.6 0.1 shard_map.57
  41.8 0.7 %copy.5 = f32[64,2,2,256]{3,2,1,0:T(2,128)} copy(f32[64,2,2,256]{3,2,1,0:T(2,128)S(1)} %shard_map.57) | data formatting | bytes 524288
  (3 shorter events, 0.0 us)
Async XLA Ops:
  0.0 2.4 %copy-start = (bf16[2,2,256,256]{3,2,1,0:T(8,128)(2,1)S(1)}, bf16[2,2,256,256]{3,2,1,0:T(8,128)(2,1)}, u32[]{:S(2)}) copy-start(bf16[2,2,256,256]{3,2,1,0:T(8,128)(2,1)} %k_hbm.1) | copy-start | bytes 1572868
  1.8 3.8 %collective-permute-start = (bf16[512,256]{1,0:T(8,128)(2,1)S(1)}, bf16[512,256]{1,0:T(8,128)(2,1)S(1)}, u32[]{:S(2)}, u32[]{:S(2)}) collective-permute-start(bf16[512,256]{1,0:T(8,128)(2,1)S(1)} %get-tuple-element.23), channel_id=1, source_target_pairs={{0,1},{1,0},{2,3},{3,2},{4,5},{5,4},{6,7},{7,6},{8,9},{9,8},{10,11... | collective-permute-start | bytes 786440 | tf_op jit(solution)/shard_map/ppermute | solution.py:350
  2.4 28.5 %collective-permute-start.8 = (bf16[2,2,256,256]{3,2,1,0:T(8,128)(2,1)S(1)}, bf16[2,2,256,256]{3,2,1,0:T(8,128)(2,1)S(1)}, u32[]{:S(2)}, u32[]{:S(2)}) collective-permute-start(bf16[2,2,256,256]{3,2,1,0:T(8,128)(2,1)S(1)} %copy-done), channel_id=1, source_target_pairs={{0,8},{8,0},{16,24},{24,16},{1,9},{9,1},{17,25},{25,17},{2,10},{10... | collective-permute-start | bytes 1572872 | tf_op jit(solution)/shard_map/ppermute | solution.py:342
  5.7 4.3 %collective-permute-start.1 = (bf16[128,256]{1,0:T(8,128)(2,1)S(1)}, bf16[128,256]{1,0:T(8,128)(2,1)S(1)}, u32[]{:S(2)}, u32[]{:S(2)}) collective-permute-start(bf16[128,256]{1,0:T(8,128)(2,1)S(1)} %get-tuple-element.26), channel_id=1, source_target_pairs={{0,2},{1,3},{2,0},{3,1},{4,6},{5,7},{6,4},{7,5},{8,10},{9,11},{10,... | collective-permute-start | bytes 196616 | tf_op jit(solution)/shard_map/ppermute | solution.py:324
  7.3 4.3 %collective-permute-start.2 = (bf16[128,256]{1,0:T(8,128)(2,1)S(1)}, bf16[128,256]{1,0:T(8,128)(2,1)S(1)}, u32[]{:S(2)}, u32[]{:S(2)}) collective-permute-start(bf16[128,256]{1,0:T(8,128)(2,1)S(1)} %get-tuple-element.27), channel_id=1, source_target_pairs={{0,4},{1,5},{2,6},{3,7},{4,0},{5,1},{6,2},{7,3},{8,12},{9,13},{10,... | collective-permute-start | bytes 196616 | tf_op jit(solution)/shard_map/ppermute | solution.py:324
  8.8 5.2 %collective-permute-start.3 = (bf16[128,256]{1,0:T(8,128)(2,1)S(1)}, bf16[128,256]{1,0:T(8,128)(2,1)S(1)}, u32[]{:S(2)}, u32[]{:S(2)}) collective-permute-start(bf16[128,256]{1,0:T(8,128)(2,1)S(1)} %get-tuple-element.28), channel_id=1, source_target_pairs={{0,6},{1,7},{2,4},{3,5},{4,2},{5,3},{6,0},{7,1},{8,14},{9,15},{10,... | collective-permute-start | bytes 196616 | tf_op jit(solution)/shard_map/ppermute | solution.py:324
  14.0 4.4 %collective-permute-start.4 = (bf16[80,256]{1,0:T(8,128)(2,1)S(1)}, bf16[80,256]{1,0:T(8,128)(2,1)S(1)}, u32[]{:S(2)}, u32[]{:S(2)}) collective-permute-start(bf16[80,256]{1,0:T(8,128)(2,1)S(1)} %get-tuple-element.30), channel_id=1, source_target_pairs={{0,8},{8,0},{16,24},{24,16},{1,9},{9,1},{17,25},{25,17},{2,10},{10... | collective-permute-start | bytes 122888 | tf_op jit(solution)/shard_map/ppermute | solution.py:327
  18.4 5.2 %collective-permute-start.7 = (bf16[128,256]{1,0:T(8,128)(2,1)S(1)}, bf16[128,256]{1,0:T(8,128)(2,1)S(1)}, u32[]{:S(2)}, u32[]{:S(2)}) collective-permute-start(bf16[128,256]{1,0:T(8,128)(2,1)S(1)} %shard_map.51.mine_ref), channel_id=1, source_target_pairs={{0,6},{1,7},{2,4},{3,5},{4,2},{5,3},{6,0},{7,1},{8,14},{9,15},{10,... | collective-permute-start | bytes 196616 | tf_op jit(solution)/shard_map/ppermute | solution.py:329
  21.1 4.3 %collective-permute-start.6 = (bf16[128,256]{1,0:T(8,128)(2,1)S(1)}, bf16[128,256]{1,0:T(8,128)(2,1)S(1)}, u32[]{:S(2)}, u32[]{:S(2)}) collective-permute-start(bf16[128,256]{1,0:T(8,128)(2,1)S(1)} %shard_map.51.mine_ref), channel_id=1, source_target_pairs={{0,4},{1,5},{2,6},{3,7},{4,0},{5,1},{6,2},{7,3},{8,12},{9,13},{10,... | collective-permute-start | bytes 196616 | tf_op jit(solution)/shard_map/ppermute | solution.py:329
  21.6 4.3 %collective-permute-start.5 = (bf16[128,256]{1,0:T(8,128)(2,1)S(1)}, bf16[128,256]{1,0:T(8,128)(2,1)S(1)}, u32[]{:S(2)}, u32[]{:S(2)}) collective-permute-start(bf16[128,256]{1,0:T(8,128)(2,1)S(1)} %shard_map.51.mine_ref), channel_id=1, source_target_pairs={{0,2},{1,3},{2,0},{3,1},{4,6},{5,7},{6,4},{7,5},{8,10},{9,11},{10,... | collective-permute-start | bytes 196616 | tf_op jit(solution)/shard_map/ppermute | solution.py:329
  25.9 6.4 %collective-permute-start.11 = (bf16[512,256]{1,0:T(8,128)(2,1)S(1)}, bf16[512,256]{1,0:T(8,128)(2,1)S(1)}, u32[]{:S(2)}, u32[]{:S(2)}) collective-permute-start(bf16[512,256]{1,0:T(8,128)(2,1)S(1)} %shard_map.52.a_ref), channel_id=1, source_target_pairs={{0,1},{1,0},{2,3},{3,2},{4,5},{5,4},{6,7},{7,6},{8,9},{9,8},{10,11... | collective-permute-start | bytes 786440 | tf_op jit(solution)/shard_map/ppermute | solution.py:331
  26.2 4.7 %collective-permute-start.10 = (bf16[8,1024]{1,0:T(8,128)(2,1)S(1)}, bf16[8,1024]{1,0:T(8,128)(2,1)S(1)}, u32[]{:S(2)}, u32[]{:S(2)}) collective-permute-start(bf16[8,1024]{1,0:T(8,128)(2,1)S(1)} %shard_map.53), channel_id=1, source_target_pairs={{8,24},{24,8},{0,16},{16,0},{9,25},{25,9},{1,17},{17,1},{10,26},{2... | collective-permute-start | bytes 49160 | tf_op jit(solution)/shard_map/ppermute | solution.py:358
  28.8 2.1 %collective-permute-start.9 = (bf16[8,1024]{1,0:T(8,128)(2,1)S(1)}, bf16[8,1024]{1,0:T(8,128)(2,1)S(1)}, u32[]{:S(2)}, u32[]{:S(2)}) collective-permute-start(bf16[8,1024]{1,0:T(8,128)(2,1)S(1)} %shard_map.53), channel_id=1, source_target_pairs={{8,16},{16,8},{9,17},{17,9},{10,18},{18,10},{11,19},{19,11},{12,20... | collective-permute-start | bytes 49160 | tf_op jit(solution)/shard_map/ppermute | solution.py:357
  32.6 9.1 %collective-permute-start.12 = (bf16[256,256]{1,0:T(8,128)(2,1)S(1)}, bf16[256,256]{1,0:T(8,128)(2,1)S(1)}, u32[]{:S(2)}, u32[]{:S(2)}) collective-permute-start(bf16[256,256]{1,0:T(8,128)(2,1)S(1)} %get-tuple-element.34), channel_id=1, source_target_pairs={{0,16},{8,24},{16,0},{24,8},{1,17},{9,25},{17,1},{25,9},{2,18},{10... | collective-permute-start | bytes 393224 | tf_op jit(solution)/shard_map/ppermute | solution.py:373

commit v10 on v9

--- a/solution.py
+++ b/solution.py
@@ -37,6 +37,10 @@
 
 def xor(a, b):
     return jnp.bitwise_xor(a, b)
+
+
+def cross(slot):
+    return 2 * slot + 1 if slot else 0
 
 
 def part(start, size):
@@ -203,7 +207,7 @@
         for mate in range(2):
             for slot in range(blocks // 2):
                 for c in range(2):
-                    lo = c * probes + xor(me, mate + 2 * slot) * block + target * size
+                    lo = c * probes + xor(me, mate ^ cross(slot)) * block + target * size
                     rows = part(lo, size)
                     ref[at:at + size] = (own_ref[rows, :] + got_ref[rows, :].astype(F32)).astype(ref.dtype)
                     at += size
@@ -299,12 +303,12 @@
     value = own + got.astype(F32)
     both = jnp.where(a == 0, jnp.stack([value, 0 * value]), jnp.stack([0 * value, value]))
     both = lax.psum(both, "col").astype(BF).reshape(2, 2, blocks, -1, width)
-    slots = 2 * jnp.arange(blocks // 2)
+    slots = jnp.array([cross(slot) for slot in range(blocks // 2)])
     me = lax.axis_index("row")
 
     def chosen(freq, mate):
         value = lax.dynamic_index_in_dim(both, freq, 0, keepdims=False)
-        value = jnp.take(value, xor(me, mate + slots), axis=1)
+        value = jnp.take(value, xor(me, xor(mate, slots)), axis=1)
         return value.transpose(1, 0, 2, 3).reshape(-1, width)
 
     tail = jnp.concatenate(three(coef) + [jnp.zeros((13, width), BF)], axis=0)
@@ -370,7 +374,7 @@
         (other, operator, *owns),
         [(half, F32)] + [((4 * size, rows), BF)] * peers,
     )
-    got = [lax.ppermute(v, "row", pair_perm("row", 2 * (d + 1))) for d, v in enumerate(sends)]
+    got = [lax.ppermute(v, "row", pair_perm("row", cross(d + 1))) for d, v in enumerate(sends)]
     return call(
         final_body,
         (x, noise, keep_own, keep_other, *got),

time: 42.6 us -> 41.7 us (0.979)
  the two profiles are of different devices: /device:TPU:0 before, /device:TPU:21 now
where the time goes in v10:
time: 41.7 us; the launch traced here: 41.6 us
  waiting for transfers between devices  19.8 us (47%)
  starting transfers between devices  16.4 us (39%)
  Pallas kernels  4.59 us (11%)
  local copies, waits for them, and re-layouts  0.71 us (2%)
    ppermute x1, waiting for transfers between devices, apply(): lax.ppermute(v, 'row', pair_perm('row', cross(d + 1)))  6.62 us
    ppermute x1, waiting for transfers between devices, chip_sum(): give = lax.ppermute(give, 'row', pair_perm('row', 1))  6.01 us
    pallas_call x12, Pallas kernels, call(): pl.pallas_call(body, in_specs=[HBM] * len(raw) + [VMEM] * len(ins), out_s...  4.59 us
    ppermute x1, starting transfers between devices, apply(): near = lax.ppermute(seam, 'row', near)  4.31 us
    ppermute x3, waiting for transfers between devices, chip_sum(): lax.ppermute(mine, 'col', pair_perm('col', 2 * (d + 1)))  3.15 us
    ppermute x3, waiting for transfers between devices, chip_sum(): lax.ppermute(v, 'col', pair_perm('col', 2 * (d + 1)))  2.91 us
    ppermute x3, starting transfers between devices, chip_sum(): lax.ppermute(v, 'col', pair_perm('col', 2 * (d + 1)))  2.71 us
    ppermute x3, starting transfers between devices, chip_sum(): lax.ppermute(mine, 'col', pair_perm('col', 2 * (d + 1)))  2.65 us
  transfers between devices with their start and end apart: 13, of which 9 were waited for; matrix products, arithmetic and copies ran while one was open for 0% of the time, Pallas kernels for 6%

profile of v10, /device:TPU:21, one launch (start us, length us, event | category | flops | bytes accessed | tf_op | source)
XLA Modules:
  0.0 41.6 jit_solution(7394082495778277289)
XLA Ops:
  0.0 0.0 copy-start
  0.0 1.8 %shard_map.46 = (bf16[512,256]{1,0:T(8,128)(2,1)S(1)}, bf16[1024,256]{1,0:T(8,128)(2,1)S(1)}, bf16[2,2,256,256]{3,2,1,0:T(8,128)(2,1)S(1)}, f32[1,256]{1,0:T(1,128)S(1)}, f32[2,256]{1,0:T(2,128)S(1)}) custom-call(bf16[256,2,2,256]{3,2,1,0:T(2,128)(2,1)} %v_hbm.1, bf16[2,2,256,256]{3,2,1,0:T(8,128)(2,1)} %k_hbm.1, f32[1,256]{1,0:T(1,128)} %bitcast.1, ...), custom_call_target="tpu_custom_call" | custom-call | tf_op jit(solution)/shard_map/pallas_call | solution.py:20
  1.8 0.7 %collective-permute-start = (bf16[512,256]{1,0:T(8,128)(2,1)S(1)}, bf16[512,256]{1,0:T(8,128)(2,1)S(1)}, u32[]{:S(2)}, u32[]{:S(2)}) collective-permute-start(bf16[512,256]{1,0:T(8,128)(2,1)S(1)} %get-tuple-element.23), channel_id=1, source_target_pairs={{0,1},{1,0},{2,3},{3,2},{4,5},{5,4},{6,7},{7,6},{8,9},{9,8},{10,11... | collective-permute-start | bytes 786440 | tf_op jit(solution)/shard_map/ppermute | solution.py:354
  2.6 0.0 copy-done
  2.6 1.3 %collective-permute-start.8 = (bf16[2,2,256,256]{3,2,1,0:T(8,128)(2,1)S(1)}, bf16[2,2,256,256]{3,2,1,0:T(8,128)(2,1)S(1)}, u32[]{:S(2)}, u32[]{:S(2)}) collective-permute-start(bf16[2,2,256,256]{3,2,1,0:T(8,128)(2,1)S(1)} %copy-done), channel_id=1, source_target_pairs={{0,8},{8,0},{16,24},{24,16},{1,9},{9,1},{17,25},{25,17},{2,10},{10... | collective-permute-start | bytes 1572872 | tf_op jit(solution)/shard_map/ppermute | solution.py:346
  3.9 0.6 %shard_map.47.own_ref = f32[512,256]{1,0:T(8,128)S(1)} custom-call(bf16[1024,256]{1,0:T(8,128)(2,1)S(1)} %get-tuple-element.20.x_ref, bf16[2,2,256,256]{3,2,1,0:T(8,128)(2,1)S(1)} %get-tuple-element.22.k_ref), custom_call_target="tpu_custom_call" | custom-call | tf_op jit(solution)/shard_map/pallas_call | solution.py:20
  4.4 0.0 collective-permute-done.got_ref
  4.5 0.1 shard_map.48
  4.5 1.3 %collective-permute-start.1 = (bf16[128,256]{1,0:T(8,128)(2,1)S(1)}, bf16[128,256]{1,0:T(8,128)(2,1)S(1)}, u32[]{:S(2)}, u32[]{:S(2)}) collective-permute-start(bf16[128,256]{1,0:T(8,128)(2,1)S(1)} %get-tuple-element.26), channel_id=1, source_target_pairs={{0,2},{1,3},{2,0},{3,1},{4,6},{5,7},{6,4},{7,5},{8,10},{9,11},{10,... | collective-permute-start | bytes 196616 | tf_op jit(solution)/shard_map/ppermute | solution.py:328
  5.8 0.2 collective-permute-start.2
  6.0 1.2 %collective-permute-start.3 = (bf16[128,256]{1,0:T(8,128)(2,1)S(1)}, bf16[128,256]{1,0:T(8,128)(2,1)S(1)}, u32[]{:S(2)}, u32[]{:S(2)}) collective-permute-start(bf16[128,256]{1,0:T(8,128)(2,1)S(1)} %get-tuple-element.28), channel_id=1, source_target_pairs={{0,6},{1,7},{2,4},{3,5},{4,2},{5,3},{6,0},{7,1},{8,14},{9,15},{10,... | collective-permute-start | bytes 196616 | tf_op jit(solution)/shard_map/ppermute | solution.py:328
  7.3 0.8 %collective-permute-done.1.refs_0_ = bf16[128,256]{1,0:T(8,128)(2,1)S(1)} collective-permute-done((bf16[128,256]{1,0:T(8,128)(2,1)S(1)}, bf16[128,256]{1,0:T(8,128)(2,1)S(1)}, u32[]{:S(2)}, u32[]{:S(2)}) %collective-permute-start.1) | collective-permute-done | bytes 65568 | tf_op jit(solution)/shard_map/ppermute | solution.py:328
  8.0 1.2 %collective-permute-done.2.refs_1_ = bf16[128,256]{1,0:T(8,128)(2,1)S(1)} collective-permute-done((bf16[128,256]{1,0:T(8,128)(2,1)S(1)}, bf16[128,256]{1,0:T(8,128)(2,1)S(1)}, u32[]{:S(2)}, u32[]{:S(2)}) %collective-permute-start.2) | collective-permute-done | bytes 65568 | tf_op jit(solution)/shard_map/ppermute | solution.py:328
  9.2 0.9 %collective-permute-done.3.refs_2_ = bf16[128,256]{1,0:T(8,128)(2,1)S(1)} collective-permute-done((bf16[128,256]{1,0:T(8,128)(2,1)S(1)}, bf16[128,256]{1,0:T(8,128)(2,1)S(1)}, u32[]{:S(2)}, u32[]{:S(2)}) %collective-permute-start.3) | collective-permute-done | bytes 65568 | tf_op jit(solution)/shard_map/ppermute | solution.py:328
  10.2 0.1 shard_map.50
  10.2 0.6 %collective-permute-start.4 = (bf16[80,256]{1,0:T(8,128)(2,1)S(1)}, bf16[80,256]{1,0:T(8,128)(2,1)S(1)}, u32[]{:S(2)}, u32[]{:S(2)}) collective-permute-start(bf16[80,256]{1,0:T(8,128)(2,1)S(1)} %get-tuple-element.30), channel_id=1, source_target_pairs={{0,8},{8,0},{16,24},{24,16},{1,9},{9,1},{17,25},{25,17},{2,10},{10... | collective-permute-start | bytes 122888 | tf_op jit(solution)/shard_map/ppermute | solution.py:331
  10.8 6.0 %collective-permute-done.4.got_ref = bf16[80,256]{1,0:T(8,128)(2,1)S(1)} collective-permute-done((bf16[80,256]{1,0:T(8,128)(2,1)S(1)}, bf16[80,256]{1,0:T(8,128)(2,1)S(1)}, u32[]{:S(2)}, u32[]{:S(2)}) %collective-permute-start.4) | collective-permute-done | bytes 40992 | tf_op jit(solution)/shard_map/ppermute | solution.py:331
  16.9 1.2 %collective-permute-start.7 = (bf16[128,256]{1,0:T(8,128)(2,1)S(1)}, bf16[128,256]{1,0:T(8,128)(2,1)S(1)}, u32[]{:S(2)}, u32[]{:S(2)}) collective-permute-start(bf16[128,256]{1,0:T(8,128)(2,1)S(1)} %shard_map.51.mine_ref), channel_id=1, source_target_pairs={{0,6},{1,7},{2,4},{3,5},{4,2},{5,3},{6,0},{7,1},{8,14},{9,15},{10,... | collective-permute-start | bytes 196616 | tf_op jit(solution)/shard_map/ppermute | solution.py:333
  18.0 1.2 %collective-permute-start.6 = (bf16[128,256]{1,0:T(8,128)(2,1)S(1)}, bf16[128,256]{1,0:T(8,128)(2,1)S(1)}, u32[]{:S(2)}, u32[]{:S(2)}) collective-permute-start(bf16[128,256]{1,0:T(8,128)(2,1)S(1)} %shard_map.51.mine_ref), channel_id=1, source_target_pairs={{0,4},{1,5},{2,6},{3,7},{4,0},{5,1},{6,2},{7,3},{8,12},{9,13},{10,... | collective-permute-start | bytes 196616 | tf_op jit(solution)/shard_map/ppermute | solution.py:333
  19.2 0.3 collective-permute-start.5
  19.5 1.4 %collective-permute-done.7.refs_2_ = bf16[128,256]{1,0:T(8,128)(2,1)S(1)} collective-permute-done((bf16[128,256]{1,0:T(8,128)(2,1)S(1)}, bf16[128,256]{1,0:T(8,128)(2,1)S(1)}, u32[]{:S(2)}, u32[]{:S(2)}) %collective-permute-start.7) | collective-permute-done | bytes 65568 | tf_op jit(solution)/shard_map/ppermute | solution.py:333
  20.9 1.0 %collective-permute-done.6.refs_1_ = bf16[128,256]{1,0:T(8,128)(2,1)S(1)} collective-permute-done((bf16[128,256]{1,0:T(8,128)(2,1)S(1)}, bf16[128,256]{1,0:T(8,128)(2,1)S(1)}, u32[]{:S(2)}, u32[]{:S(2)}) %collective-permute-start.6) | collective-permute-done | bytes 65568 | tf_op jit(solution)/shard_map/ppermute | solution.py:333
  21.9 0.8 %collective-permute-done.5.refs_0_ = bf16[128,256]{1,0:T(8,128)(2,1)S(1)} collective-permute-done((bf16[128,256]{1,0:T(8,128)(2,1)S(1)}, bf16[128,256]{1,0:T(8,128)(2,1)S(1)}, u32[]{:S(2)}, u32[]{:S(2)}) %collective-permute-start.5) | collective-permute-done | bytes 65568 | tf_op jit(solution)/shard_map/ppermute | solution.py:333
  22.7 2.4 %collective-permute-start.11 = (bf16[512,256]{1,0:T(8,128)(2,1)S(1)}, bf16[512,256]{1,0:T(8,128)(2,1)S(1)}, u32[]{:S(2)}, u32[]{:S(2)}) collective-permute-start(bf16[512,256]{1,0:T(8,128)(2,1)S(1)} %shard_map.52.a_ref), channel_id=1, source_target_pairs={{0,1},{1,0},{2,3},{3,2},{4,5},{5,4},{6,7},{7,6},{8,9},{9,8},{10,11... | collective-permute-start | bytes 786440 | tf_op jit(solution)/shard_map/ppermute | solution.py:335
  25.1 0.2 shard_map.53
  25.4 0.1 collective-permute-start.10
  25.5 4.3 %collective-permute-start.9 = (bf16[8,1024]{1,0:T(8,128)(2,1)S(1)}, bf16[8,1024]{1,0:T(8,128)(2,1)S(1)}, u32[]{:S(2)}, u32[]{:S(2)}) collective-permute-start(bf16[8,1024]{1,0:T(8,128)(2,1)S(1)} %shard_map.53), channel_id=1, source_target_pairs={{8,16},{16,8},{9,17},{17,9},{10,18},{18,10},{11,19},{19,11},{12,20... | collective-permute-start | bytes 49160 | tf_op jit(solution)/shard_map/ppermute | solution.py:361
  29.8 0.0 collective-permute-done.10.far_ref
  29.8 1.1 %collective-permute-done.9.near_ref = bf16[8,1024]{1,0:T(8,128)(2,1)S(1)} collective-permute-done((bf16[8,1024]{1,0:T(8,128)(2,1)S(1)}, bf16[8,1024]{1,0:T(8,128)(2,1)S(1)}, u32[]{:S(2)}, u32[]{:S(2)}) %collective-permute-start.9) | collective-permute-done | bytes 16416 | tf_op jit(solution)/shard_map/ppermute | solution.py:361
  30.9 0.0 collective-permute-done.8.mate_ref
  30.9 1.0 %shard_map.54.k_ref = bf16[2,2,512,256]{3,2,1,0:T(8,128)(2,1)S(1)} custom-call(bf16[2,2,256,256]{3,2,1,0:T(8,128)(2,1)S(1)} %get-tuple-element.22.k_ref, bf16[2,2,256,256]{3,2,1,0:T(8,128)(2,1)S(1)} %collective-permute-done.8.mate_ref, f32[1,256]{1,0:T(1,128)S(1)} %get-tuple-element.25.d_ref, bf16[80,256]{1,0:T(8,128)(2,1)S(1)} %collective-permute-done.4.got_ref, ...), custom_call_target="tpu_custom_call" | custom-call | tf_op jit(solution)/shard_map/pallas_call | solution.py:20
  31.9 0.3 shard_map.55
  32.3 0.0 collective-permute-done.11.a_ref
  32.3 0.3 shard_map.56
  32.6 1.5 %collective-permute-start.12 = (bf16[256,256]{1,0:T(8,128)(2,1)S(1)}, bf16[256,256]{1,0:T(8,128)(2,1)S(1)}, u32[]{:S(2)}, u32[]{:S(2)}) collective-permute-start(bf16[256,256]{1,0:T(8,128)(2,1)S(1)} %get-tuple-element.34), channel_id=1, source_target_pairs={{0,24},{8,16},{16,8},{24,0},{1,25},{9,17},{17,9},{25,1},{2,26},{10... | collective-permute-start | bytes 393224 | tf_op jit(solution)/shard_map/ppermute | solution.py:377
  34.1 6.6 %collective-permute-done.12.refs_0_ = bf16[256,256]{1,0:T(8,128)(2,1)S(1)} collective-permute-done((bf16[256,256]{1,0:T(8,128)(2,1)S(1)}, bf16[256,256]{1,0:T(8,128)(2,1)S(1)}, u32[]{:S(2)}, u32[]{:S(2)}) %collective-permute-start.12) | collective-permute-done | bytes 131104 | tf_op jit(solution)/shard_map/ppermute | solution.py:377
  40.7 0.1 shard_map.57
  40.9 0.7 %copy.5 = f32[64,2,2,256]{3,2,1,0:T(2,128)} copy(f32[64,2,2,256]{3,2,1,0:T(2,128)S(1)} %shard_map.57) | data formatting | bytes 524288
  (3 shorter events, 0.0 us)
Async XLA Ops:
  0.0 2.6 %copy-start = (bf16[2,2,256,256]{3,2,1,0:T(8,128)(2,1)S(1)}, bf16[2,2,256,256]{3,2,1,0:T(8,128)(2,1)}, u32[]{:S(2)}) copy-start(bf16[2,2,256,256]{3,2,1,0:T(8,128)(2,1)} %k_hbm.1) | copy-start | bytes 1572868
  1.8 2.6 %collective-permute-start = (bf16[512,256]{1,0:T(8,128)(2,1)S(1)}, bf16[512,256]{1,0:T(8,128)(2,1)S(1)}, u32[]{:S(2)}, u32[]{:S(2)}) collective-permute-start(bf16[512,256]{1,0:T(8,128)(2,1)S(1)} %get-tuple-element.23), channel_id=1, source_target_pairs={{0,1},{1,0},{2,3},{3,2},{4,5},{5,4},{6,7},{7,6},{8,9},{9,8},{10,11... | collective-permute-start | bytes 786440 | tf_op jit(solution)/shard_map/ppermute | solution.py:354
  2.6 28.3 %collective-permute-start.8 = (bf16[2,2,256,256]{3,2,1,0:T(8,128)(2,1)S(1)}, bf16[2,2,256,256]{3,2,1,0:T(8,128)(2,1)S(1)}, u32[]{:S(2)}, u32[]{:S(2)}) collective-permute-start(bf16[2,2,256,256]{3,2,1,0:T(8,128)(2,1)S(1)} %copy-done), channel_id=1, source_target_pairs={{0,8},{8,0},{16,24},{24,16},{1,9},{9,1},{17,25},{25,17},{2,10},{10... | collective-permute-start | bytes 1572872 | tf_op jit(solution)/shard_map/ppermute | solution.py:346
  4.5 3.5 %collective-permute-start.1 = (bf16[128,256]{1,0:T(8,128)(2,1)S(1)}, bf16[128,256]{1,0:T(8,128)(2,1)S(1)}, u32[]{:S(2)}, u32[]{:S(2)}) collective-permute-start(bf16[128,256]{1,0:T(8,128)(2,1)S(1)} %get-tuple-element.26), channel_id=1, source_target_pairs={{0,2},{1,3},{2,0},{3,1},{4,6},{5,7},{6,4},{7,5},{8,10},{9,11},{10,... | collective-permute-start | bytes 196616 | tf_op jit(solution)/shard_map/ppermute | solution.py:328
  5.8 3.4 %collective-permute-start.2 = (bf16[128,256]{1,0:T(8,128)(2,1)S(1)}, bf16[128,256]{1,0:T(8,128)(2,1)S(1)}, u32[]{:S(2)}, u32[]{:S(2)}) collective-permute-start(bf16[128,256]{1,0:T(8,128)(2,1)S(1)} %get-tuple-element.27), channel_id=1, source_target_pairs={{0,4},{1,5},{2,6},{3,7},{4,0},{5,1},{6,2},{7,3},{8,12},{9,13},{10,... | collective-permute-start | bytes 196616 | tf_op jit(solution)/shard_map/ppermute | solution.py:328
  6.0 4.1 %collective-permute-start.3 = (bf16[128,256]{1,0:T(8,128)(2,1)S(1)}, bf16[128,256]{1,0:T(8,128)(2,1)S(1)}, u32[]{:S(2)}, u32[]{:S(2)}) collective-permute-start(bf16[128,256]{1,0:T(8,128)(2,1)S(1)} %get-tuple-element.28), channel_id=1, source_target_pairs={{0,6},{1,7},{2,4},{3,5},{4,2},{5,3},{6,0},{7,1},{8,14},{9,15},{10,... | collective-permute-start | bytes 196616 | tf_op jit(solution)/shard_map/ppermute | solution.py:328
  10.2 6.6 %collective-permute-start.4 = (bf16[80,256]{1,0:T(8,128)(2,1)S(1)}, bf16[80,256]{1,0:T(8,128)(2,1)S(1)}, u32[]{:S(2)}, u32[]{:S(2)}) collective-permute-start(bf16[80,256]{1,0:T(8,128)(2,1)S(1)} %get-tuple-element.30), channel_id=1, source_target_pairs={{0,8},{8,0},{16,24},{24,16},{1,9},{9,1},{17,25},{25,17},{2,10},{10... | collective-permute-start | bytes 122888 | tf_op jit(solution)/shard_map/ppermute | solution.py:331
  16.9 4.1 %collective-permute-start.7 = (bf16[128,256]{1,0:T(8,128)(2,1)S(1)}, bf16[128,256]{1,0:T(8,128)(2,1)S(1)}, u32[]{:S(2)}, u32[]{:S(2)}) collective-permute-start(bf16[128,256]{1,0:T(8,128)(2,1)S(1)} %shard_map.51.mine_ref), channel_id=1, source_target_pairs={{0,6},{1,7},{2,4},{3,5},{4,2},{5,3},{6,0},{7,1},{8,14},{9,15},{10,... | collective-permute-start | bytes 196616 | tf_op jit(solution)/shard_map/ppermute | solution.py:333
  18.0 3.9 %collective-permute-start.6 = (bf16[128,256]{1,0:T(8,128)(2,1)S(1)}, bf16[128,256]{1,0:T(8,128)(2,1)S(1)}, u32[]{:S(2)}, u32[]{:S(2)}) collective-permute-start(bf16[128,256]{1,0:T(8,128)(2,1)S(1)} %shard_map.51.mine_ref), channel_id=1, source_target_pairs={{0,4},{1,5},{2,6},{3,7},{4,0},{5,1},{6,2},{7,3},{8,12},{9,13},{10,... | collective-permute-start | bytes 196616 | tf_op jit(solution)/shard_map/ppermute | solution.py:333
  19.2 3.4 %collective-permute-start.5 = (bf16[128,256]{1,0:T(8,128)(2,1)S(1)}, bf16[128,256]{1,0:T(8,128)(2,1)S(1)}, u32[]{:S(2)}, u32[]{:S(2)}) collective-permute-start(bf16[128,256]{1,0:T(8,128)(2,1)S(1)} %shard_map.51.mine_ref), channel_id=1, source_target_pairs={{0,2},{1,3},{2,0},{3,1},{4,6},{5,7},{6,4},{7,5},{8,10},{9,11},{10,... | collective-permute-start | bytes 196616 | tf_op jit(solution)/shard_map/ppermute | solution.py:333
  22.7 9.6 %collective-permute-start.11 = (bf16[512,256]{1,0:T(8,128)(2,1)S(1)}, bf16[512,256]{1,0:T(8,128)(2,1)S(1)}, u32[]{:S(2)}, u32[]{:S(2)}) collective-permute-start(bf16[512,256]{1,0:T(8,128)(2,1)S(1)} %shard_map.52.a_ref), channel_id=1, source_target_pairs={{0,1},{1,0},{2,3},{3,2},{4,5},{5,4},{6,7},{7,6},{8,9},{9,8},{10,11... | collective-permute-start | bytes 786440 | tf_op jit(solution)/shard_map/ppermute | solution.py:335
  25.4 4.4 %collective-permute-start.10 = (bf16[8,1024]{1,0:T(8,128)(2,1)S(1)}, bf16[8,1024]{1,0:T(8,128)(2,1)S(1)}, u32[]{:S(2)}, u32[]{:S(2)}) collective-permute-start(bf16[8,1024]{1,0:T(8,128)(2,1)S(1)} %shard_map.53), channel_id=1, source_target_pairs={{8,24},{24,8},{0,16},{16,0},{9,25},{25,9},{1,17},{17,1},{10,26},{2... | collective-permute-start | bytes 49160 | tf_op jit(solution)/shard_map/ppermute | solution.py:362
  25.5 5.4 %collective-permute-start.9 = (bf16[8,1024]{1,0:T(8,128)(2,1)S(1)}, bf16[8,1024]{1,0:T(8,128)(2,1)S(1)}, u32[]{:S(2)}, u32[]{:S(2)}) collective-permute-start(bf16[8,1024]{1,0:T(8,128)(2,1)S(1)} %shard_map.53), channel_id=1, source_target_pairs={{8,16},{16,8},{9,17},{17,9},{10,18},{18,10},{11,19},{19,11},{12,20... | collective-permute-start | bytes 49160 | tf_op jit(solution)/shard_map/ppermute | solution.py:361
  32.6 8.1 %collective-permute-start.12 = (bf16[256,256]{1,0:T(8,128)(2,1)S(1)}, bf16[256,256]{1,0:T(8,128)(2,1)S(1)}, u32[]{:S(2)}, u32[]{:S(2)}) collective-permute-start(bf16[256,256]{1,0:T(8,128)(2,1)S(1)} %get-tuple-element.34), channel_id=1, source_target_pairs={{0,24},{8,16},{16,8},{24,0},{1,25},{9,17},{17,9},{25,1},{2,26},{10... | collective-permute-start | bytes 393224 | tf_op jit(solution)/shard_map/ppermute | solution.py:377

commit v11 on v10

--- a/solution.py
+++ b/solution.py
@@ -32,7 +32,19 @@
 
 
 def parity():
-    return lax.rem(lax.axis_index("col"), 2)
+    value = lax.axis_index("col")
+    for shift in range(1, lax.axis_size("col").bit_length()):
+        value = xor(value, lax.shift_right_logical(lax.axis_index("col"), jnp.int32(shift)))
+    return lax.rem(xor(value, lax.axis_index("row")), 2)
+
+
+def hop(step):
+    return 2 * step + step.bit_count() % 2
+
+
+def mate_perm():
+    cols = lax.axis_size("col")
+    return [(i * cols + j, (i ^ 1) * cols + (j ^ 1)) for i in range(lax.axis_size("row")) for j in range(cols)]
 
 
 def xor(a, b):
@@ -255,11 +267,12 @@
         total.append(value + dot_nn(a_ref[half:], k_ref[freq, c, width:]))
     by_real, by_imag = total
     for slot, ref in enumerate(targets):
+        kind = F32 if slot == 0 else BF
         lo = 2 * slot * size
         mid = lo + size
         hi = mid + size
-        ref[:size] = (by_real[lo:mid] - by_imag[mid:hi]).astype(ref.dtype)
-        ref[size:] = (by_real[mid:hi] + by_imag[lo:mid]).astype(ref.dtype)
+        ref[:size] = (by_real[lo:mid] - by_imag[mid:hi]).astype(kind)
+        ref[size:] = (by_real[mid:hi] + by_imag[lo:mid]).astype(kind)
 
 
 def predict_own_body(a_ref, k_ref, *outs):
@@ -269,9 +282,11 @@
 def predict_other_body(peers, a_ref, k_ref, *refs):
     owns, keep_ref, sends = refs[:peers], refs[peers], refs[peers + 1:]
     size = keep_ref.shape[0]
+    freq = parity()
     for own, send in zip(owns, sends):
-        send[:size] = own[...]
-    predict(1 - parity(), a_ref, k_ref, (keep_ref,) + tuple(send.at[size:] for send in sends))
+        send[part(freq * size, size), :] = own[...]
+    rest = part((1 - freq) * size, size)
+    predict(1 - freq, a_ref, k_ref, (keep_ref,) + tuple(send.at[rest] for send in sends))
 
 
 def final_body(x_ref, noise_ref, own_ref, other_ref, *refs):
@@ -282,10 +297,10 @@
     me = lax.axis_index("row")
     freq = parity()
     for which, keep_ref in enumerate((own_ref, other_ref)):
+        f = freq if which == 0 else 1 - freq
         total = keep_ref[...]
         for ref in refs[:-2]:
-            total = total + ref[which * half:(which + 1) * half].astype(F32)
-        f = freq if which == 0 else 1 - freq
+            total = total + ref[part(f * half, half), :].astype(F32)
         for t in range(s_ref.shape[0]):
             at = slice(t * LANES, (t + 1) * LANES)
             s_ref[t, pl.ds(2 * f, size, stride=4), :] = total[:size, at]
@@ -312,12 +327,13 @@
         return value.transpose(1, 0, 2, 3).reshape(-1, width)
 
     tail = jnp.concatenate(three(coef) + [jnp.zeros((13, width), BF)], axis=0)
-    give = jnp.concatenate([chosen(1 - a, 1), chosen(a, 1), tail], axis=0)
+    give = jnp.concatenate([chosen(0, 1), chosen(1, 1), tail], axis=0)
     give = lax.ppermute(give, "row", pair_perm("row", 1))
-    half = rows // 2
-    mine = jnp.concatenate([chosen(a, 0), give[half:rows]], axis=0)
-    other = jnp.concatenate([chosen(1 - a, 0), give[:half]], axis=0)
-    return mine, other, give
+    fields = []
+    for freq in (a, 1 - a):
+        mate = lax.dynamic_slice_in_dim(give, freq * (rows // 2), rows // 2, 0)
+        fields.append(jnp.concatenate([chosen(freq, 0), mate], axis=0))
+    return (*fields, give)
 
 
 def chip_sum(own, got, coef, chips):
@@ -325,12 +341,12 @@
     size = rows // chips
     keep, *sends = call(split_body, (own, got), [((size, width), F32)] + [((size, width), BF)] * (chips - 1))
     fence = call(fence_body, (coef,), [((8, LANES), F32)])[0]
-    got = [lax.ppermute(v, "col", pair_perm("col", 2 * (d + 1))) for d, v in enumerate(sends)]
+    got = [lax.ppermute(v, "col", pair_perm("col", hop(d + 1))) for d, v in enumerate(sends)]
     stay, give = call(sum_body, (keep, coef, fence, *got), [((size // 2, width), BF), ((size // 2 + 16, width), BF)])
     fence = call(fence_body, (coef,), [((8, LANES), F32)])[0]
-    give = lax.ppermute(give, "row", pair_perm("row", 1))
+    give = lax.ppermute(give, ("row", "col"), mate_perm())
     mine = call(pack_body, (stay, give, fence), [((size, width), BF)])[0]
-    got = [lax.ppermute(mine, "col", pair_perm("col", 2 * (d + 1))) for d in range(chips - 1)]
+    got = [lax.ppermute(mine, "col", pair_perm("col", hop(d + 1))) for d in range(chips - 1)]
     mine = call(join_body, (mine, *got), [((rows, width), BF)])[0]
     return mine, lax.ppermute(mine, "col", pair_perm("col", 1)), give
 

time: 41.7 us -> 40.6 us (0.974)
  the two profiles are of different devices: /device:TPU:21 before, /device:TPU:18 now
where the time goes in v11:
time: 40.6 us; the launch traced here: 40.4 us
  waiting for transfers between devices  19.5 us (48%)
  starting transfers between devices  15.5 us (38%)
  Pallas kernels  4.64 us (11%)
  local copies, waits for them, and re-layouts  0.71 us (2%)
    ppermute x1, waiting for transfers between devices, apply(): lax.ppermute(v, 'row', pair_perm('row', cross(d + 1)))  5.41 us
    ppermute x1, waiting for transfers between devices, chip_sum(): give = lax.ppermute(give, ('row', 'col'), mate_perm())  5.2 us
    pallas_call x12, Pallas kernels, call(): pl.pallas_call(body, in_specs=[HBM] * len(raw) + [VMEM] * len(ins), out_s...  4.64 us
    ppermute x1, starting transfers between devices, apply(): near = lax.ppermute(seam, 'row', near)  4.59 us
    ppermute x3, waiting for transfers between devices, chip_sum(): lax.ppermute(v, 'col', pair_perm('col', hop(d + 1)))  3.73 us
    ppermute x3, waiting for transfers between devices, chip_sum(): lax.ppermute(mine, 'col', pair_perm('col', hop(d + 1)))  3.44 us
    ppermute x3, starting transfers between devices, chip_sum(): lax.ppermute(v, 'col', pair_perm('col', hop(d + 1)))  3.27 us
    ppermute x3, starting transfers between devices, chip_sum(): lax.ppermute(mine, 'col', pair_perm('col', hop(d + 1)))  3.21 us
  transfers between devices with their start and end apart: 13, of which 8 were waited for; matrix products, arithmetic and copies ran while one was open for 0% of the time, Pallas kernels for 6%

profile of v11, /device:TPU:18, one launch (start us, length us, event | category | flops | bytes accessed | tf_op | source)
XLA Modules:
  0.0 40.4 jit_solution(5791893927952033671)
XLA Ops:
  0.0 0.0 copy-start
  0.0 1.8 %shard_map.46 = (bf16[512,256]{1,0:T(8,128)(2,1)S(1)}, bf16[1024,256]{1,0:T(8,128)(2,1)S(1)}, bf16[2,2,256,256]{3,2,1,0:T(8,128)(2,1)S(1)}, f32[1,256]{1,0:T(1,128)S(1)}, f32[2,256]{1,0:T(2,128)S(1)}) custom-call(bf16[256,2,2,256]{3,2,1,0:T(2,128)(2,1)} %v_hbm.1, bf16[2,2,256,256]{3,2,1,0:T(8,128)(2,1)} %k_hbm.1, f32[1,256]{1,0:T(1,128)} %bitcast.1, ...), custom_call_target="tpu_custom_call" | custom-call | tf_op jit(solution)/shard_map/pallas_call | solution.py:20
  1.8 0.1 collective-permute-start
  1.9 0.0 copy-done
  1.9 1.6 %collective-permute-start.8 = (bf16[2,2,256,256]{3,2,1,0:T(8,128)(2,1)S(1)}, bf16[2,2,256,256]{3,2,1,0:T(8,128)(2,1)S(1)}, u32[]{:S(2)}, u32[]{:S(2)}) collective-permute-start(bf16[2,2,256,256]{3,2,1,0:T(8,128)(2,1)S(1)} %copy-done), channel_id=1, source_target_pairs={{0,8},{8,0},{16,24},{24,16},{1,9},{9,1},{17,25},{25,17},{2,10},{10... | collective-permute-start | bytes 1572872 | tf_op jit(solution)/shard_map/ppermute | solution.py:362
  3.6 0.6 %shard_map.47.own_ref = f32[512,256]{1,0:T(8,128)S(1)} custom-call(bf16[1024,256]{1,0:T(8,128)(2,1)S(1)} %get-tuple-element.20.x_ref, bf16[2,2,256,256]{3,2,1,0:T(8,128)(2,1)S(1)} %get-tuple-element.22.k_ref), custom_call_target="tpu_custom_call" | custom-call | tf_op jit(solution)/shard_map/pallas_call | solution.py:20
  4.1 0.0 collective-permute-done.got_ref
  4.2 0.1 shard_map.48
  4.2 0.4 collective-permute-start.1
  4.6 1.5 %collective-permute-start.2 = (bf16[128,256]{1,0:T(8,128)(2,1)S(1)}, bf16[128,256]{1,0:T(8,128)(2,1)S(1)}, u32[]{:S(2)}, u32[]{:S(2)}) collective-permute-start(bf16[128,256]{1,0:T(8,128)(2,1)S(1)} %get-tuple-element.27), channel_id=1, source_target_pairs={{0,5},{1,4},{2,7},{3,6},{4,1},{5,0},{6,3},{7,2},{8,13},{9,12},{10,... | collective-permute-start | bytes 196616 | tf_op jit(solution)/shard_map/ppermute | solution.py:344
  6.1 1.4 %collective-permute-start.3 = (bf16[128,256]{1,0:T(8,128)(2,1)S(1)}, bf16[128,256]{1,0:T(8,128)(2,1)S(1)}, u32[]{:S(2)}, u32[]{:S(2)}) collective-permute-start(bf16[128,256]{1,0:T(8,128)(2,1)S(1)} %get-tuple-element.28), channel_id=1, source_target_pairs={{0,6},{1,7},{2,4},{3,5},{4,2},{5,3},{6,0},{7,1},{8,14},{9,15},{10,... | collective-permute-start | bytes 196616 | tf_op jit(solution)/shard_map/ppermute | solution.py:344
  7.5 0.9 %collective-permute-done.1.refs_0_ = bf16[128,256]{1,0:T(8,128)(2,1)S(1)} collective-permute-done((bf16[128,256]{1,0:T(8,128)(2,1)S(1)}, bf16[128,256]{1,0:T(8,128)(2,1)S(1)}, u32[]{:S(2)}, u32[]{:S(2)}) %collective-permute-start.1) | collective-permute-done | bytes 65568 | tf_op jit(solution)/shard_map/ppermute | solution.py:344
  8.4 0.1 collective-permute-done.2.refs_1_
  8.4 2.8 %collective-permute-done.3.refs_2_ = bf16[128,256]{1,0:T(8,128)(2,1)S(1)} collective-permute-done((bf16[128,256]{1,0:T(8,128)(2,1)S(1)}, bf16[128,256]{1,0:T(8,128)(2,1)S(1)}, u32[]{:S(2)}, u32[]{:S(2)}) %collective-permute-start.3) | collective-permute-done | bytes 65568 | tf_op jit(solution)/shard_map/ppermute | solution.py:344
  11.2 0.1 shard_map.50
  11.3 0.1 collective-permute-start.4
  11.4 5.2 %collective-permute-done.4.got_ref = bf16[80,256]{1,0:T(8,128)(2,1)S(1)} collective-permute-done((bf16[80,256]{1,0:T(8,128)(2,1)S(1)}, bf16[80,256]{1,0:T(8,128)(2,1)S(1)}, u32[]{:S(2)}, u32[]{:S(2)}) %collective-permute-start.4) | collective-permute-done | bytes 40992 | tf_op jit(solution)/shard_map/ppermute | solution.py:347
  16.6 1.5 %collective-permute-start.7 = (bf16[128,256]{1,0:T(8,128)(2,1)S(1)}, bf16[128,256]{1,0:T(8,128)(2,1)S(1)}, u32[]{:S(2)}, u32[]{:S(2)}) collective-permute-start(bf16[128,256]{1,0:T(8,128)(2,1)S(1)} %shard_map.51.mine_ref), channel_id=1, source_target_pairs={{0,6},{1,7},{2,4},{3,5},{4,2},{5,3},{6,0},{7,1},{8,14},{9,15},{10,... | collective-permute-start | bytes 196616 | tf_op jit(solution)/shard_map/ppermute | solution.py:349
  18.1 0.2 collective-permute-start.6
  18.3 1.5 %collective-permute-start.5 = (bf16[128,256]{1,0:T(8,128)(2,1)S(1)}, bf16[128,256]{1,0:T(8,128)(2,1)S(1)}, u32[]{:S(2)}, u32[]{:S(2)}) collective-permute-start(bf16[128,256]{1,0:T(8,128)(2,1)S(1)} %shard_map.51.mine_ref), channel_id=1, source_target_pairs={{0,3},{1,2},{2,1},{3,0},{4,7},{5,6},{6,5},{7,4},{8,11},{9,10},{10,... | collective-permute-start | bytes 196616 | tf_op jit(solution)/shard_map/ppermute | solution.py:349
  19.8 2.1 %collective-permute-done.7.refs_2_ = bf16[128,256]{1,0:T(8,128)(2,1)S(1)} collective-permute-done((bf16[128,256]{1,0:T(8,128)(2,1)S(1)}, bf16[128,256]{1,0:T(8,128)(2,1)S(1)}, u32[]{:S(2)}, u32[]{:S(2)}) %collective-permute-start.7) | collective-permute-done | bytes 65568 | tf_op jit(solution)/shard_map/ppermute | solution.py:349
  21.9 1.3 %collective-permute-done.6.refs_1_ = bf16[128,256]{1,0:T(8,128)(2,1)S(1)} collective-permute-done((bf16[128,256]{1,0:T(8,128)(2,1)S(1)}, bf16[128,256]{1,0:T(8,128)(2,1)S(1)}, u32[]{:S(2)}, u32[]{:S(2)}) %collective-permute-start.6) | collective-permute-done | bytes 65568 | tf_op jit(solution)/shard_map/ppermute | solution.py:349
  23.2 0.0 collective-permute-done.5.refs_0_
  23.2 0.1 shard_map.52.a_ref
  23.3 0.2 collective-permute-start.11
  23.5 0.2 shard_map.53
  23.7 0.4 collective-permute-start.10
  24.1 4.6 %collective-permute-start.9 = (bf16[8,1024]{1,0:T(8,128)(2,1)S(1)}, bf16[8,1024]{1,0:T(8,128)(2,1)S(1)}, u32[]{:S(2)}, u32[]{:S(2)}) collective-permute-start(bf16[8,1024]{1,0:T(8,128)(2,1)S(1)} %shard_map.53), channel_id=1, source_target_pairs={{8,16},{16,8},{9,17},{17,9},{10,18},{18,10},{11,19},{19,11},{12,20... | collective-permute-start | bytes 49160 | tf_op jit(solution)/shard_map/ppermute | solution.py:377
  28.7 0.0 collective-permute-done.10.far_ref
  28.7 1.7 %collective-permute-done.9.near_ref = bf16[8,1024]{1,0:T(8,128)(2,1)S(1)} collective-permute-done((bf16[8,1024]{1,0:T(8,128)(2,1)S(1)}, bf16[8,1024]{1,0:T(8,128)(2,1)S(1)}, u32[]{:S(2)}, u32[]{:S(2)}) %collective-permute-start.9) | collective-permute-done | bytes 16416 | tf_op jit(solution)/shard_map/ppermute | solution.py:377
  30.4 0.0 collective-permute-done.8.mate_ref
  30.4 1.0 %shard_map.54.k_ref = bf16[2,2,512,256]{3,2,1,0:T(8,128)(2,1)S(1)} custom-call(bf16[2,2,256,256]{3,2,1,0:T(8,128)(2,1)S(1)} %get-tuple-element.22.k_ref, bf16[2,2,256,256]{3,2,1,0:T(8,128)(2,1)S(1)} %collective-permute-done.8.mate_ref, f32[1,256]{1,0:T(1,128)S(1)} %get-tuple-element.25.d_ref, bf16[80,256]{1,0:T(8,128)(2,1)S(1)} %collective-permute-done.4.got_ref, ...), custom_call_target="tpu_custom_call" | custom-call | tf_op jit(solution)/shard_map/pallas_call | solution.py:20
  31.4 0.3 shard_map.55
  31.8 0.0 collective-permute-done.11.a_ref
  31.8 0.3 shard_map.56
  32.1 2.1 %collective-permute-start.12 = (bf16[256,256]{1,0:T(8,128)(2,1)S(1)}, bf16[256,256]{1,0:T(8,128)(2,1)S(1)}, u32[]{:S(2)}, u32[]{:S(2)}) collective-permute-start(bf16[256,256]{1,0:T(8,128)(2,1)S(1)} %get-tuple-element.34), channel_id=1, source_target_pairs={{0,24},{8,16},{16,8},{24,0},{1,25},{9,17},{17,9},{25,1},{2,26},{10... | collective-permute-start | bytes 393224 | tf_op jit(solution)/shard_map/ppermute | solution.py:393
  34.2 5.4 %collective-permute-done.12.refs_0_ = bf16[256,256]{1,0:T(8,128)(2,1)S(1)} collective-permute-done((bf16[256,256]{1,0:T(8,128)(2,1)S(1)}, bf16[256,256]{1,0:T(8,128)(2,1)S(1)}, u32[]{:S(2)}, u32[]{:S(2)}) %collective-permute-start.12) | collective-permute-done | bytes 131104 | tf_op jit(solution)/shard_map/ppermute | solution.py:393
  39.6 0.1 shard_map.57
  39.7 0.7 %copy.5 = f32[64,2,2,256]{3,2,1,0:T(2,128)} copy(f32[64,2,2,256]{3,2,1,0:T(2,128)S(1)} %shard_map.57) | data formatting | bytes 524288
  (2 shorter events, 0.0 us)
Async XLA Ops:
  0.0 1.9 %copy-start = (bf16[2,2,256,256]{3,2,1,0:T(8,128)(2,1)S(1)}, bf16[2,2,256,256]{3,2,1,0:T(8,128)(2,1)}, u32[]{:S(2)}) copy-start(bf16[2,2,256,256]{3,2,1,0:T(8,128)(2,1)} %k_hbm.1) | copy-start | bytes 1572868
  1.8 2.3 %collective-permute-start = (bf16[512,256]{1,0:T(8,128)(2,1)S(1)}, bf16[512,256]{1,0:T(8,128)(2,1)S(1)}, u32[]{:S(2)}, u32[]{:S(2)}) collective-permute-start(bf16[512,256]{1,0:T(8,128)(2,1)S(1)} %get-tuple-element.23), channel_id=1, source_target_pairs={{0,1},{1,0},{2,3},{3,2},{4,5},{5,4},{6,7},{7,6},{8,9},{9,8},{10,11... | collective-permute-start | bytes 786440 | tf_op jit(solution)/shard_map/ppermute | solution.py:370
  1.9 28.5 %collective-permute-start.8 = (bf16[2,2,256,256]{3,2,1,0:T(8,128)(2,1)S(1)}, bf16[2,2,256,256]{3,2,1,0:T(8,128)(2,1)S(1)}, u32[]{:S(2)}, u32[]{:S(2)}) collective-permute-start(bf16[2,2,256,256]{3,2,1,0:T(8,128)(2,1)S(1)} %copy-done), channel_id=1, source_target_pairs={{0,8},{8,0},{16,24},{24,16},{1,9},{9,1},{17,25},{25,17},{2,10},{10... | collective-permute-start | bytes 1572872 | tf_op jit(solution)/shard_map/ppermute | solution.py:362
  4.2 4.1 %collective-permute-start.1 = (bf16[128,256]{1,0:T(8,128)(2,1)S(1)}, bf16[128,256]{1,0:T(8,128)(2,1)S(1)}, u32[]{:S(2)}, u32[]{:S(2)}) collective-permute-start(bf16[128,256]{1,0:T(8,128)(2,1)S(1)} %get-tuple-element.26), channel_id=1, source_target_pairs={{0,3},{1,2},{2,1},{3,0},{4,7},{5,6},{6,5},{7,4},{8,11},{9,10},{10,... | collective-permute-start | bytes 196616 | tf_op jit(solution)/shard_map/ppermute | solution.py:344
  4.6 3.8 %collective-permute-start.2 = (bf16[128,256]{1,0:T(8,128)(2,1)S(1)}, bf16[128,256]{1,0:T(8,128)(2,1)S(1)}, u32[]{:S(2)}, u32[]{:S(2)}) collective-permute-start(bf16[128,256]{1,0:T(8,128)(2,1)S(1)} %get-tuple-element.27), channel_id=1, source_target_pairs={{0,5},{1,4},{2,7},{3,6},{4,1},{5,0},{6,3},{7,2},{8,13},{9,12},{10,... | collective-permute-start | bytes 196616 | tf_op jit(solution)/shard_map/ppermute | solution.py:344
  6.1 5.2 %collective-permute-start.3 = (bf16[128,256]{1,0:T(8,128)(2,1)S(1)}, bf16[128,256]{1,0:T(8,128)(2,1)S(1)}, u32[]{:S(2)}, u32[]{:S(2)}) collective-permute-start(bf16[128,256]{1,0:T(8,128)(2,1)S(1)} %get-tuple-element.28), channel_id=1, source_target_pairs={{0,6},{1,7},{2,4},{3,5},{4,2},{5,3},{6,0},{7,1},{8,14},{9,15},{10,... | collective-permute-start | bytes 196616 | tf_op jit(solution)/shard_map/ppermute | solution.py:344
  11.3 5.3 %collective-permute-start.4 = (bf16[80,256]{1,0:T(8,128)(2,1)S(1)}, bf16[80,256]{1,0:T(8,128)(2,1)S(1)}, u32[]{:S(2)}, u32[]{:S(2)}) collective-permute-start(bf16[80,256]{1,0:T(8,128)(2,1)S(1)} %get-tuple-element.30), channel_id=1, source_target_pairs={{0,9},{1,8},{2,11},{3,10},{4,13},{5,12},{6,15},{7,14},{8,1},{9,0},... | collective-permute-start | bytes 122888 | tf_op jit(solution)/shard_map/ppermute | solution.py:347
  16.6 5.3 %collective-permute-start.7 = (bf16[128,256]{1,0:T(8,128)(2,1)S(1)}, bf16[128,256]{1,0:T(8,128)(2,1)S(1)}, u32[]{:S(2)}, u32[]{:S(2)}) collective-permute-start(bf16[128,256]{1,0:T(8,128)(2,1)S(1)} %shard_map.51.mine_ref), channel_id=1, source_target_pairs={{0,6},{1,7},{2,4},{3,5},{4,2},{5,3},{6,0},{7,1},{8,14},{9,15},{10,... | collective-permute-start | bytes 196616 | tf_op jit(solution)/shard_map/ppermute | solution.py:349
  18.1 5.2 %collective-permute-start.6 = (bf16[128,256]{1,0:T(8,128)(2,1)S(1)}, bf16[128,256]{1,0:T(8,128)(2,1)S(1)}, u32[]{:S(2)}, u32[]{:S(2)}) collective-permute-start(bf16[128,256]{1,0:T(8,128)(2,1)S(1)} %shard_map.51.mine_ref), channel_id=1, source_target_pairs={{0,5},{1,4},{2,7},{3,6},{4,1},{5,0},{6,3},{7,2},{8,13},{9,12},{10,... | collective-permute-start | bytes 196616 | tf_op jit(solution)/shard_map/ppermute | solution.py:349
  18.3 5.0 %collective-permute-start.5 = (bf16[128,256]{1,0:T(8,128)(2,1)S(1)}, bf16[128,256]{1,0:T(8,128)(2,1)S(1)}, u32[]{:S(2)}, u32[]{:S(2)}) collective-permute-start(bf16[128,256]{1,0:T(8,128)(2,1)S(1)} %shard_map.51.mine_ref), channel_id=1, source_target_pairs={{0,3},{1,2},{2,1},{3,0},{4,7},{5,6},{6,5},{7,4},{8,11},{9,10},{10,... | collective-permute-start | bytes 196616 | tf_op jit(solution)/shard_map/ppermute | solution.py:349
  23.3 8.5 %collective-permute-start.11 = (bf16[512,256]{1,0:T(8,128)(2,1)S(1)}, bf16[512,256]{1,0:T(8,128)(2,1)S(1)}, u32[]{:S(2)}, u32[]{:S(2)}) collective-permute-start(bf16[512,256]{1,0:T(8,128)(2,1)S(1)} %shard_map.52.a_ref), channel_id=1, source_target_pairs={{0,1},{1,0},{2,3},{3,2},{4,5},{5,4},{6,7},{7,6},{8,9},{9,8},{10,11... | collective-permute-start | bytes 786440 | tf_op jit(solution)/shard_map/ppermute | solution.py:351
  23.7 5.0 %collective-permute-start.10 = (bf16[8,1024]{1,0:T(8,128)(2,1)S(1)}, bf16[8,1024]{1,0:T(8,128)(2,1)S(1)}, u32[]{:S(2)}, u32[]{:S(2)}) collective-permute-start(bf16[8,1024]{1,0:T(8,128)(2,1)S(1)} %shard_map.53), channel_id=1, source_target_pairs={{8,24},{24,8},{0,16},{16,0},{9,25},{25,9},{1,17},{17,1},{10,26},{2... | collective-permute-start | bytes 49160 | tf_op jit(solution)/shard_map/ppermute | solution.py:378
  24.1 6.3 %collective-permute-start.9 = (bf16[8,1024]{1,0:T(8,128)(2,1)S(1)}, bf16[8,1024]{1,0:T(8,128)(2,1)S(1)}, u32[]{:S(2)}, u32[]{:S(2)}) collective-permute-start(bf16[8,1024]{1,0:T(8,128)(2,1)S(1)} %shard_map.53), channel_id=1, source_target_pairs={{8,16},{16,8},{9,17},{17,9},{10,18},{18,10},{11,19},{19,11},{12,20... | collective-permute-start | bytes 49160 | tf_op jit(solution)/shard_map/ppermute | solution.py:377
  32.1 7.5 %collective-permute-start.12 = (bf16[256,256]{1,0:T(8,128)(2,1)S(1)}, bf16[256,256]{1,0:T(8,128)(2,1)S(1)}, u32[]{:S(2)}, u32[]{:S(2)}) collective-permute-start(bf16[256,256]{1,0:T(8,128)(2,1)S(1)} %get-tuple-element.34), channel_id=1, source_target_pairs={{0,24},{8,16},{16,8},{24,0},{1,25},{9,17},{17,9},{25,1},{2,26},{10... | collective-permute-start | bytes 393224 | tf_op jit(solution)/shard_map/ppermute | solution.py:393

commit v12 on v11

--- a/solution.py
+++ b/solution.py
@@ -244,30 +244,33 @@
 
 
 def join_body(mine_ref, *refs):
-    out_ref = refs[-1]
-    pieces = (mine_ref,) + refs[:-1]
+    away_ref, stay_ref = refs[-2:]
+    pieces = (mine_ref,) + refs[:-2]
     chips = len(pieces)
-    groups = 2 * lax.axis_size("row")
-    size = mine_ref.shape[0] // groups
+    blocks = lax.axis_size("row")
+    size = mine_ref.shape[0] // (2 * blocks)
     chip = lax.div(lax.axis_index("col"), 2)
     for step, ref in enumerate(pieces):
         source = xor(chip, step)
-        for n in range(groups):
-            lo = n * chips * size + source * size
-            out_ref[part(lo, size), :] = ref[n * size:(n + 1) * size]
-
-
-def predict(freq, a_ref, k_ref, targets):
+        for n in range(2 * blocks):
+            block, inner = divmod(n, blocks)
+            if inner < 2:
+                out_ref, lo = stay_ref, block * 2 + inner
+            else:
+                out_ref, lo = away_ref, block * (blocks - 2) + inner - 2
+            out_ref[part(lo * chips * size + source * size, size), :] = ref[n * size:(n + 1) * size]
+
+
+def predict(freq, a_ref, k_ref, targets, kind):
     half = a_ref.shape[0] // 2
     width = a_ref.shape[1]
-    size = targets[0].shape[0] // 2
+    size = half // (2 * len(targets))
     total = []
     for c in range(2):
         value = dot_nn(a_ref[:half], k_ref[freq, c, :width])
         total.append(value + dot_nn(a_ref[half:], k_ref[freq, c, width:]))
     by_real, by_imag = total
     for slot, ref in enumerate(targets):
-        kind = F32 if slot == 0 else BF
         lo = 2 * slot * size
         mid = lo + size
         hi = mid + size
@@ -275,18 +278,23 @@
         ref[size:] = (by_real[mid:hi] + by_imag[lo:mid]).astype(kind)
 
 
-def predict_own_body(a_ref, k_ref, *outs):
-    predict(parity(), a_ref, k_ref, outs)
-
-
-def predict_other_body(peers, a_ref, k_ref, *refs):
-    owns, keep_ref, sends = refs[:peers], refs[peers], refs[peers + 1:]
-    size = keep_ref.shape[0]
+def predict_own_body(away_ref, stay_ref, k_ref, keep_ref, *owns):
+    predict(parity(), away_ref, k_ref, owns, BF)
+    predict(parity(), stay_ref, k_ref, (keep_ref,), F32)
+
+
+def predict_away_body(peers, away_ref, k_ref, *refs):
+    owns, sends = refs[:peers], refs[peers:]
+    size = owns[0].shape[0]
     freq = parity()
     for own, send in zip(owns, sends):
         send[part(freq * size, size), :] = own[...]
     rest = part((1 - freq) * size, size)
-    predict(1 - freq, a_ref, k_ref, (keep_ref,) + tuple(send.at[rest] for send in sends))
+    predict(1 - freq, away_ref, k_ref, tuple(send.at[rest] for send in sends), BF)
+
+
+def predict_stay_body(stay_ref, k_ref, keep_ref):
+    predict(1 - parity(), stay_ref, k_ref, (keep_ref,), F32)
 
 
 def final_body(x_ref, noise_ref, own_ref, other_ref, *refs):
@@ -332,11 +340,12 @@
     fields = []
     for freq in (a, 1 - a):
         mate = lax.dynamic_slice_in_dim(give, freq * (rows // 2), rows // 2, 0)
-        fields.append(jnp.concatenate([chosen(freq, 0), mate], axis=0))
+        field = jnp.stack([chosen(freq, 0), mate]).reshape(2, blocks // 2, -1, width)
+        fields.append((field[:, 1:].reshape(-1, width), field[:, 0].reshape(-1, width)))
     return (*fields, give)
 
 
-def chip_sum(own, got, coef, chips):
+def chip_sum(own, got, coef, blocks, chips):
     rows, width = own.shape
     size = rows // chips
     keep, *sends = call(split_body, (own, got), [((size, width), F32)] + [((size, width), BF)] * (chips - 1))
@@ -347,8 +356,10 @@
     give = lax.ppermute(give, ("row", "col"), mate_perm())
     mine = call(pack_body, (stay, give, fence), [((size, width), BF)])[0]
     got = [lax.ppermute(mine, "col", pair_perm("col", hop(d + 1))) for d in range(chips - 1)]
-    mine = call(join_body, (mine, *got), [((rows, width), BF)])[0]
-    return mine, lax.ppermute(mine, "col", pair_perm("col", 1)), give
+    stay = 4 * rows // (2 * blocks)
+    mine = call(join_body, (mine, *got), [((rows - stay, width), BF), ((stay, width), BF)])
+    other = [lax.ppermute(v, "col", pair_perm("col", 1)) for v in mine]
+    return mine, other, give
 
 
 def apply(kernel, probes, noise_var, prior_diag):
@@ -379,18 +390,17 @@
     if chips > 4:
         mine, other, give = wide_sum(own, got, coef, blocks)
     else:
-        mine, other, give = chip_sum(own, got, coef, chips)
+        mine, other, give = chip_sum(own, got, coef, blocks, chips)
     operator = call(operator_body, (kernel, mate, coef, give, near, far), [((2, 2, 2 * width, rows), BF)])[0]
     size = count // blocks
     peers = blocks // 2 - 1
     half = (2 * size, rows)
-    keep_own, *owns = call(predict_own_body, (mine, operator), [(half, F32)] + [(half, BF)] * peers)
-    keep_other, *sends = call(
-        functools.partial(predict_other_body, peers),
-        (other, operator, *owns),
-        [(half, F32)] + [((4 * size, rows), BF)] * peers,
+    keep_own, *owns = call(predict_own_body, (*mine, operator), [(half, F32)] + [(half, BF)] * peers)
+    sends = call(
+        functools.partial(predict_away_body, peers), (other[0], operator, *owns), [((4 * size, rows), BF)] * peers
     )
     got = [lax.ppermute(v, "row", pair_perm("row", cross(d + 1))) for d, v in enumerate(sends)]
+    keep_other = call(predict_stay_body, (other[1], operator), [(half, F32)])[0]
     return call(
         final_body,
         (x, noise, keep_own, keep_other, *got),

time: 40.6 us -> 40.5 us (level)
  the two profiles are of different devices: /device:TPU:18 before, /device:TPU:20 now
where the time goes in v12:
time: 40.5 us; the launch traced here: 40.3 us
  waiting for transfers between devices  18.4 us (45%)
  starting transfers between devices  16.4 us (40%)
  Pallas kernels  4.79 us (12%)
  local copies, waits for them, and re-layouts  0.71 us (2%)
    ppermute x1, waiting for transfers between devices, apply(): lax.ppermute(v, 'row', pair_perm('row', cross(d + 1)))  5.07 us
    pallas_call x13, Pallas kernels, call(): pl.pallas_call(body, in_specs=[HBM] * len(raw) + [VMEM] * len(ins), out_s...  4.79 us
    ppermute x1, starting transfers between devices, apply(): near = lax.ppermute(seam, 'row', near)  4.59 us
    ppermute x1, waiting for transfers between devices, chip_sum(): give = lax.ppermute(give, ('row', 'col'), mate_perm())  4.55 us
    ppermute x3, waiting for transfers between devices, chip_sum(): lax.ppermute(v, 'col', pair_perm('col', hop(d + 1)))  3.67 us
    ppermute x3, waiting for transfers between devices, chip_sum(): lax.ppermute(mine, 'col', pair_perm('col', hop(d + 1)))  3.44 us
    ppermute x3, starting transfers between devices, chip_sum(): lax.ppermute(v, 'col', pair_perm('col', hop(d + 1)))  3.27 us
    ppermute x3, starting transfers between devices, chip_sum(): lax.ppermute(mine, 'col', pair_perm('col', hop(d + 1)))  3.21 us
  transfers between devices with their start and end apart: 14, of which 8 were waited for; matrix products, arithmetic and copies ran while one was open for 0% of the time, Pallas kernels for 7%

profile of v12, /device:TPU:20, one launch (start us, length us, event | category | flops | bytes accessed | tf_op | source)
XLA Modules:
  0.0 40.3 jit_solution(15968865288164372064)
XLA Ops:
  0.0 0.0 copy-start
  0.0 1.8 %shard_map.46 = (bf16[512,256]{1,0:T(8,128)(2,1)S(1)}, bf16[1024,256]{1,0:T(8,128)(2,1)S(1)}, bf16[2,2,256,256]{3,2,1,0:T(8,128)(2,1)S(1)}, f32[1,256]{1,0:T(1,128)S(1)}, f32[2,256]{1,0:T(2,128)S(1)}) custom-call(bf16[256,2,2,256]{3,2,1,0:T(2,128)(2,1)} %v_hbm.1, bf16[2,2,256,256]{3,2,1,0:T(8,128)(2,1)} %k_hbm.1, f32[1,256]{1,0:T(1,128)} %bitcast.1, ...), custom_call_target="tpu_custom_call" | custom-call | tf_op jit(solution)/shard_map/pallas_call | solution.py:20
  1.8 0.1 collective-permute-start
  1.9 0.0 copy-done
  1.9 1.6 %collective-permute-start.8 = (bf16[2,2,256,256]{3,2,1,0:T(8,128)(2,1)S(1)}, bf16[2,2,256,256]{3,2,1,0:T(8,128)(2,1)S(1)}, u32[]{:S(2)}, u32[]{:S(2)}) collective-permute-start(bf16[2,2,256,256]{3,2,1,0:T(8,128)(2,1)S(1)} %copy-done), channel_id=1, source_target_pairs={{0,8},{8,0},{16,24},{24,16},{1,9},{9,1},{17,25},{25,17},{2,10},{10... | collective-permute-start | bytes 1572872 | tf_op jit(solution)/shard_map/ppermute | solution.py:373
  3.6 0.6 %shard_map.47.own_ref = f32[512,256]{1,0:T(8,128)S(1)} custom-call(bf16[1024,256]{1,0:T(8,128)(2,1)S(1)} %get-tuple-element.20.x_ref, bf16[2,2,256,256]{3,2,1,0:T(8,128)(2,1)S(1)} %get-tuple-element.22.k_ref), custom_call_target="tpu_custom_call" | custom-call | tf_op jit(solution)/shard_map/pallas_call | solution.py:20
  4.1 0.0 collective-permute-done.got_ref
  4.2 0.1 shard_map.48
  4.2 1.3 %collective-permute-start.1 = (bf16[128,256]{1,0:T(8,128)(2,1)S(1)}, bf16[128,256]{1,0:T(8,128)(2,1)S(1)}, u32[]{:S(2)}, u32[]{:S(2)}) collective-permute-start(bf16[128,256]{1,0:T(8,128)(2,1)S(1)} %get-tuple-element.26), channel_id=1, source_target_pairs={{0,3},{1,2},{2,1},{3,0},{4,7},{5,6},{6,5},{7,4},{8,11},{9,10},{10,... | collective-permute-start | bytes 196616 | tf_op jit(solution)/shard_map/ppermute | solution.py:353
  5.5 0.5 %collective-permute-start.2 = (bf16[128,256]{1,0:T(8,128)(2,1)S(1)}, bf16[128,256]{1,0:T(8,128)(2,1)S(1)}, u32[]{:S(2)}, u32[]{:S(2)}) collective-permute-start(bf16[128,256]{1,0:T(8,128)(2,1)S(1)} %get-tuple-element.27), channel_id=1, source_target_pairs={{0,5},{1,4},{2,7},{3,6},{4,1},{5,0},{6,3},{7,2},{8,13},{9,12},{10,... | collective-permute-start | bytes 196616 | tf_op jit(solution)/shard_map/ppermute | solution.py:353
  6.0 1.5 %collective-permute-start.3 = (bf16[128,256]{1,0:T(8,128)(2,1)S(1)}, bf16[128,256]{1,0:T(8,128)(2,1)S(1)}, u32[]{:S(2)}, u32[]{:S(2)}) collective-permute-start(bf16[128,256]{1,0:T(8,128)(2,1)S(1)} %get-tuple-element.28), channel_id=1, source_target_pairs={{0,6},{1,7},{2,4},{3,5},{4,2},{5,3},{6,0},{7,1},{8,14},{9,15},{10,... | collective-permute-start | bytes 196616 | tf_op jit(solution)/shard_map/ppermute | solution.py:353
  7.5 0.9 %collective-permute-done.1.refs_0_ = bf16[128,256]{1,0:T(8,128)(2,1)S(1)} collective-permute-done((bf16[128,256]{1,0:T(8,128)(2,1)S(1)}, bf16[128,256]{1,0:T(8,128)(2,1)S(1)}, u32[]{:S(2)}, u32[]{:S(2)}) %collective-permute-start.1) | collective-permute-done | bytes 65568 | tf_op jit(solution)/shard_map/ppermute | solution.py:353
  8.4 1.0 %collective-permute-done.2.refs_1_ = bf16[128,256]{1,0:T(8,128)(2,1)S(1)} collective-permute-done((bf16[128,256]{1,0:T(8,128)(2,1)S(1)}, bf16[128,256]{1,0:T(8,128)(2,1)S(1)}, u32[]{:S(2)}, u32[]{:S(2)}) %collective-permute-start.2) | collective-permute-done | bytes 65568 | tf_op jit(solution)/shard_map/ppermute | solution.py:353
  9.4 1.8 %collective-permute-done.3.refs_2_ = bf16[128,256]{1,0:T(8,128)(2,1)S(1)} collective-permute-done((bf16[128,256]{1,0:T(8,128)(2,1)S(1)}, bf16[128,256]{1,0:T(8,128)(2,1)S(1)}, u32[]{:S(2)}, u32[]{:S(2)}) %collective-permute-start.3) | collective-permute-done | bytes 65568 | tf_op jit(solution)/shard_map/ppermute | solution.py:353
  11.2 0.1 shard_map.50
  11.2 0.8 %collective-permute-start.4 = (bf16[80,256]{1,0:T(8,128)(2,1)S(1)}, bf16[80,256]{1,0:T(8,128)(2,1)S(1)}, u32[]{:S(2)}, u32[]{:S(2)}) collective-permute-start(bf16[80,256]{1,0:T(8,128)(2,1)S(1)} %get-tuple-element.30), channel_id=1, source_target_pairs={{0,9},{1,8},{2,11},{3,10},{4,13},{5,12},{6,15},{7,14},{8,1},{9,0},... | collective-permute-start | bytes 122888 | tf_op jit(solution)/shard_map/ppermute | solution.py:356
  12.0 4.6 %collective-permute-done.4.got_ref = bf16[80,256]{1,0:T(8,128)(2,1)S(1)} collective-permute-done((bf16[80,256]{1,0:T(8,128)(2,1)S(1)}, bf16[80,256]{1,0:T(8,128)(2,1)S(1)}, u32[]{:S(2)}, u32[]{:S(2)}) %collective-permute-start.4) | collective-permute-done | bytes 40992 | tf_op jit(solution)/shard_map/ppermute | solution.py:356
  16.6 1.4 %collective-permute-start.7 = (bf16[128,256]{1,0:T(8,128)(2,1)S(1)}, bf16[128,256]{1,0:T(8,128)(2,1)S(1)}, u32[]{:S(2)}, u32[]{:S(2)}) collective-permute-start(bf16[128,256]{1,0:T(8,128)(2,1)S(1)} %shard_map.51.mine_ref), channel_id=1, source_target_pairs={{0,6},{1,7},{2,4},{3,5},{4,2},{5,3},{6,0},{7,1},{8,14},{9,15},{10,... | collective-permute-start | bytes 196616 | tf_op jit(solution)/shard_map/ppermute | solution.py:358
  18.0 1.2 %collective-permute-start.6 = (bf16[128,256]{1,0:T(8,128)(2,1)S(1)}, bf16[128,256]{1,0:T(8,128)(2,1)S(1)}, u32[]{:S(2)}, u32[]{:S(2)}) collective-permute-start(bf16[128,256]{1,0:T(8,128)(2,1)S(1)} %shard_map.51.mine_ref), channel_id=1, source_target_pairs={{0,5},{1,4},{2,7},{3,6},{4,1},{5,0},{6,3},{7,2},{8,13},{9,12},{10,... | collective-permute-start | bytes 196616 | tf_op jit(solution)/shard_map/ppermute | solution.py:358
  19.2 0.6 %collective-permute-start.5 = (bf16[128,256]{1,0:T(8,128)(2,1)S(1)}, bf16[128,256]{1,0:T(8,128)(2,1)S(1)}, u32[]{:S(2)}, u32[]{:S(2)}) collective-permute-start(bf16[128,256]{1,0:T(8,128)(2,1)S(1)} %shard_map.51.mine_ref), channel_id=1, source_target_pairs={{0,3},{1,2},{2,1},{3,0},{4,7},{5,6},{6,5},{7,4},{8,11},{9,10},{10,... | collective-permute-start | bytes 196616 | tf_op jit(solution)/shard_map/ppermute | solution.py:358
  19.8 2.1 %collective-permute-done.7.refs_2_ = bf16[128,256]{1,0:T(8,128)(2,1)S(1)} collective-permute-done((bf16[128,256]{1,0:T(8,128)(2,1)S(1)}, bf16[128,256]{1,0:T(8,128)(2,1)S(1)}, u32[]{:S(2)}, u32[]{:S(2)}) %collective-permute-start.7) | collective-permute-done | bytes 65568 | tf_op jit(solution)/shard_map/ppermute | solution.py:358
  21.9 1.3 %collective-permute-done.6.refs_1_ = bf16[128,256]{1,0:T(8,128)(2,1)S(1)} collective-permute-done((bf16[128,256]{1,0:T(8,128)(2,1)S(1)}, bf16[128,256]{1,0:T(8,128)(2,1)S(1)}, u32[]{:S(2)}, u32[]{:S(2)}) %collective-permute-start.6) | collective-permute-done | bytes 65568 | tf_op jit(solution)/shard_map/ppermute | solution.py:358
  23.2 0.0 collective-permute-done.5.refs_0_
  23.3 0.3 collective-permute-start.12
  23.5 0.2 shard_map.53
  23.8 0.4 collective-permute-start.10
  24.2 4.6 %collective-permute-start.9 = (bf16[8,1024]{1,0:T(8,128)(2,1)S(1)}, bf16[8,1024]{1,0:T(8,128)(2,1)S(1)}, u32[]{:S(2)}, u32[]{:S(2)}) collective-permute-start(bf16[8,1024]{1,0:T(8,128)(2,1)S(1)} %shard_map.53), channel_id=1, source_target_pairs={{8,16},{16,8},{9,17},{17,9},{10,18},{18,10},{11,19},{19,11},{12,20... | collective-permute-start | bytes 49160 | tf_op jit(solution)/shard_map/ppermute | solution.py:388
  28.8 0.1 collective-permute-start.11
  28.8 0.0 collective-permute-done.10.far_ref
  28.9 1.6 %collective-permute-done.9.near_ref = bf16[8,1024]{1,0:T(8,128)(2,1)S(1)} collective-permute-done((bf16[8,1024]{1,0:T(8,128)(2,1)S(1)}, bf16[8,1024]{1,0:T(8,128)(2,1)S(1)}, u32[]{:S(2)}, u32[]{:S(2)}) %collective-permute-start.9) | collective-permute-done | bytes 16416 | tf_op jit(solution)/shard_map/ppermute | solution.py:388
  30.5 0.0 collective-permute-done.8.mate_ref
  30.5 1.0 %shard_map.54.k_ref = bf16[2,2,512,256]{3,2,1,0:T(8,128)(2,1)S(1)} custom-call(bf16[2,2,256,256]{3,2,1,0:T(8,128)(2,1)S(1)} %get-tuple-element.22.k_ref, bf16[2,2,256,256]{3,2,1,0:T(8,128)(2,1)S(1)} %collective-permute-done.8.mate_ref, f32[1,256]{1,0:T(1,128)S(1)} %get-tuple-element.25.d_ref, bf16[80,256]{1,0:T(8,128)(2,1)S(1)} %collective-permute-done.4.got_ref, ...), custom_call_target="tpu_custom_call" | custom-call | tf_op jit(solution)/shard_map/pallas_call | solution.py:20
  31.5 0.3 shard_map.55
  31.8 0.0 collective-permute-done.12.away_ref
  31.9 0.2 shard_map.57
  32.1 2.1 %collective-permute-start.13 = (bf16[256,256]{1,0:T(8,128)(2,1)S(1)}, bf16[256,256]{1,0:T(8,128)(2,1)S(1)}, u32[]{:S(2)}, u32[]{:S(2)}) collective-permute-start(bf16[256,256]{1,0:T(8,128)(2,1)S(1)} %shard_map.57), channel_id=1, source_target_pairs={{0,24},{8,16},{16,8},{24,0},{1,25},{9,17},{17,9},{25,1},{2,26},{10... | collective-permute-start | bytes 393224 | tf_op jit(solution)/shard_map/ppermute | solution.py:402
  34.2 0.0 collective-permute-done.11.stay_ref
  34.2 0.2 shard_map.56.other_ref
  34.4 5.1 %collective-permute-done.13.refs_0_ = bf16[256,256]{1,0:T(8,128)(2,1)S(1)} collective-permute-done((bf16[256,256]{1,0:T(8,128)(2,1)S(1)}, bf16[256,256]{1,0:T(8,128)(2,1)S(1)}, u32[]{:S(2)}, u32[]{:S(2)}) %collective-permute-start.13) | collective-permute-done | bytes 131104 | tf_op jit(solution)/shard_map/ppermute | solution.py:402
  39.5 0.1 shard_map.58
  39.6 0.7 %copy.5 = f32[64,2,2,256]{3,2,1,0:T(2,128)} copy(f32[64,2,2,256]{3,2,1,0:T(2,128)S(1)} %shard_map.58) | data formatting | bytes 524288
  (3 shorter events, 0.0 us)
Async XLA Ops:
  0.0 1.9 %copy-start = (bf16[2,2,256,256]{3,2,1,0:T(8,128)(2,1)S(1)}, bf16[2,2,256,256]{3,2,1,0:T(8,128)(2,1)}, u32[]{:S(2)}) copy-start(bf16[2,2,256,256]{3,2,1,0:T(8,128)(2,1)} %k_hbm.1) | copy-start | bytes 1572868
  1.8 2.3 %collective-permute-start = (bf16[512,256]{1,0:T(8,128)(2,1)S(1)}, bf16[512,256]{1,0:T(8,128)(2,1)S(1)}, u32[]{:S(2)}, u32[]{:S(2)}) collective-permute-start(bf16[512,256]{1,0:T(8,128)(2,1)S(1)} %get-tuple-element.23), channel_id=1, source_target_pairs={{0,1},{1,0},{2,3},{3,2},{4,5},{5,4},{6,7},{7,6},{8,9},{9,8},{10,11... | collective-permute-start | bytes 786440 | tf_op jit(solution)/shard_map/ppermute | solution.py:381
  1.9 28.5 %collective-permute-start.8 = (bf16[2,2,256,256]{3,2,1,0:T(8,128)(2,1)S(1)}, bf16[2,2,256,256]{3,2,1,0:T(8,128)(2,1)S(1)}, u32[]{:S(2)}, u32[]{:S(2)}) collective-permute-start(bf16[2,2,256,256]{3,2,1,0:T(8,128)(2,1)S(1)} %copy-done), channel_id=1, source_target_pairs={{0,8},{8,0},{16,24},{24,16},{1,9},{9,1},{17,25},{25,17},{2,10},{10... | collective-permute-start | bytes 1572872 | tf_op jit(solution)/shard_map/ppermute | solution.py:373
  4.2 4.1 %collective-permute-start.1 = (bf16[128,256]{1,0:T(8,128)(2,1)S(1)}, bf16[128,256]{1,0:T(8,128)(2,1)S(1)}, u32[]{:S(2)}, u32[]{:S(2)}) collective-permute-start(bf16[128,256]{1,0:T(8,128)(2,1)S(1)} %get-tuple-element.26), channel_id=1, source_target_pairs={{0,3},{1,2},{2,1},{3,0},{4,7},{5,6},{6,5},{7,4},{8,11},{9,10},{10,... | collective-permute-start | bytes 196616 | tf_op jit(solution)/shard_map/ppermute | solution.py:353
  5.5 3.8 %collective-permute-start.2 = (bf16[128,256]{1,0:T(8,128)(2,1)S(1)}, bf16[128,256]{1,0:T(8,128)(2,1)S(1)}, u32[]{:S(2)}, u32[]{:S(2)}) collective-permute-start(bf16[128,256]{1,0:T(8,128)(2,1)S(1)} %get-tuple-element.27), channel_id=1, source_target_pairs={{0,5},{1,4},{2,7},{3,6},{4,1},{5,0},{6,3},{7,2},{8,13},{9,12},{10,... | collective-permute-start | bytes 196616 | tf_op jit(solution)/shard_map/ppermute | solution.py:353
  6.0 5.2 %collective-permute-start.3 = (bf16[128,256]{1,0:T(8,128)(2,1)S(1)}, bf16[128,256]{1,0:T(8,128)(2,1)S(1)}, u32[]{:S(2)}, u32[]{:S(2)}) collective-permute-start(bf16[128,256]{1,0:T(8,128)(2,1)S(1)} %get-tuple-element.28), channel_id=1, source_target_pairs={{0,6},{1,7},{2,4},{3,5},{4,2},{5,3},{6,0},{7,1},{8,14},{9,15},{10,... | collective-permute-start | bytes 196616 | tf_op jit(solution)/shard_map/ppermute | solution.py:353
  11.2 5.3 %collective-permute-start.4 = (bf16[80,256]{1,0:T(8,128)(2,1)S(1)}, bf16[80,256]{1,0:T(8,128)(2,1)S(1)}, u32[]{:S(2)}, u32[]{:S(2)}) collective-permute-start(bf16[80,256]{1,0:T(8,128)(2,1)S(1)} %get-tuple-element.30), channel_id=1, source_target_pairs={{0,9},{1,8},{2,11},{3,10},{4,13},{5,12},{6,15},{7,14},{8,1},{9,0},... | collective-permute-start | bytes 122888 | tf_op jit(solution)/shard_map/ppermute | solution.py:356
  16.6 5.4 %collective-permute-start.7 = (bf16[128,256]{1,0:T(8,128)(2,1)S(1)}, bf16[128,256]{1,0:T(8,128)(2,1)S(1)}, u32[]{:S(2)}, u32[]{:S(2)}) collective-permute-start(bf16[128,256]{1,0:T(8,128)(2,1)S(1)} %shard_map.51.mine_ref), channel_id=1, source_target_pairs={{0,6},{1,7},{2,4},{3,5},{4,2},{5,3},{6,0},{7,1},{8,14},{9,15},{10,... | collective-permute-start | bytes 196616 | tf_op jit(solution)/shard_map/ppermute | solution.py:358
  18.0 5.2 %collective-permute-start.6 = (bf16[128,256]{1,0:T(8,128)(2,1)S(1)}, bf16[128,256]{1,0:T(8,128)(2,1)S(1)}, u32[]{:S(2)}, u32[]{:S(2)}) collective-permute-start(bf16[128,256]{1,0:T(8,128)(2,1)S(1)} %shard_map.51.mine_ref), channel_id=1, source_target_pairs={{0,5},{1,4},{2,7},{3,6},{4,1},{5,0},{6,3},{7,2},{8,13},{9,12},{10,... | collective-permute-start | bytes 196616 | tf_op jit(solution)/shard_map/ppermute | solution.py:358
  19.2 4.0 %collective-permute-start.5 = (bf16[128,256]{1,0:T(8,128)(2,1)S(1)}, bf16[128,256]{1,0:T(8,128)(2,1)S(1)}, u32[]{:S(2)}, u32[]{:S(2)}) collective-permute-start(bf16[128,256]{1,0:T(8,128)(2,1)S(1)} %shard_map.51.mine_ref), channel_id=1, source_target_pairs={{0,3},{1,2},{2,1},{3,0},{4,7},{5,6},{6,5},{7,4},{8,11},{9,10},{10,... | collective-permute-start | bytes 196616 | tf_op jit(solution)/shard_map/ppermute | solution.py:358
  23.3 8.6 %collective-permute-start.12 = (bf16[256,256]{1,0:T(8,128)(2,1)S(1)}, bf16[256,256]{1,0:T(8,128)(2,1)S(1)}, u32[]{:S(2)}, u32[]{:S(2)}) collective-permute-start(bf16[256,256]{1,0:T(8,128)(2,1)S(1)} %get-tuple-element.31.away_ref), channel_id=1, source_target_pairs={{0,1},{1,0},{2,3},{3,2},{4,5},{5,4},{6,7},{7,6},{8,9},{9,8},{10,11... | collective-permute-start | bytes 393224 | tf_op jit(solution)/shard_map/ppermute | solution.py:361
  23.8 5.1 %collective-permute-start.10 = (bf16[8,1024]{1,0:T(8,128)(2,1)S(1)}, bf16[8,1024]{1,0:T(8,128)(2,1)S(1)}, u32[]{:S(2)}, u32[]{:S(2)}) collective-permute-start(bf16[8,1024]{1,0:T(8,128)(2,1)S(1)} %shard_map.53), channel_id=1, source_target_pairs={{8,24},{24,8},{0,16},{16,0},{9,25},{25,9},{1,17},{17,1},{10,26},{2... | collective-permute-start | bytes 49160 | tf_op jit(solution)/shard_map/ppermute | solution.py:389
  24.2 6.3 %collective-permute-start.9 = (bf16[8,1024]{1,0:T(8,128)(2,1)S(1)}, bf16[8,1024]{1,0:T(8,128)(2,1)S(1)}, u32[]{:S(2)}, u32[]{:S(2)}) collective-permute-start(bf16[8,1024]{1,0:T(8,128)(2,1)S(1)} %shard_map.53), channel_id=1, source_target_pairs={{8,16},{16,8},{9,17},{17,9},{10,18},{18,10},{11,19},{19,11},{12,20... | collective-permute-start | bytes 49160 | tf_op jit(solution)/shard_map/ppermute | solution.py:388
  28.8 5.4 %collective-permute-start.11 = (bf16[256,256]{1,0:T(8,128)(2,1)S(1)}, bf16[256,256]{1,0:T(8,128)(2,1)S(1)}, u32[]{:S(2)}, u32[]{:S(2)}) collective-permute-start(bf16[256,256]{1,0:T(8,128)(2,1)S(1)} %get-tuple-element.32.stay_ref), channel_id=1, source_target_pairs={{0,1},{1,0},{2,3},{3,2},{4,5},{5,4},{6,7},{7,6},{8,9},{9,8},{10,11... | collective-permute-start | bytes 393224 | tf_op jit(solution)/shard_map/ppermute | solution.py:361
  32.1 7.4 %collective-permute-start.13 = (bf16[256,256]{1,0:T(8,128)(2,1)S(1)}, bf16[256,256]{1,0:T(8,128)(2,1)S(1)}, u32[]{:S(2)}, u32[]{:S(2)}) collective-permute-start(bf16[256,256]{1,0:T(8,128)(2,1)S(1)} %shard_map.57), channel_id=1, source_target_pairs={{0,24},{8,16},{16,8},{24,0},{1,25},{9,17},{17,9},{25,1},{2,26},{10... | collective-permute-start | bytes 393224 | tf_op jit(solution)/shard_map/ppermute | solution.py:402

commit v13 on v12

--- a/solution.py
+++ b/solution.py
@@ -75,61 +75,64 @@
     return pieces
 
 
-def adjoint(freq, x, k_ref, o_ref, u_ref):
-    rows = x.shape[0] // 4
-    width = k_ref.shape[3]
-    tiles = width // LANES
+def adjoint(freq, v_ref, k_ref, o_ref, u_ref):
+    rows = v_ref.shape[0]
+    tiles = u_ref.shape[0] // 2
+    x = v_ref[:, freq].reshape(2 * rows, v_ref.shape[3])
     for c in range(2):
-        y = dot_nn(x, k_ref[freq, c])
+        y = dot_nn(x, k_ref[c])
         for t in range(tiles):
             u_ref[c * tiles + t] = y[:, t * LANES:(t + 1) * LANES]
-    real = pl.ds(2 * freq, rows, stride=4)
-    imag = pl.ds(2 * freq + 1, rows, stride=4)
+    real = pl.ds(0, rows, stride=2)
+    imag = pl.ds(1, rows, stride=2)
     for t in range(tiles):
         at = slice(t * LANES, (t + 1) * LANES)
         o_ref[:rows, at] = (u_ref[t, real, :] + u_ref[tiles + t, imag, :]).astype(o_ref.dtype)
         o_ref[rows:, at] = (u_ref[t, imag, :] - u_ref[tiles + t, real, :]).astype(o_ref.dtype)
 
 
-def adjoint_other_body(v_hbm, k_hbm, d_hbm, n_hbm, o_ref, x_ref, k_ref, d_ref, n_ref, v_ref, u_ref, sems):
+def adjoint_other_body(v_hbm, k_hbm, d_hbm, n_hbm, o_ref, v_ref, mine_ref, other_ref, d_ref, n_ref, u_ref, sems):
     freq = 1 - parity()
-    copies = [
-        pltpu.make_async_copy(v_hbm, v_ref, sems.at[0]),
-        pltpu.make_async_copy(k_hbm.at[freq], k_ref.at[freq], sems.at[1]),
-        pltpu.make_async_copy(k_hbm.at[1 - freq], k_ref.at[1 - freq], sems.at[2]),
-        pltpu.make_async_copy(d_hbm, d_ref, sems.at[3]),
-        pltpu.make_async_copy(n_hbm, n_ref, sems.at[4]),
-    ]
+    pairs = (
+        (v_hbm, v_ref),
+        (k_hbm.at[freq], other_ref),
+        (k_hbm.at[1 - freq], mine_ref),
+        (d_hbm, d_ref),
+        (n_hbm, n_ref),
+    )
+    copies = [pltpu.make_async_copy(*pair, sems.at[n]) for n, pair in enumerate(pairs)]
     for copy in copies:
         copy.start()
     copies[0].wait()
-    x = v_ref[...].reshape(x_ref.shape)
-    x_ref[...] = x
     copies[1].wait()
-    adjoint(freq, x, k_ref, o_ref, u_ref)
+    adjoint(freq, v_ref, other_ref, o_ref, u_ref)
     for copy in copies[2:]:
         copy.wait()
 
 
-def adjoint_own_body(x_ref, k_ref, o_ref, u_ref):
-    adjoint(parity(), x_ref[...], k_ref, o_ref, u_ref)
-
-
-def seam_body(k_ref, d_ref, o_ref):
-    freqs, _, rows, width = k_ref.shape
+def adjoint_own_body(v_ref, k_ref, o_ref, u_ref):
+    adjoint(parity(), v_ref, k_ref, o_ref, u_ref)
+
+
+def lanes_of(freq, c, rows):
+    return part((freq * 2 + c) * rows, rows)
+
+
+def seam_body(mine_ref, other_ref, d_ref, o_ref):
+    _, rows, width = mine_ref.shape
     odd = lax.rem(lax.axis_index("row"), 2)
     at = lax.broadcasted_iota(jnp.int32, (8, width), 0)
     place = lax.broadcasted_iota(jnp.int32, (8, width), 1)
     pick = jnp.where((at < 2) & (place == at + odd * (width - 2)), 1.0, 0.0).astype(BF)
-    for f in range(freqs):
-        for c in range(2):
-            lo = (f * 2 + c) * rows
-            o_ref[:, lo:lo + rows] = dot_nt(pick, k_ref[f, c]).astype(BF)
     coef = d_ref[...]
     spot = lax.broadcasted_iota(jnp.int32, coef.shape, 1)
     edge = jnp.sum(jnp.where(spot == odd * (width - 1), coef, 0.0), axis=1, keepdims=True)
-    for n, piece in enumerate(three(edge)):
-        o_ref[2 + n:3 + n, :] = jnp.broadcast_to(piece, (1, o_ref.shape[1]))
+    lines = [jnp.zeros((2, rows), F32)]
+    lines += [jnp.broadcast_to(piece.astype(F32), (1, rows)) for piece in three(edge)]
+    lines = jnp.concatenate(lines + [jnp.zeros((3, rows), F32)], axis=0)
+    for freq, ref in ((parity(), mine_ref), (1 - parity(), other_ref)):
+        for c in range(2):
+            o_ref[:, lanes_of(freq, c, rows)] = (dot_nt(pick, ref[c]) + lines).astype(BF)
 
 
 def fence_body(d_ref, o_ref):
@@ -151,8 +154,9 @@
     return upper, (matrix - upper.astype(F32)).astype(BF)
 
 
-def operator_body(k_ref, mate_ref, d_ref, got_ref, near_ref, far_ref, o_ref):
-    freqs, _, rows, width = k_ref.shape
+def operator_body(swap, k_ref, mate_ref, d_ref, got_ref, near_ref, far_ref, o_ref):
+    _, rows, width = k_ref.shape
+    freq = 1 - parity() if swap else parity()
     me = lax.axis_index("row")
     odd = lax.rem(me, 2)
     is_odd = odd == 1
@@ -167,42 +171,38 @@
     def last_or_first(value, last):
         return jnp.where(last, value[:, width - 1:], value[:, :1])
 
-    def outer(ref, block):
+    def outer(ref, block, c):
         last = lax.axis_size("row") - 1
         there = jnp.where(lax.rem(block, 2) == 1, block < last, block > 0)
-        full = jnp.where(there, ref[...].astype(F32), 0.0)
+        full = jnp.where(there, ref[:, lanes_of(freq, c, rows)].astype(F32), 0.0)
         return full[0:2], full[2:3, :1] + full[3:4, :1] + full[4:5, :1]
 
-    near, near_coef = outer(near_ref, me)
-    far, far_coef = outer(far_ref, xor(me, 1))
     sides = (
-        (k_ref, coef, me, near, near_coef, mate_ref, mate_pick, last_or_first(mate_coef, is_odd), is_odd),
-        (mate_ref, mate_coef, xor(me, 1), far, far_coef, k_ref, own_pick, last_or_first(coef, ~is_odd), ~is_odd),
+        (k_ref, coef, me, near_ref, mate_ref, mate_pick, last_or_first(mate_coef, is_odd), is_odd),
+        (mate_ref, mate_coef, xor(me, 1), far_ref, k_ref, own_pick, last_or_first(coef, ~is_odd), ~is_odd),
     )
-    for n, (ref, c_block, block, outside, outside_coef, inner_ref, pick, inside_coef, inner_left) in enumerate(sides):
+    for n, (ref, c_block, block, outer_ref, inner_ref, pick, inside_coef, inner_left) in enumerate(sides):
         upper, lower = stencil_matrix(c_block, block)
-        left_coef = jnp.where(inner_left, inside_coef, outside_coef) + c_block[:, :1]
-        right_coef = jnp.where(inner_left, outside_coef, inside_coef) + c_block[:, width - 1:]
-        for f in range(freqs):
-            for c in range(2):
-                own = ref[f, c]
-                value = dot_nt(upper, own) + dot_nt(lower, own)
-                inside = dot_nt(pick, inner_ref[f, c])[0:2]
-                lo = (f * 2 + c) * rows
-                beyond = outside[:, lo:lo + rows]
-                left = jnp.where(inner_left, inside, beyond)
-                right = jnp.where(inner_left, beyond, inside)
-                extra = jnp.concatenate(
-                    [
-                        left[0:1] - left_coef * left[1:2],
-                        left[1:2],
-                        jnp.zeros((width - 4, rows), F32),
-                        right[0:1],
-                        right[1:2] - right_coef * right[0:1],
-                    ],
-                    axis=0,
-                )
-                o_ref[f, c, n * width:(n + 1) * width] = (value + extra).astype(BF)
+        for c in range(2):
+            beyond, outside_coef = outer(outer_ref, block, c)
+            left_coef = jnp.where(inner_left, inside_coef, outside_coef) + c_block[:, :1]
+            right_coef = jnp.where(inner_left, outside_coef, inside_coef) + c_block[:, width - 1:]
+            own = ref[c]
+            value = dot_nt(upper, own) + dot_nt(lower, own)
+            inside = dot_nt(pick, inner_ref[c])[0:2]
+            left = jnp.where(inner_left, inside, beyond)
+            right = jnp.where(inner_left, beyond, inside)
+            extra = jnp.concatenate(
+                [
+                    left[0:1] - left_coef * left[1:2],
+                    left[1:2],
+                    jnp.zeros((width - 4, rows), F32),
+                    right[0:1],
+                    right[1:2] - right_coef * right[0:1],
+                ],
+                axis=0,
+            )
+            o_ref[c, n * width:(n + 1) * width] = (value + extra).astype(BF)
 
 
 def split_body(own_ref, got_ref, keep_ref, *send_refs):
@@ -261,14 +261,14 @@
             out_ref[part(lo * chips * size + source * size, size), :] = ref[n * size:(n + 1) * size]
 
 
-def predict(freq, a_ref, k_ref, targets, kind):
+def predict(a_ref, k_ref, targets, kind):
     half = a_ref.shape[0] // 2
     width = a_ref.shape[1]
     size = half // (2 * len(targets))
     total = []
     for c in range(2):
-        value = dot_nn(a_ref[:half], k_ref[freq, c, :width])
-        total.append(value + dot_nn(a_ref[half:], k_ref[freq, c, width:]))
+        value = dot_nn(a_ref[:half], k_ref[c, :width])
+        total.append(value + dot_nn(a_ref[half:], k_ref[c, width:]))
     by_real, by_imag = total
     for slot, ref in enumerate(targets):
         lo = 2 * slot * size
@@ -279,8 +279,8 @@
 
 
 def predict_own_body(away_ref, stay_ref, k_ref, keep_ref, *owns):
-    predict(parity(), away_ref, k_ref, owns, BF)
-    predict(parity(), stay_ref, k_ref, (keep_ref,), F32)
+    predict(away_ref, k_ref, owns, BF)
+    predict(stay_ref, k_ref, (keep_ref,), F32)
 
 
 def predict_away_body(peers, away_ref, k_ref, *refs):
@@ -290,14 +290,14 @@
     for own, send in zip(owns, sends):
         send[part(freq * size, size), :] = own[...]
     rest = part((1 - freq) * size, size)
-    predict(1 - freq, away_ref, k_ref, tuple(send.at[rest] for send in sends), BF)
+    predict(away_ref, k_ref, tuple(send.at[rest] for send in sends), BF)
 
 
 def predict_stay_body(stay_ref, k_ref, keep_ref):
-    predict(1 - parity(), stay_ref, k_ref, (keep_ref,), F32)
-
-
-def final_body(x_ref, noise_ref, own_ref, other_ref, *refs):
+    predict(stay_ref, k_ref, (keep_ref,), F32)
+
+
+def final_body(v_ref, noise_ref, own_ref, other_ref, *refs):
     out_ref, s_ref = refs[-2:]
     size = out_ref.shape[0]
     rows = 4 * size
@@ -313,7 +313,7 @@
             at = slice(t * LANES, (t + 1) * LANES)
             s_ref[t, pl.ds(2 * f, size, stride=4), :] = total[:size, at]
             s_ref[t, pl.ds(2 * f + 1, size, stride=4), :] = total[size:, at]
-    x = x_ref[part(me * rows, rows), :].astype(F32)
+    x = v_ref[part(me * size, size)].reshape(rows, v_ref.shape[3]).astype(F32)
     kind = lax.rem(lax.broadcasted_iota(jnp.int32, x.shape, 0), 4)
     noise = jnp.where(kind < 2, noise_ref[0:1, :], noise_ref[1:2, :])
     values = jnp.concatenate([s_ref[t] for t in range(s_ref.shape[0])], axis=1) + noise * x
@@ -368,19 +368,27 @@
     blocks = lax.axis_size("row")
     chips = lax.axis_size("col") // 2
     coef = prior_diag[None, :]
-    flat = (4 * count, rows)
-    scratch = pltpu.VMEM((2 * width // LANES, 4 * count, LANES), F32)
-    mate = lax.ppermute(kernel, "row", pair_perm("row", 1))
-    other, x, kernel, coef, noise = call(
+    scratch = pltpu.VMEM((2 * width // LANES, 2 * count, LANES), F32)
+    block = kernel.shape[1:]
+    other, probes, k_own, k_other, coef, noise = call(
         adjoint_other_body,
         (),
-        [((2 * count, width), BF), (flat, BF), (kernel.shape, BF), (coef.shape, F32), (noise_var.shape, F32)],
-        (pltpu.VMEM(probes.shape, BF), scratch, pltpu.SemaphoreType.DMA((5,))),
+        [
+            ((2 * count, width), BF),
+            (probes.shape, BF),
+            (block, BF),
+            (block, BF),
+            (coef.shape, F32),
+            (noise_var.shape, F32),
+        ],
+        (scratch, pltpu.SemaphoreType.DMA((5,))),
         raw=(probes, kernel, coef, noise_var),
     )
     got = lax.ppermute(other, "col", pair_perm("col", 1))
-    own = call(adjoint_own_body, (x, kernel), [((2 * count, width), F32)], (scratch,))[0]
-    seam = call(seam_body, (kernel, coef), [((8, 4 * rows), BF)])[0]
+    mate_own = lax.ppermute(k_other, "row", pair_perm("row", 1))
+    mate_other = lax.ppermute(k_own, "row", pair_perm("row", 1))
+    own = call(adjoint_own_body, (probes, k_own), [((2 * count, width), F32)], (scratch,))[0]
+    seam = call(seam_body, (k_own, k_other, coef), [((8, 4 * rows), BF)])[0]
     odd = [i for i in range(blocks) if i % 2]
     even = [i for i in range(blocks) if i % 2 == 0]
     near = [(i, i + 1) for i in odd if i + 1 < blocks] + [(i, i - 1) for i in even if i]
@@ -391,19 +399,24 @@
         mine, other, give = wide_sum(own, got, coef, blocks)
     else:
         mine, other, give = chip_sum(own, got, coef, blocks, chips)
-    operator = call(operator_body, (kernel, mate, coef, give, near, far), [((2, 2, 2 * width, rows), BF)])[0]
+    operators = [
+        call(
+            functools.partial(operator_body, swap), (block_k, mate, coef, give, near, far), [((2, 2 * width, rows), BF)]
+        )[0]
+        for swap, block_k, mate in ((False, k_own, mate_own), (True, k_other, mate_other))
+    ]
     size = count // blocks
     peers = blocks // 2 - 1
     half = (2 * size, rows)
-    keep_own, *owns = call(predict_own_body, (*mine, operator), [(half, F32)] + [(half, BF)] * peers)
+    keep_own, *owns = call(predict_own_body, (*mine, operators[0]), [(half, F32)] + [(half, BF)] * peers)
     sends = call(
-        functools.partial(predict_away_body, peers), (other[0], operator, *owns), [((4 * size, rows), BF)] * peers
+        functools.partial(predict_away_body, peers), (other[0], operators[1], *owns), [((4 * size, rows), BF)] * peers
     )
     got = [lax.ppermute(v, "row", pair_perm("row", cross(d + 1))) for d, v in enumerate(sends)]
-    keep_other = call(predict_stay_body, (other[1], operator), [(half, F32)])[0]
+    keep_other = call(predict_stay_body, (other[1], operators[1]), [(half, F32)])[0]
     return call(
         final_body,
-        (x, noise, keep_own, keep_other, *got),
+        (probes, noise, keep_own, keep_other, *got),
         [((size,) + probes.shape[1:3] + (rows,), F32)],
         (pltpu.VMEM((rows // LANES, 4 * size, LANES), F32),),
     )[0]

time: 40.5 us -> 48.5 us (1.20)
  the two profiles are of different devices: /device:TPU:20 before, /device:TPU:0 now
where the time goes in v13:
time: 48.5 us; the launch traced here: 47.9 us
  waiting for transfers between devices  24.5 us (51%)
  starting transfers between devices  18.1 us (37%)
  Pallas kernels  4.53 us (9%)
  local copies, waits for them, and re-layouts  0.71 us (1%)
    ppermute x1, waiting for transfers between devices, chip_sum(): give = lax.ppermute(give, ('row', 'col'), mate_perm())  8.7 us
    ppermute x1, waiting for transfers between devices, apply(): lax.ppermute(v, 'row', pair_perm('row', cross(d + 1)))  5.13 us
    ppermute x3, waiting for transfers between devices, chip_sum(): lax.ppermute(mine, 'col', pair_perm('col', hop(d + 1)))  4.99 us
    pallas_call x14, Pallas kernels, call(): pl.pallas_call(body, in_specs=[HBM] * len(raw) + [VMEM] * len(ins), out_s...  4.53 us
    ppermute x1, starting transfers between devices, apply(): far = lax.ppermute(seam, 'row', far)  4.42 us
    ppermute x3, starting transfers between devices, chip_sum(): lax.ppermute(v, 'col', pair_perm('col', hop(d + 1)))  4.19 us
    ppermute x3, starting transfers between devices, chip_sum(): lax.ppermute(mine, 'col', pair_perm('col', hop(d + 1)))  3.35 us
    ppermute x3, waiting for transfers between devices, chip_sum(): lax.ppermute(v, 'col', pair_perm('col', hop(d + 1)))  3.07 us
  transfers between devices with their start and end apart: 15, of which 9 were waited for; matrix products, arithmetic and copies ran while one was open for 0% of the time, Pallas kernels for 6%

profile of v13, /device:TPU:0, one launch (start us, length us, event | category | flops | bytes accessed | tf_op | source)
XLA Modules:
  0.0 47.9 jit_solution(7721830971774611532)
XLA Ops:
  0.0 1.5 %shard_map.46 = (bf16[512,256]{1,0:T(8,128)(2,1)S(1)}, bf16[256,2,2,256]{3,2,1,0:T(2,128)(2,1)S(1)}, bf16[2,256,256]{2,1,0:T(8,128)(2,1)S(1)}, bf16[2,256,256]{2...) custom-call(bf16[256,2,2,256]{3,2,1,0:T(2,128)(2,1)} %v_hbm.1, bf16[2,2,256,256]{3,2,1,0:T(8,128)(2,1)} %k_hbm.1, ...), custom_call_target="tpu_custom_call" | custom-call | tf_op jit(solution)/shard_map/pallas_call | solution.py:20
  1.5 0.6 %collective-permute-start = (bf16[512,256]{1,0:T(8,128)(2,1)S(1)}, bf16[512,256]{1,0:T(8,128)(2,1)S(1)}, u32[]{:S(2)}, u32[]{:S(2)}) collective-permute-start(bf16[512,256]{1,0:T(8,128)(2,1)S(1)} %get-tuple-element.24), channel_id=1, source_target_pairs={{0,1},{1,0},{2,3},{3,2},{4,5},{5,4},{6,7},{7,6},{8,9},{9,8},{10,11... | collective-permute-start | bytes 786440 | tf_op jit(solution)/shard_map/ppermute | solution.py:387
  2.1 0.4 shard_map.47.own_ref
  2.5 0.8 %collective-permute-done.got_ref = bf16[512,256]{1,0:T(8,128)(2,1)S(1)} collective-permute-done((bf16[512,256]{1,0:T(8,128)(2,1)S(1)}, bf16[512,256]{1,0:T(8,128)(2,1)S(1)}, u32[]{:S(2)}, u32[]{:S(2)}) %collective-permute-start) | collective-permute-done | bytes 262176 | tf_op jit(solution)/shard_map/ppermute | solution.py:387
  3.3 0.1 shard_map.48
  3.3 2.7 %collective-permute-start.1 = (bf16[128,256]{1,0:T(8,128)(2,1)S(1)}, bf16[128,256]{1,0:T(8,128)(2,1)S(1)}, u32[]{:S(2)}, u32[]{:S(2)}) collective-permute-start(bf16[128,256]{1,0:T(8,128)(2,1)S(1)} %get-tuple-element.27), channel_id=1, source_target_pairs={{0,3},{1,2},{2,1},{3,0},{4,7},{5,6},{6,5},{7,4},{8,11},{9,10},{10,... | collective-permute-start | bytes 196616 | tf_op jit(solution)/shard_map/ppermute | solution.py:353
  6.0 1.5 %collective-permute-start.2 = (bf16[128,256]{1,0:T(8,128)(2,1)S(1)}, bf16[128,256]{1,0:T(8,128)(2,1)S(1)}, u32[]{:S(2)}, u32[]{:S(2)}) collective-permute-start(bf16[128,256]{1,0:T(8,128)(2,1)S(1)} %get-tuple-element.28), channel_id=1, source_target_pairs={{0,5},{1,4},{2,7},{3,6},{4,1},{5,0},{6,3},{7,2},{8,13},{9,12},{10,... | collective-permute-start | bytes 196616 | tf_op jit(solution)/shard_map/ppermute | solution.py:353
  7.5 0.0 collective-permute-start.3
  7.5 2.0 %collective-permute-start.8 = (bf16[2,256,256]{2,1,0:T(8,128)(2,1)S(1)}, bf16[2,256,256]{2,1,0:T(8,128)(2,1)S(1)}, u32[]{:S(2)}, u32[]{:S(2)}) collective-permute-start(bf16[2,256,256]{2,1,0:T(8,128)(2,1)S(1)} %get-tuple-element.34.other_ref.k_ref), channel_id=1, source_target_pairs={{0,8},{8,0},{16,24},{24,16},{1,9},{9,1},{17,25},{25,17},{2,10},{10... | collective-permute-start | bytes 786440 | tf_op jit(solution)/shard_map/ppermute | solution.py:388
  9.5 0.0 collective-permute-start.12
  9.6 0.0 collective-permute-done.1.refs_0_
  9.6 0.2 collective-permute-done.2.refs_1_
  9.8 2.8 %collective-permute-done.3.refs_2_ = bf16[128,256]{1,0:T(8,128)(2,1)S(1)} collective-permute-done((bf16[128,256]{1,0:T(8,128)(2,1)S(1)}, bf16[128,256]{1,0:T(8,128)(2,1)S(1)}, u32[]{:S(2)}, u32[]{:S(2)}) %collective-permute-start.3) | collective-permute-done | bytes 65568 | tf_op jit(solution)/shard_map/ppermute | solution.py:353
  12.7 0.2 collective-permute-start.4
  12.9 8.7 %collective-permute-done.4.got_ref = bf16[80,256]{1,0:T(8,128)(2,1)S(1)} collective-permute-done((bf16[80,256]{1,0:T(8,128)(2,1)S(1)}, bf16[80,256]{1,0:T(8,128)(2,1)S(1)}, u32[]{:S(2)}, u32[]{:S(2)}) %collective-permute-start.4) | collective-permute-done | bytes 40992 | tf_op jit(solution)/shard_map/ppermute | solution.py:356
  21.6 1.8 %collective-permute-start.5 = (bf16[128,256]{1,0:T(8,128)(2,1)S(1)}, bf16[128,256]{1,0:T(8,128)(2,1)S(1)}, u32[]{:S(2)}, u32[]{:S(2)}) collective-permute-start(bf16[128,256]{1,0:T(8,128)(2,1)S(1)} %shard_map.51.mine_ref), channel_id=1, source_target_pairs={{0,3},{1,2},{2,1},{3,0},{4,7},{5,6},{6,5},{7,4},{8,11},{9,10},{10,... | collective-permute-start | bytes 196616 | tf_op jit(solution)/shard_map/ppermute | solution.py:358
  23.4 0.9 %collective-permute-start.6 = (bf16[128,256]{1,0:T(8,128)(2,1)S(1)}, bf16[128,256]{1,0:T(8,128)(2,1)S(1)}, u32[]{:S(2)}, u32[]{:S(2)}) collective-permute-start(bf16[128,256]{1,0:T(8,128)(2,1)S(1)} %shard_map.51.mine_ref), channel_id=1, source_target_pairs={{0,5},{1,4},{2,7},{3,6},{4,1},{5,0},{6,3},{7,2},{8,13},{9,12},{10,... | collective-permute-start | bytes 196616 | tf_op jit(solution)/shard_map/ppermute | solution.py:358
  24.4 0.6 %collective-permute-start.7 = (bf16[128,256]{1,0:T(8,128)(2,1)S(1)}, bf16[128,256]{1,0:T(8,128)(2,1)S(1)}, u32[]{:S(2)}, u32[]{:S(2)}) collective-permute-start(bf16[128,256]{1,0:T(8,128)(2,1)S(1)} %shard_map.51.mine_ref), channel_id=1, source_target_pairs={{0,6},{1,7},{2,4},{3,5},{4,2},{5,3},{6,0},{7,1},{8,14},{9,15},{10,... | collective-permute-start | bytes 196616 | tf_op jit(solution)/shard_map/ppermute | solution.py:358
  25.0 0.4 collective-permute-done.5.refs_0_
  25.4 2.3 %collective-permute-done.6.refs_1_ = bf16[128,256]{1,0:T(8,128)(2,1)S(1)} collective-permute-done((bf16[128,256]{1,0:T(8,128)(2,1)S(1)}, bf16[128,256]{1,0:T(8,128)(2,1)S(1)}, u32[]{:S(2)}, u32[]{:S(2)}) %collective-permute-start.6) | collective-permute-done | bytes 65568 | tf_op jit(solution)/shard_map/ppermute | solution.py:358
  27.8 2.2 %collective-permute-done.7.refs_2_ = bf16[128,256]{1,0:T(8,128)(2,1)S(1)} collective-permute-done((bf16[128,256]{1,0:T(8,128)(2,1)S(1)}, bf16[128,256]{1,0:T(8,128)(2,1)S(1)}, u32[]{:S(2)}, u32[]{:S(2)}) %collective-permute-start.7) | collective-permute-done | bytes 65568 | tf_op jit(solution)/shard_map/ppermute | solution.py:358
  30.0 0.1 collective-permute-start.13
  30.1 0.2 shard_map.53
  30.3 0.7 %collective-permute-start.9 = (bf16[8,1024]{1,0:T(8,128)(2,1)S(1)}, bf16[8,1024]{1,0:T(8,128)(2,1)S(1)}, u32[]{:S(2)}, u32[]{:S(2)}) collective-permute-start(bf16[8,1024]{1,0:T(8,128)(2,1)S(1)} %shard_map.53), channel_id=1, source_target_pairs={{8,16},{16,8},{9,17},{17,9},{10,18},{18,10},{11,19},{19,11},{12,20... | collective-permute-start | bytes 49160 | tf_op jit(solution)/shard_map/ppermute | solution.py:396
  31.0 4.4 %collective-permute-start.10 = (bf16[8,1024]{1,0:T(8,128)(2,1)S(1)}, bf16[8,1024]{1,0:T(8,128)(2,1)S(1)}, u32[]{:S(2)}, u32[]{:S(2)}) collective-permute-start(bf16[8,1024]{1,0:T(8,128)(2,1)S(1)} %shard_map.53), channel_id=1, source_target_pairs={{8,24},{24,8},{0,16},{16,0},{9,25},{25,9},{1,17},{17,1},{10,26},{2... | collective-permute-start | bytes 49160 | tf_op jit(solution)/shard_map/ppermute | solution.py:397
  35.4 0.0 collective-permute-done.9.near_ref
  35.4 1.8 %collective-permute-done.10.far_ref = bf16[8,1024]{1,0:T(8,128)(2,1)S(1)} collective-permute-done((bf16[8,1024]{1,0:T(8,128)(2,1)S(1)}, bf16[8,1024]{1,0:T(8,128)(2,1)S(1)}, u32[]{:S(2)}, u32[]{:S(2)}) %collective-permute-start.10) | collective-permute-done | bytes 16416 | tf_op jit(solution)/shard_map/ppermute | solution.py:397
  37.2 0.0 collective-permute-done.8.mate_ref
  37.2 0.6 %shard_map.54.k_ref = bf16[2,512,256]{2,1,0:T(8,128)(2,1)S(1)} custom-call(bf16[2,256,256]{2,1,0:T(8,128)(2,1)S(1)} %get-tuple-element.23.k_ref.mine_ref, bf16[2,256,256]{2,1,0:T(8,128)(2,1)S(1)} %collective-permute-done.8.mate_ref, f32[1,256]{1,0:T(1,128)S(1)} %get-tuple-element.26.d_ref, bf16[80,256]{1,0:T(8,128)(2,1)S(1)} %collective-permute-done.4.got_ref, ...), custom_call_target="tpu_custom_call" | custom-call | tf_op jit(solution)/shard_map/pallas_call | solution.py:20
  37.9 0.0 collective-permute-done.12.mate_ref
  37.9 0.6 %shard_map.56.k_ref = bf16[2,512,256]{2,1,0:T(8,128)(2,1)S(1)} custom-call(bf16[2,256,256]{2,1,0:T(8,128)(2,1)S(1)} %get-tuple-element.34.other_ref.k_ref, bf16[2,256,256]{2,1,0:T(8,128)(2,1)S(1)} %collective-permute-done.12.mate_ref, f32[1,256]{1,0:T(1,128)S(1)} %get-tuple-element.26.d_ref, bf16[80,256]{1,0:T(8,128)(2,1)S(1)} %collective-permute-done.4.got_ref, ...), custom_call_target="tpu_custom_call" | custom-call | tf_op jit(solution)/shard_map/pallas_call | solution.py:20
  38.5 0.1 collective-permute-start.11
  38.6 0.3 shard_map.55
  38.9 0.0 collective-permute-done.13.away_ref
  38.9 0.2 shard_map.58
  39.2 2.5 %collective-permute-start.14 = (bf16[256,256]{1,0:T(8,128)(2,1)S(1)}, bf16[256,256]{1,0:T(8,128)(2,1)S(1)}, u32[]{:S(2)}, u32[]{:S(2)}) collective-permute-start(bf16[256,256]{1,0:T(8,128)(2,1)S(1)} %shard_map.58), channel_id=1, source_target_pairs={{0,24},{8,16},{16,8},{24,0},{1,25},{9,17},{17,9},{25,1},{2,26},{10... | collective-permute-start | bytes 393224 | tf_op jit(solution)/shard_map/ppermute | solution.py:415
  41.6 0.0 collective-permute-done.11.stay_ref
  41.6 0.2 shard_map.57.other_ref
  41.9 5.1 %collective-permute-done.14.refs_0_ = bf16[256,256]{1,0:T(8,128)(2,1)S(1)} collective-permute-done((bf16[256,256]{1,0:T(8,128)(2,1)S(1)}, bf16[256,256]{1,0:T(8,128)(2,1)S(1)}, u32[]{:S(2)}, u32[]{:S(2)}) %collective-permute-start.14) | collective-permute-done | bytes 131104 | tf_op jit(solution)/shard_map/ppermute | solution.py:415
  47.0 0.2 shard_map.59
  47.2 0.7 %copy.5 = f32[64,2,2,256]{3,2,1,0:T(2,128)} copy(f32[64,2,2,256]{3,2,1,0:T(2,128)S(1)} %shard_map.59) | data formatting | bytes 524288
  (4 shorter events, 0.1 us)
Async XLA Ops:
  1.5 1.7 %collective-permute-start = (bf16[512,256]{1,0:T(8,128)(2,1)S(1)}, bf16[512,256]{1,0:T(8,128)(2,1)S(1)}, u32[]{:S(2)}, u32[]{:S(2)}) collective-permute-start(bf16[512,256]{1,0:T(8,128)(2,1)S(1)} %get-tuple-element.24), channel_id=1, source_target_pairs={{0,1},{1,0},{2,3},{3,2},{4,5},{5,4},{6,7},{7,6},{8,9},{9,8},{10,11... | collective-permute-start | bytes 786440 | tf_op jit(solution)/shard_map/ppermute | solution.py:387
  3.3 6.2 %collective-permute-start.1 = (bf16[128,256]{1,0:T(8,128)(2,1)S(1)}, bf16[128,256]{1,0:T(8,128)(2,1)S(1)}, u32[]{:S(2)}, u32[]{:S(2)}) collective-permute-start(bf16[128,256]{1,0:T(8,128)(2,1)S(1)} %get-tuple-element.27), channel_id=1, source_target_pairs={{0,3},{1,2},{2,1},{3,0},{4,7},{5,6},{6,5},{7,4},{8,11},{9,10},{10,... | collective-permute-start | bytes 196616 | tf_op jit(solution)/shard_map/ppermute | solution.py:353
  6.0 3.8 %collective-permute-start.2 = (bf16[128,256]{1,0:T(8,128)(2,1)S(1)}, bf16[128,256]{1,0:T(8,128)(2,1)S(1)}, u32[]{:S(2)}, u32[]{:S(2)}) collective-permute-start(bf16[128,256]{1,0:T(8,128)(2,1)S(1)} %get-tuple-element.28), channel_id=1, source_target_pairs={{0,5},{1,4},{2,7},{3,6},{4,1},{5,0},{6,3},{7,2},{8,13},{9,12},{10,... | collective-permute-start | bytes 196616 | tf_op jit(solution)/shard_map/ppermute | solution.py:353
  7.5 5.2 %collective-permute-start.3 = (bf16[128,256]{1,0:T(8,128)(2,1)S(1)}, bf16[128,256]{1,0:T(8,128)(2,1)S(1)}, u32[]{:S(2)}, u32[]{:S(2)}) collective-permute-start(bf16[128,256]{1,0:T(8,128)(2,1)S(1)} %get-tuple-element.29), channel_id=1, source_target_pairs={{0,6},{1,7},{2,4},{3,5},{4,2},{5,3},{6,0},{7,1},{8,14},{9,15},{10,... | collective-permute-start | bytes 196616 | tf_op jit(solution)/shard_map/ppermute | solution.py:353
  7.5 29.7 %collective-permute-start.8 = (bf16[2,256,256]{2,1,0:T(8,128)(2,1)S(1)}, bf16[2,256,256]{2,1,0:T(8,128)(2,1)S(1)}, u32[]{:S(2)}, u32[]{:S(2)}) collective-permute-start(bf16[2,256,256]{2,1,0:T(8,128)(2,1)S(1)} %get-tuple-element.34.other_ref.k_ref), channel_id=1, source_target_pairs={{0,8},{8,0},{16,24},{24,16},{1,9},{9,1},{17,25},{25,17},{2,10},{10... | collective-permute-start | bytes 786440 | tf_op jit(solution)/shard_map/ppermute | solution.py:388
  9.5 28.3 %collective-permute-start.12 = (bf16[2,256,256]{2,1,0:T(8,128)(2,1)S(1)}, bf16[2,256,256]{2,1,0:T(8,128)(2,1)S(1)}, u32[]{:S(2)}, u32[]{:S(2)}) collective-permute-start(bf16[2,256,256]{2,1,0:T(8,128)(2,1)S(1)} %get-tuple-element.23.k_ref.mine_ref), channel_id=1, source_target_pairs={{0,8},{8,0},{16,24},{24,16},{1,9},{9,1},{17,25},{25,17},{2,10},{10... | collective-permute-start | bytes 786440 | tf_op jit(solution)/shard_map/ppermute | solution.py:389
  12.7 8.9 %collective-permute-start.4 = (bf16[80,256]{1,0:T(8,128)(2,1)S(1)}, bf16[80,256]{1,0:T(8,128)(2,1)S(1)}, u32[]{:S(2)}, u32[]{:S(2)}) collective-permute-start(bf16[80,256]{1,0:T(8,128)(2,1)S(1)} %get-tuple-element.31), channel_id=1, source_target_pairs={{0,9},{1,8},{2,11},{3,10},{4,13},{5,12},{6,15},{7,14},{8,1},{9,0},... | collective-permute-start | bytes 122888 | tf_op jit(solution)/shard_map/ppermute | solution.py:356
  21.6 3.8 %collective-permute-start.5 = (bf16[128,256]{1,0:T(8,128)(2,1)S(1)}, bf16[128,256]{1,0:T(8,128)(2,1)S(1)}, u32[]{:S(2)}, u32[]{:S(2)}) collective-permute-start(bf16[128,256]{1,0:T(8,128)(2,1)S(1)} %shard_map.51.mine_ref), channel_id=1, source_target_pairs={{0,3},{1,2},{2,1},{3,0},{4,7},{5,6},{6,5},{7,4},{8,11},{9,10},{10,... | collective-permute-start | bytes 196616 | tf_op jit(solution)/shard_map/ppermute | solution.py:358
  23.4 4.3 %collective-permute-start.6 = (bf16[128,256]{1,0:T(8,128)(2,1)S(1)}, bf16[128,256]{1,0:T(8,128)(2,1)S(1)}, u32[]{:S(2)}, u32[]{:S(2)}) collective-permute-start(bf16[128,256]{1,0:T(8,128)(2,1)S(1)} %shard_map.51.mine_ref), channel_id=1, source_target_pairs={{0,5},{1,4},{2,7},{3,6},{4,1},{5,0},{6,3},{7,2},{8,13},{9,12},{10,... | collective-permute-start | bytes 196616 | tf_op jit(solution)/shard_map/ppermute | solution.py:358
  24.4 5.6 %collective-permute-start.7 = (bf16[128,256]{1,0:T(8,128)(2,1)S(1)}, bf16[128,256]{1,0:T(8,128)(2,1)S(1)}, u32[]{:S(2)}, u32[]{:S(2)}) collective-permute-start(bf16[128,256]{1,0:T(8,128)(2,1)S(1)} %shard_map.51.mine_ref), channel_id=1, source_target_pairs={{0,6},{1,7},{2,4},{3,5},{4,2},{5,3},{6,0},{7,1},{8,14},{9,15},{10,... | collective-permute-start | bytes 196616 | tf_op jit(solution)/shard_map/ppermute | solution.py:358
  30.0 8.9 %collective-permute-start.13 = (bf16[256,256]{1,0:T(8,128)(2,1)S(1)}, bf16[256,256]{1,0:T(8,128)(2,1)S(1)}, u32[]{:S(2)}, u32[]{:S(2)}) collective-permute-start(bf16[256,256]{1,0:T(8,128)(2,1)S(1)} %get-tuple-element.32.away_ref), channel_id=1, source_target_pairs={{0,1},{1,0},{2,3},{3,2},{4,5},{5,4},{6,7},{7,6},{8,9},{9,8},{10,11... | collective-permute-start | bytes 393224 | tf_op jit(solution)/shard_map/ppermute | solution.py:361
  30.3 5.1 %collective-permute-start.9 = (bf16[8,1024]{1,0:T(8,128)(2,1)S(1)}, bf16[8,1024]{1,0:T(8,128)(2,1)S(1)}, u32[]{:S(2)}, u32[]{:S(2)}) collective-permute-start(bf16[8,1024]{1,0:T(8,128)(2,1)S(1)} %shard_map.53), channel_id=1, source_target_pairs={{8,16},{16,8},{9,17},{17,9},{10,18},{18,10},{11,19},{19,11},{12,20... | collective-permute-start | bytes 49160 | tf_op jit(solution)/shard_map/ppermute | solution.py:396
  31.0 6.2 %collective-permute-start.10 = (bf16[8,1024]{1,0:T(8,128)(2,1)S(1)}, bf16[8,1024]{1,0:T(8,128)(2,1)S(1)}, u32[]{:S(2)}, u32[]{:S(2)}) collective-permute-start(bf16[8,1024]{1,0:T(8,128)(2,1)S(1)} %shard_map.53), channel_id=1, source_target_pairs={{8,24},{24,8},{0,16},{16,0},{9,25},{25,9},{1,17},{17,1},{10,26},{2... | collective-permute-start | bytes 49160 | tf_op jit(solution)/shard_map/ppermute | solution.py:397
  38.5 3.1 %collective-permute-start.11 = (bf16[256,256]{1,0:T(8,128)(2,1)S(1)}, bf16[256,256]{1,0:T(8,128)(2,1)S(1)}, u32[]{:S(2)}, u32[]{:S(2)}) collective-permute-start(bf16[256,256]{1,0:T(8,128)(2,1)S(1)} %get-tuple-element.33.stay_ref), channel_id=1, source_target_pairs={{0,1},{1,0},{2,3},{3,2},{4,5},{5,4},{6,7},{7,6},{8,9},{9,8},{10,11... | collective-permute-start | bytes 393224 | tf_op jit(solution)/shard_map/ppermute | solution.py:361
  39.2 7.9 %collective-permute-start.14 = (bf16[256,256]{1,0:T(8,128)(2,1)S(1)}, bf16[256,256]{1,0:T(8,128)(2,1)S(1)}, u32[]{:S(2)}, u32[]{:S(2)}) collective-permute-start(bf16[256,256]{1,0:T(8,128)(2,1)S(1)} %shard_map.58), channel_id=1, source_target_pairs={{0,24},{8,16},{16,8},{24,0},{1,25},{9,17},{17,9},{25,1},{2,26},{10... | collective-permute-start | bytes 393224 | tf_op jit(solution)/shard_map/ppermute | solution.py:415

commit v14 on v13

--- a/solution.py
+++ b/solution.py
@@ -391,10 +391,9 @@
     seam = call(seam_body, (k_own, k_other, coef), [((8, 4 * rows), BF)])[0]
     odd = [i for i in range(blocks) if i % 2]
     even = [i for i in range(blocks) if i % 2 == 0]
-    near = [(i, i + 1) for i in odd if i + 1 < blocks] + [(i, i - 1) for i in even if i]
-    far = [(i, i + 2 if i + 2 < blocks else 1) for i in odd] + [(i, i - 2 if i else blocks - 2) for i in even]
+    near = [(i, (i + 1) % blocks) for i in odd] + [(i, (i - 1) % blocks) for i in even]
     near = lax.ppermute(seam, "row", near)
-    far = lax.ppermute(seam, "row", far)
+    far = lax.ppermute(near, "row", pair_perm("row", 1))
     if chips > 4:
         mine, other, give = wide_sum(own, got, coef, blocks)
     else:

time: 48.5 us -> 50.6 us (1.043)
  waiting for transfers between devices: 24.5 us -> 27.2 us
    ppermute x1, starting transfers between devices: 4.42 us -> 0.01 us  [apply(): far = lax.ppermute(near, 'row', pair_perm('row', 1))]
    ppermute x1, starting transfers between devices: 0.67 us -> 3.69 us  [apply(): near = lax.ppermute(seam, 'row', near)]
    ppermute x1, waiting for transfers between devices: 1.8 us -> 3.74 us  [apply(): far = lax.ppermute(near, 'row', pair_perm('row', 1))]
    ppermute x1, waiting for transfers between devices: 0.01 us -> 1.86 us  [apply(): near = lax.ppermute(seam, 'row', near)]
    ppermute x1, starting transfers between devices: 2.47 us -> 3.73 us  [apply(): lax.ppermute(v, 'row', pair_perm('row', cross(d + 1)))]
    ppermute x1, waiting for transfers between devices: 5.13 us -> 4.01 us  [apply(): lax.ppermute(v, 'row', pair_perm('row', cross(d + 1)))]
  transfers between devices with their start and end apart: 15 -> 15, of which waited for: 9 -> 10; matrix products, arithmetic and copies ran while one was open for 0% -> 0% of each run, Pallas kernels for 6% -> 5%
where the time goes in v14:
time: 50.6 us; the launch traced here: 50.5 us
  waiting for transfers between devices  27.2 us (54%)
  starting transfers between devices  17.9 us (35%)
  Pallas kernels  4.53 us (9%)
  local copies, waits for them, and re-layouts  0.71 us (1%)
    ppermute x1, waiting for transfers between devices, chip_sum(): give = lax.ppermute(give, ('row', 'col'), mate_perm())  8.7 us
    ppermute x3, waiting for transfers between devices, chip_sum(): lax.ppermute(mine, 'col', pair_perm('col', hop(d + 1)))  4.99 us
    pallas_call x14, Pallas kernels, call(): pl.pallas_call(body, in_specs=[HBM] * len(raw) + [VMEM] * len(ins), out_s...  4.53 us
    ppermute x3, starting transfers between devices, chip_sum(): lax.ppermute(v, 'col', pair_perm('col', hop(d + 1)))  4.19 us
    ppermute x1, waiting for transfers between devices, apply(): lax.ppermute(v, 'row', pair_perm('row', cross(d + 1)))  4.01 us
    ppermute x1, waiting for transfers between devices, apply(): far = lax.ppermute(near, 'row', pair_perm('row', 1))  3.74 us
    ppermute x1, starting transfers between devices, apply(): lax.ppermute(v, 'row', pair_perm('row', cross(d + 1)))  3.73 us
    ppermute x1, starting transfers between devices, apply(): near = lax.ppermute(seam, 'row', near)  3.69 us
  transfers between devices with their start and end apart: 15, of which 10 were waited for; matrix products, arithmetic and copies ran while one was open for 0% of the time, Pallas kernels for 5%

profile of v14, /device:TPU:0, one launch (start us, length us, event | category | flops | bytes accessed | tf_op | source)
XLA Modules:
  0.0 50.5 jit_solution(4740645558655712922)
XLA Ops:
  0.0 1.5 %shard_map.46 = (bf16[512,256]{1,0:T(8,128)(2,1)S(1)}, bf16[256,2,2,256]{3,2,1,0:T(2,128)(2,1)S(1)}, bf16[2,256,256]{2,1,0:T(8,128)(2,1)S(1)}, bf16[2,256,256]{2...) custom-call(bf16[256,2,2,256]{3,2,1,0:T(2,128)(2,1)} %v_hbm.1, bf16[2,2,256,256]{3,2,1,0:T(8,128)(2,1)} %k_hbm.1, ...), custom_call_target="tpu_custom_call" | custom-call | tf_op jit(solution)/shard_map/pallas_call | solution.py:20
  1.5 0.6 %collective-permute-start = (bf16[512,256]{1,0:T(8,128)(2,1)S(1)}, bf16[512,256]{1,0:T(8,128)(2,1)S(1)}, u32[]{:S(2)}, u32[]{:S(2)}) collective-permute-start(bf16[512,256]{1,0:T(8,128)(2,1)S(1)} %get-tuple-element.24), channel_id=1, source_target_pairs={{0,1},{1,0},{2,3},{3,2},{4,5},{5,4},{6,7},{7,6},{8,9},{9,8},{10,11... | collective-permute-start | bytes 786440 | tf_op jit(solution)/shard_map/ppermute | solution.py:387
  2.1 0.4 shard_map.47.own_ref
  2.5 0.8 %collective-permute-done.got_ref = bf16[512,256]{1,0:T(8,128)(2,1)S(1)} collective-permute-done((bf16[512,256]{1,0:T(8,128)(2,1)S(1)}, bf16[512,256]{1,0:T(8,128)(2,1)S(1)}, u32[]{:S(2)}, u32[]{:S(2)}) %collective-permute-start) | collective-permute-done | bytes 262176 | tf_op jit(solution)/shard_map/ppermute | solution.py:387
  3.3 0.1 shard_map.48
  3.3 2.7 %collective-permute-start.1 = (bf16[128,256]{1,0:T(8,128)(2,1)S(1)}, bf16[128,256]{1,0:T(8,128)(2,1)S(1)}, u32[]{:S(2)}, u32[]{:S(2)}) collective-permute-start(bf16[128,256]{1,0:T(8,128)(2,1)S(1)} %get-tuple-element.27), channel_id=1, source_target_pairs={{0,3},{1,2},{2,1},{3,0},{4,7},{5,6},{6,5},{7,4},{8,11},{9,10},{10,... | collective-permute-start | bytes 196616 | tf_op jit(solution)/shard_map/ppermute | solution.py:353
  6.0 1.5 %collective-permute-start.2 = (bf16[128,256]{1,0:T(8,128)(2,1)S(1)}, bf16[128,256]{1,0:T(8,128)(2,1)S(1)}, u32[]{:S(2)}, u32[]{:S(2)}) collective-permute-start(bf16[128,256]{1,0:T(8,128)(2,1)S(1)} %get-tuple-element.28), channel_id=1, source_target_pairs={{0,5},{1,4},{2,7},{3,6},{4,1},{5,0},{6,3},{7,2},{8,13},{9,12},{10,... | collective-permute-start | bytes 196616 | tf_op jit(solution)/shard_map/ppermute | solution.py:353
  7.5 0.0 collective-permute-start.3
  7.5 2.0 %collective-permute-start.8 = (bf16[2,256,256]{2,1,0:T(8,128)(2,1)S(1)}, bf16[2,256,256]{2,1,0:T(8,128)(2,1)S(1)}, u32[]{:S(2)}, u32[]{:S(2)}) collective-permute-start(bf16[2,256,256]{2,1,0:T(8,128)(2,1)S(1)} %get-tuple-element.34.other_ref.k_ref), channel_id=1, source_target_pairs={{0,8},{8,0},{16,24},{24,16},{1,9},{9,1},{17,25},{25,17},{2,10},{10... | collective-permute-start | bytes 786440 | tf_op jit(solution)/shard_map/ppermute | solution.py:388
  9.5 0.0 collective-permute-start.12
  9.6 0.0 collective-permute-done.1.refs_0_
  9.6 0.2 collective-permute-done.2.refs_1_
  9.8 2.8 %collective-permute-done.3.refs_2_ = bf16[128,256]{1,0:T(8,128)(2,1)S(1)} collective-permute-done((bf16[128,256]{1,0:T(8,128)(2,1)S(1)}, bf16[128,256]{1,0:T(8,128)(2,1)S(1)}, u32[]{:S(2)}, u32[]{:S(2)}) %collective-permute-start.3) | collective-permute-done | bytes 65568 | tf_op jit(solution)/shard_map/ppermute | solution.py:353
  12.7 0.2 collective-permute-start.4
  12.9 8.7 %collective-permute-done.4.got_ref = bf16[80,256]{1,0:T(8,128)(2,1)S(1)} collective-permute-done((bf16[80,256]{1,0:T(8,128)(2,1)S(1)}, bf16[80,256]{1,0:T(8,128)(2,1)S(1)}, u32[]{:S(2)}, u32[]{:S(2)}) %collective-permute-start.4) | collective-permute-done | bytes 40992 | tf_op jit(solution)/shard_map/ppermute | solution.py:356
  21.6 1.8 %collective-permute-start.5 = (bf16[128,256]{1,0:T(8,128)(2,1)S(1)}, bf16[128,256]{1,0:T(8,128)(2,1)S(1)}, u32[]{:S(2)}, u32[]{:S(2)}) collective-permute-start(bf16[128,256]{1,0:T(8,128)(2,1)S(1)} %shard_map.51.mine_ref), channel_id=1, source_target_pairs={{0,3},{1,2},{2,1},{3,0},{4,7},{5,6},{6,5},{7,4},{8,11},{9,10},{10,... | collective-permute-start | bytes 196616 | tf_op jit(solution)/shard_map/ppermute | solution.py:358
  23.4 0.9 %collective-permute-start.6 = (bf16[128,256]{1,0:T(8,128)(2,1)S(1)}, bf16[128,256]{1,0:T(8,128)(2,1)S(1)}, u32[]{:S(2)}, u32[]{:S(2)}) collective-permute-start(bf16[128,256]{1,0:T(8,128)(2,1)S(1)} %shard_map.51.mine_ref), channel_id=1, source_target_pairs={{0,5},{1,4},{2,7},{3,6},{4,1},{5,0},{6,3},{7,2},{8,13},{9,12},{10,... | collective-permute-start | bytes 196616 | tf_op jit(solution)/shard_map/ppermute | solution.py:358
  24.4 0.6 %collective-permute-start.7 = (bf16[128,256]{1,0:T(8,128)(2,1)S(1)}, bf16[128,256]{1,0:T(8,128)(2,1)S(1)}, u32[]{:S(2)}, u32[]{:S(2)}) collective-permute-start(bf16[128,256]{1,0:T(8,128)(2,1)S(1)} %shard_map.51.mine_ref), channel_id=1, source_target_pairs={{0,6},{1,7},{2,4},{3,5},{4,2},{5,3},{6,0},{7,1},{8,14},{9,15},{10,... | collective-permute-start | bytes 196616 | tf_op jit(solution)/shard_map/ppermute | solution.py:358
  25.0 0.4 collective-permute-done.5.refs_0_
  25.4 2.3 %collective-permute-done.6.refs_1_ = bf16[128,256]{1,0:T(8,128)(2,1)S(1)} collective-permute-done((bf16[128,256]{1,0:T(8,128)(2,1)S(1)}, bf16[128,256]{1,0:T(8,128)(2,1)S(1)}, u32[]{:S(2)}, u32[]{:S(2)}) %collective-permute-start.6) | collective-permute-done | bytes 65568 | tf_op jit(solution)/shard_map/ppermute | solution.py:358
  27.8 2.2 %collective-permute-done.7.refs_2_ = bf16[128,256]{1,0:T(8,128)(2,1)S(1)} collective-permute-done((bf16[128,256]{1,0:T(8,128)(2,1)S(1)}, bf16[128,256]{1,0:T(8,128)(2,1)S(1)}, u32[]{:S(2)}, u32[]{:S(2)}) %collective-permute-start.7) | collective-permute-done | bytes 65568 | tf_op jit(solution)/shard_map/ppermute | solution.py:358
  30.0 0.1 collective-permute-start.13
  30.1 0.2 shard_map.53
  30.3 3.7 %collective-permute-start.9 = (bf16[8,1024]{1,0:T(8,128)(2,1)S(1)}, bf16[8,1024]{1,0:T(8,128)(2,1)S(1)}, u32[]{:S(2)}, u32[]{:S(2)}) collective-permute-start(bf16[8,1024]{1,0:T(8,128)(2,1)S(1)} %shard_map.53), channel_id=1, source_target_pairs={{8,16},{24,0},{0,24},{16,8},{9,17},{25,1},{1,25},{17,9},{10,18},{2... | collective-permute-start | bytes 49160 | tf_op jit(solution)/shard_map/ppermute | solution.py:395
  34.0 1.9 %collective-permute-done.9.near_ref = bf16[8,1024]{1,0:T(8,128)(2,1)S(1)} collective-permute-done((bf16[8,1024]{1,0:T(8,128)(2,1)S(1)}, bf16[8,1024]{1,0:T(8,128)(2,1)S(1)}, u32[]{:S(2)}, u32[]{:S(2)}) %collective-permute-start.9) | collective-permute-done | bytes 16416 | tf_op jit(solution)/shard_map/ppermute | solution.py:395
  35.9 0.0 collective-permute-start.10
  35.9 3.7 %collective-permute-done.10.far_ref = bf16[8,1024]{1,0:T(8,128)(2,1)S(1)} collective-permute-done((bf16[8,1024]{1,0:T(8,128)(2,1)S(1)}, bf16[8,1024]{1,0:T(8,128)(2,1)S(1)}, u32[]{:S(2)}, u32[]{:S(2)}) %collective-permute-start.10) | collective-permute-done | bytes 16416 | tf_op jit(solution)/shard_map/ppermute | solution.py:396
  39.6 0.0 collective-permute-done.8.mate_ref
  39.6 0.6 %shard_map.54.k_ref = bf16[2,512,256]{2,1,0:T(8,128)(2,1)S(1)} custom-call(bf16[2,256,256]{2,1,0:T(8,128)(2,1)S(1)} %get-tuple-element.23.k_ref.mine_ref, bf16[2,256,256]{2,1,0:T(8,128)(2,1)S(1)} %collective-permute-done.8.mate_ref, f32[1,256]{1,0:T(1,128)S(1)} %get-tuple-element.26.d_ref, bf16[80,256]{1,0:T(8,128)(2,1)S(1)} %collective-permute-done.4.got_ref, ...), custom_call_target="tpu_custom_call" | custom-call | tf_op jit(solution)/shard_map/pallas_call | solution.py:20
  40.3 0.0 collective-permute-done.12.mate_ref
  40.3 0.6 %shard_map.56.k_ref = bf16[2,512,256]{2,1,0:T(8,128)(2,1)S(1)} custom-call(bf16[2,256,256]{2,1,0:T(8,128)(2,1)S(1)} %get-tuple-element.34.other_ref.k_ref, bf16[2,256,256]{2,1,0:T(8,128)(2,1)S(1)} %collective-permute-done.12.mate_ref, f32[1,256]{1,0:T(1,128)S(1)} %get-tuple-element.26.d_ref, bf16[80,256]{1,0:T(8,128)(2,1)S(1)} %collective-permute-done.4.got_ref, ...), custom_call_target="tpu_custom_call" | custom-call | tf_op jit(solution)/shard_map/pallas_call | solution.py:20
  40.9 0.1 collective-permute-start.11
  41.0 0.3 shard_map.55
  41.3 0.0 collective-permute-done.13.away_ref
  41.3 0.2 shard_map.58
  41.6 3.7 %collective-permute-start.14 = (bf16[256,256]{1,0:T(8,128)(2,1)S(1)}, bf16[256,256]{1,0:T(8,128)(2,1)S(1)}, u32[]{:S(2)}, u32[]{:S(2)}) collective-permute-start(bf16[256,256]{1,0:T(8,128)(2,1)S(1)} %shard_map.58), channel_id=1, source_target_pairs={{0,24},{8,16},{16,8},{24,0},{1,25},{9,17},{17,9},{25,1},{2,26},{10... | collective-permute-start | bytes 393224 | tf_op jit(solution)/shard_map/ppermute | solution.py:414
  45.3 0.0 collective-permute-done.11.stay_ref
  45.3 0.2 shard_map.57.other_ref
  45.5 4.0 %collective-permute-done.14.refs_0_ = bf16[256,256]{1,0:T(8,128)(2,1)S(1)} collective-permute-done((bf16[256,256]{1,0:T(8,128)(2,1)S(1)}, bf16[256,256]{1,0:T(8,128)(2,1)S(1)}, u32[]{:S(2)}, u32[]{:S(2)}) %collective-permute-start.14) | collective-permute-done | bytes 131104 | tf_op jit(solution)/shard_map/ppermute | solution.py:414
  49.5 0.2 shard_map.59
  49.7 0.7 %copy.5 = f32[64,2,2,256]{3,2,1,0:T(2,128)} copy(f32[64,2,2,256]{3,2,1,0:T(2,128)S(1)} %shard_map.59) | data formatting | bytes 524288
  (4 shorter events, 0.1 us)
Async XLA Ops:
  1.5 1.7 %collective-permute-start = (bf16[512,256]{1,0:T(8,128)(2,1)S(1)}, bf16[512,256]{1,0:T(8,128)(2,1)S(1)}, u32[]{:S(2)}, u32[]{:S(2)}) collective-permute-start(bf16[512,256]{1,0:T(8,128)(2,1)S(1)} %get-tuple-element.24), channel_id=1, source_target_pairs={{0,1},{1,0},{2,3},{3,2},{4,5},{5,4},{6,7},{7,6},{8,9},{9,8},{10,11... | collective-permute-start | bytes 786440 | tf_op jit(solution)/shard_map/ppermute | solution.py:387
  3.3 6.2 %collective-permute-start.1 = (bf16[128,256]{1,0:T(8,128)(2,1)S(1)}, bf16[128,256]{1,0:T(8,128)(2,1)S(1)}, u32[]{:S(2)}, u32[]{:S(2)}) collective-permute-start(bf16[128,256]{1,0:T(8,128)(2,1)S(1)} %get-tuple-element.27), channel_id=1, source_target_pairs={{0,3},{1,2},{2,1},{3,0},{4,7},{5,6},{6,5},{7,4},{8,11},{9,10},{10,... | collective-permute-start | bytes 196616 | tf_op jit(solution)/shard_map/ppermute | solution.py:353
  6.0 3.8 %collective-permute-start.2 = (bf16[128,256]{1,0:T(8,128)(2,1)S(1)}, bf16[128,256]{1,0:T(8,128)(2,1)S(1)}, u32[]{:S(2)}, u32[]{:S(2)}) collective-permute-start(bf16[128,256]{1,0:T(8,128)(2,1)S(1)} %get-tuple-element.28), channel_id=1, source_target_pairs={{0,5},{1,4},{2,7},{3,6},{4,1},{5,0},{6,3},{7,2},{8,13},{9,12},{10,... | collective-permute-start | bytes 196616 | tf_op jit(solution)/shard_map/ppermute | solution.py:353
  7.5 5.2 %collective-permute-start.3 = (bf16[128,256]{1,0:T(8,128)(2,1)S(1)}, bf16[128,256]{1,0:T(8,128)(2,1)S(1)}, u32[]{:S(2)}, u32[]{:S(2)}) collective-permute-start(bf16[128,256]{1,0:T(8,128)(2,1)S(1)} %get-tuple-element.29), channel_id=1, source_target_pairs={{0,6},{1,7},{2,4},{3,5},{4,2},{5,3},{6,0},{7,1},{8,14},{9,15},{10,... | collective-permute-start | bytes 196616 | tf_op jit(solution)/shard_map/ppermute | solution.py:353
  7.5 32.1 %collective-permute-start.8 = (bf16[2,256,256]{2,1,0:T(8,128)(2,1)S(1)}, bf16[2,256,256]{2,1,0:T(8,128)(2,1)S(1)}, u32[]{:S(2)}, u32[]{:S(2)}) collective-permute-start(bf16[2,256,256]{2,1,0:T(8,128)(2,1)S(1)} %get-tuple-element.34.other_ref.k_ref), channel_id=1, source_target_pairs={{0,8},{8,0},{16,24},{24,16},{1,9},{9,1},{17,25},{25,17},{2,10},{10... | collective-permute-start | bytes 786440 | tf_op jit(solution)/shard_map/ppermute | solution.py:388
  9.5 30.7 %collective-permute-start.12 = (bf16[2,256,256]{2,1,0:T(8,128)(2,1)S(1)}, bf16[2,256,256]{2,1,0:T(8,128)(2,1)S(1)}, u32[]{:S(2)}, u32[]{:S(2)}) collective-permute-start(bf16[2,256,256]{2,1,0:T(8,128)(2,1)S(1)} %get-tuple-element.23.k_ref.mine_ref), channel_id=1, source_target_pairs={{0,8},{8,0},{16,24},{24,16},{1,9},{9,1},{17,25},{25,17},{2,10},{10... | collective-permute-start | bytes 786440 | tf_op jit(solution)/shard_map/ppermute | solution.py:389
  12.7 8.9 %collective-permute-start.4 = (bf16[80,256]{1,0:T(8,128)(2,1)S(1)}, bf16[80,256]{1,0:T(8,128)(2,1)S(1)}, u32[]{:S(2)}, u32[]{:S(2)}) collective-permute-start(bf16[80,256]{1,0:T(8,128)(2,1)S(1)} %get-tuple-element.31), channel_id=1, source_target_pairs={{0,9},{1,8},{2,11},{3,10},{4,13},{5,12},{6,15},{7,14},{8,1},{9,0},... | collective-permute-start | bytes 122888 | tf_op jit(solution)/shard_map/ppermute | solution.py:356
  21.6 3.8 %collective-permute-start.5 = (bf16[128,256]{1,0:T(8,128)(2,1)S(1)}, bf16[128,256]{1,0:T(8,128)(2,1)S(1)}, u32[]{:S(2)}, u32[]{:S(2)}) collective-permute-start(bf16[128,256]{1,0:T(8,128)(2,1)S(1)} %shard_map.51.mine_ref), channel_id=1, source_target_pairs={{0,3},{1,2},{2,1},{3,0},{4,7},{5,6},{6,5},{7,4},{8,11},{9,10},{10,... | collective-permute-start | bytes 196616 | tf_op jit(solution)/shard_map/ppermute | solution.py:358
  23.4 4.3 %collective-permute-start.6 = (bf16[128,256]{1,0:T(8,128)(2,1)S(1)}, bf16[128,256]{1,0:T(8,128)(2,1)S(1)}, u32[]{:S(2)}, u32[]{:S(2)}) collective-permute-start(bf16[128,256]{1,0:T(8,128)(2,1)S(1)} %shard_map.51.mine_ref), channel_id=1, source_target_pairs={{0,5},{1,4},{2,7},{3,6},{4,1},{5,0},{6,3},{7,2},{8,13},{9,12},{10,... | collective-permute-start | bytes 196616 | tf_op jit(solution)/shard_map/ppermute | solution.py:358
  24.4 5.6 %collective-permute-start.7 = (bf16[128,256]{1,0:T(8,128)(2,1)S(1)}, bf16[128,256]{1,0:T(8,128)(2,1)S(1)}, u32[]{:S(2)}, u32[]{:S(2)}) collective-permute-start(bf16[128,256]{1,0:T(8,128)(2,1)S(1)} %shard_map.51.mine_ref), channel_id=1, source_target_pairs={{0,6},{1,7},{2,4},{3,5},{4,2},{5,3},{6,0},{7,1},{8,14},{9,15},{10,... | collective-permute-start | bytes 196616 | tf_op jit(solution)/shard_map/ppermute | solution.py:358
  30.0 11.3 %collective-permute-start.13 = (bf16[256,256]{1,0:T(8,128)(2,1)S(1)}, bf16[256,256]{1,0:T(8,128)(2,1)S(1)}, u32[]{:S(2)}, u32[]{:S(2)}) collective-permute-start(bf16[256,256]{1,0:T(8,128)(2,1)S(1)} %get-tuple-element.32.away_ref), channel_id=1, source_target_pairs={{0,1},{1,0},{2,3},{3,2},{4,5},{5,4},{6,7},{7,6},{8,9},{9,8},{10,11... | collective-permute-start | bytes 393224 | tf_op jit(solution)/shard_map/ppermute | solution.py:361
  30.3 5.6 %collective-permute-start.9 = (bf16[8,1024]{1,0:T(8,128)(2,1)S(1)}, bf16[8,1024]{1,0:T(8,128)(2,1)S(1)}, u32[]{:S(2)}, u32[]{:S(2)}) collective-permute-start(bf16[8,1024]{1,0:T(8,128)(2,1)S(1)} %shard_map.53), channel_id=1, source_target_pairs={{8,16},{24,0},{0,24},{16,8},{9,17},{25,1},{1,25},{17,9},{10,18},{2... | collective-permute-start | bytes 49160 | tf_op jit(solution)/shard_map/ppermute | solution.py:395
  35.9 3.7 %collective-permute-start.10 = (bf16[8,1024]{1,0:T(8,128)(2,1)S(1)}, bf16[8,1024]{1,0:T(8,128)(2,1)S(1)}, u32[]{:S(2)}, u32[]{:S(2)}) collective-permute-start(bf16[8,1024]{1,0:T(8,128)(2,1)S(1)} %collective-permute-done.9.near_ref), channel_id=1, source_target_pairs={{0,8},{8,0},{16,24},{24,16},{1,9},{9,1},{17,25},{25,17},{2,10},{10... | collective-permute-start | bytes 49160 | tf_op jit(solution)/shard_map/ppermute | solution.py:396
  40.9 4.4 %collective-permute-start.11 = (bf16[256,256]{1,0:T(8,128)(2,1)S(1)}, bf16[256,256]{1,0:T(8,128)(2,1)S(1)}, u32[]{:S(2)}, u32[]{:S(2)}) collective-permute-start(bf16[256,256]{1,0:T(8,128)(2,1)S(1)} %get-tuple-element.33.stay_ref), channel_id=1, source_target_pairs={{0,1},{1,0},{2,3},{3,2},{4,5},{5,4},{6,7},{7,6},{8,9},{9,8},{10,11... | collective-permute-start | bytes 393224 | tf_op jit(solution)/shard_map/ppermute | solution.py:361
  41.6 8.0 %collective-permute-start.14 = (bf16[256,256]{1,0:T(8,128)(2,1)S(1)}, bf16[256,256]{1,0:T(8,128)(2,1)S(1)}, u32[]{:S(2)}, u32[]{:S(2)}) collective-permute-start(bf16[256,256]{1,0:T(8,128)(2,1)S(1)} %shard_map.58), channel_id=1, source_target_pairs={{0,24},{8,16},{16,8},{24,0},{1,25},{9,17},{17,9},{25,1},{2,26},{10... | collective-permute-start | bytes 393224 | tf_op jit(solution)/shard_map/ppermute | solution.py:414

commit v15 on v13

--- a/solution.py
+++ b/solution.py
@@ -11,6 +11,7 @@
 BF = jnp.bfloat16
 F32 = jnp.float32
 LANES = 128
+PIECES = 2
 LIMIT = 24 * 2**20
 VMEM = pl.BlockSpec(memory_space=pltpu.VMEM)
 HBM = pl.BlockSpec(memory_space=pltpu.HBM)
@@ -91,12 +92,11 @@
         o_ref[rows:, at] = (u_ref[t, imag, :] - u_ref[tiles + t, real, :]).astype(o_ref.dtype)
 
 
-def adjoint_other_body(v_hbm, k_hbm, d_hbm, n_hbm, o_ref, v_ref, mine_ref, other_ref, d_ref, n_ref, u_ref, sems):
+def adjoint_other_body(v_hbm, k_hbm, d_hbm, n_hbm, o_ref, v_ref, other_ref, d_ref, n_ref, u_ref, sems):
     freq = 1 - parity()
     pairs = (
         (v_hbm, v_ref),
         (k_hbm.at[freq], other_ref),
-        (k_hbm.at[1 - freq], mine_ref),
         (d_hbm, d_ref),
         (n_hbm, n_ref),
     )
@@ -110,8 +110,12 @@
         copy.wait()
 
 
-def adjoint_own_body(v_ref, k_ref, o_ref, u_ref):
-    adjoint(parity(), v_ref, k_ref, o_ref, u_ref)
+def adjoint_own_body(k_hbm, v_ref, o_ref, k_ref, u_ref, sem):
+    freq = parity()
+    copy = pltpu.make_async_copy(k_hbm.at[freq], k_ref, sem)
+    copy.start()
+    copy.wait()
+    adjoint(freq, v_ref, k_ref, o_ref, u_ref)
 
 
 def lanes_of(freq, c, rows):
@@ -298,26 +302,52 @@
 
 
 def final_body(v_ref, noise_ref, own_ref, other_ref, *refs):
-    out_ref, s_ref = refs[-2:]
-    size = out_ref.shape[0]
-    rows = 4 * size
+    out_hbm, s_ref, y_ref, sems = refs[-4:]
+    size = y_ref.shape[0]
     half = 2 * size
+    step = size // PIECES
     me = lax.axis_index("row")
     freq = parity()
-    for which, keep_ref in enumerate((own_ref, other_ref)):
-        f = freq if which == 0 else 1 - freq
-        total = keep_ref[...]
-        for ref in refs[:-2]:
-            total = total + ref[part(f * half, half), :].astype(F32)
-        for t in range(s_ref.shape[0]):
-            at = slice(t * LANES, (t + 1) * LANES)
-            s_ref[t, pl.ds(2 * f, size, stride=4), :] = total[:size, at]
-            s_ref[t, pl.ds(2 * f + 1, size, stride=4), :] = total[size:, at]
-    x = v_ref[part(me * size, size)].reshape(rows, v_ref.shape[3]).astype(F32)
-    kind = lax.rem(lax.broadcasted_iota(jnp.int32, x.shape, 0), 4)
-    noise = jnp.where(kind < 2, noise_ref[0:1, :], noise_ref[1:2, :])
-    values = jnp.concatenate([s_ref[t] for t in range(s_ref.shape[0])], axis=1) + noise * x
-    out_ref[...] = values.reshape(out_ref.shape)
+    copies = []
+    for n in range(PIECES):
+        lo = n * step
+        for which, keep_ref in enumerate((own_ref, other_ref)):
+            f = freq if which == 0 else 1 - freq
+            for c in range(2):
+                at = c * size + lo
+                total = keep_ref[at:at + step]
+                for ref in refs[:-4]:
+                    total = total + ref[part(f * half + at, step), :].astype(F32)
+                for t in range(s_ref.shape[0]):
+                    s_ref[t, pl.ds(4 * lo + 2 * f + c, step, stride=4), :] = total[:, t * LANES:(t + 1) * LANES]
+        x = v_ref[part(me * size + lo, step)].reshape(4 * step, v_ref.shape[3]).astype(F32)
+        kind = lax.rem(lax.broadcasted_iota(jnp.int32, x.shape, 0), 4)
+        noise = jnp.where(kind < 2, noise_ref[0:1, :], noise_ref[1:2, :])
+        sums = [s_ref[t, 4 * lo:4 * (lo + step)] for t in range(s_ref.shape[0])]
+        values = jnp.concatenate(sums, axis=1) + noise * x
+        y_ref[lo:lo + step] = values.reshape((step,) + y_ref.shape[1:])
+        rows = pl.ds(lo, step)
+        copies.append(pltpu.make_async_copy(y_ref.at[rows], out_hbm.at[rows], sems.at[n]))
+        copies[-1].start()
+    for copy in copies:
+        copy.wait()
+
+
+def finish(ins, shape):
+    ins = [pltpu.with_memory_space_constraint(v, pltpu.VMEM) for v in ins]
+    return pl.pallas_call(
+        final_body,
+        name="final",
+        in_specs=[VMEM] * len(ins),
+        out_specs=HBM,
+        out_shape=jax.ShapeDtypeStruct(shape, F32),
+        scratch_shapes=[
+            pltpu.VMEM((shape[3] // LANES, 4 * shape[0], LANES), F32),
+            pltpu.VMEM(shape, F32),
+            pltpu.SemaphoreType.DMA((PIECES,)),
+        ],
+        compiler_params=pltpu.CompilerParams(vmem_limit_bytes=LIMIT),
+    )(*ins)
 
 
 def wide_sum(own, got, coef, blocks):
@@ -370,28 +400,33 @@
     coef = prior_diag[None, :]
     scratch = pltpu.VMEM((2 * width // LANES, 2 * count, LANES), F32)
     block = kernel.shape[1:]
-    other, probes, k_own, k_other, coef, noise = call(
+    other, probes, k_other, coef, noise = call(
         adjoint_other_body,
         (),
         [
             ((2 * count, width), BF),
             (probes.shape, BF),
             (block, BF),
-            (block, BF),
             (coef.shape, F32),
             (noise_var.shape, F32),
         ],
-        (scratch, pltpu.SemaphoreType.DMA((5,))),
+        (scratch, pltpu.SemaphoreType.DMA((4,))),
         raw=(probes, kernel, coef, noise_var),
     )
     got = lax.ppermute(other, "col", pair_perm("col", 1))
     mate_own = lax.ppermute(k_other, "row", pair_perm("row", 1))
+    own, k_own = call(
+        adjoint_own_body,
+        (probes,),
+        [((2 * count, width), F32), (block, BF)],
+        (scratch, pltpu.SemaphoreType.DMA),
+        raw=(kernel,),
+    )
     mate_other = lax.ppermute(k_own, "row", pair_perm("row", 1))
-    own = call(adjoint_own_body, (probes, k_own), [((2 * count, width), F32)], (scratch,))[0]
     seam = call(seam_body, (k_own, k_other, coef), [((8, 4 * rows), BF)])[0]
     odd = [i for i in range(blocks) if i % 2]
     even = [i for i in range(blocks) if i % 2 == 0]
-    near = [(i, i + 1) for i in odd if i + 1 < blocks] + [(i, i - 1) for i in even if i]
+    near = [(i, (i + 1) % blocks) for i in odd] + [(i, (i - 1) % blocks) for i in even]
     far = [(i, i + 2 if i + 2 < blocks else 1) for i in odd] + [(i, i - 2 if i else blocks - 2) for i in even]
     near = lax.ppermute(seam, "row", near)
     far = lax.ppermute(seam, "row", far)
@@ -414,12 +449,8 @@
     )
     got = [lax.ppermute(v, "row", pair_perm("row", cross(d + 1))) for d, v in enumerate(sends)]
     keep_other = call(predict_stay_body, (other[1], operators[1]), [(half, F32)])[0]
-    return call(
-        final_body,
-        (probes, noise, keep_own, keep_other, *got),
-        [((size,) + probes.shape[1:3] + (rows,), F32)],
-        (pltpu.VMEM((rows // LANES, 4 * size, LANES), F32),),
-    )[0]
+    shape = (size,) + probes.shape[1:3] + (rows,)
+    return finish((probes, noise, keep_own, keep_other, *got), shape)
 
 
 def solution(mesh):

time: 48.5 us -> 49.5 us (1.021)
  waiting for transfers between devices: 24.5 us -> 27.5 us
  starting transfers between devices: 18.1 us -> 15.6 us
  Pallas kernels: 4.53 us -> 6.12 us
  local copies, waits for them, and re-layouts: 0.71 us -> 0 us
    ppermute x1, starting transfers between devices: 4.42 us -> 0.01 us  [apply(): far = lax.ppermute(seam, 'row', far)]
    ppermute x1, starting transfers between devices: 0.67 us -> 3.62 us  [apply(): near = lax.ppermute(seam, 'row', near)]
    ppermute x1, waiting for transfers between devices: 0.01 us -> 1.93 us  [apply(): near = lax.ppermute(seam, 'row', near)]
    ppermute x1, starting transfers between devices: 2.47 us -> 0.97 us  [apply(): lax.ppermute(v, 'row', pair_perm('row', cross(d + 1)))]
    ppermute x1, waiting for transfers between devices: 5.13 us -> 6.54 us  [apply(): lax.ppermute(v, 'row', pair_perm('row', cross(d + 1)))]
    ppermute x1, waiting for transfers between devices: 1.8 us -> 2.71 us  [apply(): far = lax.ppermute(seam, 'row', far)]
    pallas_call x0 -> x1, Pallas kernels: none -> 0.84 us  [finish(): pl.pallas_call(final_body, name='final', in_specs=[VMEM] * len(ins), out_...]
    ppermute x1, waiting for transfers between devices: 0.78 us -> 0.01 us  [apply(): got = lax.ppermute(other, 'col', pair_perm('col', 1))]
  transfers between devices with their start and end apart: 15 -> 15, of which waited for: 9 -> 9; matrix products, arithmetic and copies ran while one was open for 0% -> 0% of each run, Pallas kernels for 6% -> 7%
where the time goes in v15:
time: 49.5 us; the launch traced here: 49.3 us
  waiting for transfers between devices  27.5 us (56%)
  starting transfers between devices  15.6 us (32%)
  Pallas kernels  6.12 us (12%)
    ppermute x1, waiting for transfers between devices, chip_sum(): give = lax.ppermute(give, ('row', 'col'), mate_perm())  8.32 us
    ppermute x1, waiting for transfers between devices, apply(): lax.ppermute(v, 'row', pair_perm('row', cross(d + 1)))  6.54 us
    pallas_call x13, Pallas kernels, call(): pl.pallas_call(body, in_specs=[HBM] * len(raw) + [VMEM] * len(ins), out_s...  5.28 us
    ppermute x3, waiting for transfers between devices, chip_sum(): lax.ppermute(mine, 'col', pair_perm('col', hop(d + 1)))  5 us
    ppermute x3, starting transfers between devices, chip_sum(): lax.ppermute(v, 'col', pair_perm('col', hop(d + 1)))  4.19 us
    ppermute x1, starting transfers between devices, apply(): near = lax.ppermute(seam, 'row', near)  3.62 us
    ppermute x3, starting transfers between devices, chip_sum(): lax.ppermute(mine, 'col', pair_perm('col', hop(d + 1)))  3.35 us
    ppermute x3, waiting for transfers between devices, chip_sum(): lax.ppermute(v, 'col', pair_perm('col', hop(d + 1)))  2.96 us
  transfers between devices with their start and end apart: 15, of which 9 were waited for; matrix products, arithmetic and copies ran while one was open for 0% of the time, Pallas kernels for 7%

profile of v15, /device:TPU:0, one launch (start us, length us, event | category | flops | bytes accessed | tf_op | source)
XLA Modules:
  0.0 49.3 jit_solution(14247424593252651839)
XLA Ops:
  0.0 1.5 %shard_map.46 = (bf16[512,256]{1,0:T(8,128)(2,1)S(1)}, bf16[256,2,2,256]{3,2,1,0:T(2,128)(2,1)S(1)}, bf16[2,256,256]{2,1,0:T(8,128)(2,1)S(1)}, f32[1,256]{1,0:T(1,128)S(1)}, f32[2,256]{1,0:T(2,128)S(1)}) custom-call(bf16[256,2,2,256]{3,2,1,0:T(2,128)(2,1)} %v_hbm.1, bf16[2,2,256,256]{3,2,1,0:T(8,128)(2,1)} %k_hbm.3, f32[1,256]{1,0:T(1,128)} %bitcast.1, ...), custom_call_target="tpu_custom_call" | custom-call | tf_op jit(solution)/shard_map/pallas_call | solution.py:21
  1.5 0.6 %collective-permute-start = (bf16[512,256]{1,0:T(8,128)(2,1)S(1)}, bf16[512,256]{1,0:T(8,128)(2,1)S(1)}, u32[]{:S(2)}, u32[]{:S(2)}) collective-permute-start(bf16[512,256]{1,0:T(8,128)(2,1)S(1)} %get-tuple-element.25), channel_id=1, source_target_pairs={{0,1},{1,0},{2,3},{3,2},{4,5},{5,4},{6,7},{7,6},{8,9},{9,8},{10,11... | collective-permute-start | bytes 786440 | tf_op jit(solution)/shard_map/ppermute | solution.py:416
  2.1 1.3 %shard_map.47 = (f32[512,256]{1,0:T(8,128)S(1)}, bf16[2,256,256]{2,1,0:T(8,128)(2,1)S(1)}) custom-call(bf16[2,2,256,256]{3,2,1,0:T(8,128)(2,1)} %k_hbm.3, bf16[256,2,2,256]{3,2,1,0:T(2,128)(2,1)S(1)} %get-tuple-element.22.v_ref), custom_call_target="tpu_custom_call" | custom-call | tf_op jit(solution)/shard_map/pallas_call | solution.py:21
  3.4 0.0 collective-permute-done.got_ref
  3.4 0.1 shard_map.48
  3.5 2.7 %collective-permute-start.1 = (bf16[128,256]{1,0:T(8,128)(2,1)S(1)}, bf16[128,256]{1,0:T(8,128)(2,1)S(1)}, u32[]{:S(2)}, u32[]{:S(2)}) collective-permute-start(bf16[128,256]{1,0:T(8,128)(2,1)S(1)} %get-tuple-element.28), channel_id=1, source_target_pairs={{0,3},{1,2},{2,1},{3,0},{4,7},{5,6},{6,5},{7,4},{8,11},{9,10},{10,... | collective-permute-start | bytes 196616 | tf_op jit(solution)/shard_map/ppermute | solution.py:383
  6.2 1.3 %collective-permute-start.2 = (bf16[128,256]{1,0:T(8,128)(2,1)S(1)}, bf16[128,256]{1,0:T(8,128)(2,1)S(1)}, u32[]{:S(2)}, u32[]{:S(2)}) collective-permute-start(bf16[128,256]{1,0:T(8,128)(2,1)S(1)} %get-tuple-element.29), channel_id=1, source_target_pairs={{0,5},{1,4},{2,7},{3,6},{4,1},{5,0},{6,3},{7,2},{8,13},{9,12},{10,... | collective-permute-start | bytes 196616 | tf_op jit(solution)/shard_map/ppermute | solution.py:383
  7.5 0.2 collective-permute-start.3
  7.7 1.8 %collective-permute-start.8 = (bf16[2,256,256]{2,1,0:T(8,128)(2,1)S(1)}, bf16[2,256,256]{2,1,0:T(8,128)(2,1)S(1)}, u32[]{:S(2)}, u32[]{:S(2)}) collective-permute-start(bf16[2,256,256]{2,1,0:T(8,128)(2,1)S(1)} %get-tuple-element.36.other_ref.k_ref), channel_id=1, source_target_pairs={{0,8},{8,0},{16,24},{24,16},{1,9},{9,1},{17,25},{25,17},{2,10},{10... | collective-permute-start | bytes 786440 | tf_op jit(solution)/shard_map/ppermute | solution.py:417
  9.5 0.2 collective-permute-start.12
  9.7 0.0 collective-permute-done.1.refs_0_
  9.7 1.3 %collective-permute-done.2.refs_1_ = bf16[128,256]{1,0:T(8,128)(2,1)S(1)} collective-permute-done((bf16[128,256]{1,0:T(8,128)(2,1)S(1)}, bf16[128,256]{1,0:T(8,128)(2,1)S(1)}, u32[]{:S(2)}, u32[]{:S(2)}) %collective-permute-start.2) | collective-permute-done | bytes 65568 | tf_op jit(solution)/shard_map/ppermute | solution.py:383
  11.0 1.7 %collective-permute-done.3.refs_2_ = bf16[128,256]{1,0:T(8,128)(2,1)S(1)} collective-permute-done((bf16[128,256]{1,0:T(8,128)(2,1)S(1)}, bf16[128,256]{1,0:T(8,128)(2,1)S(1)}, u32[]{:S(2)}, u32[]{:S(2)}) %collective-permute-start.3) | collective-permute-done | bytes 65568 | tf_op jit(solution)/shard_map/ppermute | solution.py:383
  12.7 0.1 shard_map.50
  12.8 0.7 %collective-permute-start.4 = (bf16[80,256]{1,0:T(8,128)(2,1)S(1)}, bf16[80,256]{1,0:T(8,128)(2,1)S(1)}, u32[]{:S(2)}, u32[]{:S(2)}) collective-permute-start(bf16[80,256]{1,0:T(8,128)(2,1)S(1)} %get-tuple-element.32), channel_id=1, source_target_pairs={{0,9},{1,8},{2,11},{3,10},{4,13},{5,12},{6,15},{7,14},{8,1},{9,0},... | collective-permute-start | bytes 122888 | tf_op jit(solution)/shard_map/ppermute | solution.py:386
  13.5 8.3 %collective-permute-done.4.got_ref = bf16[80,256]{1,0:T(8,128)(2,1)S(1)} collective-permute-done((bf16[80,256]{1,0:T(8,128)(2,1)S(1)}, bf16[80,256]{1,0:T(8,128)(2,1)S(1)}, u32[]{:S(2)}, u32[]{:S(2)}) %collective-permute-start.4) | collective-permute-done | bytes 40992 | tf_op jit(solution)/shard_map/ppermute | solution.py:386
  21.8 1.8 %collective-permute-start.5 = (bf16[128,256]{1,0:T(8,128)(2,1)S(1)}, bf16[128,256]{1,0:T(8,128)(2,1)S(1)}, u32[]{:S(2)}, u32[]{:S(2)}) collective-permute-start(bf16[128,256]{1,0:T(8,128)(2,1)S(1)} %shard_map.51.mine_ref), channel_id=1, source_target_pairs={{0,3},{1,2},{2,1},{3,0},{4,7},{5,6},{6,5},{7,4},{8,11},{9,10},{10,... | collective-permute-start | bytes 196616 | tf_op jit(solution)/shard_map/ppermute | solution.py:388
  23.6 0.9 %collective-permute-start.6 = (bf16[128,256]{1,0:T(8,128)(2,1)S(1)}, bf16[128,256]{1,0:T(8,128)(2,1)S(1)}, u32[]{:S(2)}, u32[]{:S(2)}) collective-permute-start(bf16[128,256]{1,0:T(8,128)(2,1)S(1)} %shard_map.51.mine_ref), channel_id=1, source_target_pairs={{0,5},{1,4},{2,7},{3,6},{4,1},{5,0},{6,3},{7,2},{8,13},{9,12},{10,... | collective-permute-start | bytes 196616 | tf_op jit(solution)/shard_map/ppermute | solution.py:388
  24.6 0.6 %collective-permute-start.7 = (bf16[128,256]{1,0:T(8,128)(2,1)S(1)}, bf16[128,256]{1,0:T(8,128)(2,1)S(1)}, u32[]{:S(2)}, u32[]{:S(2)}) collective-permute-start(bf16[128,256]{1,0:T(8,128)(2,1)S(1)} %shard_map.51.mine_ref), channel_id=1, source_target_pairs={{0,6},{1,7},{2,4},{3,5},{4,2},{5,3},{6,0},{7,1},{8,14},{9,15},{10,... | collective-permute-start | bytes 196616 | tf_op jit(solution)/shard_map/ppermute | solution.py:388
  25.2 0.4 collective-permute-done.5.refs_0_
  25.6 2.3 %collective-permute-done.6.refs_1_ = bf16[128,256]{1,0:T(8,128)(2,1)S(1)} collective-permute-done((bf16[128,256]{1,0:T(8,128)(2,1)S(1)}, bf16[128,256]{1,0:T(8,128)(2,1)S(1)}, u32[]{:S(2)}, u32[]{:S(2)}) %collective-permute-start.6) | collective-permute-done | bytes 65568 | tf_op jit(solution)/shard_map/ppermute | solution.py:388
  28.0 2.2 %collective-permute-done.7.refs_2_ = bf16[128,256]{1,0:T(8,128)(2,1)S(1)} collective-permute-done((bf16[128,256]{1,0:T(8,128)(2,1)S(1)}, bf16[128,256]{1,0:T(8,128)(2,1)S(1)}, u32[]{:S(2)}, u32[]{:S(2)}) %collective-permute-start.7) | collective-permute-done | bytes 65568 | tf_op jit(solution)/shard_map/ppermute | solution.py:388
  30.2 0.1 collective-permute-start.13
  30.3 0.2 shard_map.53
  30.5 3.6 %collective-permute-start.9 = (bf16[8,1024]{1,0:T(8,128)(2,1)S(1)}, bf16[8,1024]{1,0:T(8,128)(2,1)S(1)}, u32[]{:S(2)}, u32[]{:S(2)}) collective-permute-start(bf16[8,1024]{1,0:T(8,128)(2,1)S(1)} %shard_map.53), channel_id=1, source_target_pairs={{8,16},{24,0},{0,24},{16,8},{9,17},{25,1},{1,25},{17,9},{10,18},{2... | collective-permute-start | bytes 49160 | tf_op jit(solution)/shard_map/ppermute | solution.py:431
  34.2 0.0 collective-permute-start.10
  34.2 1.9 %collective-permute-done.9.near_ref = bf16[8,1024]{1,0:T(8,128)(2,1)S(1)} collective-permute-done((bf16[8,1024]{1,0:T(8,128)(2,1)S(1)}, bf16[8,1024]{1,0:T(8,128)(2,1)S(1)}, u32[]{:S(2)}, u32[]{:S(2)}) %collective-permute-start.9) | collective-permute-done | bytes 16416 | tf_op jit(solution)/shard_map/ppermute | solution.py:431
  36.1 2.7 %collective-permute-done.10.far_ref = bf16[8,1024]{1,0:T(8,128)(2,1)S(1)} collective-permute-done((bf16[8,1024]{1,0:T(8,128)(2,1)S(1)}, bf16[8,1024]{1,0:T(8,128)(2,1)S(1)}, u32[]{:S(2)}, u32[]{:S(2)}) %collective-permute-start.10) | collective-permute-done | bytes 16416 | tf_op jit(solution)/shard_map/ppermute | solution.py:432
  38.8 0.0 collective-permute-done.8.mate_ref
  38.8 0.6 %shard_map.54.k_ref = bf16[2,512,256]{2,1,0:T(8,128)(2,1)S(1)} custom-call(bf16[2,256,256]{2,1,0:T(8,128)(2,1)S(1)} %get-tuple-element.35.mine_ref.k_ref, bf16[2,256,256]{2,1,0:T(8,128)(2,1)S(1)} %collective-permute-done.8.mate_ref, f32[1,256]{1,0:T(1,128)S(1)} %get-tuple-element.27.d_ref, bf16[80,256]{1,0:T(8,128)(2,1)S(1)} %collective-permute-done.4.got_ref, ...), custom_call_target="tpu_custom_call" | custom-call | tf_op jit(solution)/shard_map/pallas_call | solution.py:21
  39.4 0.0 collective-permute-done.12.mate_ref
  39.4 0.6 %shard_map.56.k_ref = bf16[2,512,256]{2,1,0:T(8,128)(2,1)S(1)} custom-call(bf16[2,256,256]{2,1,0:T(8,128)(2,1)S(1)} %get-tuple-element.36.other_ref.k_ref, bf16[2,256,256]{2,1,0:T(8,128)(2,1)S(1)} %collective-permute-done.12.mate_ref, f32[1,256]{1,0:T(1,128)S(1)} %get-tuple-element.27.d_ref, bf16[80,256]{1,0:T(8,128)(2,1)S(1)} %collective-permute-done.4.got_ref, ...), custom_call_target="tpu_custom_call" | custom-call | tf_op jit(solution)/shard_map/pallas_call | solution.py:21
  40.0 0.1 collective-permute-start.11
  40.1 0.3 shard_map.55
  40.4 0.0 collective-permute-done.13.away_ref
  40.5 0.2 shard_map.58
  40.7 1.0 %collective-permute-start.14 = (bf16[256,256]{1,0:T(8,128)(2,1)S(1)}, bf16[256,256]{1,0:T(8,128)(2,1)S(1)}, u32[]{:S(2)}, u32[]{:S(2)}) collective-permute-start(bf16[256,256]{1,0:T(8,128)(2,1)S(1)} %shard_map.58), channel_id=1, source_target_pairs={{0,24},{8,16},{16,8},{24,0},{1,25},{9,17},{17,9},{25,1},{2,26},{10... | collective-permute-start | bytes 393224 | tf_op jit(solution)/shard_map/ppermute | solution.py:450
  41.7 0.0 collective-permute-done.11.stay_ref
  41.7 0.2 shard_map.57.other_ref
  41.9 6.5 %collective-permute-done.14.refs_0_ = bf16[256,256]{1,0:T(8,128)(2,1)S(1)} collective-permute-done((bf16[256,256]{1,0:T(8,128)(2,1)S(1)}, bf16[256,256]{1,0:T(8,128)(2,1)S(1)}, u32[]{:S(2)}, u32[]{:S(2)}) %collective-permute-start.14) | collective-permute-done | bytes 131104 | tf_op jit(solution)/shard_map/ppermute | solution.py:450
  48.5 0.8 %final.1 = f32[64,2,2,256]{3,2,1,0:T(2,128)} custom-call(bf16[256,2,2,256]{3,2,1,0:T(2,128)(2,1)S(1)} %get-tuple-element.22.v_ref, f32[2,256]{1,0:T(2,128)S(1)} %get-tuple-element.23.noise_ref, f32[128,256]{1,0:T(8,128)S(1)} %get-tuple-element.37.own_ref, f32[128,256]{1,0:T(8,128)S(1)} %shard_map.57.other_ref, ...), custom_call_target="tpu_custom_call" | custom-call | tf_op jit(solution)/shard_map/final/pallas_call | solution.py:338
  (3 shorter events, 0.0 us)
Async XLA Ops:
  1.5 1.9 %collective-permute-start = (bf16[512,256]{1,0:T(8,128)(2,1)S(1)}, bf16[512,256]{1,0:T(8,128)(2,1)S(1)}, u32[]{:S(2)}, u32[]{:S(2)}) collective-permute-start(bf16[512,256]{1,0:T(8,128)(2,1)S(1)} %get-tuple-element.25), channel_id=1, source_target_pairs={{0,1},{1,0},{2,3},{3,2},{4,5},{5,4},{6,7},{7,6},{8,9},{9,8},{10,11... | collective-permute-start | bytes 786440 | tf_op jit(solution)/shard_map/ppermute | solution.py:416
  3.5 6.2 %collective-permute-start.1 = (bf16[128,256]{1,0:T(8,128)(2,1)S(1)}, bf16[128,256]{1,0:T(8,128)(2,1)S(1)}, u32[]{:S(2)}, u32[]{:S(2)}) collective-permute-start(bf16[128,256]{1,0:T(8,128)(2,1)S(1)} %get-tuple-element.28), channel_id=1, source_target_pairs={{0,3},{1,2},{2,1},{3,0},{4,7},{5,6},{6,5},{7,4},{8,11},{9,10},{10,... | collective-permute-start | bytes 196616 | tf_op jit(solution)/shard_map/ppermute | solution.py:383
  6.2 4.9 %collective-permute-start.2 = (bf16[128,256]{1,0:T(8,128)(2,1)S(1)}, bf16[128,256]{1,0:T(8,128)(2,1)S(1)}, u32[]{:S(2)}, u32[]{:S(2)}) collective-permute-start(bf16[128,256]{1,0:T(8,128)(2,1)S(1)} %get-tuple-element.29), channel_id=1, source_target_pairs={{0,5},{1,4},{2,7},{3,6},{4,1},{5,0},{6,3},{7,2},{8,13},{9,12},{10,... | collective-permute-start | bytes 196616 | tf_op jit(solution)/shard_map/ppermute | solution.py:383
  7.5 5.2 %collective-permute-start.3 = (bf16[128,256]{1,0:T(8,128)(2,1)S(1)}, bf16[128,256]{1,0:T(8,128)(2,1)S(1)}, u32[]{:S(2)}, u32[]{:S(2)}) collective-permute-start(bf16[128,256]{1,0:T(8,128)(2,1)S(1)} %get-tuple-element.30), channel_id=1, source_target_pairs={{0,6},{1,7},{2,4},{3,5},{4,2},{5,3},{6,0},{7,1},{8,14},{9,15},{10,... | collective-permute-start | bytes 196616 | tf_op jit(solution)/shard_map/ppermute | solution.py:383
  7.7 31.1 %collective-permute-start.8 = (bf16[2,256,256]{2,1,0:T(8,128)(2,1)S(1)}, bf16[2,256,256]{2,1,0:T(8,128)(2,1)S(1)}, u32[]{:S(2)}, u32[]{:S(2)}) collective-permute-start(bf16[2,256,256]{2,1,0:T(8,128)(2,1)S(1)} %get-tuple-element.36.other_ref.k_ref), channel_id=1, source_target_pairs={{0,8},{8,0},{16,24},{24,16},{1,9},{9,1},{17,25},{25,17},{2,10},{10... | collective-permute-start | bytes 786440 | tf_op jit(solution)/shard_map/ppermute | solution.py:417
  9.5 29.9 %collective-permute-start.12 = (bf16[2,256,256]{2,1,0:T(8,128)(2,1)S(1)}, bf16[2,256,256]{2,1,0:T(8,128)(2,1)S(1)}, u32[]{:S(2)}, u32[]{:S(2)}) collective-permute-start(bf16[2,256,256]{2,1,0:T(8,128)(2,1)S(1)} %get-tuple-element.35.mine_ref.k_ref), channel_id=1, source_target_pairs={{0,8},{8,0},{16,24},{24,16},{1,9},{9,1},{17,25},{25,17},{2,10},{10... | collective-permute-start | bytes 786440 | tf_op jit(solution)/shard_map/ppermute | solution.py:425
  12.8 9.0 %collective-permute-start.4 = (bf16[80,256]{1,0:T(8,128)(2,1)S(1)}, bf16[80,256]{1,0:T(8,128)(2,1)S(1)}, u32[]{:S(2)}, u32[]{:S(2)}) collective-permute-start(bf16[80,256]{1,0:T(8,128)(2,1)S(1)} %get-tuple-element.32), channel_id=1, source_target_pairs={{0,9},{1,8},{2,11},{3,10},{4,13},{5,12},{6,15},{7,14},{8,1},{9,0},... | collective-permute-start | bytes 122888 | tf_op jit(solution)/shard_map/ppermute | solution.py:386
  21.8 3.8 %collective-permute-start.5 = (bf16[128,256]{1,0:T(8,128)(2,1)S(1)}, bf16[128,256]{1,0:T(8,128)(2,1)S(1)}, u32[]{:S(2)}, u32[]{:S(2)}) collective-permute-start(bf16[128,256]{1,0:T(8,128)(2,1)S(1)} %shard_map.51.mine_ref), channel_id=1, source_target_pairs={{0,3},{1,2},{2,1},{3,0},{4,7},{5,6},{6,5},{7,4},{8,11},{9,10},{10,... | collective-permute-start | bytes 196616 | tf_op jit(solution)/shard_map/ppermute | solution.py:388
  23.6 4.3 %collective-permute-start.6 = (bf16[128,256]{1,0:T(8,128)(2,1)S(1)}, bf16[128,256]{1,0:T(8,128)(2,1)S(1)}, u32[]{:S(2)}, u32[]{:S(2)}) collective-permute-start(bf16[128,256]{1,0:T(8,128)(2,1)S(1)} %shard_map.51.mine_ref), channel_id=1, source_target_pairs={{0,5},{1,4},{2,7},{3,6},{4,1},{5,0},{6,3},{7,2},{8,13},{9,12},{10,... | collective-permute-start | bytes 196616 | tf_op jit(solution)/shard_map/ppermute | solution.py:388
  24.6 5.6 %collective-permute-start.7 = (bf16[128,256]{1,0:T(8,128)(2,1)S(1)}, bf16[128,256]{1,0:T(8,128)(2,1)S(1)}, u32[]{:S(2)}, u32[]{:S(2)}) collective-permute-start(bf16[128,256]{1,0:T(8,128)(2,1)S(1)} %shard_map.51.mine_ref), channel_id=1, source_target_pairs={{0,6},{1,7},{2,4},{3,5},{4,2},{5,3},{6,0},{7,1},{8,14},{9,15},{10,... | collective-permute-start | bytes 196616 | tf_op jit(solution)/shard_map/ppermute | solution.py:388
  30.2 10.2 %collective-permute-start.13 = (bf16[256,256]{1,0:T(8,128)(2,1)S(1)}, bf16[256,256]{1,0:T(8,128)(2,1)S(1)}, u32[]{:S(2)}, u32[]{:S(2)}) collective-permute-start(bf16[256,256]{1,0:T(8,128)(2,1)S(1)} %get-tuple-element.33.away_ref), channel_id=1, source_target_pairs={{0,1},{1,0},{2,3},{3,2},{4,5},{5,4},{6,7},{7,6},{8,9},{9,8},{10,11... | collective-permute-start | bytes 393224 | tf_op jit(solution)/shard_map/ppermute | solution.py:391
  30.5 5.6 %collective-permute-start.9 = (bf16[8,1024]{1,0:T(8,128)(2,1)S(1)}, bf16[8,1024]{1,0:T(8,128)(2,1)S(1)}, u32[]{:S(2)}, u32[]{:S(2)}) collective-permute-start(bf16[8,1024]{1,0:T(8,128)(2,1)S(1)} %shard_map.53), channel_id=1, source_target_pairs={{8,16},{24,0},{0,24},{16,8},{9,17},{25,1},{1,25},{17,9},{10,18},{2... | collective-permute-start | bytes 49160 | tf_op jit(solution)/shard_map/ppermute | solution.py:431
  34.2 4.6 %collective-permute-start.10 = (bf16[8,1024]{1,0:T(8,128)(2,1)S(1)}, bf16[8,1024]{1,0:T(8,128)(2,1)S(1)}, u32[]{:S(2)}, u32[]{:S(2)}) collective-permute-start(bf16[8,1024]{1,0:T(8,128)(2,1)S(1)} %shard_map.53), channel_id=1, source_target_pairs={{8,24},{24,8},{0,16},{16,0},{9,25},{25,9},{1,17},{17,1},{10,26},{2... | collective-permute-start | bytes 49160 | tf_op jit(solution)/shard_map/ppermute | solution.py:432
  40.0 1.6 %collective-permute-start.11 = (bf16[256,256]{1,0:T(8,128)(2,1)S(1)}, bf16[256,256]{1,0:T(8,128)(2,1)S(1)}, u32[]{:S(2)}, u32[]{:S(2)}) collective-permute-start(bf16[256,256]{1,0:T(8,128)(2,1)S(1)} %get-tuple-element.34.stay_ref), channel_id=1, source_target_pairs={{0,1},{1,0},{2,3},{3,2},{4,5},{5,4},{6,7},{7,6},{8,9},{9,8},{10,11... | collective-permute-start | bytes 393224 | tf_op jit(solution)/shard_map/ppermute | solution.py:391
  40.7 7.8 %collective-permute-start.14 = (bf16[256,256]{1,0:T(8,128)(2,1)S(1)}, bf16[256,256]{1,0:T(8,128)(2,1)S(1)}, u32[]{:S(2)}, u32[]{:S(2)}) collective-permute-start(bf16[256,256]{1,0:T(8,128)(2,1)S(1)} %shard_map.58), channel_id=1, source_target_pairs={{0,24},{8,16},{16,8},{24,0},{1,25},{9,17},{17,9},{25,1},{2,26},{10... | collective-permute-start | bytes 393224 | tf_op jit(solution)/shard_map/ppermute | solution.py:450

commit v16 on v15

--- a/solution.py
+++ b/solution.py
@@ -11,7 +11,7 @@
 BF = jnp.bfloat16
 F32 = jnp.float32
 LANES = 128
-PIECES = 2
+PIECES = 4
 LIMIT = 24 * 2**20
 VMEM = pl.BlockSpec(memory_space=pltpu.VMEM)
 HBM = pl.BlockSpec(memory_space=pltpu.HBM)
@@ -92,11 +92,12 @@
         o_ref[rows:, at] = (u_ref[t, imag, :] - u_ref[tiles + t, real, :]).astype(o_ref.dtype)
 
 
-def adjoint_other_body(v_hbm, k_hbm, d_hbm, n_hbm, o_ref, v_ref, other_ref, d_ref, n_ref, u_ref, sems):
+def adjoint_other_body(v_hbm, k_hbm, d_hbm, n_hbm, o_ref, v_ref, mine_ref, other_ref, d_ref, n_ref, u_ref, sems):
     freq = 1 - parity()
     pairs = (
         (v_hbm, v_ref),
         (k_hbm.at[freq], other_ref),
+        (k_hbm.at[1 - freq], mine_ref),
         (d_hbm, d_ref),
         (n_hbm, n_ref),
     )
@@ -110,12 +111,8 @@
         copy.wait()
 
 
-def adjoint_own_body(k_hbm, v_ref, o_ref, k_ref, u_ref, sem):
-    freq = parity()
-    copy = pltpu.make_async_copy(k_hbm.at[freq], k_ref, sem)
-    copy.start()
-    copy.wait()
-    adjoint(freq, v_ref, k_ref, o_ref, u_ref)
+def adjoint_own_body(v_ref, k_ref, o_ref, u_ref):
+    adjoint(parity(), v_ref, k_ref, o_ref, u_ref)
 
 
 def lanes_of(freq, c, rows):
@@ -400,29 +397,24 @@
     coef = prior_diag[None, :]
     scratch = pltpu.VMEM((2 * width // LANES, 2 * count, LANES), F32)
     block = kernel.shape[1:]
-    other, probes, k_other, coef, noise = call(
+    other, probes, k_own, k_other, coef, noise = call(
         adjoint_other_body,
         (),
         [
             ((2 * count, width), BF),
             (probes.shape, BF),
             (block, BF),
+            (block, BF),
             (coef.shape, F32),
             (noise_var.shape, F32),
         ],
-        (scratch, pltpu.SemaphoreType.DMA((4,))),
+        (scratch, pltpu.SemaphoreType.DMA((5,))),
         raw=(probes, kernel, coef, noise_var),
     )
     got = lax.ppermute(other, "col", pair_perm("col", 1))
     mate_own = lax.ppermute(k_other, "row", pair_perm("row", 1))
-    own, k_own = call(
-        adjoint_own_body,
-        (probes,),
-        [((2 * count, width), F32), (block, BF)],
-        (scratch, pltpu.SemaphoreType.DMA),
-        raw=(kernel,),
-    )
     mate_other = lax.ppermute(k_own, "row", pair_perm("row", 1))
+    own = call(adjoint_own_body, (probes, k_own), [((2 * count, width), F32)], (scratch,))[0]
     seam = call(seam_body, (k_own, k_other, coef), [((8, 4 * rows), BF)])[0]
     odd = [i for i in range(blocks) if i % 2]
     even = [i for i in range(blocks) if i % 2 == 0]

time: 49.5 us -> 49.3 us (level)
  waiting for transfers between devices: 27.5 us -> 28.7 us
  Pallas kernels: 6.12 us -> 5.14 us
    pallas_call x13, Pallas kernels: 5.28 us -> 4.34 us  [call(): pl.pallas_call(body, in_specs=[HBM] * len(raw) + [VMEM] * len(ins), out_s...]
    ppermute x1, waiting for transfers between devices: 0.01 us -> 0.78 us  [apply(): got = lax.ppermute(other, 'col', pair_perm('col', 1))]
  transfers between devices with their start and end apart: 15 -> 15, of which waited for: 9 -> 10; matrix products, arithmetic and copies ran while one was open for 0% -> 0% of each run, Pallas kernels for 7% -> 6%
where the time goes in v16:
time: 49.3 us; the launch traced here: 49.1 us
  waiting for transfers between devices  28.7 us (58%)
  starting transfers between devices  15.2 us (31%)
  Pallas kernels  5.14 us (10%)
    ppermute x1, waiting for transfers between devices, chip_sum(): give = lax.ppermute(give, ('row', 'col'), mate_perm())  8.7 us
    ppermute x1, waiting for transfers between devices, apply(): lax.ppermute(v, 'row', pair_perm('row', cross(d + 1)))  6.54 us
    ppermute x3, waiting for transfers between devices, chip_sum(): lax.ppermute(mine, 'col', pair_perm('col', hop(d + 1)))  4.99 us
    pallas_call x13, Pallas kernels, call(): pl.pallas_call(body, in_specs=[HBM] * len(raw) + [VMEM] * len(ins), out_s...  4.34 us
    ppermute x3, starting transfers between devices, chip_sum(): lax.ppermute(v, 'col', pair_perm('col', hop(d + 1)))  4.19 us
    ppermute x1, starting transfers between devices, apply(): near = lax.ppermute(seam, 'row', near)  3.69 us
    ppermute x3, starting transfers between devices, chip_sum(): lax.ppermute(mine, 'col', pair_perm('col', hop(d + 1)))  3.35 us
    ppermute x3, waiting for transfers between devices, chip_sum(): lax.ppermute(v, 'col', pair_perm('col', hop(d + 1)))  3.07 us
  transfers between devices with their start and end apart: 15, of which 10 were waited for; matrix products, arithmetic and copies ran while one was open for 0% of the time, Pallas kernels for 6%

profile of v16, /device:TPU:0, one launch (start us, length us, event | category | flops | bytes accessed | tf_op | source)
XLA Modules:
  0.0 49.1 jit_solution(895429882037318556)
XLA Ops:
  0.0 1.5 %shard_map.46 = (bf16[512,256]{1,0:T(8,128)(2,1)S(1)}, bf16[256,2,2,256]{3,2,1,0:T(2,128)(2,1)S(1)}, bf16[2,256,256]{2,1,0:T(8,128)(2,1)S(1)}, bf16[2,256,256]{2...) custom-call(bf16[256,2,2,256]{3,2,1,0:T(2,128)(2,1)} %v_hbm.1, bf16[2,2,256,256]{3,2,1,0:T(8,128)(2,1)} %k_hbm.1, ...), custom_call_target="tpu_custom_call" | custom-call | tf_op jit(solution)/shard_map/pallas_call | solution.py:21
  1.5 0.6 %collective-permute-start = (bf16[512,256]{1,0:T(8,128)(2,1)S(1)}, bf16[512,256]{1,0:T(8,128)(2,1)S(1)}, u32[]{:S(2)}, u32[]{:S(2)}) collective-permute-start(bf16[512,256]{1,0:T(8,128)(2,1)S(1)} %get-tuple-element.24), channel_id=1, source_target_pairs={{0,1},{1,0},{2,3},{3,2},{4,5},{5,4},{6,7},{7,6},{8,9},{9,8},{10,11... | collective-permute-start | bytes 786440 | tf_op jit(solution)/shard_map/ppermute | solution.py:414
  2.1 0.4 shard_map.47.own_ref
  2.5 0.8 %collective-permute-done.got_ref = bf16[512,256]{1,0:T(8,128)(2,1)S(1)} collective-permute-done((bf16[512,256]{1,0:T(8,128)(2,1)S(1)}, bf16[512,256]{1,0:T(8,128)(2,1)S(1)}, u32[]{:S(2)}, u32[]{:S(2)}) %collective-permute-start) | collective-permute-done | bytes 262176 | tf_op jit(solution)/shard_map/ppermute | solution.py:414
  3.3 0.1 shard_map.48
  3.3 2.7 %collective-permute-start.1 = (bf16[128,256]{1,0:T(8,128)(2,1)S(1)}, bf16[128,256]{1,0:T(8,128)(2,1)S(1)}, u32[]{:S(2)}, u32[]{:S(2)}) collective-permute-start(bf16[128,256]{1,0:T(8,128)(2,1)S(1)} %get-tuple-element.27), channel_id=1, source_target_pairs={{0,3},{1,2},{2,1},{3,0},{4,7},{5,6},{6,5},{7,4},{8,11},{9,10},{10,... | collective-permute-start | bytes 196616 | tf_op jit(solution)/shard_map/ppermute | solution.py:380
  6.0 1.5 %collective-permute-start.2 = (bf16[128,256]{1,0:T(8,128)(2,1)S(1)}, bf16[128,256]{1,0:T(8,128)(2,1)S(1)}, u32[]{:S(2)}, u32[]{:S(2)}) collective-permute-start(bf16[128,256]{1,0:T(8,128)(2,1)S(1)} %get-tuple-element.28), channel_id=1, source_target_pairs={{0,5},{1,4},{2,7},{3,6},{4,1},{5,0},{6,3},{7,2},{8,13},{9,12},{10,... | collective-permute-start | bytes 196616 | tf_op jit(solution)/shard_map/ppermute | solution.py:380
  7.5 0.0 collective-permute-start.3
  7.5 2.0 %collective-permute-start.8 = (bf16[2,256,256]{2,1,0:T(8,128)(2,1)S(1)}, bf16[2,256,256]{2,1,0:T(8,128)(2,1)S(1)}, u32[]{:S(2)}, u32[]{:S(2)}) collective-permute-start(bf16[2,256,256]{2,1,0:T(8,128)(2,1)S(1)} %get-tuple-element.34.other_ref.k_ref), channel_id=1, source_target_pairs={{0,8},{8,0},{16,24},{24,16},{1,9},{9,1},{17,25},{25,17},{2,10},{10... | collective-permute-start | bytes 786440 | tf_op jit(solution)/shard_map/ppermute | solution.py:415
  9.5 0.0 collective-permute-start.12
  9.6 0.0 collective-permute-done.1.refs_0_
  9.6 0.2 collective-permute-done.2.refs_1_
  9.8 2.8 %collective-permute-done.3.refs_2_ = bf16[128,256]{1,0:T(8,128)(2,1)S(1)} collective-permute-done((bf16[128,256]{1,0:T(8,128)(2,1)S(1)}, bf16[128,256]{1,0:T(8,128)(2,1)S(1)}, u32[]{:S(2)}, u32[]{:S(2)}) %collective-permute-start.3) | collective-permute-done | bytes 65568 | tf_op jit(solution)/shard_map/ppermute | solution.py:380
  12.7 0.2 collective-permute-start.4
  12.9 8.7 %collective-permute-done.4.got_ref = bf16[80,256]{1,0:T(8,128)(2,1)S(1)} collective-permute-done((bf16[80,256]{1,0:T(8,128)(2,1)S(1)}, bf16[80,256]{1,0:T(8,128)(2,1)S(1)}, u32[]{:S(2)}, u32[]{:S(2)}) %collective-permute-start.4) | collective-permute-done | bytes 40992 | tf_op jit(solution)/shard_map/ppermute | solution.py:383
  21.6 1.8 %collective-permute-start.5 = (bf16[128,256]{1,0:T(8,128)(2,1)S(1)}, bf16[128,256]{1,0:T(8,128)(2,1)S(1)}, u32[]{:S(2)}, u32[]{:S(2)}) collective-permute-start(bf16[128,256]{1,0:T(8,128)(2,1)S(1)} %shard_map.51.mine_ref), channel_id=1, source_target_pairs={{0,3},{1,2},{2,1},{3,0},{4,7},{5,6},{6,5},{7,4},{8,11},{9,10},{10,... | collective-permute-start | bytes 196616 | tf_op jit(solution)/shard_map/ppermute | solution.py:385
  23.4 0.9 %collective-permute-start.6 = (bf16[128,256]{1,0:T(8,128)(2,1)S(1)}, bf16[128,256]{1,0:T(8,128)(2,1)S(1)}, u32[]{:S(2)}, u32[]{:S(2)}) collective-permute-start(bf16[128,256]{1,0:T(8,128)(2,1)S(1)} %shard_map.51.mine_ref), channel_id=1, source_target_pairs={{0,5},{1,4},{2,7},{3,6},{4,1},{5,0},{6,3},{7,2},{8,13},{9,12},{10,... | collective-permute-start | bytes 196616 | tf_op jit(solution)/shard_map/ppermute | solution.py:385
  24.4 0.6 %collective-permute-start.7 = (bf16[128,256]{1,0:T(8,128)(2,1)S(1)}, bf16[128,256]{1,0:T(8,128)(2,1)S(1)}, u32[]{:S(2)}, u32[]{:S(2)}) collective-permute-start(bf16[128,256]{1,0:T(8,128)(2,1)S(1)} %shard_map.51.mine_ref), channel_id=1, source_target_pairs={{0,6},{1,7},{2,4},{3,5},{4,2},{5,3},{6,0},{7,1},{8,14},{9,15},{10,... | collective-permute-start | bytes 196616 | tf_op jit(solution)/shard_map/ppermute | solution.py:385
  25.0 0.4 collective-permute-done.5.refs_0_
  25.4 2.3 %collective-permute-done.6.refs_1_ = bf16[128,256]{1,0:T(8,128)(2,1)S(1)} collective-permute-done((bf16[128,256]{1,0:T(8,128)(2,1)S(1)}, bf16[128,256]{1,0:T(8,128)(2,1)S(1)}, u32[]{:S(2)}, u32[]{:S(2)}) %collective-permute-start.6) | collective-permute-done | bytes 65568 | tf_op jit(solution)/shard_map/ppermute | solution.py:385
  27.8 2.2 %collective-permute-done.7.refs_2_ = bf16[128,256]{1,0:T(8,128)(2,1)S(1)} collective-permute-done((bf16[128,256]{1,0:T(8,128)(2,1)S(1)}, bf16[128,256]{1,0:T(8,128)(2,1)S(1)}, u32[]{:S(2)}, u32[]{:S(2)}) %collective-permute-start.7) | collective-permute-done | bytes 65568 | tf_op jit(solution)/shard_map/ppermute | solution.py:385
  30.0 0.1 collective-permute-start.13
  30.1 0.2 shard_map.53
  30.3 3.7 %collective-permute-start.9 = (bf16[8,1024]{1,0:T(8,128)(2,1)S(1)}, bf16[8,1024]{1,0:T(8,128)(2,1)S(1)}, u32[]{:S(2)}, u32[]{:S(2)}) collective-permute-start(bf16[8,1024]{1,0:T(8,128)(2,1)S(1)} %shard_map.53), channel_id=1, source_target_pairs={{8,16},{24,0},{0,24},{16,8},{9,17},{25,1},{1,25},{17,9},{10,18},{2... | collective-permute-start | bytes 49160 | tf_op jit(solution)/shard_map/ppermute | solution.py:423
  34.0 0.0 collective-permute-start.10
  34.0 1.9 %collective-permute-done.9.near_ref = bf16[8,1024]{1,0:T(8,128)(2,1)S(1)} collective-permute-done((bf16[8,1024]{1,0:T(8,128)(2,1)S(1)}, bf16[8,1024]{1,0:T(8,128)(2,1)S(1)}, u32[]{:S(2)}, u32[]{:S(2)}) %collective-permute-start.9) | collective-permute-done | bytes 16416 | tf_op jit(solution)/shard_map/ppermute | solution.py:423
  35.9 2.8 %collective-permute-done.10.far_ref = bf16[8,1024]{1,0:T(8,128)(2,1)S(1)} collective-permute-done((bf16[8,1024]{1,0:T(8,128)(2,1)S(1)}, bf16[8,1024]{1,0:T(8,128)(2,1)S(1)}, u32[]{:S(2)}, u32[]{:S(2)}) %collective-permute-start.10) | collective-permute-done | bytes 16416 | tf_op jit(solution)/shard_map/ppermute | solution.py:424
  38.7 0.0 collective-permute-done.8.mate_ref
  38.7 0.6 %shard_map.54.k_ref = bf16[2,512,256]{2,1,0:T(8,128)(2,1)S(1)} custom-call(bf16[2,256,256]{2,1,0:T(8,128)(2,1)S(1)} %get-tuple-element.23.k_ref.mine_ref, bf16[2,256,256]{2,1,0:T(8,128)(2,1)S(1)} %collective-permute-done.8.mate_ref, f32[1,256]{1,0:T(1,128)S(1)} %get-tuple-element.26.d_ref, bf16[80,256]{1,0:T(8,128)(2,1)S(1)} %collective-permute-done.4.got_ref, ...), custom_call_target="tpu_custom_call" | custom-call | tf_op jit(solution)/shard_map/pallas_call | solution.py:21
  39.3 0.0 collective-permute-done.12.mate_ref
  39.3 0.6 %shard_map.56.k_ref = bf16[2,512,256]{2,1,0:T(8,128)(2,1)S(1)} custom-call(bf16[2,256,256]{2,1,0:T(8,128)(2,1)S(1)} %get-tuple-element.34.other_ref.k_ref, bf16[2,256,256]{2,1,0:T(8,128)(2,1)S(1)} %collective-permute-done.12.mate_ref, f32[1,256]{1,0:T(1,128)S(1)} %get-tuple-element.26.d_ref, bf16[80,256]{1,0:T(8,128)(2,1)S(1)} %collective-permute-done.4.got_ref, ...), custom_call_target="tpu_custom_call" | custom-call | tf_op jit(solution)/shard_map/pallas_call | solution.py:21
  39.9 0.1 collective-permute-start.11
  40.0 0.3 shard_map.55
  40.3 0.0 collective-permute-done.13.away_ref
  40.3 0.2 shard_map.58
  40.6 1.0 %collective-permute-start.14 = (bf16[256,256]{1,0:T(8,128)(2,1)S(1)}, bf16[256,256]{1,0:T(8,128)(2,1)S(1)}, u32[]{:S(2)}, u32[]{:S(2)}) collective-permute-start(bf16[256,256]{1,0:T(8,128)(2,1)S(1)} %shard_map.58), channel_id=1, source_target_pairs={{0,24},{8,16},{16,8},{24,0},{1,25},{9,17},{17,9},{25,1},{2,26},{10... | collective-permute-start | bytes 393224 | tf_op jit(solution)/shard_map/ppermute | solution.py:442
  41.6 0.0 collective-permute-done.11.stay_ref
  41.6 0.2 shard_map.57.other_ref
  41.8 6.5 %collective-permute-done.14.refs_0_ = bf16[256,256]{1,0:T(8,128)(2,1)S(1)} collective-permute-done((bf16[256,256]{1,0:T(8,128)(2,1)S(1)}, bf16[256,256]{1,0:T(8,128)(2,1)S(1)}, u32[]{:S(2)}, u32[]{:S(2)}) %collective-permute-start.14) | collective-permute-done | bytes 131104 | tf_op jit(solution)/shard_map/ppermute | solution.py:442
  48.3 0.8 %final.1 = f32[64,2,2,256]{3,2,1,0:T(2,128)} custom-call(bf16[256,2,2,256]{3,2,1,0:T(2,128)(2,1)S(1)} %get-tuple-element.21.v_ref, f32[2,256]{1,0:T(2,128)S(1)} %get-tuple-element.22.noise_ref, f32[128,256]{1,0:T(8,128)S(1)} %get-tuple-element.35.own_ref, f32[128,256]{1,0:T(8,128)S(1)} %shard_map.57.other_ref, ...), custom_call_target="tpu_custom_call" | custom-call | tf_op jit(solution)/shard_map/final/pallas_call | solution.py:335
  (4 shorter events, 0.1 us)
Async XLA Ops:
  1.5 1.7 %collective-permute-start = (bf16[512,256]{1,0:T(8,128)(2,1)S(1)}, bf16[512,256]{1,0:T(8,128)(2,1)S(1)}, u32[]{:S(2)}, u32[]{:S(2)}) collective-permute-start(bf16[512,256]{1,0:T(8,128)(2,1)S(1)} %get-tuple-element.24), channel_id=1, source_target_pairs={{0,1},{1,0},{2,3},{3,2},{4,5},{5,4},{6,7},{7,6},{8,9},{9,8},{10,11... | collective-permute-start | bytes 786440 | tf_op jit(solution)/shard_map/ppermute | solution.py:414
  3.3 6.2 %collective-permute-start.1 = (bf16[128,256]{1,0:T(8,128)(2,1)S(1)}, bf16[128,256]{1,0:T(8,128)(2,1)S(1)}, u32[]{:S(2)}, u32[]{:S(2)}) collective-permute-start(bf16[128,256]{1,0:T(8,128)(2,1)S(1)} %get-tuple-element.27), channel_id=1, source_target_pairs={{0,3},{1,2},{2,1},{3,0},{4,7},{5,6},{6,5},{7,4},{8,11},{9,10},{10,... | collective-permute-start | bytes 196616 | tf_op jit(solution)/shard_map/ppermute | solution.py:380
  6.0 3.8 %collective-permute-start.2 = (bf16[128,256]{1,0:T(8,128)(2,1)S(1)}, bf16[128,256]{1,0:T(8,128)(2,1)S(1)}, u32[]{:S(2)}, u32[]{:S(2)}) collective-permute-start(bf16[128,256]{1,0:T(8,128)(2,1)S(1)} %get-tuple-element.28), channel_id=1, source_target_pairs={{0,5},{1,4},{2,7},{3,6},{4,1},{5,0},{6,3},{7,2},{8,13},{9,12},{10,... | collective-permute-start | bytes 196616 | tf_op jit(solution)/shard_map/ppermute | solution.py:380
  7.5 5.2 %collective-permute-start.3 = (bf16[128,256]{1,0:T(8,128)(2,1)S(1)}, bf16[128,256]{1,0:T(8,128)(2,1)S(1)}, u32[]{:S(2)}, u32[]{:S(2)}) collective-permute-start(bf16[128,256]{1,0:T(8,128)(2,1)S(1)} %get-tuple-element.29), channel_id=1, source_target_pairs={{0,6},{1,7},{2,4},{3,5},{4,2},{5,3},{6,0},{7,1},{8,14},{9,15},{10,... | collective-permute-start | bytes 196616 | tf_op jit(solution)/shard_map/ppermute | solution.py:380
  7.5 31.1 %collective-permute-start.8 = (bf16[2,256,256]{2,1,0:T(8,128)(2,1)S(1)}, bf16[2,256,256]{2,1,0:T(8,128)(2,1)S(1)}, u32[]{:S(2)}, u32[]{:S(2)}) collective-permute-start(bf16[2,256,256]{2,1,0:T(8,128)(2,1)S(1)} %get-tuple-element.34.other_ref.k_ref), channel_id=1, source_target_pairs={{0,8},{8,0},{16,24},{24,16},{1,9},{9,1},{17,25},{25,17},{2,10},{10... | collective-permute-start | bytes 786440 | tf_op jit(solution)/shard_map/ppermute | solution.py:415
  9.5 29.8 %collective-permute-start.12 = (bf16[2,256,256]{2,1,0:T(8,128)(2,1)S(1)}, bf16[2,256,256]{2,1,0:T(8,128)(2,1)S(1)}, u32[]{:S(2)}, u32[]{:S(2)}) collective-permute-start(bf16[2,256,256]{2,1,0:T(8,128)(2,1)S(1)} %get-tuple-element.23.k_ref.mine_ref), channel_id=1, source_target_pairs={{0,8},{8,0},{16,24},{24,16},{1,9},{9,1},{17,25},{25,17},{2,10},{10... | collective-permute-start | bytes 786440 | tf_op jit(solution)/shard_map/ppermute | solution.py:416
  12.7 8.9 %collective-permute-start.4 = (bf16[80,256]{1,0:T(8,128)(2,1)S(1)}, bf16[80,256]{1,0:T(8,128)(2,1)S(1)}, u32[]{:S(2)}, u32[]{:S(2)}) collective-permute-start(bf16[80,256]{1,0:T(8,128)(2,1)S(1)} %get-tuple-element.31), channel_id=1, source_target_pairs={{0,9},{1,8},{2,11},{3,10},{4,13},{5,12},{6,15},{7,14},{8,1},{9,0},... | collective-permute-start | bytes 122888 | tf_op jit(solution)/shard_map/ppermute | solution.py:383
  21.6 3.8 %collective-permute-start.5 = (bf16[128,256]{1,0:T(8,128)(2,1)S(1)}, bf16[128,256]{1,0:T(8,128)(2,1)S(1)}, u32[]{:S(2)}, u32[]{:S(2)}) collective-permute-start(bf16[128,256]{1,0:T(8,128)(2,1)S(1)} %shard_map.51.mine_ref), channel_id=1, source_target_pairs={{0,3},{1,2},{2,1},{3,0},{4,7},{5,6},{6,5},{7,4},{8,11},{9,10},{10,... | collective-permute-start | bytes 196616 | tf_op jit(solution)/shard_map/ppermute | solution.py:385
  23.4 4.3 %collective-permute-start.6 = (bf16[128,256]{1,0:T(8,128)(2,1)S(1)}, bf16[128,256]{1,0:T(8,128)(2,1)S(1)}, u32[]{:S(2)}, u32[]{:S(2)}) collective-permute-start(bf16[128,256]{1,0:T(8,128)(2,1)S(1)} %shard_map.51.mine_ref), channel_id=1, source_target_pairs={{0,5},{1,4},{2,7},{3,6},{4,1},{5,0},{6,3},{7,2},{8,13},{9,12},{10,... | collective-permute-start | bytes 196616 | tf_op jit(solution)/shard_map/ppermute | solution.py:385
  24.4 5.6 %collective-permute-start.7 = (bf16[128,256]{1,0:T(8,128)(2,1)S(1)}, bf16[128,256]{1,0:T(8,128)(2,1)S(1)}, u32[]{:S(2)}, u32[]{:S(2)}) collective-permute-start(bf16[128,256]{1,0:T(8,128)(2,1)S(1)} %shard_map.51.mine_ref), channel_id=1, source_target_pairs={{0,6},{1,7},{2,4},{3,5},{4,2},{5,3},{6,0},{7,1},{8,14},{9,15},{10,... | collective-permute-start | bytes 196616 | tf_op jit(solution)/shard_map/ppermute | solution.py:385
  30.0 10.3 %collective-permute-start.13 = (bf16[256,256]{1,0:T(8,128)(2,1)S(1)}, bf16[256,256]{1,0:T(8,128)(2,1)S(1)}, u32[]{:S(2)}, u32[]{:S(2)}) collective-permute-start(bf16[256,256]{1,0:T(8,128)(2,1)S(1)} %get-tuple-element.32.away_ref), channel_id=1, source_target_pairs={{0,1},{1,0},{2,3},{3,2},{4,5},{5,4},{6,7},{7,6},{8,9},{9,8},{10,11... | collective-permute-start | bytes 393224 | tf_op jit(solution)/shard_map/ppermute | solution.py:388
  30.3 5.6 %collective-permute-start.9 = (bf16[8,1024]{1,0:T(8,128)(2,1)S(1)}, bf16[8,1024]{1,0:T(8,128)(2,1)S(1)}, u32[]{:S(2)}, u32[]{:S(2)}) collective-permute-start(bf16[8,1024]{1,0:T(8,128)(2,1)S(1)} %shard_map.53), channel_id=1, source_target_pairs={{8,16},{24,0},{0,24},{16,8},{9,17},{25,1},{1,25},{17,9},{10,18},{2... | collective-permute-start | bytes 49160 | tf_op jit(solution)/shard_map/ppermute | solution.py:423
  34.0 4.6 %collective-permute-start.10 = (bf16[8,1024]{1,0:T(8,128)(2,1)S(1)}, bf16[8,1024]{1,0:T(8,128)(2,1)S(1)}, u32[]{:S(2)}, u32[]{:S(2)}) collective-permute-start(bf16[8,1024]{1,0:T(8,128)(2,1)S(1)} %shard_map.53), channel_id=1, source_target_pairs={{8,24},{24,8},{0,16},{16,0},{9,25},{25,9},{1,17},{17,1},{10,26},{2... | collective-permute-start | bytes 49160 | tf_op jit(solution)/shard_map/ppermute | solution.py:424
  39.9 1.6 %collective-permute-start.11 = (bf16[256,256]{1,0:T(8,128)(2,1)S(1)}, bf16[256,256]{1,0:T(8,128)(2,1)S(1)}, u32[]{:S(2)}, u32[]{:S(2)}) collective-permute-start(bf16[256,256]{1,0:T(8,128)(2,1)S(1)} %get-tuple-element.33.stay_ref), channel_id=1, source_target_pairs={{0,1},{1,0},{2,3},{3,2},{4,5},{5,4},{6,7},{7,6},{8,9},{9,8},{10,11... | collective-permute-start | bytes 393224 | tf_op jit(solution)/shard_map/ppermute | solution.py:388
  40.6 7.8 %collective-permute-start.14 = (bf16[256,256]{1,0:T(8,128)(2,1)S(1)}, bf16[256,256]{1,0:T(8,128)(2,1)S(1)}, u32[]{:S(2)}, u32[]{:S(2)}) collective-permute-start(bf16[256,256]{1,0:T(8,128)(2,1)S(1)} %shard_map.58), channel_id=1, source_target_pairs={{0,24},{8,16},{16,8},{24,0},{1,25},{9,17},{17,9},{25,1},{2,26},{10... | collective-permute-start | bytes 393224 | tf_op jit(solution)/shard_map/ppermute | solution.py:442
